TPU v7x, 32 devices: a whole 2x2x4 slice. The times are simulated.
32 devices in a mesh: groups: 1, ctx: 8 (over z, y), head: 2 (over x), rep: 2 (over core).
Axes of the slice: x: 2, y: 2, z: 4, core: 2. Of those that a mesh axis runs over, the one named last changes fastest.
Arguments:
- queries: bfloat16 [16, 512, 4096], P(('groups', 'ctx'), 'rep', 'head'), may hold values from -6 to 6
- prefill_keys: bfloat16 [16, 512, 1024], P(('groups', 'ctx'), 'rep', 'head'), may hold values from -6 to 6
- prefill_values: bfloat16 [16, 512, 1024], P(('groups', 'ctx'), 'rep', 'head'), may hold values from -6 to 6
- context_keys: bfloat16 [16384, 1024], P(('groups', 'ctx'), 'head'), may hold values from -6 to 6
- context_values: bfloat16 [16384, 1024], P(('groups', 'ctx'), 'head'), may hold values from -6 to 6
- picks: int32 [16, 32, 3], P(('groups', 'ctx'), 'head'), may hold values from 0 to 47, as said below
Outputs:
- attended: bfloat16 [16, 512, 4096], P(('groups', 'ctx'), 'rep', 'head')
Inputs may be any that keep to these rules, and one draw needn't show every extreme that they name: `picks`: row [b, h] is increasing; its last entry is 32 + b and its first two are cache blocks. Among the first two entries of the rows of the 2 query blocks that start at a multiple of 2 and the 16 heads of one run that starts at a multiple of 16, at most 16 lie in the 4 blocks that start at one multiple of 4, and for every such set of rows some such set of blocks holds exactly 16 of them.
All inputs are finite; a program needn't handle non-finite values.
Results may differ from a plain program's by a relative error of at most 0.0055.
Values may be sent and summed in bfloat16 or wider, within the bound.
No kernel may reach another device: no remote copies, remote signals or barrier semaphores. Data moves between devices by JAX's collectives and lax.ppermute only.
A program may use at most 64 MiB of HBM per device.

v0:
```python
import jax
import jax.numpy as jnp
from jax import lax
from jax.sharding import PartitionSpec as P

HEAD_WIDTH = 128
BLOCK_TOKENS = 512


NEGATIVE = -1e30


def from_behind(value, axis, steps):
    count = lax.axis_size(axis)
    first, last = (max(0, -steps), min(count, count - steps))
    return lax.ppermute(value, axis, [(source, source + steps) for source in range(first, last)])


def partial_attention(scores, values, allowed, pattern):
    scores = jnp.where(allowed, scores, NEGATIVE)
    highest = jnp.max(scores, axis=-1, keepdims=True)
    weights = jnp.exp(scores - highest)
    totals = jnp.sum(weights, axis=-1, keepdims=True)
    mixed = jnp.einsum(
        pattern, weights.astype(jnp.bfloat16), values, preferred_element_type=jnp.float32
    )
    return (mixed / totals, highest[..., 0] + jnp.log(totals[..., 0]))


def assign_slots(chosen, blocks_here, capacity):
    flat = chosen.reshape(-1)
    holders = flat // blocks_here
    places = jnp.arange(flat.shape[0])
    earlier = jnp.sum(
        (holders[:, None] == holders[None, :]) & (places[None, :] < places[:, None]), axis=1
    )
    return (holders * capacity + earlier, flat - holders * blocks_here)


def body(queries, prefill_keys, prefill_values, context_keys, context_values, picks):
    local_count = queries.shape[0]
    stack_height = queries.shape[1]
    query_heads = queries.shape[2] // HEAD_WIDTH
    key_heads = prefill_keys.shape[2] // HEAD_WIDTH
    head_grouping = query_heads // key_heads
    blocks_here = context_keys.shape[0] // BLOCK_TOKENS
    ctx_size = lax.axis_size("ctx")
    pick_count = 2 * local_count * query_heads
    capacity = max(2, 2 * pick_count // ctx_size)
    slot_count = ctx_size * capacity
    scale = HEAD_WIDTH ** (-0.5)
    rep_index = lax.axis_index("rep")
    earlier_keys, earlier_values = from_behind((prefill_keys, prefill_values), "rep", 1)
    selected_block_keys = jnp.concatenate([earlier_keys, prefill_keys], 1).reshape(
        local_count, 2 * stack_height, key_heads, HEAD_WIDTH
    )
    selected_block_values = jnp.concatenate([earlier_values, prefill_values], 1).reshape(
        local_count, 2 * stack_height, key_heads, HEAD_WIDTH
    )
    grouped = queries.reshape(local_count, stack_height, key_heads, head_grouping, HEAD_WIDTH)
    query_place = rep_index * stack_height + jnp.arange(stack_height)
    key_place = (rep_index - 1) * stack_height + jnp.arange(2 * stack_height)
    allowed = (key_place[None, :] <= query_place[:, None]) & (key_place[None, :] >= 0)

    def own_block(paired):
        rows_here, keys_here, values_here = paired
        scores = (
            jnp.einsum("rkgd,jkd->kgrj", rows_here, keys_here, preferred_element_type=jnp.float32)
            * scale
        )
        return partial_attention(scores, values_here, allowed, "kgrj,jkd->kgrd")

    own_mixed, own_log = lax.map(own_block, (grouped, selected_block_keys, selected_block_values))
    own_mixed = own_mixed.reshape(local_count, query_heads, stack_height, HEAD_WIDTH)
    own_log = own_log.reshape(local_count, query_heads, stack_height)
    targets, local_blocks = assign_slots(picks[:, :, :2], blocks_here, capacity)
    routing = targets[:, None] == jnp.arange(slot_count)[None, :]
    sending = routing.astype(jnp.bfloat16).reshape(local_count, query_heads, 2, slot_count)
    by_head = queries.reshape(local_count, stack_height, query_heads, HEAD_WIDTH)
    outbound = jnp.einsum("qhps,qrhd->srd", sending, by_head, preferred_element_type=jnp.float32)
    outbound = outbound.astype(jnp.bfloat16).reshape(ctx_size, capacity, stack_height, HEAD_WIDTH)
    pick_heads = jnp.arange(pick_count) // 2 % query_heads // head_grouping
    key_tiles = context_keys.reshape(blocks_here, BLOCK_TOKENS, key_heads, HEAD_WIDTH)
    value_tiles = context_values.reshape(blocks_here, BLOCK_TOKENS, key_heads, HEAD_WIDTH)
    block_label = jnp.sum(jnp.where(routing, local_blocks[:, None], 0), axis=0)
    head_label = jnp.sum(jnp.where(routing, pick_heads[:, None], 0), axis=0)
    labels = jnp.stack([block_label, head_label], axis=-1).reshape(ctx_size, capacity, 2)
    inbound = lax.all_to_all(outbound, "ctx", split_axis=0, concat_axis=0, tiled=True)
    arrived = lax.all_to_all(labels, "ctx", split_axis=0, concat_axis=0, tiled=True)
    leading = inbound.shape[:2]

    def single(paired):
        rows_in, position = paired
        anchor = (position[0], 0, position[1], 0)
        keys_tile = lax.dynamic_slice(key_tiles, anchor, (1, BLOCK_TOKENS, 1, HEAD_WIDTH)).reshape(
            BLOCK_TOKENS, HEAD_WIDTH
        )
        values_tile = lax.dynamic_slice(
            value_tiles, anchor, (1, BLOCK_TOKENS, 1, HEAD_WIDTH)
        ).reshape(BLOCK_TOKENS, HEAD_WIDTH)
        scores = (
            lax.dot_general(
                rows_in, keys_tile, (((1,), (1,)), ((), ())), preferred_element_type=jnp.float32
            )
            * scale
        )
        mixed, logged = partial_attention(scores, values_tile, True, "rj,jd->rd")
        return (mixed.astype(jnp.bfloat16), logged)

    flat_rows = inbound.reshape((-1,) + inbound.shape[2:])
    flat_labels = arrived.reshape(-1, 2)
    mixed, logged = lax.map(single, (flat_rows, flat_labels), batch_size=8)
    served = mixed.reshape(leading + mixed.shape[1:])
    served_logs = logged.reshape(leading + logged.shape[1:])
    answers = lax.all_to_all(served, "ctx", split_axis=0, concat_axis=0, tiled=True)
    answer_logs = lax.all_to_all(served_logs, "ctx", split_axis=0, concat_axis=0, tiled=True)
    gathered = answers.reshape(slot_count, stack_height, HEAD_WIDTH)[targets]
    gathered_logs = answer_logs.reshape(slot_count, stack_height)[targets]
    remote_mixed = gathered.astype(jnp.float32).reshape(
        local_count, query_heads, 2, stack_height, HEAD_WIDTH
    )
    remote_logs = gathered_logs.reshape(local_count, query_heads, 2, stack_height)
    all_logs = jnp.concatenate([own_log[:, :, None], remote_logs], axis=2)
    all_mixed = jnp.concatenate([own_mixed[:, :, None], remote_mixed], axis=2)
    peak = jnp.max(all_logs, axis=2, keepdims=True)
    shares = jnp.exp(all_logs - peak)
    merged = jnp.sum(shares[..., None] * all_mixed, axis=2) / jnp.sum(shares, axis=2)[..., None]
    return (
        jnp.transpose(merged, (0, 2, 1, 3))
        .reshape(local_count, stack_height, query_heads * HEAD_WIDTH)
        .astype(jnp.bfloat16)
    )


def solution(mesh):
    return jax.shard_map(
        body,
        mesh=mesh,
        in_specs=(
            P(("groups", "ctx"), "rep", "head"),
            P(("groups", "ctx"), "rep", "head"),
            P(("groups", "ctx"), "rep", "head"),
            P(("groups", "ctx"), "head"),
            P(("groups", "ctx"), "head"),
            P(("groups", "ctx"), "head", None),
        ),
        out_specs=P(("groups", "ctx"), "rep", "head"),
        check_vma=False,
    )
```

profile of v0, /device:TPU:0, one launch (start us, length us, event | category | flops | bytes accessed | tf_op | source)
XLA Modules:
  0.0 637.1 jit_solution(9051729560354161578)
XLA Ops:
  2.0 7.3 %all-to-all-start.1 = ((s32[8,16,2]{1,2,0:T(2,128)}), s32[8,16,2]{1,2,0:T(2,128)S(1)}, u32[]{:S(2)}, u32[]{:S(2)}) async-start(s32[8,16,2]{1,2,0:T(2,128)} %copy.96), calls=%async_computation.1 | async-start | bytes 16384 | tf_op jit(solution)/shard_map/all_to_all | solution.py:89
  11.8 5.6 bitcast_convert_fusion
  17.4 8.1 %copy.94 = bf16[8,16,256,128]{3,1,2,0:T(8,128)(2,1)} copy(bf16[8,16,256,128]{3,1,0,2:T(8,128)(2,1)} %bitcast.133) | data formatting | bytes 16777216 | tf_op jit(solution)/shard_map/reshape | solution.py:81
  25.5 6.1 all-to-all-start
  33.7 3.0 copy.100
  36.7 4.0 reshape.332
  40.6 4.3 copy.99
  45.0 169.3 %all-to-all-done = bf16[8,16,256,128]{3,1,2,0:T(8,128)(2,1)} async-done(((bf16[8,16,256,128]{3,1,2,0:T(8,128)(2,1)}), bf16[8,16,256,128]{3,1,2,0:T(8,128)(2,1)}, u32[]{:S(2)}, u32[]{:S(2)}) %all-to-all-start) | async-done | bytes 8388640 | tf_op jit(solution)/shard_map/all_to_all | solution.py:88
  214.3 8.9 %copy.95 = bf16[8,16,256,128]{3,2,1,0:T(8,128)(2,1)} copy(bf16[8,16,256,128]{3,1,2,0:T(8,128)(2,1)} %all-to-all-done) | data formatting | bytes 16777216 | tf_op jit(solution)/shard_map/all_to_all | solution.py:88
  223.2 191.2 %while.25 = (s32[]{:T(128)}, bf16[16,8,256,128]{3,2,1,0:T(8,128)(2,1)}, f32[16,8,256]{2,1,0:T(8,128)S(1)}, bf16[16,8,256,128]{3,2,1,0:T(8,128)(2,1)}, s32[16,8,2...) while((s32[]{:T(128)}, ...), condition=%wide.region_11.12_spmd, body=%wide.region_8.11_spmd.sunk | while | flops 545781888 | bytes 36767320 | solution.py:112
  231.1 4.1 fusion.80
  235.2 2.2 gather_fusion.1
  243.1 4.1 fusion.80
  247.2 2.2 gather_fusion.1
  255.1 4.1 fusion.80
  259.1 2.2 gather_fusion.1
  267.0 4.0 fusion.80
  271.1 2.2 gather_fusion.1
  278.9 4.1 fusion.80
  283.0 2.2 gather_fusion.1
  290.9 4.1 fusion.80
  295.0 2.2 gather_fusion.1
  302.8 4.1 fusion.80
  314.8 4.1 fusion.80
  326.7 4.1 fusion.80
  338.7 4.1 fusion.80
  350.7 4.0 fusion.80
  354.7 2.2 gather_fusion.1
  362.6 4.1 fusion.80
  374.5 4.1 fusion.80
  386.5 4.1 fusion.80
  390.6 2.2 gather_fusion.1
  398.4 4.0 fusion.80
  410.4 4.1 fusion.80
  414.4 10.8 %all_to_all.20 = f32[8,16,256]{2,1,0:T(8,128)S(1)} all-to-all(f32[8,16,256]{2,1,0:T(8,128)S(1)} %bitcast.143), channel_id=1, replica_groups=mesh['groups'=1,'ctx'=8,'head'=2,'rep'=2] {'ctx'}, dimensions={0} | all-to-all | bytes 262144 | tf_op jit(solution)/shard_map/all_to_all | solution.py:116
  425.2 5.1 all-to-all-start.3
  430.5 2.3 collective-permute-start
  436.1 2.9 copy.85
  440.3 2.2 pad_maximum_fusion.1
  442.5 14.5 %while.26 = (s32[]{:T(128)}, f32[2,4,4,256,128]{4,3,2,1,0:T(8,128)}, f32[2,4,4,256]{3,2,1,0:T(4,128)S(1)}, bf16[2,512,4,128]{1,3,2,0:T(8,128)(2,1)S(1)}, bf16[2,...) while((s32[]{:T(128)}, ...), condition=%wide.region_3.4_spmd.clone, body=%wide.region_0.3_spmd.clone.sunk | while | flops 1097592832 | bytes 34215556 | solution.py:73
  446.0 3.8 bitcast_dynamic-update-slice_fusion.7
  453.3 3.7 bitcast_dynamic-update-slice_fusion.7
  458.1 154.3 %all-to-all-done.3 = bf16[8,16,256,128]{3,2,1,0:T(8,128)(2,1)} async-done(((bf16[8,16,256,128]{3,2,1,0:T(8,128)(2,1)}), bf16[8,16,256,128]{3,2,1,0:T(8,128)(2,1)}, u32[]{:S(2)}, u32[]{:S(2)}) %all-to-all-start.3) | async-done | bytes 8388640 | tf_op jit(solution)/shard_map/all_to_all | solution.py:115
  612.4 6.4 %gather_fusion.3 = bf16[64,256,128]{2,1,0:T(8,128)(2,1)} fusion(bf16[128,256,128]{2,1,0:T(8,128)(2,1)} %bitcast.20, s32[1024]{0:T(1024)S(1)} %pad_clamp_fusion), kind=kCustom, calls=%fused_computation.3 | custom fusion | bytes 8388864 | tf_op jit(solution)/shard_map/gather | solution.py:117
  618.8 3.3 bitcast_convert_fusion.1
  622.1 7.0 %fusion.49 = f32[2,16,256,128]{3,2,1,0:T(8,128)S(1)} fusion(f32[2,16,2,256,128]{4,3,2,1,0:T(8,128)S(1)} %bitcast_convert_fusion.1, f32[2,16,1,256,128]{4,3,2,1,0:T(8,128)} %bitcast.18, f32[2,16,3,256]{3,2,1,0:T(4,128)S(1)} %get-tuple-element.220), kind=kLoop, calls=%fused_computation.56 | loop fusion | flops 8388608 | bytes 16875520 | tf_op jit(solution)/shard_map/reduce_sum | solution.py:127
  630.5 2.6 copy.103
  633.2 3.9 copy.104
  (200 shorter events, 128.4 us)
Async XLA Ops:
  2.0 23.5 %all-to-all-start.1 = ((s32[8,16,2]{1,2,0:T(2,128)}), s32[8,16,2]{1,2,0:T(2,128)S(1)}, u32[]{:S(2)}, u32[]{:S(2)}) async-start(s32[8,16,2]{1,2,0:T(2,128)} %copy.96), calls=%async_computation.1 | async-start | bytes 16384 | tf_op jit(solution)/shard_map/all_to_all | solution.py:89
  25.5 6.1 copy-start.1
  25.5 188.7 %all-to-all-start = ((bf16[8,16,256,128]{3,1,2,0:T(8,128)(2,1)}), bf16[8,16,256,128]{3,1,2,0:T(8,128)(2,1)}, u32[]{:S(2)}, u32[]{:S(2)}) async-start(bf16[8,16,256,128]{3,1,2,0:T(8,128)(2,1)} %copy.94), calls=%async_computation | async-start | bytes 16777216 | tf_op jit(solution)/shard_map/all_to_all | solution.py:88
  227.3 1.9 copy-start
  239.2 1.9 copy-start
  251.2 1.9 copy-start
  263.2 1.9 copy-start
  275.1 1.9 copy-start
  287.1 1.9 copy-start
  299.0 1.9 copy-start
  311.0 1.9 copy-start
  322.9 1.9 copy-start
  334.9 1.9 copy-start
  346.9 1.9 copy-start
  358.8 1.9 copy-start
  370.7 1.9 copy-start
  382.7 1.9 copy-start
  394.6 1.9 copy-start
  406.5 1.9 copy-start
  425.2 5.1 copy-start.4
  425.2 7.6 %copy-start.5 = (bf16[2,256,512]{2,1,0:T(8,128)(2,1)S(1)}, bf16[2,256,512]{2,1,0:T(8,128)(2,1)}, u32[]{:S(2)}) copy-start(bf16[2,256,512]{2,1,0:T(8,128)(2,1)} %param.12) | copy-start | bytes 1572868
  425.2 187.2 %all-to-all-start.3 = ((bf16[8,16,256,128]{3,2,1,0:T(8,128)(2,1)}), bf16[8,16,256,128]{3,2,1,0:T(8,128)(2,1)}, u32[]{:S(2)}, u32[]{:S(2)}) async-start(bf16[8,16,256,128]{3,2,1,0:T(8,128)(2,1)} %bitcast.137), calls=%async_computation.3 | async-start | bytes 16777216 | tf_op jit(solution)/shard_map/all_to_all | solution.py:115
  430.5 8.4 %copy-start.2 = (bf16[2,256,512]{1,2,0:T(8,128)(2,1)}, bf16[2,256,512]{1,2,0:T(8,128)(2,1)S(1)}, u32[]{:S(2)}) copy-start(bf16[2,256,512]{1,2,0:T(8,128)(2,1)S(1)} %copy.83) | copy-start | bytes 1572868
  430.5 8.4 %collective-permute-start = (bf16[2,256,512]{1,2,0:T(8,128)(2,1)S(1)}, bf16[2,256,512]{1,2,0:T(8,128)(2,1)}, u32[]{:S(2)}, u32[]{:S(2)}) collective-permute-start(bf16[2,256,512]{1,2,0:T(8,128)(2,1)S(1)} %copy.83), channel_id=1, source_target_pairs={{0,1},{2,3},{4,5},{6,7},{8,9},{10,11},{12,13},{14,15},{16,17},{18,... | collective-permute-start | bytes 1572872 | tf_op jit(solution)/shard_map/ppermute | solution.py:16
  433.8 6.4 %collective-permute-start.1 = (bf16[2,256,512]{1,2,0:T(8,128)(2,1)}, bf16[2,256,512]{1,2,0:T(8,128)(2,1)}, u32[]{:S(2)}, u32[]{:S(2)}) collective-permute-start(bf16[2,256,512]{1,2,0:T(8,128)(2,1)} %copy.86), channel_id=1, source_target_pairs={{0,1},{2,3},{4,5},{6,7},{8,9},{10,11},{12,13},{14,15},{16,17},{18,... | collective-permute-start | bytes 1572872 | tf_op jit(solution)/shard_map/ppermute | solution.py:16
  444.2 1.8 copy-start.3
  451.5 1.8 copy-start.3
where the time goes:
time: 640 us; the launch traced here: 637 us
  waiting for transfers between devices  324 us (51%)
  local copies, waits for them, and re-layouts  128 us (20%)
  matrix products  110 us (17%)
  other arithmetic  40.1 us (6%)
  starting transfers between devices  22.9 us (4%)
  blocking collectives  10.8 us (2%)
    all_to_all x1, waiting for transfers between devices, body(): lax.all_to_all(outbound, 'ctx', split_axis=0, concat_axis=0, tiled=True)  169 us
    all_to_all x1, waiting for transfers between devices, body(): lax.all_to_all(served, 'ctx', split_axis=0, concat_axis=0, tiled=True)  154 us
    dot_general x18, matrix products, partial_attention(): jnp.einsum(pattern, weights.astype(jnp.bfloat16), values, preferred_eleme...  72.6 us
    gather x16, local copies, waits for them, and re-layouts, single(): lax.dynamic_slice(key_tiles, anchor, (1, BLOCK_TOKENS, 1, HEAD_WIDTH))  35.3 us
    while x36, local copies, waits for them, and re-layouts  30.7 us
    dot_general x16, matrix products, single(): lax.dot_general(rows_in, keys_tile, (((1,), (1,)), ((), ())), preferred_e...  29 us
    reduce_sum x18, other arithmetic, partial_attention(): totals = jnp.sum(weights, axis=-1, keepdims=True)  23.6 us
  transfers between devices with their start and end apart: 5, of which 2 were waited for; matrix products, arithmetic and copies ran while one was open for 8% of the time, Pallas kernels for 0%

commit v1 on v0

v1 whole, which is shorter than its diff:
```python
import functools

import jax
import jax.numpy as jnp
from jax import lax
from jax.experimental import pallas as pl
from jax.experimental.pallas import tpu as pltpu
from jax.sharding import PartitionSpec as P

HEAD_WIDTH = 128
BLOCK_TOKENS = 512
SCALE = HEAD_WIDTH ** (-0.5)
LOG2E = 1.4426950408889634
NEGATIVE = -1e30


def scores_by_key(keys, queries):
    return lax.dot_general(
        keys, queries, (((1,), (1,)), ((), ())), preferred_element_type=jnp.float32
    )


def mix_by_width(values, weights):
    return lax.dot_general(
        values,
        weights.astype(jnp.bfloat16),
        (((0,), (0,)), ((), ())),
        preferred_element_type=jnp.float32,
    )


def own_kernel(q_ref, k_ref, v_ref, part_ref, log_ref, picked_ref, picked_log_ref):
    half = q_ref.shape[1] // 2
    visible = lax.broadcasted_iota(jnp.int32, (half, half), 0) <= lax.broadcasted_iota(
        jnp.int32, (half, half), 1
    )
    early_keys, late_keys = k_ref[0, :half], k_ref[0, half:]
    early_queries, late_queries = q_ref[0, :half], q_ref[0, half:]

    first = jnp.where(visible, scores_by_key(early_keys, early_queries), NEGATIVE)
    highest = jnp.max(first, axis=0, keepdims=True)
    weights = jnp.exp2((first - highest) * (SCALE * LOG2E))
    total = jnp.sum(weights, axis=0, keepdims=True)
    part_ref[0, :, :half] = mix_by_width(v_ref[0, :half], weights) / total
    log_ref[0, :, :half] = highest * SCALE + jnp.log(total)

    before = scores_by_key(early_keys, late_queries)
    within = jnp.where(visible, scores_by_key(late_keys, late_queries), NEGATIVE)
    highest = jnp.maximum(
        jnp.max(before, axis=0, keepdims=True), jnp.max(within, axis=0, keepdims=True)
    )
    before = jnp.exp2((before - highest) * (SCALE * LOG2E))
    within = jnp.exp2((within - highest) * (SCALE * LOG2E))
    total = jnp.sum(before, axis=0, keepdims=True) + jnp.sum(within, axis=0, keepdims=True)
    mixed = mix_by_width(v_ref[0, :half], before) + mix_by_width(v_ref[0, half:], within)
    part_ref[0, :, half:] = mixed / total
    log_ref[0, :, half:] = highest * SCALE + jnp.log(total)


def own_attention(queries, keys, values, head_grouping):
    blocks, rows, width = queries.shape
    heads = width // HEAD_WIDTH
    count = blocks * heads
    items = 2 * count
    query_spec = pl.BlockSpec((1, rows, HEAD_WIDTH), lambda n: (lax.div(n, heads), 0, lax.rem(n, heads)))
    key_spec = pl.BlockSpec(
        (1, rows, HEAD_WIDTH), lambda n: (lax.div(n, heads), 0, lax.div(lax.rem(n, heads), head_grouping))
    )
    return pl.pallas_call(
        own_kernel,
        grid=(count,),
        in_specs=[query_spec, key_spec, key_spec],
        out_specs=[
            pl.BlockSpec((1, HEAD_WIDTH, rows), lambda n: (n, 0, 0)),
            pl.BlockSpec((1, 1, rows), lambda n: (n, 0, 0)),
            pl.BlockSpec(memory_space=pl.ANY),
            pl.BlockSpec(memory_space=pl.ANY),
        ],
        out_shape=[
            jax.ShapeDtypeStruct((count, HEAD_WIDTH, rows), jnp.float32),
            jax.ShapeDtypeStruct((count, 1, rows), jnp.float32),
            jax.ShapeDtypeStruct((items + 2, HEAD_WIDTH, rows), jnp.bfloat16),
            jax.ShapeDtypeStruct((items + 2, 1, rows), jnp.float32),
        ],
        cost_estimate=pl.CostEstimate(
            flops=count * rows * rows * HEAD_WIDTH * 4,
            transcendentals=count * rows * rows,
            bytes_accessed=count * rows * HEAD_WIDTH * 8,
        ),
        name="own_attention",
    )(queries, keys, values)


def pick_kernel(table, count, q_hbm, k_hbm, v_hbm, part_in, log_in, part_hbm, log_hbm):
    rows = q_hbm.shape[1]

    def attend(q_ref, k_ref, v_ref, part_ref, log_ref):
        scores = scores_by_key(k_ref[...], q_ref[0])
        highest = jnp.max(scores, axis=0, keepdims=True)
        weights = jnp.exp2((scores - highest) * (SCALE * LOG2E))
        total = jnp.sum(weights, axis=0, keepdims=True)
        part_ref[0] = (mix_by_width(v_ref[...], weights) / total).astype(part_ref.dtype)
        log_ref[0] = highest * SCALE + jnp.log(total)

    tile = pl.BlockSpec((BLOCK_TOKENS, HEAD_WIDTH), lambda n: (table[1, n], table[2, n]))
    pltpu.emit_pipeline(
        attend,
        grid=(count[0],),
        in_specs=[
            pl.BlockSpec((1, rows, HEAD_WIDTH), lambda n: (table[3, n], 0, table[4, n])),
            tile,
            tile,
        ],
        out_specs=[
            pl.BlockSpec((1, HEAD_WIDTH, rows), lambda n: (table[0, n], 0, 0)),
            pl.BlockSpec((1, 1, rows), lambda n: (table[0, n], 0, 0)),
        ],
    )(q_hbm, k_hbm, v_hbm, part_hbm, log_hbm)


def pick_attention(table, count, queries, keys, values, parts, logs):
    blocks, rows, width = queries.shape
    expected = 2 * blocks * (width // HEAD_WIDTH) // 8
    smem = pl.BlockSpec(memory_space=pltpu.SMEM)
    anywhere = pl.BlockSpec(memory_space=pl.ANY)
    return pl.pallas_call(
        pick_kernel,
        in_specs=[smem, smem] + [anywhere] * 5,
        out_specs=[anywhere, anywhere],
        out_shape=[
            jax.ShapeDtypeStruct(parts.shape, parts.dtype),
            jax.ShapeDtypeStruct(logs.shape, logs.dtype),
        ],
        input_output_aliases={5: 0, 6: 1},
        cost_estimate=pl.CostEstimate(
            flops=expected * rows * BLOCK_TOKENS * HEAD_WIDTH * 4,
            transcendentals=expected * rows * BLOCK_TOKENS,
            bytes_accessed=expected * rows * HEAD_WIDTH * 8,
        ),
        name="pick_attention",
    )(table, count.reshape(1), queries, keys, values, parts, logs)


def merge_kernel(rep, own_ref, own_log_ref, part_ref, log_ref, keep_ref, send_ref):
    half = keep_ref.shape[1]
    own_log, first_log, second_log = own_log_ref[0], log_ref[0], log_ref[1]
    top = jnp.maximum(own_log, jnp.maximum(first_log, second_log))
    own_share = jnp.exp(own_log - top)
    first_share = jnp.exp(first_log - top)
    second_share = jnp.exp(second_log - top)
    merged = (
        own_share * own_ref[0]
        + first_share * part_ref[0].astype(jnp.float32)
        + second_share * part_ref[1].astype(jnp.float32)
    ) / (own_share + first_share + second_share)
    early = merged[:, :half].T.astype(keep_ref.dtype)
    late = merged[:, half:].T.astype(keep_ref.dtype)
    keep_ref[0] = jnp.where(rep[0] == 0, early, late)
    send_ref[0] = jnp.where(rep[0] == 0, late, early)


def merge(rep, own, own_log, parts, logs, blocks, full_width):
    count, _, rows = own.shape
    heads = count // blocks
    half = rows // 2
    return pl.pallas_call(
        merge_kernel,
        grid_spec=pltpu.PrefetchScalarGridSpec(
            num_scalar_prefetch=1,
            grid=(count,),
            in_specs=[
                pl.BlockSpec((1, HEAD_WIDTH, rows), lambda n, r: (n, 0, 0)),
                pl.BlockSpec((1, 1, rows), lambda n, r: (n, 0, 0)),
                pl.BlockSpec((2, HEAD_WIDTH, rows), lambda n, r: (n, 0, 0)),
                pl.BlockSpec((2, 1, rows), lambda n, r: (n, 0, 0)),
            ],
            out_specs=[
                pl.BlockSpec(
                    (1, half, HEAD_WIDTH),
                    lambda n, r: (lax.div(n, heads), 0, r[0] * heads + lax.rem(n, heads)),
                ),
                pl.BlockSpec((1, half, HEAD_WIDTH), lambda n, r: (lax.div(n, heads), 0, lax.rem(n, heads))),
            ],
        ),
        out_shape=[
            jax.ShapeDtypeStruct((blocks, half, full_width), jnp.bfloat16),
            jax.ShapeDtypeStruct((blocks, half, heads * HEAD_WIDTH), jnp.bfloat16),
        ],
        cost_estimate=pl.CostEstimate(
            flops=count * rows * HEAD_WIDTH * 8,
            transcendentals=count * rows * 3,
            bytes_accessed=count * rows * HEAD_WIDTH * 10,
        ),
        name="merge_parts",
    )(rep, own, own_log, parts, logs)


def ring_order(count):
    return list(range(0, count, 2)) + list(range(count - 1, 0, -2))


def item_tables(holders, tiles, key_heads, blocks, heads, wanted, items):
    mine = holders[None, :] == wanted[:, None]
    place = jnp.cumsum(mine.astype(jnp.int32), axis=1) - 1
    slot = jnp.arange(items)
    chosen = mine[:, :, None] & (place[:, :, None] == slot[None, None, :])
    columns = jnp.stack([jnp.arange(items), tiles, key_heads, blocks, heads])
    filled = jnp.sum(jnp.where(chosen[:, None], columns[None, :, :, None], 0), axis=2)
    counts = jnp.sum(mine.astype(jnp.int32), axis=1)
    spare = (slot[None, :] >= counts[:, None])[:, None, :] & (jnp.arange(5) == 0)[None, :, None]
    return jnp.where(spare, items, filled), jnp.maximum(counts, 1)


def body(queries, prefill_keys, prefill_values, context_keys, context_values, picks):
    local_count, stack_height, full_width = queries.shape
    rep_size = lax.axis_size("rep")
    ctx_size = lax.axis_size("ctx")
    rep_index = lax.axis_index("rep")
    ctx_index = lax.axis_index("ctx")
    width = full_width // rep_size
    key_width = prefill_keys.shape[2] // rep_size
    heads = width // HEAD_WIDTH
    head_grouping = width // key_width
    blocks_here = context_keys.shape[0] // BLOCK_TOKENS
    items = 2 * local_count * heads
    swap = [(0, 1), (1, 0)]

    def columns_of(value, which, size):
        return lax.dynamic_slice_in_dim(value, which * size, size, axis=value.ndim - 1)

    own_shard = (
        columns_of(context_keys, rep_index, key_width),
        columns_of(context_values, rep_index, key_width),
    )
    order = ring_order(ctx_size)
    onward = [(order[n], order[(n + 1) % ctx_size]) for n in range(ctx_size)]
    backward = [(target, source) for source, target in onward]
    shards = {0: own_shard}
    ahead, behind = own_shard, own_shard
    for step in range(1, (ctx_size - 1) // 2 + 1):
        ahead = tuple(lax.ppermute(part, "ctx", onward) for part in ahead)
        behind = tuple(lax.ppermute(part, "ctx", backward) for part in behind)
        shards[-step], shards[step] = ahead, behind
    if ctx_size % 2 == 0:
        shards[ctx_size // 2] = (
            lax.ppermute(ahead[0], "ctx", onward),
            lax.ppermute(behind[1], "ctx", backward),
        )

    other = rep_size - 1 - rep_index

    def all_rows(value, size):
        kept = columns_of(value, rep_index, size)
        came = lax.ppermute(columns_of(value, other, size), "rep", swap)
        return jnp.where(
            rep_index == 0,
            jnp.concatenate([kept, came], axis=1),
            jnp.concatenate([came, kept], axis=1),
        )

    block_queries = all_rows(queries, width)
    block_keys = all_rows(prefill_keys, key_width)
    block_values = all_rows(prefill_values, key_width)

    position_of = [0] * ctx_size
    for position, device in enumerate(order):
        position_of[device] = position
    here = jnp.array(position_of, jnp.int32)[ctx_index]
    distances = sorted(shards, key=abs)
    wanted = jnp.array(order, jnp.int32)[(here + jnp.array(distances, jnp.int32)) % ctx_size]
    mine = lax.dynamic_slice_in_dim(picks[:, :, :2], rep_index * heads, heads, axis=1).reshape(-1)
    place = jnp.arange(items)
    head = place // 2 % heads
    holders = mine // blocks_here
    tables, counts = item_tables(
        holders,
        mine - holders * blocks_here,
        head // head_grouping,
        place // (2 * heads),
        head,
        wanted,
        items,
    )

    own, own_log, parts, logs = own_attention(
        block_queries, block_keys, block_values, head_grouping
    )
    for n, distance in enumerate(distances):
        keys, values = shards[distance]
        parts, logs = pick_attention(
            tables[n], counts[n], block_queries, keys, values, parts, logs
        )
    result, leaving = merge(
        rep_index.reshape(1), own, own_log, parts, logs, local_count, full_width
    )
    arriving = lax.ppermute(leaving, "rep", swap)
    return lax.dynamic_update_slice_in_dim(result, arriving, other * width, axis=2)


def solution(mesh):
    return jax.shard_map(
        body,
        mesh=mesh,
        in_specs=(
            P(("groups", "ctx"), "rep", "head"),
            P(("groups", "ctx"), "rep", "head"),
            P(("groups", "ctx"), "rep", "head"),
            P(("groups", "ctx"), "head"),
            P(("groups", "ctx"), "head"),
            P(("groups", "ctx"), "head", None),
        ),
        out_specs=P(("groups", "ctx"), "rep", "head"),
        check_vma=False,
    )
```

time: 640 us -> 220 us (0.34)
  waiting for transfers between devices: 324 us -> 99.1 us
  local copies, waits for them, and re-layouts: 128 us -> 13.7 us
  matrix products: 110 us -> 0 us
  Pallas kernels: 0 us -> 78.8 us
  other arithmetic: 40.1 us -> 9.69 us
  blocking collectives: 10.8 us -> 0 us
    all_to_all x3 -> x0, waiting for transfers between devices: 324 us -> none  [the longest x1 169 us: body(): lax.all_to_all(outbound, 'ctx', split_axis=0, concat_axis=0, tiled=True)]
    dot_general x37 -> x0, matrix products: 110 us -> none  [the longest x18 72.6 us: partial_attention(): jnp.einsum(pattern, weights.astype(jnp.bfloat16), values, preferred_eleme...]
    ppermute x2 -> x18, waiting for transfers between devices: 0.01 us -> 99.1 us  [the longest x6 48.1 us: body(): behind = tuple((lax.ppermute(part, 'ctx', backward) for part in behind))]
    pallas_call x0 -> x10, Pallas kernels: none -> 78.8 us  [the longest x8 51.1 us: pick_attention(): pl.pallas_call(pick_kernel, in_specs=[smem, smem] + [anywhere] * 5, out_s...]
    gather x34 -> x1, local copies, waits for them, and re-layouts: 52.4 us -> 0.64 us  [body(): jnp.array(order, jnp.int32)]
    while x38 -> x0, local copies, waits for them, and re-layouts: 38 us -> none
    reduce_sum x23 -> x2, other arithmetic: 31.1 us -> 0.36 us  [the longest x1 0.18 us: item_tables(): counts = jnp.sum(mine.astype(jnp.int32), axis=1)]
    all_to_all x3 -> x0, starting transfers between devices: 18.5 us -> none  [the longest x1 7.31 us: body(): lax.all_to_all(labels, 'ctx', split_axis=0, concat_axis=0, tiled=True)]
  transfers between devices with their start and end apart: 5 -> 18, of which waited for: 2 -> 8; matrix products, arithmetic and copies ran while one was open for 8% -> 9% of each run, Pallas kernels for 0% -> 26%
where the time goes in v1:
time: 220 us; the launch traced here: 218 us
  waiting for transfers between devices  99.1 us (45%)
  Pallas kernels  78.8 us (36%)
  starting transfers between devices  16.5 us (8%)
  local copies, waits for them, and re-layouts  13.7 us (6%)
  other arithmetic  9.69 us (4%)
    pallas_call x8, Pallas kernels, pick_attention(): pl.pallas_call(pick_kernel, in_specs=[smem, smem] + [anywhere] * 5, out_s...  51.1 us
    ppermute x6, waiting for transfers between devices, body(): behind = tuple((lax.ppermute(part, 'ctx', backward) for part in behind))  48.1 us
    ppermute x6, waiting for transfers between devices, body(): ahead = tuple((lax.ppermute(part, 'ctx', onward) for part in ahead))  48.1 us
    pallas_call x1, Pallas kernels, own_attention(): pl.pallas_call(own_kernel, grid=(count,), in_specs=[query_spec, key_spec,...  16.2 us
    ppermute x6, starting transfers between devices, body(): ahead = tuple((lax.ppermute(part, 'ctx', onward) for part in ahead))  13.1 us
    pallas_call x1, Pallas kernels, merge(): pl.pallas_call(merge_kernel, grid_spec=pltpu.PrefetchScalarGridSpec(num_s...  11.6 us
    select_n x3, other arithmetic, all_rows(): jnp.where(rep_index == 0, jnp.concatenate([kept, came], axis=1), jnp.conc...  8.07 us
    dynamic_slice x5, local copies, waits for them, and re-layouts, columns_of(): lax.dynamic_slice_in_dim(value, which * size, size, axis=value.ndim - 1)  7.4 us
  transfers between devices with their start and end apart: 18, of which 8 were waited for; matrix products, arithmetic and copies ran while one was open for 9% of the time, Pallas kernels for 26%

profile of v1, /device:TPU:0, one launch (start us, length us, event | category | flops | bytes accessed | tf_op | source)
XLA Modules:
  0.0 218.0 jit_solution(5581756517322502756)
XLA Ops:
  0.0 1.6 copy-done
  1.6 1.0 constant_dynamic-slice_fusion.1.k_hbm
  2.6 3.1 %collective-permute-start.3 = (bf16[2048,256]{1,0:T(8,128)(2,1)}, bf16[2048,256]{1,0:T(8,128)(2,1)}, u32[]{:S(2)}, u32[]{:S(2)}) collective-permute-start(bf16[2048,256]{1,0:T(8,128)(2,1)} %constant_dynamic-slice_fusion.1.k_hbm), channel_id=1, source_target_pairs={{0,8},{8,16},{16,24},{24,28},{28,20},{20,12},{12,4},{4,0},{1,9},{9... | collective-permute-start | bytes 3145736 | tf_op jit(solution)/shard_map/ppermute | solution.py:241
  5.8 2.1 collective-permute-start.14
  7.9 1.8 constant_dynamic-slice_fusion.6
  10.0 0.6 dynamic_slice.37
  10.5 0.7 compare_select_fusion
  11.2 0.6 gather_fusion
  12.0 0.2 reduce_window_sum.11
  12.3 17.8 %collective-permute-done.3.k_hbm = bf16[2048,256]{1,0:T(8,128)(2,1)} collective-permute-done((bf16[2048,256]{1,0:T(8,128)(2,1)}, bf16[2048,256]{1,0:T(8,128)(2,1)}, u32[]{:S(2)}, u32[]{:S(2)}) %collective-permute-start.3) | collective-permute-done | bytes 1048608 | tf_op jit(solution)/shard_map/ppermute | solution.py:241
  30.0 2.1 collective-permute-start.4
  32.1 21.1 %collective-permute-done.7.v_hbm = bf16[2048,256]{1,0:T(8,128)(2,1)} collective-permute-done((bf16[2048,256]{1,0:T(8,128)(2,1)S(1)}, bf16[2048,256]{1,0:T(8,128)(2,1)}, u32[]{:S(2)}, u32[]{:S(2)}) %collective-permute-start.7) | collective-permute-done | bytes 1048608 | tf_op jit(solution)/shard_map/ppermute | solution.py:242
  53.2 0.3 collective-permute-start.8
  53.7 0.2 select_reduce_fusion
  53.9 1.8 constant_dynamic-slice_fusion.4
  55.6 1.7 collective-permute-start.15
  57.4 2.8 %constant_dynamic-slice_fusion.8 = (bf16[2,256,1024]{2,1,0:T(8,128)(2,1)S(1)}, bf16[2,256,1024]{2,1,0:T(8,128)(2,1)}) fusion(bf16[2,256,2048]{2,1,0:T(8,128)(2,1)} %param.9, s32[]{:T(128)S(6)} %select_n.134, s32[]{:T(128)S(6)} %select_n.135), kind=kLoop, calls=%fused_computation.28 | loop fusion | bytes 4194312 | tf_op jit(solution)/shard_map/dynamic_slice | solution.py:229
  60.1 0.4 collective-permute-start.12
  60.5 14.5 %collective-permute-done.4.k_hbm = bf16[2048,256]{1,0:T(8,128)(2,1)} collective-permute-done((bf16[2048,256]{1,0:T(8,128)(2,1)}, bf16[2048,256]{1,0:T(8,128)(2,1)}, u32[]{:S(2)}, u32[]{:S(2)}) %collective-permute-start.4) | collective-permute-done | bytes 1048608 | tf_op jit(solution)/shard_map/ppermute | solution.py:241
  75.0 2.1 collective-permute-start.5
  77.0 2.5 %collective-permute-done.8.v_hbm = bf16[2048,256]{1,0:T(8,128)(2,1)} collective-permute-done((bf16[2048,256]{1,0:T(8,128)(2,1)}, bf16[2048,256]{1,0:T(8,128)(2,1)}, u32[]{:S(2)}, u32[]{:S(2)}) %collective-permute-start.8) | collective-permute-done | bytes 1048608 | tf_op jit(solution)/shard_map/ppermute | solution.py:242
  79.5 0.3 collective-permute-start.9
  79.8 0.2 convert_reduce_fusion
  80.1 0.7 copy-done.4
  80.9 0.7 slice_bitcast_fusion
  81.5 15.9 %collective-permute-done.15.v_hbm = bf16[2048,256]{1,0:T(8,128)(2,1)} collective-permute-done((bf16[2048,256]{1,0:T(8,128)(2,1)}, bf16[2048,256]{1,0:T(8,128)(2,1)}, u32[]{:S(2)}, u32[]{:S(2)}) %collective-permute-start.15) | collective-permute-done | bytes 1048608 | tf_op jit(solution)/shard_map/ppermute | solution.py:241
  97.4 2.1 collective-permute-start.16
  99.5 2.5 %collective-permute-done.12.k_hbm = bf16[2048,256]{1,0:T(8,128)(2,1)} collective-permute-done((bf16[2048,256]{1,0:T(8,128)(2,1)}, bf16[2048,256]{1,0:T(8,128)(2,1)}, u32[]{:S(2)}, u32[]{:S(2)}) %collective-permute-start.12) | collective-permute-done | bytes 1048608 | tf_op jit(solution)/shard_map/ppermute | solution.py:242
  102.0 0.3 collective-permute-start.13
  102.3 22.2 %collective-permute-done.9.v_hbm = bf16[2048,256]{1,0:T(8,128)(2,1)} collective-permute-done((bf16[2048,256]{1,0:T(8,128)(2,1)}, bf16[2048,256]{1,0:T(8,128)(2,1)}, u32[]{:S(2)}, u32[]{:S(2)}) %collective-permute-start.9) | collective-permute-done | bytes 1048608 | tf_op jit(solution)/shard_map/ppermute | solution.py:242
  124.4 0.3 collective-permute-start.10
  124.8 1.7 collective-permute-start.6
  126.5 0.7 fusion.4
  127.2 2.0 maximum_select_fusion.1.k_ref
  129.2 2.1 maximum_select_fusion.2.v_ref
  131.3 3.9 %maximum_select_fusion.q_ref.q_hbm = bf16[2,512,1024]{2,1,0:T(8,128)(2,1)} fusion(bf16[2,256,1024]{2,1,0:T(8,128)(2,1)} %collective-permute-done, bf16[2,256,1024]{2,1,0:T(8,128)(2,1)S(1)} %get-tuple-element.49, pred[]{:T(512)S(6)} %eq.54), kind=kLoop, calls=%fused_computation.1 | loop fusion | flops 9437184 | bytes 4194305 | tf_op jit(solution)/shard_map/jit(_where)/select_n | solution.py:255
  135.2 16.2 %own_attention.1 = (f32[16,128,512]{2,1,0:T(8,128)}, f32[16,1,512]{2,1,0:T(1,128)}, bf16[34,128,512]{2,1,0:T(8,128)(2,1)}, f32[34,1,512]{2,1,0:T(1,128)}) custom-call(bf16[2,512,1024]{2,1,0:T(8,128)(2,1)} %maximum_select_fusion.q_ref.q_hbm, bf16[2,512,256]{2,1,0:T(8,128)(2,1)} %maximum_select_fusion.1.k_ref, bf16[2,512,256]{2,1,0:T(8,128)(2,1)} %maximum_select_fusion.2.v_ref), custom_call_target="tpu_custom_call" | custom-call | flops 2147483648 | bytes 8388608 | tf_op jit(solution)/shard_map/own_attention/pallas_call | solution.py:69
  151.4 6.4 %pick_attention.8 = (bf16[34,128,512]{2,1,0:T(8,128)(2,1)}, f32[34,1,512]{2,1,0:T(1,128)}) custom-call(s32[5,32]{1,0:T(8,128)} %get-tuple-element.55.table, s32[1]{0:T(128)} %get-tuple-element.65.count, bf16[2,512,1024]{2,1,0:T(8,128)(2,1)} %maximum_select_fusion.q_ref.q_hbm, ...), custom_call_target="tpu_custom_call", output_to_operand_aliasing={{0}: (5, {}), {1}: (6, {})} | custom-call | flops 536870912 | bytes 2097152 | tf_op jit(solution)/shard_map/pick_attention/pallas_call | solution.py:126
  157.8 6.3 %pick_attention.9 = (bf16[34,128,512]{2,1,0:T(8,128)(2,1)}, f32[34,1,512]{2,1,0:T(1,128)}) custom-call(s32[5,32]{1,0:T(8,128)} %get-tuple-element.56.table, s32[1]{0:T(128)} %get-tuple-element.66.count, bf16[2,512,1024]{2,1,0:T(8,128)(2,1)} %maximum_select_fusion.q_ref.q_hbm, ...), custom_call_target="tpu_custom_call", output_to_operand_aliasing={{0}: (5, {}), {1}: (6, {})} | custom-call | flops 536870912 | bytes 2097152 | tf_op jit(solution)/shard_map/pick_attention/pallas_call | solution.py:126
  164.1 3.7 %pick_attention.10 = (bf16[34,128,512]{2,1,0:T(8,128)(2,1)}, f32[34,1,512]{2,1,0:T(1,128)}) custom-call(s32[5,32]{1,0:T(8,128)} %get-tuple-element.57.table, s32[1]{0:T(128)} %get-tuple-element.67.count, bf16[2,512,1024]{2,1,0:T(8,128)(2,1)} %maximum_select_fusion.q_ref.q_hbm, ...), custom_call_target="tpu_custom_call", output_to_operand_aliasing={{0}: (5, {}), {1}: (6, {})} | custom-call | flops 536870912 | bytes 2097152 | tf_op jit(solution)/shard_map/pick_attention/pallas_call | solution.py:126
  167.8 6.4 %pick_attention.11 = (bf16[34,128,512]{2,1,0:T(8,128)(2,1)}, f32[34,1,512]{2,1,0:T(1,128)}) custom-call(s32[5,32]{1,0:T(8,128)} %get-tuple-element.58.table, s32[1]{0:T(128)} %get-tuple-element.68.count, bf16[2,512,1024]{2,1,0:T(8,128)(2,1)} %maximum_select_fusion.q_ref.q_hbm, ...), custom_call_target="tpu_custom_call", output_to_operand_aliasing={{0}: (5, {}), {1}: (6, {})} | custom-call | flops 536870912 | bytes 2097152 | tf_op jit(solution)/shard_map/pick_attention/pallas_call | solution.py:126
  174.3 6.3 %pick_attention.12 = (bf16[34,128,512]{2,1,0:T(8,128)(2,1)}, f32[34,1,512]{2,1,0:T(1,128)}) custom-call(s32[5,32]{1,0:T(8,128)} %get-tuple-element.59.table, s32[1]{0:T(128)} %get-tuple-element.69.count, bf16[2,512,1024]{2,1,0:T(8,128)(2,1)} %maximum_select_fusion.q_ref.q_hbm, ...), custom_call_target="tpu_custom_call", output_to_operand_aliasing={{0}: (5, {}), {1}: (6, {})} | custom-call | flops 536870912 | bytes 2097152 | tf_op jit(solution)/shard_map/pick_attention/pallas_call | solution.py:126
  180.6 6.4 %pick_attention.13 = (bf16[34,128,512]{2,1,0:T(8,128)(2,1)}, f32[34,1,512]{2,1,0:T(1,128)}) custom-call(s32[5,32]{1,0:T(8,128)} %get-tuple-element.60.table, s32[1]{0:T(128)} %get-tuple-element.70.count, bf16[2,512,1024]{2,1,0:T(8,128)(2,1)} %maximum_select_fusion.q_ref.q_hbm, ...), custom_call_target="tpu_custom_call", output_to_operand_aliasing={{0}: (5, {}), {1}: (6, {})} | custom-call | flops 536870912 | bytes 2097152 | tf_op jit(solution)/shard_map/pick_attention/pallas_call | solution.py:126
  187.0 4.5 %pick_attention.14 = (bf16[34,128,512]{2,1,0:T(8,128)(2,1)}, f32[34,1,512]{2,1,0:T(1,128)}) custom-call(s32[5,32]{1,0:T(8,128)} %get-tuple-element.61.table, s32[1]{0:T(128)} %get-tuple-element.71.count, bf16[2,512,1024]{2,1,0:T(8,128)(2,1)} %maximum_select_fusion.q_ref.q_hbm, ...), custom_call_target="tpu_custom_call", output_to_operand_aliasing={{0}: (5, {}), {1}: (6, {})} | custom-call | flops 536870912 | bytes 2097152 | tf_op jit(solution)/shard_map/pick_attention/pallas_call | solution.py:126
  191.5 11.0 %pick_attention.15 = (bf16[34,128,512]{2,1,0:T(8,128)(2,1)}, f32[34,1,512]{2,1,0:T(1,128)}) custom-call(s32[5,32]{1,0:T(8,128)} %get-tuple-element.62.table, s32[1]{0:T(128)} %get-tuple-element.72.count, bf16[2,512,1024]{2,1,0:T(8,128)(2,1)} %maximum_select_fusion.q_ref.q_hbm, ...), custom_call_target="tpu_custom_call", output_to_operand_aliasing={{0}: (5, {}), {1}: (6, {})} | custom-call | flops 536870912 | bytes 2097152 | tf_op jit(solution)/shard_map/pick_attention/pallas_call | solution.py:126
  202.5 11.6 %merge_parts.1 = (bf16[2,256,2048]{2,1,0:T(8,128)(2,1)}, bf16[2,256,1024]{2,1,0:T(8,128)(2,1)}) custom-call(s32[1]{0:T(128)} %bitcast.rep, f32[16,128,512]{2,1,0:T(8,128)} %get-tuple-element.27.own_ref, f32[16,1,512]{2,1,0:T(1,128)} %get-tuple-element.28.own_log_ref, bf16[34,128,512]{2,1,0:T(8,128)(2,1)} %get-tuple-element.45.part_ref, ...), custom_call_target="tpu_custom_call" | custom-call | flops 8388608 | bytes 10485760 | tf_op jit(solution)/shard_map/merge_parts/pallas_call | solution.py:166
  214.0 2.9 %collective-permute-done.17 = bf16[2,256,1024]{2,1,0:T(8,128)(2,1)S(1)} collective-permute-done((bf16[2,256,1024]{2,1,0:T(8,128)(2,1)}, bf16[2,256,1024]{2,1,0:T(8,128)(2,1)S(1)}, u32[]{:S(2)}, u32[]{:S(2)}) %collective-permute-start.17) | collective-permute-done | bytes 1048608 | tf_op jit(solution)/shard_map/ppermute | solution.py:296
  216.9 1.0 constant_dynamic-update-slice_fusion
  (48 shorter events, 0.9 us)
Async XLA Ops:
  0.0 1.6 copy-start
  1.6 4.2 %copy-start.3 = (bf16[2048,512]{1,0:T(8,128)(2,1)S(1)}, bf16[2048,512]{1,0:T(8,128)(2,1)}, u32[]{:S(2)}) copy-start(bf16[2048,512]{1,0:T(8,128)(2,1)} %param.13) | copy-start | bytes 6291460
  2.6 7.1 %slice-start = ((s32[2,16,3]{1,0,2:T(2,128)}), s32[2,16,2]{1,0,2:T(2,128)S(1)}, s32[]{:S(2)}) async-start(s32[2,16,3]{1,0,2:T(2,128)} %param.14), calls=%async_computation | async-start | bytes 4096 | tf_op jit(solution)/shard_map/slice | solution.py:271
  2.6 7.3 %copy-start.6 = (s32[8]{0:T(128)S(1)}, s32[8]{0:T(128)}, u32[]{:S(2)}) copy-start(s32[8]{0:T(128)} %constant.110.clone) | copy-start | bytes 100
  2.6 7.9 %copy-start.5 = (s32[8]{0:T(128)S(1)}, s32[8]{0:T(128)}, u32[]{:S(2)}) copy-start(s32[8]{0:T(128)} %constant.112.clone) | copy-start | bytes 100
  2.6 8.6 %copy-start.1 = (s32[8]{0:T(128)S(1)}, s32[8]{0:T(128)}, u32[]{:S(2)}) copy-start(s32[8]{0:T(128)} %constant.111.clone) | copy-start | bytes 100
  2.6 27.4 %collective-permute-start.3 = (bf16[2048,256]{1,0:T(8,128)(2,1)}, bf16[2048,256]{1,0:T(8,128)(2,1)}, u32[]{:S(2)}, u32[]{:S(2)}) collective-permute-start(bf16[2048,256]{1,0:T(8,128)(2,1)} %constant_dynamic-slice_fusion.1.k_hbm), channel_id=1, source_target_pairs={{0,8},{8,16},{16,24},{24,28},{28,20},{20,12},{12,4},{4,0},{1,9},{9... | collective-permute-start | bytes 3145736 | tf_op jit(solution)/shard_map/ppermute | solution.py:241
  5.8 54.4 %collective-permute-start.11 = (bf16[2048,256]{1,0:T(8,128)(2,1)}, bf16[2048,256]{1,0:T(8,128)(2,1)}, u32[]{:S(2)}, u32[]{:S(2)}) collective-permute-start(bf16[2048,256]{1,0:T(8,128)(2,1)} %constant_dynamic-slice_fusion.1.k_hbm), channel_id=1, source_target_pairs={{8,0},{16,8},{24,16},{28,24},{20,28},{12,20},{4,12},{0,4},{9,1},{1... | collective-permute-start | bytes 3145736 | tf_op jit(solution)/shard_map/ppermute | solution.py:242
  5.8 49.8 %copy-start.2 = (bf16[2048,256]{1,0:T(8,128)(2,1)}, bf16[2048,256]{1,0:T(8,128)(2,1)S(1)}, u32[]{:S(2)}) copy-start(bf16[2048,256]{1,0:T(8,128)(2,1)S(1)} %constant_dynamic-slice_fusion.v_hbm) | copy-start | bytes 3145732
  5.8 49.8 %collective-permute-start.14 = (bf16[2048,256]{1,0:T(8,128)(2,1)S(1)}, bf16[2048,256]{1,0:T(8,128)(2,1)}, u32[]{:S(2)}, u32[]{:S(2)}) collective-permute-start(bf16[2048,256]{1,0:T(8,128)(2,1)S(1)} %constant_dynamic-slice_fusion.v_hbm), channel_id=1, source_target_pairs={{0,8},{8,16},{16,24},{24,28},{28,20},{20,12},{12,4},{4,0},{1,9},{9... | collective-permute-start | bytes 3145736 | tf_op jit(solution)/shard_map/ppermute | solution.py:241
  7.9 45.2 %collective-permute-start.7 = (bf16[2048,256]{1,0:T(8,128)(2,1)S(1)}, bf16[2048,256]{1,0:T(8,128)(2,1)}, u32[]{:S(2)}, u32[]{:S(2)}) collective-permute-start(bf16[2048,256]{1,0:T(8,128)(2,1)S(1)} %constant_dynamic-slice_fusion.v_hbm), channel_id=1, source_target_pairs={{8,0},{16,8},{24,16},{28,24},{20,28},{12,20},{4,12},{0,4},{9,1},{1... | collective-permute-start | bytes 3145736 | tf_op jit(solution)/shard_map/ppermute | solution.py:242
  9.7 50.4 %collective-permute-start.1 = (bf16[2,256,256]{2,1,0:T(8,128)(2,1)}, bf16[2,256,256]{2,1,0:T(8,128)(2,1)}, u32[]{:S(2)}, u32[]{:S(2)}) collective-permute-start(bf16[2,256,256]{2,1,0:T(8,128)(2,1)} %get-tuple-element.54), channel_id=1, source_target_pairs={{0,1},{1,0},{2,3},{3,2},{4,5},{5,4},{6,7},{7,6},{8,9},{9,8},{10,11... | collective-permute-start | bytes 786440 | tf_op jit(solution)/shard_map/ppermute | solution.py:254
  30.0 44.9 %collective-permute-start.4 = (bf16[2048,256]{1,0:T(8,128)(2,1)}, bf16[2048,256]{1,0:T(8,128)(2,1)}, u32[]{:S(2)}, u32[]{:S(2)}) collective-permute-start(bf16[2048,256]{1,0:T(8,128)(2,1)} %collective-permute-done.3.k_hbm), channel_id=1, source_target_pairs={{0,8},{8,16},{16,24},{24,28},{28,20},{20,12},{12,4},{4,0},{1,9},{9... | collective-permute-start | bytes 3145736 | tf_op jit(solution)/shard_map/ppermute | solution.py:241
  53.2 26.3 %collective-permute-start.8 = (bf16[2048,256]{1,0:T(8,128)(2,1)}, bf16[2048,256]{1,0:T(8,128)(2,1)}, u32[]{:S(2)}, u32[]{:S(2)}) collective-permute-start(bf16[2048,256]{1,0:T(8,128)(2,1)} %collective-permute-done.7.v_hbm), channel_id=1, source_target_pairs={{8,0},{16,8},{24,16},{28,24},{20,28},{12,20},{4,12},{0,4},{9,1},{1... | collective-permute-start | bytes 3145736 | tf_op jit(solution)/shard_map/ppermute | solution.py:242
  55.6 41.8 %collective-permute-start.15 = (bf16[2048,256]{1,0:T(8,128)(2,1)}, bf16[2048,256]{1,0:T(8,128)(2,1)}, u32[]{:S(2)}, u32[]{:S(2)}) collective-permute-start(bf16[2048,256]{1,0:T(8,128)(2,1)} %collective-permute-done.14.v_hbm), channel_id=1, source_target_pairs={{0,8},{8,16},{16,24},{24,28},{28,20},{20,12},{12,4},{4,0},{1,9},{9... | collective-permute-start | bytes 3145736 | tf_op jit(solution)/shard_map/ppermute | solution.py:241
  60.1 20.0 %collective-permute-start.2 = (bf16[2,256,256]{2,1,0:T(8,128)(2,1)S(1)}, bf16[2,256,256]{2,1,0:T(8,128)(2,1)S(1)}, u32[]{:S(2)}, u32[]{:S(2)}) collective-permute-start(bf16[2,256,256]{2,1,0:T(8,128)(2,1)S(1)} %get-tuple-element.52), channel_id=1, source_target_pairs={{0,1},{1,0},{2,3},{3,2},{4,5},{5,4},{6,7},{7,6},{8,9},{9,8},{10,11... | collective-permute-start | bytes 786440 | tf_op jit(solution)/shard_map/ppermute | solution.py:254
  60.1 41.8 %collective-permute-start.12 = (bf16[2048,256]{1,0:T(8,128)(2,1)}, bf16[2048,256]{1,0:T(8,128)(2,1)}, u32[]{:S(2)}, u32[]{:S(2)}) collective-permute-start(bf16[2048,256]{1,0:T(8,128)(2,1)} %collective-permute-done.11.k_hbm), channel_id=1, source_target_pairs={{8,0},{16,8},{24,16},{28,24},{20,28},{12,20},{4,12},{0,4},{9,1},{1... | collective-permute-start | bytes 3145736 | tf_op jit(solution)/shard_map/ppermute | solution.py:242
  75.0 49.8 %collective-permute-start.5 = (bf16[2048,256]{1,0:T(8,128)(2,1)}, bf16[2048,256]{1,0:T(8,128)(2,1)}, u32[]{:S(2)}, u32[]{:S(2)}) collective-permute-start(bf16[2048,256]{1,0:T(8,128)(2,1)} %collective-permute-done.4.k_hbm), channel_id=1, source_target_pairs={{0,8},{8,16},{16,24},{24,28},{28,20},{20,12},{12,4},{4,0},{1,9},{9... | collective-permute-start | bytes 3145736 | tf_op jit(solution)/shard_map/ppermute | solution.py:241
  79.5 44.9 %collective-permute-start.9 = (bf16[2048,256]{1,0:T(8,128)(2,1)}, bf16[2048,256]{1,0:T(8,128)(2,1)}, u32[]{:S(2)}, u32[]{:S(2)}) collective-permute-start(bf16[2048,256]{1,0:T(8,128)(2,1)} %collective-permute-done.8.v_hbm), channel_id=1, source_target_pairs={{8,0},{16,8},{24,16},{28,24},{20,28},{12,20},{4,12},{0,4},{9,1},{1... | collective-permute-start | bytes 3145736 | tf_op jit(solution)/shard_map/ppermute | solution.py:242
  80.1 0.7 copy-start.4
  80.8 50.5 %collective-permute-start = (bf16[2,256,1024]{2,1,0:T(8,128)(2,1)}, bf16[2,256,1024]{2,1,0:T(8,128)(2,1)}, u32[]{:S(2)}, u32[]{:S(2)}) collective-permute-start(bf16[2,256,1024]{2,1,0:T(8,128)(2,1)} %get-tuple-element.50), channel_id=1, source_target_pairs={{0,1},{1,0},{2,3},{3,2},{4,5},{5,4},{6,7},{7,6},{8,9},{9,8},{10,11... | collective-permute-start | bytes 3145736 | tf_op jit(solution)/shard_map/ppermute | solution.py:254
  97.4 83.2 %collective-permute-start.16 = (bf16[2048,256]{1,0:T(8,128)(2,1)}, bf16[2048,256]{1,0:T(8,128)(2,1)}, u32[]{:S(2)}, u32[]{:S(2)}) collective-permute-start(bf16[2048,256]{1,0:T(8,128)(2,1)} %collective-permute-done.15.v_hbm), channel_id=1, source_target_pairs={{0,8},{8,16},{16,24},{24,28},{28,20},{20,12},{12,4},{4,0},{1,9},{9... | collective-permute-start | bytes 3145736 | tf_op jit(solution)/shard_map/ppermute | solution.py:241
  102.0 85.0 %collective-permute-start.13 = (bf16[2048,256]{1,0:T(8,128)(2,1)}, bf16[2048,256]{1,0:T(8,128)(2,1)}, u32[]{:S(2)}, u32[]{:S(2)}) collective-permute-start(bf16[2048,256]{1,0:T(8,128)(2,1)} %collective-permute-done.12.k_hbm), channel_id=1, source_target_pairs={{8,0},{16,8},{24,16},{28,24},{20,28},{12,20},{4,12},{0,4},{9,1},{1... | collective-permute-start | bytes 3145736 | tf_op jit(solution)/shard_map/ppermute | solution.py:242
  124.4 67.0 %collective-permute-start.10 = (bf16[2048,256]{1,0:T(8,128)(2,1)}, bf16[2048,256]{1,0:T(8,128)(2,1)}, u32[]{:S(2)}, u32[]{:S(2)}) collective-permute-start(bf16[2048,256]{1,0:T(8,128)(2,1)} %collective-permute-done.9.v_hbm), channel_id=1, source_target_pairs={{8,0},{16,8},{24,16},{28,24},{20,28},{12,20},{4,12},{0,4},{9,1},{1... | collective-permute-start | bytes 3145736 | tf_op jit(solution)/shard_map/ppermute | solution.py:247
  124.8 66.7 %collective-permute-start.6 = (bf16[2048,256]{1,0:T(8,128)(2,1)}, bf16[2048,256]{1,0:T(8,128)(2,1)}, u32[]{:S(2)}, u32[]{:S(2)}) collective-permute-start(bf16[2048,256]{1,0:T(8,128)(2,1)} %collective-permute-done.5.k_hbm), channel_id=1, source_target_pairs={{0,8},{8,16},{16,24},{24,28},{28,20},{20,12},{12,4},{4,0},{1,9},{9... | collective-permute-start | bytes 3145736 | tf_op jit(solution)/shard_map/ppermute | solution.py:246
  214.0 2.9 %collective-permute-start.17 = (bf16[2,256,1024]{2,1,0:T(8,128)(2,1)}, bf16[2,256,1024]{2,1,0:T(8,128)(2,1)S(1)}, u32[]{:S(2)}, u32[]{:S(2)}) collective-permute-start(bf16[2,256,1024]{2,1,0:T(8,128)(2,1)} %get-tuple-element.48), channel_id=1, source_target_pairs={{0,1},{1,0},{2,3},{3,2},{4,5},{5,4},{6,7},{7,6},{8,9},{9,8},{10,11... | collective-permute-start | bytes 3145736 | tf_op jit(solution)/shard_map/ppermute | solution.py:296

commit v2 on v1

--- a/solution.py
+++ b/solution.py
@@ -1,5 +1,3 @@
-import functools
-
 import jax
 import jax.numpy as jnp
 from jax import lax
@@ -7,6 +5,7 @@
 from jax.experimental.pallas import tpu as pltpu
 from jax.sharding import PartitionSpec as P
 
+
 HEAD_WIDTH = 128
 BLOCK_TOKENS = 512
 SCALE = HEAD_WIDTH ** (-0.5)
@@ -29,7 +28,7 @@
     )
 
 
-def own_kernel(q_ref, k_ref, v_ref, part_ref, log_ref, picked_ref, picked_log_ref):
+def own_kernel(q_ref, k_ref, v_ref, part_ref, log_ref, *unwritten):
     half = q_ref.shape[1] // 2
     visible = lax.broadcasted_iota(jnp.int32, (half, half), 0) <= lax.broadcasted_iota(
         jnp.int32, (half, half), 1
@@ -57,7 +56,7 @@
     log_ref[0, :, half:] = highest * SCALE + jnp.log(total)
 
 
-def own_attention(queries, keys, values, head_grouping):
+def own_attention(queries, keys, values, head_grouping, full_width):
     blocks, rows, width = queries.shape
     heads = width // HEAD_WIDTH
     count = blocks * heads
@@ -73,14 +72,15 @@
         out_specs=[
             pl.BlockSpec((1, HEAD_WIDTH, rows), lambda n: (n, 0, 0)),
             pl.BlockSpec((1, 1, rows), lambda n: (n, 0, 0)),
-            pl.BlockSpec(memory_space=pl.ANY),
-            pl.BlockSpec(memory_space=pl.ANY),
-        ],
+        ]
+        + [pl.BlockSpec(memory_space=pl.ANY)] * 4,
         out_shape=[
             jax.ShapeDtypeStruct((count, HEAD_WIDTH, rows), jnp.float32),
             jax.ShapeDtypeStruct((count, 1, rows), jnp.float32),
             jax.ShapeDtypeStruct((items + 2, HEAD_WIDTH, rows), jnp.bfloat16),
             jax.ShapeDtypeStruct((items + 2, 1, rows), jnp.float32),
+            jax.ShapeDtypeStruct((blocks, rows // 2, full_width), jnp.bfloat16),
+            jax.ShapeDtypeStruct((blocks, rows // 2, width), jnp.bfloat16),
         ],
         cost_estimate=pl.CostEstimate(
             flops=count * rows * rows * HEAD_WIDTH * 4,
@@ -141,78 +141,88 @@
     )(table, count.reshape(1), queries, keys, values, parts, logs)
 
 
-def merge_kernel(rep, own_ref, own_log_ref, part_ref, log_ref, keep_ref, send_ref):
-    half = keep_ref.shape[1]
-    own_log, first_log, second_log = own_log_ref[0], log_ref[0], log_ref[1]
-    top = jnp.maximum(own_log, jnp.maximum(first_log, second_log))
-    own_share = jnp.exp(own_log - top)
-    first_share = jnp.exp(first_log - top)
-    second_share = jnp.exp(second_log - top)
-    merged = (
-        own_share * own_ref[0]
-        + first_share * part_ref[0].astype(jnp.float32)
-        + second_share * part_ref[1].astype(jnp.float32)
-    ) / (own_share + first_share + second_share)
-    early = merged[:, :half].T.astype(keep_ref.dtype)
-    late = merged[:, half:].T.astype(keep_ref.dtype)
-    keep_ref[0] = jnp.where(rep[0] == 0, early, late)
-    send_ref[0] = jnp.where(rep[0] == 0, late, early)
-
-
-def merge(rep, own, own_log, parts, logs, blocks, full_width):
-    count, _, rows = own.shape
-    heads = count // blocks
+def merge_kernel(
+    rep, ready, count, own_hbm, own_log_hbm, part_hbm, log_hbm, keep_in, send_in, keep_hbm, send_hbm
+):
+    rows = own_hbm.shape[2]
     half = rows // 2
+    heads = send_hbm.shape[2] // HEAD_WIDTH
+
+    def combine(own_ref, own_log_ref, part_ref, log_ref, keep_ref, send_ref):
+        own_log, first_log, second_log = own_log_ref[0], log_ref[0], log_ref[1]
+        top = jnp.maximum(own_log, jnp.maximum(first_log, second_log))
+        own_share = jnp.exp(own_log - top)
+        first_share = jnp.exp(first_log - top)
+        second_share = jnp.exp(second_log - top)
+        merged = (
+            own_share * own_ref[0]
+            + first_share * part_ref[0].astype(jnp.float32)
+            + second_share * part_ref[1].astype(jnp.float32)
+        ) / (own_share + first_share + second_share)
+        early = merged[:, :half].T.astype(keep_ref.dtype)
+        late = merged[:, half:].T.astype(keep_ref.dtype)
+        keep_ref[0] = jnp.where(rep[0] == 0, early, late)
+        send_ref[0] = jnp.where(rep[0] == 0, late, early)
+
+    def place(n):
+        return lax.div(ready[n], heads), lax.rem(ready[n], heads)
+
+    pltpu.emit_pipeline(
+        combine,
+        grid=(count[0],),
+        in_specs=[
+            pl.BlockSpec((1, HEAD_WIDTH, rows), lambda n: (ready[n], 0, 0)),
+            pl.BlockSpec((1, 1, rows), lambda n: (ready[n], 0, 0)),
+            pl.BlockSpec((2, HEAD_WIDTH, rows), lambda n: (ready[n], 0, 0)),
+            pl.BlockSpec((2, 1, rows), lambda n: (ready[n], 0, 0)),
+        ],
+        out_specs=[
+            pl.BlockSpec(
+                (1, half, HEAD_WIDTH), lambda n: (place(n)[0], 0, rep[0] * heads + place(n)[1])
+            ),
+            pl.BlockSpec((1, half, HEAD_WIDTH), lambda n: (place(n)[0], 0, place(n)[1])),
+        ],
+    )(own_hbm, own_log_hbm, part_hbm, log_hbm, keep_hbm, send_hbm)
+
+
+def merge(rep, ready, count, own, own_log, parts, logs, keep, send):
+    heads, _, rows = own.shape
+    smem = pl.BlockSpec(memory_space=pltpu.SMEM)
+    anywhere = pl.BlockSpec(memory_space=pl.ANY)
     return pl.pallas_call(
         merge_kernel,
-        grid_spec=pltpu.PrefetchScalarGridSpec(
-            num_scalar_prefetch=1,
-            grid=(count,),
-            in_specs=[
-                pl.BlockSpec((1, HEAD_WIDTH, rows), lambda n, r: (n, 0, 0)),
-                pl.BlockSpec((1, 1, rows), lambda n, r: (n, 0, 0)),
-                pl.BlockSpec((2, HEAD_WIDTH, rows), lambda n, r: (n, 0, 0)),
-                pl.BlockSpec((2, 1, rows), lambda n, r: (n, 0, 0)),
-            ],
-            out_specs=[
-                pl.BlockSpec(
-                    (1, half, HEAD_WIDTH),
-                    lambda n, r: (lax.div(n, heads), 0, r[0] * heads + lax.rem(n, heads)),
-                ),
-                pl.BlockSpec((1, half, HEAD_WIDTH), lambda n, r: (lax.div(n, heads), 0, lax.rem(n, heads))),
-            ],
-        ),
+        in_specs=[smem] * 3 + [anywhere] * 6,
+        out_specs=[anywhere, anywhere],
         out_shape=[
-            jax.ShapeDtypeStruct((blocks, half, full_width), jnp.bfloat16),
-            jax.ShapeDtypeStruct((blocks, half, heads * HEAD_WIDTH), jnp.bfloat16),
-        ],
+            jax.ShapeDtypeStruct(keep.shape, keep.dtype),
+            jax.ShapeDtypeStruct(send.shape, send.dtype),
+        ],
+        input_output_aliases={7: 0, 8: 1},
         cost_estimate=pl.CostEstimate(
-            flops=count * rows * HEAD_WIDTH * 8,
-            transcendentals=count * rows * 3,
-            bytes_accessed=count * rows * HEAD_WIDTH * 10,
+            flops=heads * rows * HEAD_WIDTH * 8,
+            transcendentals=heads * rows * 3,
+            bytes_accessed=heads * rows * HEAD_WIDTH * 10,
         ),
         name="merge_parts",
-    )(rep, own, own_log, parts, logs)
+    )(rep.reshape(1), ready, count.reshape(1), own, own_log, parts, logs, keep, send)
 
 
 def ring_order(count):
     return list(range(0, count, 2)) + list(range(count - 1, 0, -2))
 
 
-def item_tables(holders, tiles, key_heads, blocks, heads, wanted, items):
-    mine = holders[None, :] == wanted[:, None]
-    place = jnp.cumsum(mine.astype(jnp.int32), axis=1) - 1
-    slot = jnp.arange(items)
-    chosen = mine[:, :, None] & (place[:, :, None] == slot[None, None, :])
-    columns = jnp.stack([jnp.arange(items), tiles, key_heads, blocks, heads])
+def compacted(mask, columns, spare):
+    place = jnp.cumsum(mask.astype(jnp.int32), axis=1) - 1
+    slot = jnp.arange(mask.shape[1])
+    chosen = mask[:, :, None] & (place[:, :, None] == slot[None, None, :])
     filled = jnp.sum(jnp.where(chosen[:, None], columns[None, :, :, None], 0), axis=2)
-    counts = jnp.sum(mine.astype(jnp.int32), axis=1)
-    spare = (slot[None, :] >= counts[:, None])[:, None, :] & (jnp.arange(5) == 0)[None, :, None]
-    return jnp.where(spare, items, filled), jnp.maximum(counts, 1)
+    counts = jnp.sum(mask.astype(jnp.int32), axis=1)
+    empty = (slot[None, :] >= counts[:, None])[:, None, :]
+    return jnp.where(empty, spare[None, :, None], filled), counts
 
 
 def body(queries, prefill_keys, prefill_values, context_keys, context_values, picks):
-    local_count, stack_height, full_width = queries.shape
+    local_count, _, full_width = queries.shape
     rep_size = lax.axis_size("rep")
     ctx_size = lax.axis_size("ctx")
     rep_index = lax.axis_index("rep")
@@ -235,17 +245,20 @@
     order = ring_order(ctx_size)
     onward = [(order[n], order[(n + 1) % ctx_size]) for n in range(ctx_size)]
     backward = [(target, source) for source, target in onward]
+
+    def hop(value, pairs):
+        return lax.ppermute(value, "ctx", pairs)
+
     shards = {0: own_shard}
     ahead, behind = own_shard, own_shard
-    for step in range(1, (ctx_size - 1) // 2 + 1):
-        ahead = tuple(lax.ppermute(part, "ctx", onward) for part in ahead)
-        behind = tuple(lax.ppermute(part, "ctx", backward) for part in behind)
+    full_steps = (ctx_size - 1) // 2
+    for step in range(1, full_steps + 1):
+        ahead = (hop(ahead[0], onward), hop(ahead[1], onward))
+        behind = (hop(behind[0], backward), hop(behind[1], backward))
         shards[-step], shards[step] = ahead, behind
     if ctx_size % 2 == 0:
-        shards[ctx_size // 2] = (
-            lax.ppermute(ahead[0], "ctx", onward),
-            lax.ppermute(behind[1], "ctx", backward),
-        )
+        step = full_steps + 1
+        shards[step] = (hop(ahead[0], onward), hop(behind[1], backward))
 
     other = rep_size - 1 - rep_index
 
@@ -272,29 +285,41 @@
     place = jnp.arange(items)
     head = place // 2 % heads
     holders = mine // blocks_here
-    tables, counts = item_tables(
-        holders,
-        mine - holders * blocks_here,
-        head // head_grouping,
-        place // (2 * heads),
-        head,
-        wanted,
-        items,
-    )
-
-    own, own_log, parts, logs = own_attention(
-        block_queries, block_keys, block_values, head_grouping
+    columns = jnp.stack(
+        [
+            place,
+            mine - holders * blocks_here,
+            head // head_grouping,
+            place // (2 * heads),
+            head,
+        ]
+    )
+    spare = jnp.array([items, 0, 0, 0, 0], jnp.int32)
+    tables, counts = compacted(holders[None, :] == wanted[:, None], columns, spare)
+    counts = jnp.maximum(counts, 1)
+    waiting = jnp.any(holders.reshape(-1, 2) == wanted[-1], axis=1)
+    ready, ready_counts = compacted(
+        jnp.stack([~waiting, waiting]),
+        jnp.arange(items // 2)[None],
+        jnp.zeros((1,), jnp.int32),
+    )
+    ready_counts = jnp.maximum(ready_counts, 1)
+
+    own, own_log, parts, logs, keep, send = own_attention(
+        block_queries, block_keys, block_values, head_grouping, full_width
     )
     for n, distance in enumerate(distances):
         keys, values = shards[distance]
-        parts, logs = pick_attention(
-            tables[n], counts[n], block_queries, keys, values, parts, logs
-        )
-    result, leaving = merge(
-        rep_index.reshape(1), own, own_log, parts, logs, local_count, full_width
-    )
-    arriving = lax.ppermute(leaving, "rep", swap)
-    return lax.dynamic_update_slice_in_dim(result, arriving, other * width, axis=2)
+        if n == len(distances) - 1:
+            keep, send = merge(
+                rep_index, ready[0, 0], ready_counts[0], own, own_log, parts, logs, keep, send
+            )
+        parts, logs = pick_attention(tables[n], counts[n], block_queries, keys, values, parts, logs)
+    keep, send = merge(
+        rep_index, ready[1, 0], ready_counts[1], own, own_log, parts, logs, keep, send
+    )
+    arriving = lax.ppermute(send, "rep", swap)
+    return lax.dynamic_update_slice_in_dim(keep, arriving, other * width, axis=2)
 
 
 def solution(mesh):

time: 220 us -> 224 us (1.018)
  Pallas kernels: 78.8 us -> 83.2 us
    pallas_call x1 -> x2, Pallas kernels: 11.6 us -> 15.2 us  [merge(): pl.pallas_call(merge_kernel, in_specs=[smem] * 3 + [anywhere] * 6, out_sp...]
    ppermute x15, waiting for transfers between devices: 99.1 us -> 95.9 us  [the longest x14 93.1 us: hop(): return lax.ppermute(value, 'ctx', pairs)]
  transfers between devices with their start and end apart: 18 -> 18, of which waited for: 8 -> 9; matrix products, arithmetic and copies ran while one was open for 9% -> 9% of each run, Pallas kernels for 26% -> 33%
where the time goes in v2:
time: 224 us; the launch traced here: 222 us
  waiting for transfers between devices  97.6 us (44%)
  Pallas kernels  83.2 us (37%)
  starting transfers between devices  16.6 us (7%)
  local copies, waits for them, and re-layouts  13.8 us (6%)
  other arithmetic  10.9 us (5%)
    ppermute x14, waiting for transfers between devices, hop(): return lax.ppermute(value, 'ctx', pairs)  93.1 us
    pallas_call x8, Pallas kernels, pick_attention(): pl.pallas_call(pick_kernel, in_specs=[smem, smem] + [anywhere] * 5, out_s...  51.9 us
    ppermute x14, starting transfers between devices, hop(): return lax.ppermute(value, 'ctx', pairs)  16.5 us
    pallas_call x1, Pallas kernels, own_attention(): pl.pallas_call(own_kernel, grid=(count,), in_specs=[query_spec, key_spec,...  16.2 us
    pallas_call x2, Pallas kernels, merge(): pl.pallas_call(merge_kernel, in_specs=[smem] * 3 + [anywhere] * 6, out_sp...  15.2 us
    select_n x3, other arithmetic, all_rows(): jnp.where(rep_index == 0, jnp.concatenate([kept, came], axis=1), jnp.conc...  8.09 us
    dynamic_slice x5, local copies, waits for them, and re-layouts, columns_of(): lax.dynamic_slice_in_dim(value, which * size, size, axis=value.ndim - 1)  6.48 us
  transfers between devices with their start and end apart: 18, of which 9 were waited for; matrix products, arithmetic and copies ran while one was open for 9% of the time, Pallas kernels for 33%

profile of v2, /device:TPU:0, one launch (start us, length us, event | category | flops | bytes accessed | tf_op | source)
XLA Modules:
  0.0 222.3 jit_solution(9801847547456375435)
XLA Ops:
  0.0 1.6 copy-done
  1.6 1.0 constant_dynamic-slice_fusion.k_hbm
  2.6 3.1 %collective-permute-start.3 = (bf16[2048,256]{1,0:T(8,128)(2,1)}, bf16[2048,256]{1,0:T(8,128)(2,1)}, u32[]{:S(2)}, u32[]{:S(2)}) collective-permute-start(bf16[2048,256]{1,0:T(8,128)(2,1)} %constant_dynamic-slice_fusion.k_hbm), channel_id=1, source_target_pairs={{0,8},{8,16},{16,24},{24,28},{28,20},{20,12},{12,4},{4,0},{1,9},{9... | collective-permute-start | bytes 3145736 | tf_op jit(solution)/shard_map/ppermute | solution.py:250
  5.8 2.1 collective-permute-start.14
  7.9 1.8 constant_dynamic-slice_fusion.4
  9.7 0.6 dynamic_slice.31
  10.3 0.7 compare_select_fusion
  11.0 0.6 gather_fusion
  11.6 0.6 slice.67
  12.2 0.7 compare_reduce_fusion
  14.3 15.7 %collective-permute-done.3.k_hbm = bf16[2048,256]{1,0:T(8,128)(2,1)} collective-permute-done((bf16[2048,256]{1,0:T(8,128)(2,1)}, bf16[2048,256]{1,0:T(8,128)(2,1)}, u32[]{:S(2)}, u32[]{:S(2)}) %collective-permute-start.3) | collective-permute-done | bytes 1048608 | tf_op jit(solution)/shard_map/ppermute | solution.py:250
  30.0 2.1 collective-permute-start.4
  32.1 21.1 %collective-permute-done.7.v_hbm = bf16[2048,256]{1,0:T(8,128)(2,1)} collective-permute-done((bf16[2048,256]{1,0:T(8,128)(2,1)S(1)}, bf16[2048,256]{1,0:T(8,128)(2,1)}, u32[]{:S(2)}, u32[]{:S(2)}) %collective-permute-start.7) | collective-permute-done | bytes 1048608 | tf_op jit(solution)/shard_map/ppermute | solution.py:250
  53.5 0.5 slice_bitcast_fusion.8
  54.1 1.8 collective-permute-start.15
  55.9 2.8 %constant_dynamic-slice_fusion.6 = (bf16[2,256,1024]{2,1,0:T(8,128)(2,1)S(1)}, bf16[2,256,1024]{2,1,0:T(8,128)(2,1)}) fusion(bf16[2,256,2048]{2,1,0:T(8,128)(2,1)} %param.10, s32[]{:T(128)S(6)} %select_n.169, s32[]{:T(128)S(6)} %select_n.170), kind=kLoop, calls=%fused_computation.34 | loop fusion | bytes 4194312 | tf_op jit(solution)/shard_map/dynamic_slice | solution.py:239
  58.7 0.3 collective-permute-start.12
  59.0 16.0 %collective-permute-done.4.k_hbm = bf16[2048,256]{1,0:T(8,128)(2,1)} collective-permute-done((bf16[2048,256]{1,0:T(8,128)(2,1)}, bf16[2048,256]{1,0:T(8,128)(2,1)}, u32[]{:S(2)}, u32[]{:S(2)}) %collective-permute-start.4) | collective-permute-done | bytes 1048608 | tf_op jit(solution)/shard_map/ppermute | solution.py:250
  75.0 2.1 collective-permute-start.5
  77.0 2.5 %collective-permute-done.8.v_hbm = bf16[2048,256]{1,0:T(8,128)(2,1)} collective-permute-done((bf16[2048,256]{1,0:T(8,128)(2,1)}, bf16[2048,256]{1,0:T(8,128)(2,1)}, u32[]{:S(2)}, u32[]{:S(2)}) %collective-permute-start.8) | collective-permute-done | bytes 1048608 | tf_op jit(solution)/shard_map/ppermute | solution.py:250
  79.8 0.8 constant_dynamic-slice_fusion.2
  80.9 1.7 collective-permute-done.2
  82.9 0.6 slice_bitcast_fusion
  83.6 13.8 %collective-permute-done.15.v_hbm = bf16[2048,256]{1,0:T(8,128)(2,1)} collective-permute-done((bf16[2048,256]{1,0:T(8,128)(2,1)}, bf16[2048,256]{1,0:T(8,128)(2,1)}, u32[]{:S(2)}, u32[]{:S(2)}) %collective-permute-start.15) | collective-permute-done | bytes 1048608 | tf_op jit(solution)/shard_map/ppermute | solution.py:250
  97.4 2.1 collective-permute-start.16
  99.5 0.7 fusion.6
  100.2 1.8 collective-permute-done.12.k_hbm
  102.0 0.3 collective-permute-start.13
  102.3 22.2 %collective-permute-done.9.v_hbm = bf16[2048,256]{1,0:T(8,128)(2,1)} collective-permute-done((bf16[2048,256]{1,0:T(8,128)(2,1)}, bf16[2048,256]{1,0:T(8,128)(2,1)}, u32[]{:S(2)}, u32[]{:S(2)}) %collective-permute-start.9) | collective-permute-done | bytes 1048608 | tf_op jit(solution)/shard_map/ppermute | solution.py:250
  124.4 0.3 collective-permute-start.10
  124.8 1.7 collective-permute-start.6
  126.5 0.6 fusion.5
  127.1 2.0 maximum_select_fusion.1.k_ref
  129.1 2.2 %maximum_select_fusion.2.v_ref = bf16[2,512,256]{2,1,0:T(8,128)(2,1)} fusion(bf16[2,256,256]{2,1,0:T(8,128)(2,1)} %collective-permute-done.2, bf16[2,256,256]{2,1,0:T(8,128)(2,1)} %get-tuple-element.63, pred[]{:T(512)S(6)} %eq.79), kind=kLoop, calls=%fused_computation.4 | loop fusion | flops 2359296 | bytes 1048577 | tf_op jit(solution)/shard_map/jit(_where)/select_n | solution.py:268
  131.3 3.9 %maximum_select_fusion.q_ref.q_hbm = bf16[2,512,1024]{2,1,0:T(8,128)(2,1)} fusion(bf16[2,256,1024]{2,1,0:T(8,128)(2,1)} %collective-permute-done, bf16[2,256,1024]{2,1,0:T(8,128)(2,1)S(1)} %get-tuple-element.61, pred[]{:T(512)S(6)} %eq.79), kind=kLoop, calls=%fused_computation.1 | loop fusion | flops 9437184 | bytes 4194305 | tf_op jit(solution)/shard_map/jit(_where)/select_n | solution.py:268
  135.2 16.2 %own_attention.1 = (f32[16,128,512]{2,1,0:T(8,128)}, f32[16,1,512]{2,1,0:T(1,128)}, bf16[34,128,512]{2,1,0:T(8,128)(2,1)}, f32[34,1,512]{2,1,0:T(1,128)}, bf16[2...) custom-call(bf16[2,512,1024]{2,1,0:T(8,128)(2,1)} %maximum_select_fusion.q_ref.q_hbm, ...), custom_call_target="tpu_custom_call" | custom-call | flops 2147483648 | bytes 8388608 | tf_op jit(solution)/shard_map/own_attention/pallas_call | solution.py:68
  151.3 6.3 %pick_attention.8 = (bf16[34,128,512]{2,1,0:T(8,128)(2,1)}, f32[34,1,512]{2,1,0:T(1,128)}) custom-call(s32[5,32]{1,0:T(8,128)} %get-tuple-element.67.table, s32[1]{0:T(128)} %get-tuple-element.81.count, bf16[2,512,1024]{2,1,0:T(8,128)(2,1)} %maximum_select_fusion.q_ref.q_hbm, ...), custom_call_target="tpu_custom_call", output_to_operand_aliasing={{0}: (5, {}), {1}: (6, {})} | custom-call | flops 536870912 | bytes 2097152 | tf_op jit(solution)/shard_map/pick_attention/pallas_call | solution.py:126
  157.7 8.1 %pick_attention.9 = (bf16[34,128,512]{2,1,0:T(8,128)(2,1)}, f32[34,1,512]{2,1,0:T(1,128)}) custom-call(s32[5,32]{1,0:T(8,128)} %get-tuple-element.68.table, s32[1]{0:T(128)} %get-tuple-element.82.count, bf16[2,512,1024]{2,1,0:T(8,128)(2,1)} %maximum_select_fusion.q_ref.q_hbm, ...), custom_call_target="tpu_custom_call", output_to_operand_aliasing={{0}: (5, {}), {1}: (6, {})} | custom-call | flops 536870912 | bytes 2097152 | tf_op jit(solution)/shard_map/pick_attention/pallas_call | solution.py:126
  165.8 6.3 %pick_attention.10 = (bf16[34,128,512]{2,1,0:T(8,128)(2,1)}, f32[34,1,512]{2,1,0:T(1,128)}) custom-call(s32[5,32]{1,0:T(8,128)} %get-tuple-element.69.table, s32[1]{0:T(128)} %get-tuple-element.83.count, bf16[2,512,1024]{2,1,0:T(8,128)(2,1)} %maximum_select_fusion.q_ref.q_hbm, ...), custom_call_target="tpu_custom_call", output_to_operand_aliasing={{0}: (5, {}), {1}: (6, {})} | custom-call | flops 536870912 | bytes 2097152 | tf_op jit(solution)/shard_map/pick_attention/pallas_call | solution.py:126
  172.2 6.4 %pick_attention.11 = (bf16[34,128,512]{2,1,0:T(8,128)(2,1)}, f32[34,1,512]{2,1,0:T(1,128)}) custom-call(s32[5,32]{1,0:T(8,128)} %get-tuple-element.70.table, s32[1]{0:T(128)} %get-tuple-element.84.count, bf16[2,512,1024]{2,1,0:T(8,128)(2,1)} %maximum_select_fusion.q_ref.q_hbm, ...), custom_call_target="tpu_custom_call", output_to_operand_aliasing={{0}: (5, {}), {1}: (6, {})} | custom-call | flops 536870912 | bytes 2097152 | tf_op jit(solution)/shard_map/pick_attention/pallas_call | solution.py:126
  178.5 3.8 %pick_attention.12 = (bf16[34,128,512]{2,1,0:T(8,128)(2,1)}, f32[34,1,512]{2,1,0:T(1,128)}) custom-call(s32[5,32]{1,0:T(8,128)} %get-tuple-element.71.table, s32[1]{0:T(128)} %get-tuple-element.85.count, bf16[2,512,1024]{2,1,0:T(8,128)(2,1)} %maximum_select_fusion.q_ref.q_hbm, ...), custom_call_target="tpu_custom_call", output_to_operand_aliasing={{0}: (5, {}), {1}: (6, {})} | custom-call | flops 536870912 | bytes 2097152 | tf_op jit(solution)/shard_map/pick_attention/pallas_call | solution.py:126
  182.3 10.7 %pick_attention.13 = (bf16[34,128,512]{2,1,0:T(8,128)(2,1)}, f32[34,1,512]{2,1,0:T(1,128)}) custom-call(s32[5,32]{1,0:T(8,128)} %get-tuple-element.72.table, s32[1]{0:T(128)} %get-tuple-element.86.count, bf16[2,512,1024]{2,1,0:T(8,128)(2,1)} %maximum_select_fusion.q_ref.q_hbm, ...), custom_call_target="tpu_custom_call", output_to_operand_aliasing={{0}: (5, {}), {1}: (6, {})} | custom-call | flops 536870912 | bytes 2097152 | tf_op jit(solution)/shard_map/pick_attention/pallas_call | solution.py:126
  193.0 4.6 %pick_attention.14 = (bf16[34,128,512]{2,1,0:T(8,128)(2,1)}, f32[34,1,512]{2,1,0:T(1,128)}) custom-call(s32[5,32]{1,0:T(8,128)} %get-tuple-element.73.table, s32[1]{0:T(128)} %get-tuple-element.87.count, bf16[2,512,1024]{2,1,0:T(8,128)(2,1)} %maximum_select_fusion.q_ref.q_hbm, ...), custom_call_target="tpu_custom_call", output_to_operand_aliasing={{0}: (5, {}), {1}: (6, {})} | custom-call | flops 536870912 | bytes 2097152 | tf_op jit(solution)/shard_map/pick_attention/pallas_call | solution.py:126
  197.6 10.8 %merge_parts.2 = (bf16[2,256,2048]{2,1,0:T(8,128)(2,1)}, bf16[2,256,1024]{2,1,0:T(8,128)(2,1)}) custom-call(s32[1]{0:T(128)} %bitcast.rep, s32[16]{0:T(128)} %get-tuple-element.75.ready, s32[1]{0:T(128)} %get-tuple-element.79.count, f32[16,128,512]{2,1,0:T(8,128)} %get-tuple-element.31.own_hbm, ...), custom_call_target="tpu_custom_call", output_to_operand_aliasing={{0}: (7, {}), {1}: (8, {})} | custom-call | flops 8388608 | bytes 10485760 | tf_op jit(solution)/shard_map/merge_parts/pallas_call | solution.py:192
  208.5 5.6 %pick_attention.15 = (bf16[34,128,512]{2,1,0:T(8,128)(2,1)}, f32[34,1,512]{2,1,0:T(1,128)}) custom-call(s32[5,32]{1,0:T(8,128)} %get-tuple-element.74.table, s32[1]{0:T(128)} %get-tuple-element.88.count, bf16[2,512,1024]{2,1,0:T(8,128)(2,1)} %maximum_select_fusion.q_ref.q_hbm, ...), custom_call_target="tpu_custom_call", output_to_operand_aliasing={{0}: (5, {}), {1}: (6, {})} | custom-call | flops 536870912 | bytes 2097152 | tf_op jit(solution)/shard_map/pick_attention/pallas_call | solution.py:126
  214.0 4.4 %merge_parts.3 = (bf16[2,256,2048]{2,1,0:T(8,128)(2,1)}, bf16[2,256,1024]{2,1,0:T(8,128)(2,1)}) custom-call(s32[1]{0:T(128)} %bitcast.rep, s32[16]{0:T(128)} %get-tuple-element.76.ready, s32[1]{0:T(128)} %get-tuple-element.80.count, f32[16,128,512]{2,1,0:T(8,128)} %get-tuple-element.31.own_hbm, ...), custom_call_target="tpu_custom_call", output_to_operand_aliasing={{0}: (7, {}), {1}: (8, {})} | custom-call | flops 8388608 | bytes 10485760 | tf_op jit(solution)/shard_map/merge_parts/pallas_call | solution.py:192
  218.4 2.9 %collective-permute-done.17 = bf16[2,256,1024]{2,1,0:T(8,128)(2,1)S(1)} collective-permute-done((bf16[2,256,1024]{2,1,0:T(8,128)(2,1)}, bf16[2,256,1024]{2,1,0:T(8,128)(2,1)S(1)}, u32[]{:S(2)}, u32[]{:S(2)}) %collective-permute-start.17) | collective-permute-done | bytes 1048608 | tf_op jit(solution)/shard_map/ppermute | solution.py:321
  221.3 1.0 constant_dynamic-update-slice_fusion
  (62 shorter events, 2.7 us)
Async XLA Ops:
  0.0 1.6 copy-start
  1.6 4.2 %copy-start.3 = (bf16[2048,512]{1,0:T(8,128)(2,1)S(1)}, bf16[2048,512]{1,0:T(8,128)(2,1)}, u32[]{:S(2)}) copy-start(bf16[2048,512]{1,0:T(8,128)(2,1)} %param.14) | copy-start | bytes 6291460
  2.6 7.1 %copy-start.7 = (s32[8]{0:T(128)S(1)}, s32[8]{0:T(128)}, u32[]{:S(2)}) copy-start(s32[8]{0:T(128)} %constant.119.clone) | copy-start | bytes 100
  2.6 7.7 %copy-start.6 = (s32[8]{0:T(128)S(1)}, s32[8]{0:T(128)}, u32[]{:S(2)}) copy-start(s32[8]{0:T(128)} %constant.121.clone) | copy-start | bytes 100
  2.6 8.3 %copy-start.1 = (s32[8]{0:T(128)S(1)}, s32[8]{0:T(128)}, u32[]{:S(2)}) copy-start(s32[8]{0:T(128)} %constant.120.clone) | copy-start | bytes 100
  2.6 9.6 %slice-start = ((s32[2,16,3]{1,0,2:T(2,128)}), s32[2,16,2]{1,0,2:T(2,128)S(1)}, s32[]{:S(2)}) async-start(s32[2,16,3]{1,0,2:T(2,128)} %param.15), calls=%async_computation | async-start | bytes 4096 | tf_op jit(solution)/shard_map/slice | solution.py:284
  2.6 27.4 %collective-permute-start.3 = (bf16[2048,256]{1,0:T(8,128)(2,1)}, bf16[2048,256]{1,0:T(8,128)(2,1)}, u32[]{:S(2)}, u32[]{:S(2)}) collective-permute-start(bf16[2048,256]{1,0:T(8,128)(2,1)} %constant_dynamic-slice_fusion.k_hbm), channel_id=1, source_target_pairs={{0,8},{8,16},{16,24},{24,28},{28,20},{20,12},{12,4},{4,0},{1,9},{9... | collective-permute-start | bytes 3145736 | tf_op jit(solution)/shard_map/ppermute | solution.py:250
  5.7 52.9 %collective-permute-start.11 = (bf16[2048,256]{1,0:T(8,128)(2,1)}, bf16[2048,256]{1,0:T(8,128)(2,1)}, u32[]{:S(2)}, u32[]{:S(2)}) collective-permute-start(bf16[2048,256]{1,0:T(8,128)(2,1)} %constant_dynamic-slice_fusion.k_hbm), channel_id=1, source_target_pairs={{8,0},{16,8},{24,16},{28,24},{20,28},{12,20},{4,12},{0,4},{9,1},{1... | collective-permute-start | bytes 3145736 | tf_op jit(solution)/shard_map/ppermute | solution.py:250
  5.8 48.3 %copy-start.2 = (bf16[2048,256]{1,0:T(8,128)(2,1)}, bf16[2048,256]{1,0:T(8,128)(2,1)S(1)}, u32[]{:S(2)}) copy-start(bf16[2048,256]{1,0:T(8,128)(2,1)S(1)} %constant_dynamic-slice_fusion.7.v_hbm) | copy-start | bytes 3145732
  5.8 48.3 %collective-permute-start.14 = (bf16[2048,256]{1,0:T(8,128)(2,1)S(1)}, bf16[2048,256]{1,0:T(8,128)(2,1)}, u32[]{:S(2)}, u32[]{:S(2)}) collective-permute-start(bf16[2048,256]{1,0:T(8,128)(2,1)S(1)} %constant_dynamic-slice_fusion.7.v_hbm), channel_id=1, source_target_pairs={{0,8},{8,16},{16,24},{24,28},{28,20},{20,12},{12,4},{4,0},{1,9},{9... | collective-permute-start | bytes 3145736 | tf_op jit(solution)/shard_map/ppermute | solution.py:250
  7.9 45.2 %collective-permute-start.7 = (bf16[2048,256]{1,0:T(8,128)(2,1)S(1)}, bf16[2048,256]{1,0:T(8,128)(2,1)}, u32[]{:S(2)}, u32[]{:S(2)}) collective-permute-start(bf16[2048,256]{1,0:T(8,128)(2,1)S(1)} %constant_dynamic-slice_fusion.7.v_hbm), channel_id=1, source_target_pairs={{8,0},{16,8},{24,16},{28,24},{20,28},{12,20},{4,12},{0,4},{9,1},{1... | collective-permute-start | bytes 3145736 | tf_op jit(solution)/shard_map/ppermute | solution.py:250
  9.7 71.0 %collective-permute-start.1 = (bf16[2,256,256]{2,1,0:T(8,128)(2,1)}, bf16[2,256,256]{2,1,0:T(8,128)(2,1)}, u32[]{:S(2)}, u32[]{:S(2)}) collective-permute-start(bf16[2,256,256]{2,1,0:T(8,128)(2,1)} %get-tuple-element.66), channel_id=1, source_target_pairs={{0,1},{1,0},{2,3},{3,2},{4,5},{5,4},{6,7},{7,6},{8,9},{9,8},{10,11... | collective-permute-start | bytes 786440 | tf_op jit(solution)/shard_map/ppermute | solution.py:267
  30.0 44.9 %collective-permute-start.4 = (bf16[2048,256]{1,0:T(8,128)(2,1)}, bf16[2048,256]{1,0:T(8,128)(2,1)}, u32[]{:S(2)}, u32[]{:S(2)}) collective-permute-start(bf16[2048,256]{1,0:T(8,128)(2,1)} %collective-permute-done.3.k_hbm), channel_id=1, source_target_pairs={{0,8},{8,16},{16,24},{24,28},{28,20},{20,12},{12,4},{4,0},{1,9},{9... | collective-permute-start | bytes 3145736 | tf_op jit(solution)/shard_map/ppermute | solution.py:250
  53.2 26.3 %collective-permute-start.8 = (bf16[2048,256]{1,0:T(8,128)(2,1)}, bf16[2048,256]{1,0:T(8,128)(2,1)}, u32[]{:S(2)}, u32[]{:S(2)}) collective-permute-start(bf16[2048,256]{1,0:T(8,128)(2,1)} %collective-permute-done.7.v_hbm), channel_id=1, source_target_pairs={{8,0},{16,8},{24,16},{28,24},{20,28},{12,20},{4,12},{0,4},{9,1},{1... | collective-permute-start | bytes 3145736 | tf_op jit(solution)/shard_map/ppermute | solution.py:250
  54.1 25.7 %copy-start.4 = (bf16[2,256,512]{2,1,0:T(8,128)(2,1)S(1)}, bf16[2,256,512]{2,1,0:T(8,128)(2,1)}, u32[]{:S(2)}) copy-start(bf16[2,256,512]{2,1,0:T(8,128)(2,1)} %param.12) | copy-start | bytes 1572868
  54.1 28.8 %copy-start.5 = (s32[5]{0:T(128)S(1)}, s32[5]{0:T(128)}, u32[]{:S(2)}) copy-start(s32[5]{0:T(128)} %constant.122.clone) | copy-start | bytes 64
  54.1 43.3 %collective-permute-start.15 = (bf16[2048,256]{1,0:T(8,128)(2,1)}, bf16[2048,256]{1,0:T(8,128)(2,1)}, u32[]{:S(2)}, u32[]{:S(2)}) collective-permute-start(bf16[2048,256]{1,0:T(8,128)(2,1)} %collective-permute-done.14.v_hbm), channel_id=1, source_target_pairs={{0,8},{8,16},{16,24},{24,28},{28,20},{20,12},{12,4},{4,0},{1,9},{9... | collective-permute-start | bytes 3145736 | tf_op jit(solution)/shard_map/ppermute | solution.py:250
  58.7 43.3 %collective-permute-start.12 = (bf16[2048,256]{1,0:T(8,128)(2,1)}, bf16[2048,256]{1,0:T(8,128)(2,1)}, u32[]{:S(2)}, u32[]{:S(2)}) collective-permute-start(bf16[2048,256]{1,0:T(8,128)(2,1)} %collective-permute-done.11.k_hbm), channel_id=1, source_target_pairs={{8,0},{16,8},{24,16},{28,24},{20,28},{12,20},{4,12},{0,4},{9,1},{1... | collective-permute-start | bytes 3145736 | tf_op jit(solution)/shard_map/ppermute | solution.py:250
  75.0 49.8 %collective-permute-start.5 = (bf16[2048,256]{1,0:T(8,128)(2,1)}, bf16[2048,256]{1,0:T(8,128)(2,1)}, u32[]{:S(2)}, u32[]{:S(2)}) collective-permute-start(bf16[2048,256]{1,0:T(8,128)(2,1)} %collective-permute-done.4.k_hbm), channel_id=1, source_target_pairs={{0,8},{8,16},{16,24},{24,28},{28,20},{20,12},{12,4},{4,0},{1,9},{9... | collective-permute-start | bytes 3145736 | tf_op jit(solution)/shard_map/ppermute | solution.py:250
  79.5 44.9 %collective-permute-start.9 = (bf16[2048,256]{1,0:T(8,128)(2,1)}, bf16[2048,256]{1,0:T(8,128)(2,1)}, u32[]{:S(2)}, u32[]{:S(2)}) collective-permute-start(bf16[2048,256]{1,0:T(8,128)(2,1)} %collective-permute-done.8.v_hbm), channel_id=1, source_target_pairs={{8,0},{16,8},{24,16},{28,24},{20,28},{12,20},{4,12},{0,4},{9,1},{1... | collective-permute-start | bytes 3145736 | tf_op jit(solution)/shard_map/ppermute | solution.py:250
  80.7 1.9 collective-permute-start.2
  82.5 48.8 %collective-permute-start = (bf16[2,256,1024]{2,1,0:T(8,128)(2,1)}, bf16[2,256,1024]{2,1,0:T(8,128)(2,1)}, u32[]{:S(2)}, u32[]{:S(2)}) collective-permute-start(bf16[2,256,1024]{2,1,0:T(8,128)(2,1)} %get-tuple-element.62), channel_id=1, source_target_pairs={{0,1},{1,0},{2,3},{3,2},{4,5},{5,4},{6,7},{7,6},{8,9},{9,8},{10,11... | collective-permute-start | bytes 3145736 | tf_op jit(solution)/shard_map/ppermute | solution.py:267
  97.4 84.9 %collective-permute-start.16 = (bf16[2048,256]{1,0:T(8,128)(2,1)}, bf16[2048,256]{1,0:T(8,128)(2,1)}, u32[]{:S(2)}, u32[]{:S(2)}) collective-permute-start(bf16[2048,256]{1,0:T(8,128)(2,1)} %collective-permute-done.15.v_hbm), channel_id=1, source_target_pairs={{0,8},{8,16},{16,24},{24,28},{28,20},{20,12},{12,4},{4,0},{1,9},{9... | collective-permute-start | bytes 3145736 | tf_op jit(solution)/shard_map/ppermute | solution.py:250
  102.0 91.1 %collective-permute-start.13 = (bf16[2048,256]{1,0:T(8,128)(2,1)}, bf16[2048,256]{1,0:T(8,128)(2,1)}, u32[]{:S(2)}, u32[]{:S(2)}) collective-permute-start(bf16[2048,256]{1,0:T(8,128)(2,1)} %collective-permute-done.12.k_hbm), channel_id=1, source_target_pairs={{8,0},{16,8},{24,16},{28,24},{20,28},{12,20},{4,12},{0,4},{9,1},{1... | collective-permute-start | bytes 3145736 | tf_op jit(solution)/shard_map/ppermute | solution.py:250
  124.4 84.0 %collective-permute-start.10 = (bf16[2048,256]{1,0:T(8,128)(2,1)}, bf16[2048,256]{1,0:T(8,128)(2,1)}, u32[]{:S(2)}, u32[]{:S(2)}) collective-permute-start(bf16[2048,256]{1,0:T(8,128)(2,1)} %collective-permute-done.9.v_hbm), channel_id=1, source_target_pairs={{8,0},{16,8},{24,16},{28,24},{20,28},{12,20},{4,12},{0,4},{9,1},{1... | collective-permute-start | bytes 3145736 | tf_op jit(solution)/shard_map/ppermute | solution.py:250
  124.8 83.7 %collective-permute-start.6 = (bf16[2048,256]{1,0:T(8,128)(2,1)}, bf16[2048,256]{1,0:T(8,128)(2,1)}, u32[]{:S(2)}, u32[]{:S(2)}) collective-permute-start(bf16[2048,256]{1,0:T(8,128)(2,1)} %collective-permute-done.5.k_hbm), channel_id=1, source_target_pairs={{0,8},{8,16},{16,24},{24,28},{28,20},{20,12},{12,4},{4,0},{1,9},{9... | collective-permute-start | bytes 3145736 | tf_op jit(solution)/shard_map/ppermute | solution.py:250
  218.4 2.9 %collective-permute-start.17 = (bf16[2,256,1024]{2,1,0:T(8,128)(2,1)}, bf16[2,256,1024]{2,1,0:T(8,128)(2,1)S(1)}, u32[]{:S(2)}, u32[]{:S(2)}) collective-permute-start(bf16[2,256,1024]{2,1,0:T(8,128)(2,1)} %get-tuple-element.56), channel_id=1, source_target_pairs={{0,1},{1,0},{2,3},{3,2},{4,5},{5,4},{6,7},{7,6},{8,9},{9,8},{10,11... | collective-permute-start | bytes 3145736 | tf_op jit(solution)/shard_map/ppermute | solution.py:321

commit v3 on v2

--- a/solution.py
+++ b/solution.py
@@ -11,6 +11,7 @@
 SCALE = HEAD_WIDTH ** (-0.5)
 LOG2E = 1.4426950408889634
 NEGATIVE = -1e30
+PIECES = 2
 
 
 def scores_by_key(keys, queries):
@@ -91,19 +92,29 @@
     )(queries, keys, values)
 
 
+def attend_tile(queries, keys, values):
+    scores = scores_by_key(keys, queries)
+    highest = jnp.max(scores, axis=0, keepdims=True)
+    weights = jnp.exp2((scores - highest) * (SCALE * LOG2E))
+    total = jnp.sum(weights, axis=0, keepdims=True)
+    part = (mix_by_width(values, weights) / total).astype(jnp.bfloat16)
+    return part, highest * SCALE + jnp.log(total)
+
+
+def when_any(count, pipeline, *arrays):
+    @pl.when(count > 0)
+    def _():
+        pipeline(*arrays)
+
+
 def pick_kernel(table, count, q_hbm, k_hbm, v_hbm, part_in, log_in, part_hbm, log_hbm):
     rows = q_hbm.shape[1]
 
     def attend(q_ref, k_ref, v_ref, part_ref, log_ref):
-        scores = scores_by_key(k_ref[...], q_ref[0])
-        highest = jnp.max(scores, axis=0, keepdims=True)
-        weights = jnp.exp2((scores - highest) * (SCALE * LOG2E))
-        total = jnp.sum(weights, axis=0, keepdims=True)
-        part_ref[0] = (mix_by_width(v_ref[...], weights) / total).astype(part_ref.dtype)
-        log_ref[0] = highest * SCALE + jnp.log(total)
+        part_ref[0], log_ref[0] = attend_tile(q_ref[0], k_ref[...], v_ref[...])
 
     tile = pl.BlockSpec((BLOCK_TOKENS, HEAD_WIDTH), lambda n: (table[1, n], table[2, n]))
-    pltpu.emit_pipeline(
+    pipeline = pltpu.emit_pipeline(
         attend,
         grid=(count[0],),
         in_specs=[
@@ -115,7 +126,8 @@
             pl.BlockSpec((1, HEAD_WIDTH, rows), lambda n: (table[0, n], 0, 0)),
             pl.BlockSpec((1, 1, rows), lambda n: (table[0, n], 0, 0)),
         ],
-    )(q_hbm, k_hbm, v_hbm, part_hbm, log_hbm)
+    )
+    when_any(count[0], pipeline, q_hbm, k_hbm, v_hbm, part_hbm, log_hbm)
 
 
 def pick_attention(table, count, queries, keys, values, parts, logs):
@@ -141,6 +153,22 @@
     )(table, count.reshape(1), queries, keys, values, parts, logs)
 
 
+def merged_rows(rep, own, own_log, first, first_log, second, second_log):
+    half = own.shape[1] // 2
+    top = jnp.maximum(own_log, jnp.maximum(first_log, second_log))
+    own_share = jnp.exp(own_log - top)
+    first_share = jnp.exp(first_log - top)
+    second_share = jnp.exp(second_log - top)
+    merged = (
+        own_share * own
+        + first_share * first.astype(jnp.float32)
+        + second_share * second.astype(jnp.float32)
+    ) / (own_share + first_share + second_share)
+    early = merged[:, :half].T.astype(jnp.bfloat16)
+    late = merged[:, half:].T.astype(jnp.bfloat16)
+    return jnp.where(rep == 0, early, late), jnp.where(rep == 0, late, early)
+
+
 def merge_kernel(
     rep, ready, count, own_hbm, own_log_hbm, part_hbm, log_hbm, keep_in, send_in, keep_hbm, send_hbm
 ):
@@ -149,25 +177,14 @@
     heads = send_hbm.shape[2] // HEAD_WIDTH
 
     def combine(own_ref, own_log_ref, part_ref, log_ref, keep_ref, send_ref):
-        own_log, first_log, second_log = own_log_ref[0], log_ref[0], log_ref[1]
-        top = jnp.maximum(own_log, jnp.maximum(first_log, second_log))
-        own_share = jnp.exp(own_log - top)
-        first_share = jnp.exp(first_log - top)
-        second_share = jnp.exp(second_log - top)
-        merged = (
-            own_share * own_ref[0]
-            + first_share * part_ref[0].astype(jnp.float32)
-            + second_share * part_ref[1].astype(jnp.float32)
-        ) / (own_share + first_share + second_share)
-        early = merged[:, :half].T.astype(keep_ref.dtype)
-        late = merged[:, half:].T.astype(keep_ref.dtype)
-        keep_ref[0] = jnp.where(rep[0] == 0, early, late)
-        send_ref[0] = jnp.where(rep[0] == 0, late, early)
+        keep_ref[0], send_ref[0] = merged_rows(
+            rep[0], own_ref[0], own_log_ref[0], part_ref[0], log_ref[0], part_ref[1], log_ref[1]
+        )
 
     def place(n):
         return lax.div(ready[n], heads), lax.rem(ready[n], heads)
 
-    pltpu.emit_pipeline(
+    pipeline = pltpu.emit_pipeline(
         combine,
         grid=(count[0],),
         in_specs=[
@@ -182,7 +199,8 @@
             ),
             pl.BlockSpec((1, half, HEAD_WIDTH), lambda n: (place(n)[0], 0, place(n)[1])),
         ],
-    )(own_hbm, own_log_hbm, part_hbm, log_hbm, keep_hbm, send_hbm)
+    )
+    when_any(count[0], pipeline, own_hbm, own_log_hbm, part_hbm, log_hbm, keep_hbm, send_hbm)
 
 
 def merge(rep, ready, count, own, own_log, parts, logs, keep, send):
@@ -205,6 +223,143 @@
         ),
         name="merge_parts",
     )(rep.reshape(1), ready, count.reshape(1), own, own_log, parts, logs, keep, send)
+
+
+def final_kernel(
+    rep,
+    table,
+    count,
+    q_hbm,
+    k_hbm,
+    v_hbm,
+    own_hbm,
+    own_log_hbm,
+    part_in,
+    log_in,
+    keep_in,
+    send_in,
+    part_hbm,
+    log_hbm,
+    keep_hbm,
+    send_hbm,
+    step,
+    held,
+    held_log,
+):
+    rows = q_hbm.shape[1]
+    half = rows // 2
+    heads = send_hbm.shape[2] // HEAD_WIDTH
+    step[0] = 0
+
+    def attend(
+        q_ref,
+        k_ref,
+        v_ref,
+        own_ref,
+        own_log_ref,
+        other_ref,
+        other_log_ref,
+        part_ref,
+        log_ref,
+        keep_ref,
+        send_ref,
+    ):
+        part, log = attend_tile(q_ref[0], k_ref[...], v_ref[...])
+        second = table[6, step[0]] == 1
+        other = jnp.where(second, held[...], other_ref[0])
+        other_log = jnp.where(second, held_log[...], other_log_ref[0])
+        keep_ref[0], send_ref[0] = merged_rows(
+            rep[0], own_ref[0], own_log_ref[0], part, log, other, other_log
+        )
+        part_ref[0], log_ref[0] = part, log
+        held[...], held_log[...] = part, log
+        step[0] += 1
+
+    tile = pl.BlockSpec((BLOCK_TOKENS, HEAD_WIDTH), lambda n: (table[1, n], table[2, n]))
+    wide = (1, HEAD_WIDTH, rows)
+    pipeline = pltpu.emit_pipeline(
+        attend,
+        grid=(count[0],),
+        in_specs=[
+            pl.BlockSpec((1, rows, HEAD_WIDTH), lambda n: (table[3, n], 0, table[4, n])),
+            tile,
+            tile,
+            pl.BlockSpec(wide, lambda n: (table[3, n] * heads + table[4, n], 0, 0)),
+            pl.BlockSpec((1, 1, rows), lambda n: (table[3, n] * heads + table[4, n], 0, 0)),
+            pl.BlockSpec(wide, lambda n: (table[5, n], 0, 0)),
+            pl.BlockSpec((1, 1, rows), lambda n: (table[5, n], 0, 0)),
+        ],
+        out_specs=[
+            pl.BlockSpec(wide, lambda n: (table[0, n], 0, 0)),
+            pl.BlockSpec((1, 1, rows), lambda n: (table[0, n], 0, 0)),
+            pl.BlockSpec(
+                (1, half, HEAD_WIDTH), lambda n: (table[3, n], 0, rep[0] * heads + table[4, n])
+            ),
+            pl.BlockSpec((1, half, HEAD_WIDTH), lambda n: (table[3, n], 0, table[4, n])),
+        ],
+    )
+    when_any(
+        count[0],
+        pipeline,
+        q_hbm,
+        k_hbm,
+        v_hbm,
+        own_hbm,
+        own_log_hbm,
+        part_hbm,
+        log_hbm,
+        part_hbm,
+        log_hbm,
+        keep_hbm,
+        send_hbm,
+    )
+
+
+def final_attention(rep, table, count, queries, keys, values, own, own_log, state):
+    rows = queries.shape[1]
+    expected = own.shape[0] // 8
+    smem = pl.BlockSpec(memory_space=pltpu.SMEM)
+    anywhere = pl.BlockSpec(memory_space=pl.ANY)
+    return pl.pallas_call(
+        final_kernel,
+        in_specs=[smem] * 3 + [anywhere] * 9,
+        out_specs=[anywhere] * 4,
+        out_shape=[jax.ShapeDtypeStruct(value.shape, value.dtype) for value in state],
+        scratch_shapes=[
+            pltpu.SMEM((1,), jnp.int32),
+            pltpu.VMEM((HEAD_WIDTH, rows), jnp.bfloat16),
+            pltpu.VMEM((1, rows), jnp.float32),
+        ],
+        input_output_aliases={8: 0, 9: 1, 10: 2, 11: 3},
+        cost_estimate=pl.CostEstimate(
+            flops=expected * rows * BLOCK_TOKENS * HEAD_WIDTH * 4,
+            transcendentals=expected * rows * BLOCK_TOKENS,
+            bytes_accessed=expected * rows * HEAD_WIDTH * 18,
+        ),
+        name="final_attention",
+    )(rep.reshape(1), table, count.reshape(1), queries, keys, values, own, own_log, *state)
+
+
+def half_kernel(rep, from_ref, to_ref):
+    to_ref[...] = from_ref[...]
+
+
+def columns_kept(value, rep, size):
+    rows = value.shape[0]
+    return pl.pallas_call(
+        half_kernel,
+        grid_spec=pltpu.PrefetchScalarGridSpec(
+            num_scalar_prefetch=1,
+            grid=(rows // BLOCK_TOKENS,),
+            in_specs=[pl.BlockSpec((BLOCK_TOKENS, size), lambda n, r: (n, r[0]))],
+            out_specs=pl.BlockSpec((BLOCK_TOKENS, size), lambda n, r: (n, 0)),
+        ),
+        out_shape=jax.ShapeDtypeStruct((rows, size), value.dtype),
+        cost_estimate=pl.CostEstimate(
+            flops=0, transcendentals=0, bytes_accessed=rows * size * 4
+        ),
+        name="columns_kept",
+    )(rep.reshape(1), value)
 
 
 def ring_order(count):
@@ -239,8 +394,8 @@
         return lax.dynamic_slice_in_dim(value, which * size, size, axis=value.ndim - 1)
 
     own_shard = (
-        columns_of(context_keys, rep_index, key_width),
-        columns_of(context_values, rep_index, key_width),
+        columns_kept(context_keys, rep_index, key_width),
+        columns_kept(context_values, rep_index, key_width),
     )
     order = ring_order(ctx_size)
     onward = [(order[n], order[(n + 1) % ctx_size]) for n in range(ctx_size)]
@@ -256,9 +411,15 @@
         ahead = (hop(ahead[0], onward), hop(ahead[1], onward))
         behind = (hop(behind[0], backward), hop(behind[1], backward))
         shards[-step], shards[step] = ahead, behind
-    if ctx_size % 2 == 0:
-        step = full_steps + 1
-        shards[step] = (hop(ahead[0], onward), hop(behind[1], backward))
+    step = full_steps + 1
+    piece = context_keys.shape[0] // PIECES
+    last_pieces = [
+        (
+            hop(ahead[0][n * piece : (n + 1) * piece], onward),
+            hop(behind[1][n * piece : (n + 1) * piece], backward),
+        )
+        for n in range(PIECES)
+    ]
 
     other = rep_size - 1 - rep_index
 
@@ -280,46 +441,68 @@
         position_of[device] = position
     here = jnp.array(position_of, jnp.int32)[ctx_index]
     distances = sorted(shards, key=abs)
-    wanted = jnp.array(order, jnp.int32)[(here + jnp.array(distances, jnp.int32)) % ctx_size]
+    wanted = jnp.array(order, jnp.int32)[
+        (here + jnp.array([*distances, ctx_size // 2], jnp.int32)) % ctx_size
+    ]
     mine = lax.dynamic_slice_in_dim(picks[:, :, :2], rep_index * heads, heads, axis=1).reshape(-1)
     place = jnp.arange(items)
     head = place // 2 % heads
     holders = mine // blocks_here
-    columns = jnp.stack(
-        [
-            place,
-            mine - holders * blocks_here,
-            head // head_grouping,
-            place // (2 * heads),
-            head,
-        ]
-    )
-    spare = jnp.array([items, 0, 0, 0, 0], jnp.int32)
-    tables, counts = compacted(holders[None, :] == wanted[:, None], columns, spare)
-    counts = jnp.maximum(counts, 1)
-    waiting = jnp.any(holders.reshape(-1, 2) == wanted[-1], axis=1)
+    tile = mine - holders * blocks_here
+    facts = [head // head_grouping, place // (2 * heads), head]
+    tables, counts = compacted(
+        holders[None, :] == wanted[:-1, None],
+        jnp.stack([place, tile, *facts]),
+        jnp.zeros((5,), jnp.int32),
+    )
+    tiles = blocks_here // PIECES
+    waits = holders == wanted[-1]
+    inside = waits[None, :] & (tile[None, :] // tiles == jnp.arange(PIECES)[:, None])
+    both = jnp.any(jnp.all(inside.reshape(PIECES, -1, 2), axis=2), axis=0)
+    both = jnp.stack([both, both], axis=1).reshape(-1)
+    last_tables, last_counts = compacted(
+        inside,
+        jnp.stack(
+            [
+                place,
+                tile % tiles,
+                *facts,
+                jnp.where(both, items, place + 1 - 2 * (place % 2)),
+                jnp.where(both, place % 2, 0),
+            ]
+        ),
+        jnp.zeros((7,), jnp.int32),
+    )
     ready, ready_counts = compacted(
-        jnp.stack([~waiting, waiting]),
+        ~jnp.any(waits.reshape(1, -1, 2), axis=2),
         jnp.arange(items // 2)[None],
         jnp.zeros((1,), jnp.int32),
     )
-    ready_counts = jnp.maximum(ready_counts, 1)
 
     own, own_log, parts, logs, keep, send = own_attention(
         block_queries, block_keys, block_values, head_grouping, full_width
     )
     for n, distance in enumerate(distances):
         keys, values = shards[distance]
-        if n == len(distances) - 1:
-            keep, send = merge(
-                rep_index, ready[0, 0], ready_counts[0], own, own_log, parts, logs, keep, send
-            )
         parts, logs = pick_attention(tables[n], counts[n], block_queries, keys, values, parts, logs)
     keep, send = merge(
-        rep_index, ready[1, 0], ready_counts[1], own, own_log, parts, logs, keep, send
-    )
-    arriving = lax.ppermute(send, "rep", swap)
-    return lax.dynamic_update_slice_in_dim(keep, arriving, other * width, axis=2)
+        rep_index, ready[0, 0], ready_counts[0], own, own_log, parts, logs, keep, send
+    )
+    state = (parts, logs, keep, send)
+    for n, (keys, values) in enumerate(last_pieces):
+        state = final_attention(
+            rep_index,
+            last_tables[n],
+            last_counts[n],
+            block_queries,
+            keys,
+            values,
+            own,
+            own_log,
+            state,
+        )
+    arriving = lax.ppermute(state[3], "rep", swap)
+    return lax.dynamic_update_slice_in_dim(state[2], arriving, other * width, axis=2)
 
 
 def solution(mesh):

time: 224 us -> 234 us (1.045)
  starting transfers between devices: 16.6 us -> 20.9 us
  Pallas kernels: 83.2 us -> 86.7 us
  other arithmetic: 10.9 us -> 14.4 us
    pallas_call x0 -> x4, Pallas kernels: none -> 15.9 us  [the longest x2 9.21 us: final_attention(): pl.pallas_call(final_kernel, in_specs=[smem] * 3 + [anywhere] * 9, out_sp...]
    pallas_call x8 -> x7, Pallas kernels: 51.9 us -> 43.7 us  [pick_attention(): pl.pallas_call(pick_kernel, in_specs=[smem, smem] + [anywhere] * 5, out_s...]
    pallas_call x2 -> x1, Pallas kernels: 15.2 us -> 10.9 us  [merge(): pl.pallas_call(merge_kernel, in_specs=[smem] * 3 + [anywhere] * 6, out_sp...]
    ppermute x14 -> x16, starting transfers between devices: 16.5 us -> 20.6 us  [hop(): return lax.ppermute(value, 'ctx', pairs)]
    dynamic_slice x5 -> x3, local copies, waits for them, and re-layouts: 6.48 us -> 2.74 us  [columns_of(): lax.dynamic_slice_in_dim(value, which * size, size, axis=value.ndim - 1)]
    ppermute x14 -> x16, waiting for transfers between devices: 93.1 us -> 92.9 us  [hop(): return lax.ppermute(value, 'ctx', pairs)]
  transfers between devices with their start and end apart: 18 -> 20, of which waited for: 9 -> 9; matrix products, arithmetic and copies ran while one was open for 9% -> 11% of each run, Pallas kernels for 33% -> 34%
where the time goes in v3:
time: 234 us; the launch traced here: 231 us
  waiting for transfers between devices  95.8 us (41%)
  Pallas kernels  86.7 us (37%)
  starting transfers between devices  20.9 us (9%)
  other arithmetic  14.4 us (6%)
  local copies, waits for them, and re-layouts  13 us (6%)
    ppermute x16, waiting for transfers between devices, hop(): return lax.ppermute(value, 'ctx', pairs)  92.9 us
    pallas_call x7, Pallas kernels, pick_attention(): pl.pallas_call(pick_kernel, in_specs=[smem, smem] + [anywhere] * 5, out_s...  43.7 us
    ppermute x16, starting transfers between devices, hop(): return lax.ppermute(value, 'ctx', pairs)  20.6 us
    pallas_call x1, Pallas kernels, own_attention(): pl.pallas_call(own_kernel, grid=(count,), in_specs=[query_spec, key_spec,...  16.2 us
    pallas_call x1, Pallas kernels, merge(): pl.pallas_call(merge_kernel, in_specs=[smem] * 3 + [anywhere] * 6, out_sp...  10.9 us
    pallas_call x2, Pallas kernels, final_attention(): pl.pallas_call(final_kernel, in_specs=[smem] * 3 + [anywhere] * 9, out_sp...  9.21 us
    select_n x3, other arithmetic, all_rows(): jnp.where(rep_index == 0, jnp.concatenate([kept, came], axis=1), jnp.conc...  8.1 us
    pallas_call x2, Pallas kernels, columns_kept(): pl.pallas_call(half_kernel, grid_spec=pltpu.PrefetchScalarGridSpec(num_sc...  6.72 us
  transfers between devices with their start and end apart: 20, of which 9 were waited for; matrix products, arithmetic and copies ran while one was open for 11% of the time, Pallas kernels for 34%

profile of v3, /device:TPU:0, one launch (start us, length us, event | category | flops | bytes accessed | tf_op | source)
XLA Modules:
  0.0 230.9 jit_solution(13179692587168264186)
XLA Ops:
  0.0 3.4 %columns_kept.2.k_hbm = bf16[2048,256]{1,0:T(8,128)(2,1)} custom-call(s32[1]{0:T(128)} %bitcast.rep, bf16[2048,512]{1,0:T(8,128)(2,1)} %from_ref.2), custom_call_target="tpu_custom_call" | custom-call | bytes 2097152 | tf_op jit(solution)/shard_map/columns_kept/pallas_call | solution.py:349
  3.4 3.1 %collective-permute-start.1 = (bf16[2048,256]{1,0:T(8,128)(2,1)}, bf16[2048,256]{1,0:T(8,128)(2,1)}, u32[]{:S(2)}, u32[]{:S(2)}) collective-permute-start(bf16[2048,256]{1,0:T(8,128)(2,1)} %columns_kept.2.k_hbm), channel_id=1, source_target_pairs={{0,8},{8,16},{16,24},{24,28},{28,20},{20,12},{12,4},{4,0},{1,9},{9... | collective-permute-start | bytes 3145736 | tf_op jit(solution)/shard_map/ppermute | solution.py:405
  6.5 3.4 %columns_kept.3.v_hbm = bf16[2048,256]{1,0:T(8,128)(2,1)} custom-call(s32[1]{0:T(128)} %bitcast.rep, bf16[2048,512]{1,0:T(8,128)(2,1)} %from_ref.3), custom_call_target="tpu_custom_call" | custom-call | bytes 2097152 | tf_op jit(solution)/shard_map/columns_kept/pallas_call | solution.py:349
  9.9 2.0 collective-permute-start.16
  11.9 0.7 constant_dynamic-slice_fusion.3
  13.2 0.7 compare_select_fusion
  15.1 0.7 compare_reduce_fusion
  16.3 0.7 broadcast_compare_fusion.2
  17.2 0.7 broadcast_compare_fusion.1
  19.5 0.8 constant_dynamic-slice_fusion.1
  20.6 10.1 %collective-permute-done.1.k_hbm = bf16[2048,256]{1,0:T(8,128)(2,1)} collective-permute-done((bf16[2048,256]{1,0:T(8,128)(2,1)}, bf16[2048,256]{1,0:T(8,128)(2,1)}, u32[]{:S(2)}, u32[]{:S(2)}) %collective-permute-start.1) | collective-permute-done | bytes 1048608 | tf_op jit(solution)/shard_map/ppermute | solution.py:405
  30.8 2.1 collective-permute-start.2
  33.1 20.8 %collective-permute-done.5.v_hbm = bf16[2048,256]{1,0:T(8,128)(2,1)} collective-permute-done((bf16[2048,256]{1,0:T(8,128)(2,1)}, bf16[2048,256]{1,0:T(8,128)(2,1)}, u32[]{:S(2)}, u32[]{:S(2)}) %collective-permute-start.5) | collective-permute-done | bytes 1048608 | tf_op jit(solution)/shard_map/ppermute | solution.py:405
  54.2 1.2 constant_dynamic-slice_fusion.5
  55.4 1.8 collective-permute-start.17
  58.2 0.7 collective-permute-start.14
  59.2 16.5 %collective-permute-done.2.k_hbm = bf16[2048,256]{1,0:T(8,128)(2,1)} collective-permute-done((bf16[2048,256]{1,0:T(8,128)(2,1)}, bf16[2048,256]{1,0:T(8,128)(2,1)}, u32[]{:S(2)}, u32[]{:S(2)}) %collective-permute-start.2) | collective-permute-done | bytes 1048608 | tf_op jit(solution)/shard_map/ppermute | solution.py:405
  75.7 2.1 collective-permute-start.3
  79.0 1.2 collective-permute-done.6.v_hbm
  80.6 1.1 compare_select_fusion.7.ready
  81.7 16.5 %collective-permute-done.17.v_hbm = bf16[2048,256]{1,0:T(8,128)(2,1)} collective-permute-done((bf16[2048,256]{1,0:T(8,128)(2,1)}, bf16[2048,256]{1,0:T(8,128)(2,1)}, u32[]{:S(2)}, u32[]{:S(2)}) %collective-permute-start.17) | collective-permute-done | bytes 1048608 | tf_op jit(solution)/shard_map/ppermute | solution.py:405
  98.2 2.1 collective-permute-start.18
  100.8 2.0 maximum_select_fusion.1.k_ref
  102.8 2.1 maximum_select_fusion.2.v_ref
  105.0 4.0 %maximum_select_fusion.q_ref.q_hbm = bf16[2,512,1024]{2,1,0:T(8,128)(2,1)} fusion(bf16[2,256,1024]{2,1,0:T(8,128)(2,1)} %collective-permute-done, bf16[2,256,1024]{2,1,0:T(8,128)(2,1)S(1)} %get-tuple-element.71, pred[]{:T(512)S(6)} %eq.152), kind=kLoop, calls=%fused_computation.1 | loop fusion | flops 9437184 | bytes 4194305 | tf_op jit(solution)/shard_map/jit(_where)/select_n | solution.py:429
  109.0 11.6 %collective-permute-done.3.k_hbm = bf16[2048,256]{1,0:T(8,128)(2,1)S(1)} collective-permute-done((bf16[2048,256]{1,0:T(8,128)(2,1)}, bf16[2048,256]{1,0:T(8,128)(2,1)S(1)}, u32[]{:S(2)}, u32[]{:S(2)}) %collective-permute-start.3) | collective-permute-done | bytes 1048608 | tf_op jit(solution)/shard_map/ppermute | solution.py:405
  120.5 1.2 fusion.8
  121.7 2.1 collective-permute-start.11
  123.8 1.3 collective-permute-done.7.v_hbm
  125.1 1.1 fusion.7
  126.5 1.7 collective-permute-start.4
  128.2 14.9 %collective-permute-done.18.v_hbm = bf16[2048,256]{1,0:T(8,128)(2,1)} collective-permute-done((bf16[2048,256]{1,0:T(8,128)(2,1)}, bf16[2048,256]{1,0:T(8,128)(2,1)}, u32[]{:S(2)}, u32[]{:S(2)}) %collective-permute-start.18) | collective-permute-done | bytes 1048608 | tf_op jit(solution)/shard_map/ppermute | solution.py:405
  143.1 2.0 collective-permute-start.8
  145.1 16.2 %own_attention.1 = (f32[16,128,512]{2,1,0:T(8,128)}, f32[16,1,512]{2,1,0:T(1,128)}, bf16[34,128,512]{2,1,0:T(8,128)(2,1)}, f32[34,1,512]{2,1,0:T(1,128)}, bf16[2...) custom-call(bf16[2,512,1024]{2,1,0:T(8,128)(2,1)} %maximum_select_fusion.q_ref.q_hbm, ...), custom_call_target="tpu_custom_call" | custom-call | flops 2147483648 | bytes 8388608 | tf_op jit(solution)/shard_map/own_attention/pallas_call | solution.py:69
  161.3 6.3 %pick_attention.7 = (bf16[34,128,512]{2,1,0:T(8,128)(2,1)}, f32[34,1,512]{2,1,0:T(1,128)}) custom-call(s32[5,32]{1,0:T(8,128)} %get-tuple-element.81.table, s32[1]{0:T(128)} %get-tuple-element.94.count, bf16[2,512,1024]{2,1,0:T(8,128)(2,1)} %maximum_select_fusion.q_ref.q_hbm, ...), custom_call_target="tpu_custom_call", output_to_operand_aliasing={{0}: (5, {}), {1}: (6, {})} | custom-call | flops 536870912 | bytes 2097152 | tf_op jit(solution)/shard_map/pick_attention/pallas_call | solution.py:138
  167.6 8.1 %pick_attention.8 = (bf16[34,128,512]{2,1,0:T(8,128)(2,1)}, f32[34,1,512]{2,1,0:T(1,128)}) custom-call(s32[5,32]{1,0:T(8,128)} %get-tuple-element.82.table, s32[1]{0:T(128)} %get-tuple-element.95.count, bf16[2,512,1024]{2,1,0:T(8,128)(2,1)} %maximum_select_fusion.q_ref.q_hbm, ...), custom_call_target="tpu_custom_call", output_to_operand_aliasing={{0}: (5, {}), {1}: (6, {})} | custom-call | flops 536870912 | bytes 2097152 | tf_op jit(solution)/shard_map/pick_attention/pallas_call | solution.py:138
  175.8 6.3 %pick_attention.9 = (bf16[34,128,512]{2,1,0:T(8,128)(2,1)}, f32[34,1,512]{2,1,0:T(1,128)}) custom-call(s32[5,32]{1,0:T(8,128)} %get-tuple-element.83.table, s32[1]{0:T(128)} %get-tuple-element.96.count, bf16[2,512,1024]{2,1,0:T(8,128)(2,1)} %maximum_select_fusion.q_ref.q_hbm, ...), custom_call_target="tpu_custom_call", output_to_operand_aliasing={{0}: (5, {}), {1}: (6, {})} | custom-call | flops 536870912 | bytes 2097152 | tf_op jit(solution)/shard_map/pick_attention/pallas_call | solution.py:138
  182.1 6.4 %pick_attention.10 = (bf16[34,128,512]{2,1,0:T(8,128)(2,1)}, f32[34,1,512]{2,1,0:T(1,128)}) custom-call(s32[5,32]{1,0:T(8,128)} %get-tuple-element.84.table, s32[1]{0:T(128)} %get-tuple-element.97.count, bf16[2,512,1024]{2,1,0:T(8,128)(2,1)} %maximum_select_fusion.q_ref.q_hbm, ...), custom_call_target="tpu_custom_call", output_to_operand_aliasing={{0}: (5, {}), {1}: (6, {})} | custom-call | flops 536870912 | bytes 2097152 | tf_op jit(solution)/shard_map/pick_attention/pallas_call | solution.py:138
  188.4 1.3 pick_attention.11
  189.7 10.8 %pick_attention.12 = (bf16[34,128,512]{2,1,0:T(8,128)(2,1)}, f32[34,1,512]{2,1,0:T(1,128)}) custom-call(s32[5,32]{1,0:T(8,128)} %get-tuple-element.86.table, s32[1]{0:T(128)} %get-tuple-element.99.count, bf16[2,512,1024]{2,1,0:T(8,128)(2,1)} %maximum_select_fusion.q_ref.q_hbm, ...), custom_call_target="tpu_custom_call", output_to_operand_aliasing={{0}: (5, {}), {1}: (6, {})} | custom-call | flops 536870912 | bytes 2097152 | tf_op jit(solution)/shard_map/pick_attention/pallas_call | solution.py:138
  200.6 4.5 %pick_attention.13 = (bf16[34,128,512]{2,1,0:T(8,128)(2,1)}, f32[34,1,512]{2,1,0:T(1,128)}) custom-call(s32[5,32]{1,0:T(8,128)} %get-tuple-element.87.table, s32[1]{0:T(128)} %get-tuple-element.100.count, bf16[2,512,1024]{2,1,0:T(8,128)(2,1)} %maximum_select_fusion.q_ref.q_hbm, ...), custom_call_target="tpu_custom_call", output_to_operand_aliasing={{0}: (5, {}), {1}: (6, {})} | custom-call | flops 536870912 | bytes 2097152 | tf_op jit(solution)/shard_map/pick_attention/pallas_call | solution.py:138
  205.0 10.9 %merge_parts.1 = (bf16[2,256,2048]{2,1,0:T(8,128)(2,1)}, bf16[2,256,1024]{2,1,0:T(8,128)(2,1)}) custom-call(s32[1]{0:T(128)} %bitcast.rep, s32[16]{0:T(128)} %compare_select_fusion.7.ready, s32[1]{0:T(128)} %bitcast.13.count, f32[16,128,512]{2,1,0:T(8,128)} %get-tuple-element.33.own_hbm, ...), custom_call_target="tpu_custom_call", output_to_operand_aliasing={{0}: (7, {}), {1}: (8, {})} | custom-call | flops 8388608 | bytes 10485760 | tf_op jit(solution)/shard_map/merge_parts/pallas_call | solution.py:210
  215.9 0.8 copy-done.6
  216.9 5.2 %final_attention.2 = (bf16[34,128,512]{2,1,0:T(8,128)(2,1)}, f32[34,1,512]{2,1,0:T(1,128)}, bf16[2,256,2048]{2,1,0:T(8,128)(2,1)}, bf16[2,256,1024]{2,1,0:T(8,128)(2,1)}) custom-call(s32[1]{0:T(128)} %bitcast.rep, s32[7,32]{1,0:T(8,128)} %get-tuple-element.88.table, ...), custom_call_target="tpu_custom_call", output_to_operand_aliasing={{0}: (8, {}), {1}: (9, {}), {2}: (10, {}), {3}: (11, {})} | custom-call | flops 268435456 | bytes 2359296 | tf_op jit(solution)/shard_map/final_attention/pallas_call | solution.py:323
  222.0 0.8 copy-done.4
  223.0 4.1 %final_attention.3 = (bf16[34,128,512]{2,1,0:T(8,128)(2,1)}, f32[34,1,512]{2,1,0:T(1,128)}, bf16[2,256,2048]{2,1,0:T(8,128)(2,1)}, bf16[2,256,1024]{2,1,0:T(8,128)(2,1)}) custom-call(s32[1]{0:T(128)} %bitcast.rep, s32[7,32]{1,0:T(8,128)} %get-tuple-element.89.table, ...), custom_call_target="tpu_custom_call", output_to_operand_aliasing={{0}: (8, {}), {1}: (9, {}), {2}: (10, {}), {3}: (11, {})} | custom-call | flops 268435456 | bytes 2359296 | tf_op jit(solution)/shard_map/final_attention/pallas_call | solution.py:323
  227.0 2.9 %collective-permute-done.19 = bf16[2,256,1024]{2,1,0:T(8,128)(2,1)S(1)} collective-permute-done((bf16[2,256,1024]{2,1,0:T(8,128)(2,1)}, bf16[2,256,1024]{2,1,0:T(8,128)(2,1)S(1)}, u32[]{:S(2)}, u32[]{:S(2)}) %collective-permute-start.19) | collective-permute-done | bytes 1048608 | tf_op jit(solution)/shard_map/ppermute | solution.py:504
  229.9 1.0 constant_dynamic-update-slice_fusion
  (96 shorter events, 9.1 us)
Async XLA Ops:
  3.4 8.6 %copy-start.8 = (bf16[2,256,512]{2,1,0:T(8,128)(2,1)S(1)}, bf16[2,256,512]{2,1,0:T(8,128)(2,1)}, u32[]{:S(2)}) copy-start(bf16[2,256,512]{2,1,0:T(8,128)(2,1)} %param.10) | copy-start | bytes 1572868
  3.4 9.3 %copy-start.12 = (s32[8]{0:T(128)S(1)}, s32[8]{0:T(128)}, u32[]{:S(2)}) copy-start(s32[8]{0:T(128)} %constant.154.clone) | copy-start | bytes 100
  3.4 9.9 %copy-start.11 = (s32[8]{0:T(128)S(1)}, s32[8]{0:T(128)}, u32[]{:S(2)}) copy-start(s32[8]{0:T(128)} %constant.156.clone) | copy-start | bytes 100
  3.4 10.5 %copy-start = (s32[8]{0:T(128)S(1)}, s32[8]{0:T(128)}, u32[]{:S(2)}) copy-start(s32[8]{0:T(128)} %constant.155.clone) | copy-start | bytes 100
  3.4 11.8 %slice-start = ((s32[2,16,3]{1,0,2:T(2,128)}), s32[2,16,2]{1,0,2:T(2,128)S(1)}, s32[]{:S(2)}) async-start(s32[2,16,3]{1,0,2:T(2,128)} %param.14), calls=%async_computation | async-start | bytes 4096 | tf_op jit(solution)/shard_map/slice | solution.py:447
  3.4 16.1 %copy-start.9 = (bf16[2,256,512]{2,1,0:T(8,128)(2,1)S(1)}, bf16[2,256,512]{2,1,0:T(8,128)(2,1)}, u32[]{:S(2)}) copy-start(bf16[2,256,512]{2,1,0:T(8,128)(2,1)} %param.11) | copy-start | bytes 1572868
  3.4 27.4 %collective-permute-start.1 = (bf16[2048,256]{1,0:T(8,128)(2,1)}, bf16[2048,256]{1,0:T(8,128)(2,1)}, u32[]{:S(2)}, u32[]{:S(2)}) collective-permute-start(bf16[2048,256]{1,0:T(8,128)(2,1)} %columns_kept.2.k_hbm), channel_id=1, source_target_pairs={{0,8},{8,16},{16,24},{24,28},{28,20},{20,12},{12,4},{4,0},{1,9},{9... | collective-permute-start | bytes 3145736 | tf_op jit(solution)/shard_map/ppermute | solution.py:405
  6.5 51.7 %collective-permute-start.13 = (bf16[2048,256]{1,0:T(8,128)(2,1)}, bf16[2048,256]{1,0:T(8,128)(2,1)}, u32[]{:S(2)}, u32[]{:S(2)}) collective-permute-start(bf16[2048,256]{1,0:T(8,128)(2,1)} %columns_kept.2.k_hbm), channel_id=1, source_target_pairs={{8,0},{16,8},{24,16},{28,24},{20,28},{12,20},{4,12},{0,4},{9,1},{1... | collective-permute-start | bytes 3145736 | tf_op jit(solution)/shard_map/ppermute | solution.py:405
  9.9 44.3 %copy-start.3 = (bf16[2,256,2048]{2,1,0:T(8,128)(2,1)S(1)}, bf16[2,256,2048]{2,1,0:T(8,128)(2,1)}, u32[]{:S(2)}) copy-start(bf16[2,256,2048]{2,1,0:T(8,128)(2,1)} %param.9) | copy-start | bytes 6291460
  9.9 45.5 %collective-permute-start.16 = (bf16[2048,256]{1,0:T(8,128)(2,1)}, bf16[2048,256]{1,0:T(8,128)(2,1)}, u32[]{:S(2)}, u32[]{:S(2)}) collective-permute-start(bf16[2048,256]{1,0:T(8,128)(2,1)} %columns_kept.3.v_hbm), channel_id=1, source_target_pairs={{0,8},{8,16},{16,24},{24,28},{28,20},{20,12},{12,4},{4,0},{1,9},{9... | collective-permute-start | bytes 3145736 | tf_op jit(solution)/shard_map/ppermute | solution.py:405
  11.9 42.0 %collective-permute-start.5 = (bf16[2048,256]{1,0:T(8,128)(2,1)}, bf16[2048,256]{1,0:T(8,128)(2,1)}, u32[]{:S(2)}, u32[]{:S(2)}) collective-permute-start(bf16[2048,256]{1,0:T(8,128)(2,1)} %columns_kept.3.v_hbm), channel_id=1, source_target_pairs={{8,0},{16,8},{24,16},{28,24},{20,28},{12,20},{4,12},{0,4},{9,1},{1... | collective-permute-start | bytes 3145736 | tf_op jit(solution)/shard_map/ppermute | solution.py:405
  12.6 42.8 %collective-permute-start.9 = (bf16[2,256,256]{2,1,0:T(8,128)(2,1)}, bf16[2,256,256]{2,1,0:T(8,128)(2,1)}, u32[]{:S(2)}, u32[]{:S(2)}) collective-permute-start(bf16[2,256,256]{2,1,0:T(8,128)(2,1)} %get-tuple-element.80), channel_id=1, source_target_pairs={{0,1},{1,0},{2,3},{3,2},{4,5},{5,4},{6,7},{7,6},{8,9},{9,8},{10,11... | collective-permute-start | bytes 786440 | tf_op jit(solution)/shard_map/ppermute | solution.py:428
  30.8 44.9 %collective-permute-start.2 = (bf16[2048,256]{1,0:T(8,128)(2,1)}, bf16[2048,256]{1,0:T(8,128)(2,1)}, u32[]{:S(2)}, u32[]{:S(2)}) collective-permute-start(bf16[2048,256]{1,0:T(8,128)(2,1)} %collective-permute-done.1.k_hbm), channel_id=1, source_target_pairs={{0,8},{8,16},{16,24},{24,28},{28,20},{20,12},{12,4},{4,0},{1,9},{9... | collective-permute-start | bytes 3145736 | tf_op jit(solution)/shard_map/ppermute | solution.py:405
  53.9 26.3 %collective-permute-start.6 = (bf16[2048,256]{1,0:T(8,128)(2,1)}, bf16[2048,256]{1,0:T(8,128)(2,1)}, u32[]{:S(2)}, u32[]{:S(2)}) collective-permute-start(bf16[2048,256]{1,0:T(8,128)(2,1)} %collective-permute-done.5.v_hbm), channel_id=1, source_target_pairs={{8,0},{16,8},{24,16},{28,24},{20,28},{12,20},{4,12},{0,4},{9,1},{1... | collective-permute-start | bytes 3145736 | tf_op jit(solution)/shard_map/ppermute | solution.py:405
  55.4 2.6 %collective-permute-start.10 = (bf16[2,256,256]{2,1,0:T(8,128)(2,1)}, bf16[2,256,256]{2,1,0:T(8,128)(2,1)S(1)}, u32[]{:S(2)}, u32[]{:S(2)}) collective-permute-start(bf16[2,256,256]{2,1,0:T(8,128)(2,1)} %get-tuple-element.78), channel_id=1, source_target_pairs={{0,1},{1,0},{2,3},{3,2},{4,5},{5,4},{6,7},{7,6},{8,9},{9,8},{10,11... | collective-permute-start | bytes 786440 | tf_op jit(solution)/shard_map/ppermute | solution.py:428
  55.4 42.8 %collective-permute-start.17 = (bf16[2048,256]{1,0:T(8,128)(2,1)}, bf16[2048,256]{1,0:T(8,128)(2,1)}, u32[]{:S(2)}, u32[]{:S(2)}) collective-permute-start(bf16[2048,256]{1,0:T(8,128)(2,1)} %collective-permute-done.16.v_hbm), channel_id=1, source_target_pairs={{0,8},{8,16},{16,24},{24,28},{28,20},{20,12},{12,4},{4,0},{1,9},{9... | collective-permute-start | bytes 3145736 | tf_op jit(solution)/shard_map/ppermute | solution.py:405
  58.0 21.1 %copy-start.10 = (bf16[2,256,256]{2,1,0:T(8,128)(2,1)}, bf16[2,256,256]{2,1,0:T(8,128)(2,1)S(1)}, u32[]{:S(2)}) copy-start(bf16[2,256,256]{2,1,0:T(8,128)(2,1)S(1)} %collective-permute-done.10) | copy-start | bytes 786436
  58.0 47.0 %collective-permute-start = (bf16[2,256,1024]{2,1,0:T(8,128)(2,1)}, bf16[2,256,1024]{2,1,0:T(8,128)(2,1)}, u32[]{:S(2)}, u32[]{:S(2)}) collective-permute-start(bf16[2,256,1024]{2,1,0:T(8,128)(2,1)} %get-tuple-element.72), channel_id=1, source_target_pairs={{0,1},{1,0},{2,3},{3,2},{4,5},{5,4},{6,7},{7,6},{8,9},{9,8},{10,11... | collective-permute-start | bytes 3145736 | tf_op jit(solution)/shard_map/ppermute | solution.py:428
  58.2 46.8 %collective-permute-start.14 = (bf16[2048,256]{1,0:T(8,128)(2,1)}, bf16[2048,256]{1,0:T(8,128)(2,1)}, u32[]{:S(2)}, u32[]{:S(2)}) collective-permute-start(bf16[2048,256]{1,0:T(8,128)(2,1)} %collective-permute-done.13.k_hbm), channel_id=1, source_target_pairs={{8,0},{16,8},{24,16},{28,24},{20,28},{12,20},{4,12},{0,4},{9,1},{1... | collective-permute-start | bytes 3145736 | tf_op jit(solution)/shard_map/ppermute | solution.py:405
  75.7 44.8 %collective-permute-start.3 = (bf16[2048,256]{1,0:T(8,128)(2,1)}, bf16[2048,256]{1,0:T(8,128)(2,1)S(1)}, u32[]{:S(2)}, u32[]{:S(2)}) collective-permute-start(bf16[2048,256]{1,0:T(8,128)(2,1)} %collective-permute-done.2.k_hbm), channel_id=1, source_target_pairs={{0,8},{8,16},{16,24},{24,28},{28,20},{20,12},{12,4},{4,0},{1,9},{9... | collective-permute-start | bytes 3145736 | tf_op jit(solution)/shard_map/ppermute | solution.py:405
  80.2 44.8 %collective-permute-start.7 = (bf16[2048,256]{1,0:T(8,128)(2,1)}, bf16[2048,256]{1,0:T(8,128)(2,1)S(1)}, u32[]{:S(2)}, u32[]{:S(2)}) collective-permute-start(bf16[2048,256]{1,0:T(8,128)(2,1)} %collective-permute-done.6.v_hbm), channel_id=1, source_target_pairs={{8,0},{16,8},{24,16},{28,24},{20,28},{12,20},{4,12},{0,4},{9,1},{1... | collective-permute-start | bytes 3145736 | tf_op jit(solution)/shard_map/ppermute | solution.py:405
  98.2 44.9 %collective-permute-start.18 = (bf16[2048,256]{1,0:T(8,128)(2,1)}, bf16[2048,256]{1,0:T(8,128)(2,1)}, u32[]{:S(2)}, u32[]{:S(2)}) collective-permute-start(bf16[2048,256]{1,0:T(8,128)(2,1)} %collective-permute-done.17.v_hbm), channel_id=1, source_target_pairs={{0,8},{8,16},{16,24},{24,28},{28,20},{20,12},{12,4},{4,0},{1,9},{9... | collective-permute-start | bytes 3145736 | tf_op jit(solution)/shard_map/ppermute | solution.py:405
  105.0 95.6 %collective-permute-start.15 = (bf16[2048,256]{1,0:T(8,128)(2,1)}, bf16[2048,256]{1,0:T(8,128)(2,1)}, u32[]{:S(2)}, u32[]{:S(2)}) collective-permute-start(bf16[2048,256]{1,0:T(8,128)(2,1)} %collective-permute-done.14.k_hbm), channel_id=1, source_target_pairs={{8,0},{16,8},{24,16},{28,24},{20,28},{12,20},{4,12},{0,4},{9,1},{1... | collective-permute-start | bytes 3145736 | tf_op jit(solution)/shard_map/ppermute | solution.py:405
  120.5 5.6 %copy-start.1 = (bf16[2048,256]{1,0:T(8,128)(2,1)}, bf16[2048,256]{1,0:T(8,128)(2,1)S(1)}, u32[]{:S(2)}) copy-start(bf16[2048,256]{1,0:T(8,128)(2,1)S(1)} %collective-permute-done.3.k_hbm) | copy-start | bytes 3145732
  121.7 94.2 %collective-permute-start.11 = (bf16[1024,256]{1,0:T(8,128)(2,1)}, bf16[1024,256]{1,0:T(8,128)(2,1)S(1)}, u32[]{:S(2)}, u32[]{:S(2)}) collective-permute-start(bf16[1024,256]{1,0:T(8,128)(2,1)} %get-tuple-element.75), channel_id=1, source_target_pairs={{0,8},{8,16},{16,24},{24,28},{28,20},{20,12},{12,4},{4,0},{1,9},{9... | collective-permute-start | bytes 1572872 | tf_op jit(solution)/shard_map/ppermute | solution.py:405
  125.1 36.2 %copy-start.2 = (bf16[2048,256]{1,0:T(8,128)(2,1)}, bf16[2048,256]{1,0:T(8,128)(2,1)S(1)}, u32[]{:S(2)}) copy-start(bf16[2048,256]{1,0:T(8,128)(2,1)S(1)} %collective-permute-done.7.v_hbm) | copy-start | bytes 3145732
  126.2 89.7 %collective-permute-start.12 = (bf16[1024,256]{1,0:T(8,128)(2,1)}, bf16[1024,256]{1,0:T(8,128)(2,1)S(1)}, u32[]{:S(2)}, u32[]{:S(2)}) collective-permute-start(bf16[1024,256]{1,0:T(8,128)(2,1)} %get-tuple-element.73), channel_id=1, source_target_pairs={{8,0},{16,8},{24,16},{28,24},{20,28},{12,20},{4,12},{0,4},{9,1},{1... | collective-permute-start | bytes 1572872 | tf_op jit(solution)/shard_map/ppermute | solution.py:405
  126.5 95.5 %collective-permute-start.4 = (bf16[1024,256]{1,0:T(8,128)(2,1)}, bf16[1024,256]{1,0:T(8,128)(2,1)S(1)}, u32[]{:S(2)}, u32[]{:S(2)}) collective-permute-start(bf16[1024,256]{1,0:T(8,128)(2,1)} %get-tuple-element.76), channel_id=1, source_target_pairs={{0,8},{8,16},{16,24},{24,28},{28,20},{20,12},{12,4},{4,0},{1,9},{9... | collective-permute-start | bytes 1572872 | tf_op jit(solution)/shard_map/ppermute | solution.py:405
  143.1 78.9 %collective-permute-start.8 = (bf16[1024,256]{1,0:T(8,128)(2,1)}, bf16[1024,256]{1,0:T(8,128)(2,1)S(1)}, u32[]{:S(2)}, u32[]{:S(2)}) collective-permute-start(bf16[1024,256]{1,0:T(8,128)(2,1)} %get-tuple-element.74), channel_id=1, source_target_pairs={{8,0},{16,8},{24,16},{28,24},{20,28},{12,20},{4,12},{0,4},{9,1},{1... | collective-permute-start | bytes 1572872 | tf_op jit(solution)/shard_map/ppermute | solution.py:405
  215.9 0.8 copy-start.6
  215.9 1.0 copy-start.7
  222.0 0.8 copy-start.4
  222.0 1.0 copy-start.5
  227.0 2.9 %collective-permute-start.19 = (bf16[2,256,1024]{2,1,0:T(8,128)(2,1)}, bf16[2,256,1024]{2,1,0:T(8,128)(2,1)S(1)}, u32[]{:S(2)}, u32[]{:S(2)}) collective-permute-start(bf16[2,256,1024]{2,1,0:T(8,128)(2,1)} %get-tuple-element.60), channel_id=1, source_target_pairs={{0,1},{1,0},{2,3},{3,2},{4,5},{5,4},{6,7},{7,6},{8,9},{9,8},{10,11... | collective-permute-start | bytes 3145736 | tf_op jit(solution)/shard_map/ppermute | solution.py:504

commit v4 on v3

--- a/solution.py
+++ b/solution.py
@@ -451,21 +451,26 @@
     tile = mine - holders * blocks_here
     facts = [head // head_grouping, place // (2 * heads), head]
     tables, counts = compacted(
-        holders[None, :] == wanted[:-1, None],
+        holders[None, :] == wanted[:-3, None],
         jnp.stack([place, tile, *facts]),
         jnp.zeros((5,), jnp.int32),
     )
     tiles = blocks_here // PIECES
-    waits = holders == wanted[-1]
-    inside = waits[None, :] & (tile[None, :] // tiles == jnp.arange(PIECES)[:, None])
-    both = jnp.any(jnp.all(inside.reshape(PIECES, -1, 2), axis=2), axis=0)
+    piece_of = tile // tiles
+    inside = jnp.concatenate(
+        [
+            holders[None, :] == wanted[-3:-1, None],
+            (holders == wanted[-1])[None, :] & (piece_of[None, :] == jnp.arange(PIECES)[:, None]),
+        ]
+    )
+    both = jnp.any(jnp.all(inside.reshape(2 + PIECES, -1, 2), axis=2), axis=0)
     both = jnp.stack([both, both], axis=1).reshape(-1)
     last_tables, last_counts = compacted(
         inside,
         jnp.stack(
             [
                 place,
-                tile % tiles,
+                jnp.where(holders == wanted[-1], tile - piece_of * tiles, tile),
                 *facts,
                 jnp.where(both, items, place + 1 - 2 * (place % 2)),
                 jnp.where(both, place % 2, 0),
@@ -474,7 +479,7 @@
         jnp.zeros((7,), jnp.int32),
     )
     ready, ready_counts = compacted(
-        ~jnp.any(waits.reshape(1, -1, 2), axis=2),
+        ~jnp.any(inside.reshape(1, -1, items // 2, 2), axis=(1, 3)),
         jnp.arange(items // 2)[None],
         jnp.zeros((1,), jnp.int32),
     )
@@ -482,14 +487,15 @@
     own, own_log, parts, logs, keep, send = own_attention(
         block_queries, block_keys, block_values, head_grouping, full_width
     )
-    for n, distance in enumerate(distances):
+    for n, distance in enumerate(distances[:-2]):
         keys, values = shards[distance]
         parts, logs = pick_attention(tables[n], counts[n], block_queries, keys, values, parts, logs)
     keep, send = merge(
         rep_index, ready[0, 0], ready_counts[0], own, own_log, parts, logs, keep, send
     )
     state = (parts, logs, keep, send)
-    for n, (keys, values) in enumerate(last_pieces):
+    late_arrivals = [shards[distance] for distance in distances[-2:]] + last_pieces
+    for n, (keys, values) in enumerate(late_arrivals):
         state = final_attention(
             rep_index,
             last_tables[n],

time: 234 us -> 232 us (level)
  Pallas kernels: 86.7 us -> 83.1 us
  local copies, waits for them, and re-layouts: 13 us -> 16.1 us
  waiting for transfers between devices: 95.8 us -> 92.9 us
    pallas_call x2 -> x4, Pallas kernels: 9.21 us -> 26.7 us  [final_attention(): pl.pallas_call(final_kernel, in_specs=[smem] * 3 + [anywhere] * 9, out_sp...]
    pallas_call x7 -> x5, Pallas kernels: 43.7 us -> 28.5 us  [pick_attention(): pl.pallas_call(pick_kernel, in_specs=[smem, smem] + [anywhere] * 5, out_s...]
    pallas_call x1, Pallas kernels: 10.9 us -> 4.94 us  [merge(): pl.pallas_call(merge_kernel, in_specs=[smem] * 3 + [anywhere] * 6, out_sp...]
    ppermute x16, waiting for transfers between devices: 92.9 us -> 90 us  [hop(): return lax.ppermute(value, 'ctx', pairs)]
  transfers between devices with their start and end apart: 20 -> 20, of which waited for: 9 -> 8; matrix products, arithmetic and copies ran while one was open for 11% -> 12% of each run, Pallas kernels for 34% -> 33%
where the time goes in v4:
time: 232 us; the launch traced here: 227 us
  waiting for transfers between devices  92.9 us (40%)
  Pallas kernels  83.1 us (36%)
  starting transfers between devices  20.4 us (9%)
  local copies, waits for them, and re-layouts  16.1 us (7%)
  other arithmetic  14.6 us (6%)
    ppermute x16, waiting for transfers between devices, hop(): return lax.ppermute(value, 'ctx', pairs)  90 us
    pallas_call x5, Pallas kernels, pick_attention(): pl.pallas_call(pick_kernel, in_specs=[smem, smem] + [anywhere] * 5, out_s...  28.5 us
    pallas_call x4, Pallas kernels, final_attention(): pl.pallas_call(final_kernel, in_specs=[smem] * 3 + [anywhere] * 9, out_sp...  26.7 us
    ppermute x16, starting transfers between devices, hop(): return lax.ppermute(value, 'ctx', pairs)  19.8 us
    pallas_call x1, Pallas kernels, own_attention(): pl.pallas_call(own_kernel, grid=(count,), in_specs=[query_spec, key_spec,...  16.2 us
    select_n x3, other arithmetic, all_rows(): jnp.where(rep_index == 0, jnp.concatenate([kept, came], axis=1), jnp.conc...  8.09 us
    pallas_call x2, Pallas kernels, columns_kept(): pl.pallas_call(half_kernel, grid_spec=pltpu.PrefetchScalarGridSpec(num_sc...  6.73 us
    pallas_call x1, Pallas kernels, merge(): pl.pallas_call(merge_kernel, in_specs=[smem] * 3 + [anywhere] * 6, out_sp...  4.94 us
  transfers between devices with their start and end apart: 20, of which 8 were waited for; matrix products, arithmetic and copies ran while one was open for 12% of the time, Pallas kernels for 33%

profile of v4, /device:TPU:0, one launch (start us, length us, event | category | flops | bytes accessed | tf_op | source)
XLA Modules:
  0.0 227.2 jit_solution(51948863736665938)
XLA Ops:
  0.0 3.4 %columns_kept.2.k_hbm = bf16[2048,256]{1,0:T(8,128)(2,1)} custom-call(s32[1]{0:T(128)} %bitcast.rep, bf16[2048,512]{1,0:T(8,128)(2,1)} %from_ref.2), custom_call_target="tpu_custom_call" | custom-call | bytes 2097152 | tf_op jit(solution)/shard_map/columns_kept/pallas_call | solution.py:349
  3.4 3.1 %collective-permute-start.1 = (bf16[2048,256]{1,0:T(8,128)(2,1)}, bf16[2048,256]{1,0:T(8,128)(2,1)S(1)}, u32[]{:S(2)}, u32[]{:S(2)}) collective-permute-start(bf16[2048,256]{1,0:T(8,128)(2,1)} %columns_kept.2.k_hbm), channel_id=1, source_target_pairs={{0,8},{8,16},{16,24},{24,28},{28,20},{20,12},{12,4},{4,0},{1,9},{9... | collective-permute-start | bytes 3145736 | tf_op jit(solution)/shard_map/ppermute | solution.py:405
  6.5 3.4 %columns_kept.3.v_hbm = bf16[2048,256]{1,0:T(8,128)(2,1)} custom-call(s32[1]{0:T(128)} %bitcast.rep, bf16[2048,512]{1,0:T(8,128)(2,1)} %from_ref.3), custom_call_target="tpu_custom_call" | custom-call | bytes 2097152 | tf_op jit(solution)/shard_map/columns_kept/pallas_call | solution.py:349
  9.9 2.0 collective-permute-start.16
  11.9 0.7 constant_dynamic-slice_fusion.3
  13.7 0.7 compare_select_fusion
  16.2 0.7 broadcast_compare_fusion.4
  16.9 0.7 and_select_fusion.5
  17.9 0.7 broadcast_compare_fusion.2
  20.6 10.1 %collective-permute-done.1.k_hbm = bf16[2048,256]{1,0:T(8,128)(2,1)S(1)} collective-permute-done((bf16[2048,256]{1,0:T(8,128)(2,1)}, bf16[2048,256]{1,0:T(8,128)(2,1)S(1)}, u32[]{:S(2)}, u32[]{:S(2)}) %collective-permute-start.1) | collective-permute-done | bytes 1048608 | tf_op jit(solution)/shard_map/ppermute | solution.py:405
  30.7 2.1 collective-permute-start.2
  32.9 21.0 %collective-permute-done.5.v_hbm = bf16[2048,256]{1,0:T(8,128)(2,1)S(1)} collective-permute-done((bf16[2048,256]{1,0:T(8,128)(2,1)}, bf16[2048,256]{1,0:T(8,128)(2,1)S(1)}, u32[]{:S(2)}, u32[]{:S(2)}) %collective-permute-start.5) | collective-permute-done | bytes 1048608 | tf_op jit(solution)/shard_map/ppermute | solution.py:405
  55.3 1.7 collective-permute-start.17
  57.2 0.7 constant_dynamic-slice_fusion.1
  58.3 17.5 %collective-permute-done.2.k_hbm = bf16[2048,256]{1,0:T(8,128)(2,1)} collective-permute-done((bf16[2048,256]{1,0:T(8,128)(2,1)S(1)}, bf16[2048,256]{1,0:T(8,128)(2,1)}, u32[]{:S(2)}, u32[]{:S(2)}) %collective-permute-start.2) | collective-permute-done | bytes 1048608 | tf_op jit(solution)/shard_map/ppermute | solution.py:405
  75.7 2.1 collective-permute-start.3
  77.9 0.7 copy-done.10
  78.6 2.8 %constant_dynamic-slice_fusion.5 = (bf16[2,256,1024]{2,1,0:T(8,128)(2,1)S(1)}, bf16[2,256,1024]{2,1,0:T(8,128)(2,1)}) fusion(bf16[2,256,2048]{2,1,0:T(8,128)(2,1)} %param.9, s32[]{:T(128)S(6)} %select_n.275, s32[]{:T(128)S(6)} %select_n.276), kind=kLoop, calls=%fused_computation.44 | loop fusion | bytes 4194312 | tf_op jit(solution)/shard_map/dynamic_slice | solution.py:394
  81.5 0.7 copy-done.11
  82.7 1.1 compare_select_fusion.5.ready
  84.5 13.7 %collective-permute-done.17.v_hbm = bf16[2048,256]{1,0:T(8,128)(2,1)} collective-permute-done((bf16[2048,256]{1,0:T(8,128)(2,1)}, bf16[2048,256]{1,0:T(8,128)(2,1)}, u32[]{:S(2)}, u32[]{:S(2)}) %collective-permute-start.17) | collective-permute-done | bytes 1048608 | tf_op jit(solution)/shard_map/ppermute | solution.py:405
  98.2 2.1 collective-permute-start.18
  100.9 2.0 maximum_select_fusion.1.k_ref
  102.9 2.1 maximum_select_fusion.2.v_ref
  105.1 15.5 %collective-permute-done.3.k_hbm = bf16[2048,256]{1,0:T(8,128)(2,1)S(1)} collective-permute-done((bf16[2048,256]{1,0:T(8,128)(2,1)}, bf16[2048,256]{1,0:T(8,128)(2,1)S(1)}, u32[]{:S(2)}, u32[]{:S(2)}) %collective-permute-start.3) | collective-permute-done | bytes 1048608 | tf_op jit(solution)/shard_map/ppermute | solution.py:405
  120.6 1.1 fusion.7
  121.7 2.1 collective-permute-start.11
  123.7 1.0 collective-permute-done.7.v_hbm
  124.8 1.1 fusion.6
  126.2 3.9 %maximum_select_fusion.q_ref.q_hbm = bf16[2,512,1024]{2,1,0:T(8,128)(2,1)} fusion(bf16[2,256,1024]{2,1,0:T(8,128)(2,1)} %collective-permute-done, bf16[2,256,1024]{2,1,0:T(8,128)(2,1)S(1)} %get-tuple-element.79, pred[]{:T(512)S(6)} %eq.207), kind=kLoop, calls=%fused_computation.1 | loop fusion | flops 9437184 | bytes 4194305 | tf_op jit(solution)/shard_map/jit(_where)/select_n | solution.py:429
  130.2 1.7 collective-permute-start.4
  131.9 11.2 %collective-permute-done.18.v_hbm = bf16[2048,256]{1,0:T(8,128)(2,1)} collective-permute-done((bf16[2048,256]{1,0:T(8,128)(2,1)}, bf16[2048,256]{1,0:T(8,128)(2,1)}, u32[]{:S(2)}, u32[]{:S(2)}) %collective-permute-start.18) | collective-permute-done | bytes 1048608 | tf_op jit(solution)/shard_map/ppermute | solution.py:405
  143.1 2.0 collective-permute-start.8
  145.2 16.2 %own_attention.1 = (f32[16,128,512]{2,1,0:T(8,128)}, f32[16,1,512]{2,1,0:T(1,128)}, bf16[34,128,512]{2,1,0:T(8,128)(2,1)}, f32[34,1,512]{2,1,0:T(1,128)}, bf16[2...) custom-call(bf16[2,512,1024]{2,1,0:T(8,128)(2,1)} %maximum_select_fusion.q_ref.q_hbm, ...), custom_call_target="tpu_custom_call" | custom-call | flops 2147483648 | bytes 8388608 | tf_op jit(solution)/shard_map/own_attention/pallas_call | solution.py:69
  161.3 6.4 %pick_attention.5 = (bf16[34,128,512]{2,1,0:T(8,128)(2,1)}, f32[34,1,512]{2,1,0:T(1,128)}) custom-call(s32[5,32]{1,0:T(8,128)} %get-tuple-element.89.table, s32[1]{0:T(128)} %get-tuple-element.100.count, bf16[2,512,1024]{2,1,0:T(8,128)(2,1)} %maximum_select_fusion.q_ref.q_hbm, ...), custom_call_target="tpu_custom_call", output_to_operand_aliasing={{0}: (5, {}), {1}: (6, {})} | custom-call | flops 536870912 | bytes 2097152 | tf_op jit(solution)/shard_map/pick_attention/pallas_call | solution.py:138
  167.8 8.1 %pick_attention.6 = (bf16[34,128,512]{2,1,0:T(8,128)(2,1)}, f32[34,1,512]{2,1,0:T(1,128)}) custom-call(s32[5,32]{1,0:T(8,128)} %get-tuple-element.90.table, s32[1]{0:T(128)} %get-tuple-element.101.count, bf16[2,512,1024]{2,1,0:T(8,128)(2,1)} %maximum_select_fusion.q_ref.q_hbm, ...), custom_call_target="tpu_custom_call", output_to_operand_aliasing={{0}: (5, {}), {1}: (6, {})} | custom-call | flops 536870912 | bytes 2097152 | tf_op jit(solution)/shard_map/pick_attention/pallas_call | solution.py:138
  175.9 6.3 %pick_attention.7 = (bf16[34,128,512]{2,1,0:T(8,128)(2,1)}, f32[34,1,512]{2,1,0:T(1,128)}) custom-call(s32[5,32]{1,0:T(8,128)} %get-tuple-element.91.table, s32[1]{0:T(128)} %get-tuple-element.102.count, bf16[2,512,1024]{2,1,0:T(8,128)(2,1)} %maximum_select_fusion.q_ref.q_hbm, ...), custom_call_target="tpu_custom_call", output_to_operand_aliasing={{0}: (5, {}), {1}: (6, {})} | custom-call | flops 536870912 | bytes 2097152 | tf_op jit(solution)/shard_map/pick_attention/pallas_call | solution.py:138
  182.2 6.3 %pick_attention.8 = (bf16[34,128,512]{2,1,0:T(8,128)(2,1)}, f32[34,1,512]{2,1,0:T(1,128)}) custom-call(s32[5,32]{1,0:T(8,128)} %get-tuple-element.92.table, s32[1]{0:T(128)} %get-tuple-element.103.count, bf16[2,512,1024]{2,1,0:T(8,128)(2,1)} %maximum_select_fusion.q_ref.q_hbm, ...), custom_call_target="tpu_custom_call", output_to_operand_aliasing={{0}: (5, {}), {1}: (6, {})} | custom-call | flops 536870912 | bytes 2097152 | tf_op jit(solution)/shard_map/pick_attention/pallas_call | solution.py:138
  188.5 1.4 pick_attention.9
  189.9 4.9 %merge_parts.1 = (bf16[2,256,2048]{2,1,0:T(8,128)(2,1)}, bf16[2,256,1024]{2,1,0:T(8,128)(2,1)}) custom-call(s32[1]{0:T(128)} %bitcast.rep, s32[16]{0:T(128)} %compare_select_fusion.5.ready, s32[1]{0:T(128)} %bitcast.14.count, f32[16,128,512]{2,1,0:T(8,128)} %get-tuple-element.37.own_hbm, ...), custom_call_target="tpu_custom_call", output_to_operand_aliasing={{0}: (7, {}), {1}: (8, {})} | custom-call | flops 8388608 | bytes 10485760 | tf_op jit(solution)/shard_map/merge_parts/pallas_call | solution.py:210
  194.8 12.4 %final_attention.4 = (bf16[34,128,512]{2,1,0:T(8,128)(2,1)}, f32[34,1,512]{2,1,0:T(1,128)}, bf16[2,256,2048]{2,1,0:T(8,128)(2,1)}, bf16[2,256,1024]{2,1,0:T(8,128)(2,1)}) custom-call(s32[1]{0:T(128)} %bitcast.rep, s32[7,32]{1,0:T(8,128)} %get-tuple-element.94.table, ...), custom_call_target="tpu_custom_call", output_to_operand_aliasing={{0}: (8, {}), {1}: (9, {}), {2}: (10, {}), {3}: (11, {})} | custom-call | flops 268435456 | bytes 2359296 | tf_op jit(solution)/shard_map/final_attention/pallas_call | solution.py:323
  207.2 5.1 %final_attention.5 = (bf16[34,128,512]{2,1,0:T(8,128)(2,1)}, f32[34,1,512]{2,1,0:T(1,128)}, bf16[2,256,2048]{2,1,0:T(8,128)(2,1)}, bf16[2,256,1024]{2,1,0:T(8,128)(2,1)}) custom-call(s32[1]{0:T(128)} %bitcast.rep, s32[7,32]{1,0:T(8,128)} %get-tuple-element.95.table, ...), custom_call_target="tpu_custom_call", output_to_operand_aliasing={{0}: (8, {}), {1}: (9, {}), {2}: (10, {}), {3}: (11, {})} | custom-call | flops 268435456 | bytes 2359296 | tf_op jit(solution)/shard_map/final_attention/pallas_call | solution.py:323
  212.3 0.8 copy-done.7
  213.1 5.1 %final_attention.6 = (bf16[34,128,512]{2,1,0:T(8,128)(2,1)}, f32[34,1,512]{2,1,0:T(1,128)}, bf16[2,256,2048]{2,1,0:T(8,128)(2,1)}, bf16[2,256,1024]{2,1,0:T(8,128)(2,1)}) custom-call(s32[1]{0:T(128)} %bitcast.rep, s32[7,32]{1,0:T(8,128)} %get-tuple-element.96.table, ...), custom_call_target="tpu_custom_call", output_to_operand_aliasing={{0}: (8, {}), {1}: (9, {}), {2}: (10, {}), {3}: (11, {})} | custom-call | flops 268435456 | bytes 2359296 | tf_op jit(solution)/shard_map/final_attention/pallas_call | solution.py:323
  218.3 0.8 copy-done.5
  219.2 4.1 %final_attention.7 = (bf16[34,128,512]{2,1,0:T(8,128)(2,1)}, f32[34,1,512]{2,1,0:T(1,128)}, bf16[2,256,2048]{2,1,0:T(8,128)(2,1)}, bf16[2,256,1024]{2,1,0:T(8,128)(2,1)}) custom-call(s32[1]{0:T(128)} %bitcast.rep, s32[7,32]{1,0:T(8,128)} %get-tuple-element.97.table, ...), custom_call_target="tpu_custom_call", output_to_operand_aliasing={{0}: (8, {}), {1}: (9, {}), {2}: (10, {}), {3}: (11, {})} | custom-call | flops 268435456 | bytes 2359296 | tf_op jit(solution)/shard_map/final_attention/pallas_call | solution.py:323
  223.3 2.9 %collective-permute-done.19 = bf16[2,256,1024]{2,1,0:T(8,128)(2,1)S(1)} collective-permute-done((bf16[2,256,1024]{2,1,0:T(8,128)(2,1)}, bf16[2,256,1024]{2,1,0:T(8,128)(2,1)S(1)}, u32[]{:S(2)}, u32[]{:S(2)}) %collective-permute-start.19) | collective-permute-done | bytes 1048608 | tf_op jit(solution)/shard_map/ppermute | solution.py:510
  226.1 1.0 constant_dynamic-update-slice_fusion
  (102 shorter events, 9.7 us)
Async XLA Ops:
  3.4 8.5 %copy-start.8 = (bf16[2,256,512]{2,1,0:T(8,128)(2,1)S(1)}, bf16[2,256,512]{2,1,0:T(8,128)(2,1)}, u32[]{:S(2)}) copy-start(bf16[2,256,512]{2,1,0:T(8,128)(2,1)} %param.10) | copy-start | bytes 1572868
  3.4 9.3 %slice-start = ((s32[2,16,3]{1,0,2:T(2,128)}), s32[2,16,2]{1,0,2:T(2,128)S(1)}, s32[]{:S(2)}) async-start(s32[2,16,3]{1,0,2:T(2,128)} %param.14), calls=%async_computation | async-start | bytes 4096 | tf_op jit(solution)/shard_map/slice | solution.py:447
  3.4 9.6 %copy-start.13 = (s32[8]{0:T(128)S(1)}, s32[8]{0:T(128)}, u32[]{:S(2)}) copy-start(s32[8]{0:T(128)} %constant.147.clone) | copy-start | bytes 100
  3.4 10.3 %copy-start.12 = (s32[8]{0:T(128)S(1)}, s32[8]{0:T(128)}, u32[]{:S(2)}) copy-start(s32[8]{0:T(128)} %constant.149.clone) | copy-start | bytes 100
  3.4 11.0 %copy-start = (s32[8]{0:T(128)S(1)}, s32[8]{0:T(128)}, u32[]{:S(2)}) copy-start(s32[8]{0:T(128)} %constant.148.clone) | copy-start | bytes 100
  3.4 53.8 %copy-start.9 = (bf16[2,256,512]{2,1,0:T(8,128)(2,1)S(1)}, bf16[2,256,512]{2,1,0:T(8,128)(2,1)}, u32[]{:S(2)}) copy-start(bf16[2,256,512]{2,1,0:T(8,128)(2,1)} %param.11) | copy-start | bytes 1572868
  3.4 27.3 %collective-permute-start.1 = (bf16[2048,256]{1,0:T(8,128)(2,1)}, bf16[2048,256]{1,0:T(8,128)(2,1)S(1)}, u32[]{:S(2)}, u32[]{:S(2)}) collective-permute-start(bf16[2048,256]{1,0:T(8,128)(2,1)} %columns_kept.2.k_hbm), channel_id=1, source_target_pairs={{0,8},{8,16},{16,24},{24,28},{28,20},{20,12},{12,4},{4,0},{1,9},{9... | collective-permute-start | bytes 3145736 | tf_op jit(solution)/shard_map/ppermute | solution.py:405
  6.5 51.4 %collective-permute-start.13 = (bf16[2048,256]{1,0:T(8,128)(2,1)}, bf16[2048,256]{1,0:T(8,128)(2,1)}, u32[]{:S(2)}, u32[]{:S(2)}) collective-permute-start(bf16[2048,256]{1,0:T(8,128)(2,1)} %columns_kept.2.k_hbm), channel_id=1, source_target_pairs={{8,0},{16,8},{24,16},{28,24},{20,28},{12,20},{4,12},{0,4},{9,1},{1... | collective-permute-start | bytes 3145736 | tf_op jit(solution)/shard_map/ppermute | solution.py:405
  9.9 45.5 %collective-permute-start.16 = (bf16[2048,256]{1,0:T(8,128)(2,1)}, bf16[2048,256]{1,0:T(8,128)(2,1)}, u32[]{:S(2)}, u32[]{:S(2)}) collective-permute-start(bf16[2048,256]{1,0:T(8,128)(2,1)} %columns_kept.3.v_hbm), channel_id=1, source_target_pairs={{0,8},{8,16},{16,24},{24,28},{28,20},{20,12},{12,4},{4,0},{1,9},{9... | collective-permute-start | bytes 3145736 | tf_op jit(solution)/shard_map/ppermute | solution.py:405
  11.9 41.9 %collective-permute-start.5 = (bf16[2048,256]{1,0:T(8,128)(2,1)}, bf16[2048,256]{1,0:T(8,128)(2,1)S(1)}, u32[]{:S(2)}, u32[]{:S(2)}) collective-permute-start(bf16[2048,256]{1,0:T(8,128)(2,1)} %columns_kept.3.v_hbm), channel_id=1, source_target_pairs={{8,0},{16,8},{24,16},{28,24},{20,28},{12,20},{4,12},{0,4},{9,1},{1... | collective-permute-start | bytes 3145736 | tf_op jit(solution)/shard_map/ppermute | solution.py:405
  12.6 65.3 %collective-permute-start.9 = (bf16[2,256,256]{2,1,0:T(8,128)(2,1)}, bf16[2,256,256]{2,1,0:T(8,128)(2,1)S(1)}, u32[]{:S(2)}, u32[]{:S(2)}) collective-permute-start(bf16[2,256,256]{2,1,0:T(8,128)(2,1)} %get-tuple-element.88), channel_id=1, source_target_pairs={{0,1},{1,0},{2,3},{3,2},{4,5},{5,4},{6,7},{7,6},{8,9},{9,8},{10,11... | collective-permute-start | bytes 786440 | tf_op jit(solution)/shard_map/ppermute | solution.py:428
  30.7 27.6 %copy-start.3 = (bf16[2048,256]{1,0:T(8,128)(2,1)}, bf16[2048,256]{1,0:T(8,128)(2,1)S(1)}, u32[]{:S(2)}) copy-start(bf16[2048,256]{1,0:T(8,128)(2,1)S(1)} %collective-permute-done.1.k_hbm) | copy-start | bytes 3145732
  30.7 45.0 %collective-permute-start.2 = (bf16[2048,256]{1,0:T(8,128)(2,1)S(1)}, bf16[2048,256]{1,0:T(8,128)(2,1)}, u32[]{:S(2)}, u32[]{:S(2)}) collective-permute-start(bf16[2048,256]{1,0:T(8,128)(2,1)S(1)} %collective-permute-done.1.k_hbm), channel_id=1, source_target_pairs={{0,8},{8,16},{16,24},{24,28},{28,20},{20,12},{12,4},{4,0},{1,9},{9... | collective-permute-start | bytes 3145736 | tf_op jit(solution)/shard_map/ppermute | solution.py:405
  53.8 27.6 %copy-start.4 = (bf16[2048,256]{1,0:T(8,128)(2,1)}, bf16[2048,256]{1,0:T(8,128)(2,1)S(1)}, u32[]{:S(2)}) copy-start(bf16[2048,256]{1,0:T(8,128)(2,1)S(1)} %collective-permute-done.5.v_hbm) | copy-start | bytes 3145732
  53.8 27.6 %collective-permute-start.6 = (bf16[2048,256]{1,0:T(8,128)(2,1)S(1)}, bf16[2048,256]{1,0:T(8,128)(2,1)}, u32[]{:S(2)}, u32[]{:S(2)}) collective-permute-start(bf16[2048,256]{1,0:T(8,128)(2,1)S(1)} %collective-permute-done.5.v_hbm), channel_id=1, source_target_pairs={{8,0},{16,8},{24,16},{28,24},{20,28},{12,20},{4,12},{0,4},{9,1},{1... | collective-permute-start | bytes 3145736 | tf_op jit(solution)/shard_map/ppermute | solution.py:405
  55.3 42.8 %collective-permute-start.17 = (bf16[2048,256]{1,0:T(8,128)(2,1)}, bf16[2048,256]{1,0:T(8,128)(2,1)}, u32[]{:S(2)}, u32[]{:S(2)}) collective-permute-start(bf16[2048,256]{1,0:T(8,128)(2,1)} %collective-permute-done.16.v_hbm), channel_id=1, source_target_pairs={{0,8},{8,16},{16,24},{24,28},{28,20},{20,12},{12,4},{4,0},{1,9},{9... | collective-permute-start | bytes 3145736 | tf_op jit(solution)/shard_map/ppermute | solution.py:405
  57.9 47.1 %collective-permute-start.14 = (bf16[2048,256]{1,0:T(8,128)(2,1)}, bf16[2048,256]{1,0:T(8,128)(2,1)}, u32[]{:S(2)}, u32[]{:S(2)}) collective-permute-start(bf16[2048,256]{1,0:T(8,128)(2,1)} %collective-permute-done.13.k_hbm), channel_id=1, source_target_pairs={{8,0},{16,8},{24,16},{28,24},{20,28},{12,20},{4,12},{0,4},{9,1},{1... | collective-permute-start | bytes 3145736 | tf_op jit(solution)/shard_map/ppermute | solution.py:405
  75.7 44.8 %collective-permute-start.3 = (bf16[2048,256]{1,0:T(8,128)(2,1)}, bf16[2048,256]{1,0:T(8,128)(2,1)S(1)}, u32[]{:S(2)}, u32[]{:S(2)}) collective-permute-start(bf16[2048,256]{1,0:T(8,128)(2,1)} %collective-permute-done.2.k_hbm), channel_id=1, source_target_pairs={{0,8},{8,16},{16,24},{24,28},{28,20},{20,12},{12,4},{4,0},{1,9},{9... | collective-permute-start | bytes 3145736 | tf_op jit(solution)/shard_map/ppermute | solution.py:405
  77.9 0.7 copy-start.10
  78.6 2.9 %collective-permute-start.10 = (bf16[2,256,256]{2,1,0:T(8,128)(2,1)S(1)}, bf16[2,256,256]{2,1,0:T(8,128)(2,1)S(1)}, u32[]{:S(2)}, u32[]{:S(2)}) collective-permute-start(bf16[2,256,256]{2,1,0:T(8,128)(2,1)S(1)} %get-tuple-element.86), channel_id=1, source_target_pairs={{0,1},{1,0},{2,3},{3,2},{4,5},{5,4},{6,7},{7,6},{8,9},{9,8},{10,11... | collective-permute-start | bytes 786440 | tf_op jit(solution)/shard_map/ppermute | solution.py:428
  81.4 43.4 %collective-permute-start.7 = (bf16[2048,256]{1,0:T(8,128)(2,1)}, bf16[2048,256]{1,0:T(8,128)(2,1)S(1)}, u32[]{:S(2)}, u32[]{:S(2)}) collective-permute-start(bf16[2048,256]{1,0:T(8,128)(2,1)} %collective-permute-done.6.v_hbm), channel_id=1, source_target_pairs={{8,0},{16,8},{24,16},{28,24},{20,28},{12,20},{4,12},{0,4},{9,1},{1... | collective-permute-start | bytes 3145736 | tf_op jit(solution)/shard_map/ppermute | solution.py:405
  81.5 0.7 copy-start.11
  82.2 44.0 %collective-permute-start = (bf16[2,256,1024]{2,1,0:T(8,128)(2,1)}, bf16[2,256,1024]{2,1,0:T(8,128)(2,1)}, u32[]{:S(2)}, u32[]{:S(2)}) collective-permute-start(bf16[2,256,1024]{2,1,0:T(8,128)(2,1)} %get-tuple-element.80), channel_id=1, source_target_pairs={{0,1},{1,0},{2,3},{3,2},{4,5},{5,4},{6,7},{7,6},{8,9},{9,8},{10,11... | collective-permute-start | bytes 3145736 | tf_op jit(solution)/shard_map/ppermute | solution.py:428
  98.2 44.9 %collective-permute-start.18 = (bf16[2048,256]{1,0:T(8,128)(2,1)}, bf16[2048,256]{1,0:T(8,128)(2,1)}, u32[]{:S(2)}, u32[]{:S(2)}) collective-permute-start(bf16[2048,256]{1,0:T(8,128)(2,1)} %collective-permute-done.17.v_hbm), channel_id=1, source_target_pairs={{0,8},{8,16},{16,24},{24,28},{28,20},{20,12},{12,4},{4,0},{1,9},{9... | collective-permute-start | bytes 3145736 | tf_op jit(solution)/shard_map/ppermute | solution.py:405
  105.1 102.1 %collective-permute-start.15 = (bf16[2048,256]{1,0:T(8,128)(2,1)}, bf16[2048,256]{1,0:T(8,128)(2,1)}, u32[]{:S(2)}, u32[]{:S(2)}) collective-permute-start(bf16[2048,256]{1,0:T(8,128)(2,1)} %collective-permute-done.14.k_hbm), channel_id=1, source_target_pairs={{8,0},{16,8},{24,16},{28,24},{20,28},{12,20},{4,12},{0,4},{9,1},{1... | collective-permute-start | bytes 3145736 | tf_op jit(solution)/shard_map/ppermute | solution.py:405
  120.6 5.4 %copy-start.1 = (bf16[2048,256]{1,0:T(8,128)(2,1)}, bf16[2048,256]{1,0:T(8,128)(2,1)S(1)}, u32[]{:S(2)}) copy-start(bf16[2048,256]{1,0:T(8,128)(2,1)S(1)} %collective-permute-done.3.k_hbm) | copy-start | bytes 3145732
  121.7 90.6 %collective-permute-start.11 = (bf16[1024,256]{1,0:T(8,128)(2,1)}, bf16[1024,256]{1,0:T(8,128)(2,1)}, u32[]{:S(2)}, u32[]{:S(2)}) collective-permute-start(bf16[1024,256]{1,0:T(8,128)(2,1)} %get-tuple-element.83), channel_id=1, source_target_pairs={{0,8},{8,16},{16,24},{24,28},{28,20},{20,12},{12,4},{4,0},{1,9},{9... | collective-permute-start | bytes 1572872 | tf_op jit(solution)/shard_map/ppermute | solution.py:405
  124.8 5.4 %copy-start.2 = (bf16[2048,256]{1,0:T(8,128)(2,1)}, bf16[2048,256]{1,0:T(8,128)(2,1)S(1)}, u32[]{:S(2)}) copy-start(bf16[2048,256]{1,0:T(8,128)(2,1)S(1)} %collective-permute-done.7.v_hbm) | copy-start | bytes 3145732
  125.9 86.4 %collective-permute-start.12 = (bf16[1024,256]{1,0:T(8,128)(2,1)}, bf16[1024,256]{1,0:T(8,128)(2,1)S(1)}, u32[]{:S(2)}, u32[]{:S(2)}) collective-permute-start(bf16[1024,256]{1,0:T(8,128)(2,1)} %get-tuple-element.81), channel_id=1, source_target_pairs={{8,0},{16,8},{24,16},{28,24},{20,28},{12,20},{4,12},{0,4},{9,1},{1... | collective-permute-start | bytes 1572872 | tf_op jit(solution)/shard_map/ppermute | solution.py:405
  130.2 88.1 %collective-permute-start.4 = (bf16[1024,256]{1,0:T(8,128)(2,1)}, bf16[1024,256]{1,0:T(8,128)(2,1)S(1)}, u32[]{:S(2)}, u32[]{:S(2)}) collective-permute-start(bf16[1024,256]{1,0:T(8,128)(2,1)} %get-tuple-element.84), channel_id=1, source_target_pairs={{0,8},{8,16},{16,24},{24,28},{28,20},{20,12},{12,4},{4,0},{1,9},{9... | collective-permute-start | bytes 1572872 | tf_op jit(solution)/shard_map/ppermute | solution.py:405
  143.1 75.1 %collective-permute-start.8 = (bf16[1024,256]{1,0:T(8,128)(2,1)}, bf16[1024,256]{1,0:T(8,128)(2,1)S(1)}, u32[]{:S(2)}, u32[]{:S(2)}) collective-permute-start(bf16[1024,256]{1,0:T(8,128)(2,1)} %get-tuple-element.82), channel_id=1, source_target_pairs={{8,0},{16,8},{24,16},{28,24},{20,28},{12,20},{4,12},{0,4},{9,1},{1... | collective-permute-start | bytes 1572872 | tf_op jit(solution)/shard_map/ppermute | solution.py:405
  212.3 0.8 copy-start.7
  218.2 0.8 copy-start.5
  218.3 1.0 copy-start.6
  223.3 2.9 %collective-permute-start.19 = (bf16[2,256,1024]{2,1,0:T(8,128)(2,1)}, bf16[2,256,1024]{2,1,0:T(8,128)(2,1)S(1)}, u32[]{:S(2)}, u32[]{:S(2)}) collective-permute-start(bf16[2,256,1024]{2,1,0:T(8,128)(2,1)} %get-tuple-element.68), channel_id=1, source_target_pairs={{0,1},{1,0},{2,3},{3,2},{4,5},{5,4},{6,7},{7,6},{8,9},{9,8},{10,11... | collective-permute-start | bytes 3145736 | tf_op jit(solution)/shard_map/ppermute | solution.py:510

commit v5 on v4

--- a/solution.py
+++ b/solution.py
@@ -11,7 +11,10 @@
 SCALE = HEAD_WIDTH ** (-0.5)
 LOG2E = 1.4426950408889634
 NEGATIVE = -1e30
-PIECES = 2
+
+
+def fetched(shape, index_map):
+    return pl.BlockSpec(shape, index_map, pipeline_mode=pl.Buffered(3))
 
 
 def scores_by_key(keys, queries):
@@ -113,12 +116,12 @@
     def attend(q_ref, k_ref, v_ref, part_ref, log_ref):
         part_ref[0], log_ref[0] = attend_tile(q_ref[0], k_ref[...], v_ref[...])
 
-    tile = pl.BlockSpec((BLOCK_TOKENS, HEAD_WIDTH), lambda n: (table[1, n], table[2, n]))
+    tile = fetched((BLOCK_TOKENS, HEAD_WIDTH), lambda n: (table[1, n], table[2, n]))
     pipeline = pltpu.emit_pipeline(
         attend,
         grid=(count[0],),
         in_specs=[
-            pl.BlockSpec((1, rows, HEAD_WIDTH), lambda n: (table[3, n], 0, table[4, n])),
+            fetched((1, rows, HEAD_WIDTH), lambda n: (table[3, n], 0, table[4, n])),
             tile,
             tile,
         ],
@@ -188,10 +191,10 @@
         combine,
         grid=(count[0],),
         in_specs=[
-            pl.BlockSpec((1, HEAD_WIDTH, rows), lambda n: (ready[n], 0, 0)),
-            pl.BlockSpec((1, 1, rows), lambda n: (ready[n], 0, 0)),
-            pl.BlockSpec((2, HEAD_WIDTH, rows), lambda n: (ready[n], 0, 0)),
-            pl.BlockSpec((2, 1, rows), lambda n: (ready[n], 0, 0)),
+            fetched((1, HEAD_WIDTH, rows), lambda n: (ready[n], 0, 0)),
+            fetched((1, 1, rows), lambda n: (ready[n], 0, 0)),
+            fetched((2, HEAD_WIDTH, rows), lambda n: (ready[n], 0, 0)),
+            fetched((2, 1, rows), lambda n: (ready[n], 0, 0)),
         ],
         out_specs=[
             pl.BlockSpec(
@@ -275,19 +278,19 @@
         held[...], held_log[...] = part, log
         step[0] += 1
 
-    tile = pl.BlockSpec((BLOCK_TOKENS, HEAD_WIDTH), lambda n: (table[1, n], table[2, n]))
+    tile = fetched((BLOCK_TOKENS, HEAD_WIDTH), lambda n: (table[1, n], table[2, n]))
     wide = (1, HEAD_WIDTH, rows)
     pipeline = pltpu.emit_pipeline(
         attend,
         grid=(count[0],),
         in_specs=[
-            pl.BlockSpec((1, rows, HEAD_WIDTH), lambda n: (table[3, n], 0, table[4, n])),
+            fetched((1, rows, HEAD_WIDTH), lambda n: (table[3, n], 0, table[4, n])),
             tile,
             tile,
-            pl.BlockSpec(wide, lambda n: (table[3, n] * heads + table[4, n], 0, 0)),
-            pl.BlockSpec((1, 1, rows), lambda n: (table[3, n] * heads + table[4, n], 0, 0)),
-            pl.BlockSpec(wide, lambda n: (table[5, n], 0, 0)),
-            pl.BlockSpec((1, 1, rows), lambda n: (table[5, n], 0, 0)),
+            fetched(wide, lambda n: (table[3, n] * heads + table[4, n], 0, 0)),
+            fetched((1, 1, rows), lambda n: (table[3, n] * heads + table[4, n], 0, 0)),
+            fetched(wide, lambda n: (table[5, n], 0, 0)),
+            fetched((1, 1, rows), lambda n: (table[5, n], 0, 0)),
         ],
         out_specs=[
             pl.BlockSpec(wide, lambda n: (table[0, n], 0, 0)),
@@ -340,26 +343,52 @@
     )(rep.reshape(1), table, count.reshape(1), queries, keys, values, own, own_log, *state)
 
 
-def half_kernel(rep, from_ref, to_ref):
-    to_ref[...] = from_ref[...]
+def kept_kernel(rep, from_ref, to_ref, held, arrived, left):
+    size = to_ref.shape[1]
+    columns = pl.ds(pl.multiple_of(rep[0] * size, HEAD_WIDTH), size)
+    pieces = [pl.ds(n * BLOCK_TOKENS, BLOCK_TOKENS) for n in range(to_ref.shape[0] // BLOCK_TOKENS)]
+    incoming = [
+        pltpu.make_async_copy(from_ref.at[piece, columns], held.at[piece], arrived.at[n])
+        for n, piece in enumerate(pieces)
+    ]
+    outgoing = [
+        pltpu.make_async_copy(held.at[piece], to_ref.at[piece], left.at[n])
+        for n, piece in enumerate(pieces)
+    ]
+    for copy in incoming:
+        copy.start()
+    for copy, onward in zip(incoming, outgoing):
+        copy.wait()
+        onward.start()
+    for copy in outgoing:
+        copy.wait()
 
 
 def columns_kept(value, rep, size):
     rows = value.shape[0]
+    pieces = rows // BLOCK_TOKENS
     return pl.pallas_call(
-        half_kernel,
-        grid_spec=pltpu.PrefetchScalarGridSpec(
-            num_scalar_prefetch=1,
-            grid=(rows // BLOCK_TOKENS,),
-            in_specs=[pl.BlockSpec((BLOCK_TOKENS, size), lambda n, r: (n, r[0]))],
-            out_specs=pl.BlockSpec((BLOCK_TOKENS, size), lambda n, r: (n, 0)),
-        ),
+        kept_kernel,
+        in_specs=[pl.BlockSpec(memory_space=pltpu.SMEM), pl.BlockSpec(memory_space=pl.ANY)],
+        out_specs=pl.BlockSpec(memory_space=pl.ANY),
         out_shape=jax.ShapeDtypeStruct((rows, size), value.dtype),
+        scratch_shapes=[
+            pltpu.VMEM((rows, size), value.dtype),
+            pltpu.SemaphoreType.DMA((pieces,)),
+            pltpu.SemaphoreType.DMA((pieces,)),
+        ],
         cost_estimate=pl.CostEstimate(
             flops=0, transcendentals=0, bytes_accessed=rows * size * 4
         ),
         name="columns_kept",
     )(rep.reshape(1), value)
+
+
+def piece_starts(blocks):
+    starts = [0]
+    while blocks - starts[-1] > 1:
+        starts.append(starts[-1] + (blocks - starts[-1] + 1) // 2)
+    return starts
 
 
 def ring_order(count):
@@ -412,14 +441,11 @@
         behind = (hop(behind[0], backward), hop(behind[1], backward))
         shards[-step], shards[step] = ahead, behind
     step = full_steps + 1
-    piece = context_keys.shape[0] // PIECES
-    last_pieces = [
-        (
-            hop(ahead[0][n * piece : (n + 1) * piece], onward),
-            hop(behind[1][n * piece : (n + 1) * piece], backward),
-        )
-        for n in range(PIECES)
-    ]
+    starts = piece_starts(blocks_here)
+    last_pieces = []
+    for first, end in zip(starts, starts[1:] + [blocks_here]):
+        rows = slice(first * BLOCK_TOKENS, end * BLOCK_TOKENS)
+        last_pieces.append((hop(ahead[0][rows], onward), hop(behind[1][rows], backward)))
 
     other = rep_size - 1 - rep_index
 
@@ -455,22 +481,26 @@
         jnp.stack([place, tile, *facts]),
         jnp.zeros((5,), jnp.int32),
     )
-    tiles = blocks_here // PIECES
-    piece_of = tile // tiles
+    first_tiles = jnp.array(starts, jnp.int32)
+    piece_of = jnp.sum(tile[:, None] >= first_tiles[None, 1:], axis=1)
+    piece_start = jnp.sum(
+        jnp.where(piece_of[:, None] == jnp.arange(len(starts))[None, :], first_tiles[None, :], 0),
+        axis=1,
+    )
     inside = jnp.concatenate(
         [
             holders[None, :] == wanted[-3:-1, None],
-            (holders == wanted[-1])[None, :] & (piece_of[None, :] == jnp.arange(PIECES)[:, None]),
+            (holders == wanted[-1])[None, :] & (piece_of[None, :] == jnp.arange(len(starts))[:, None]),
         ]
     )
-    both = jnp.any(jnp.all(inside.reshape(2 + PIECES, -1, 2), axis=2), axis=0)
+    both = jnp.any(jnp.all(inside.reshape(2 + len(starts), -1, 2), axis=2), axis=0)
     both = jnp.stack([both, both], axis=1).reshape(-1)
     last_tables, last_counts = compacted(
         inside,
         jnp.stack(
             [
                 place,
-                jnp.where(holders == wanted[-1], tile - piece_of * tiles, tile),
+                jnp.where(holders == wanted[-1], tile - piece_start, tile),
                 *facts,
                 jnp.where(both, items, place + 1 - 2 * (place % 2)),
                 jnp.where(both, place % 2, 0),

time: 232 us -> 219 us (0.944); the launches traced: 227 us -> 217 us
  waiting for transfers between devices: 92.9 us -> 81.2 us
  starting transfers between devices: 20.4 us -> 26 us
  Pallas kernels: 83.1 us -> 80 us
    ppermute x16 -> x18, waiting for transfers between devices: 90 us -> 78.7 us  [hop(): return lax.ppermute(value, 'ctx', pairs)]
    ppermute x16 -> x18, starting transfers between devices: 19.8 us -> 23.8 us  [hop(): return lax.ppermute(value, 'ctx', pairs)]
    pallas_call x2, Pallas kernels: 6.73 us -> 4.05 us  [columns_kept(): pl.pallas_call(kept_kernel, in_specs=[pl.BlockSpec(memory_space=pltpu.SME...]
    pallas_call x4 -> x5, Pallas kernels: 26.7 us -> 28 us  [final_attention(): pl.pallas_call(final_kernel, in_specs=[smem] * 3 + [anywhere] * 9, out_sp...]
  transfers between devices with their start and end apart: 20 -> 22, of which waited for: 8 -> 10; matrix products, arithmetic and copies ran while one was open for 12% -> 12% of each run, Pallas kernels for 33% -> 35%
where the time goes in v5:
time: 219 us; the launch traced here: 217 us
  waiting for transfers between devices  81.2 us (37%)
  Pallas kernels  80 us (37%)
  starting transfers between devices  26 us (12%)
  local copies, waits for them, and re-layouts  15.1 us (7%)
  other arithmetic  14.2 us (6%)
    ppermute x18, waiting for transfers between devices, hop(): return lax.ppermute(value, 'ctx', pairs)  78.7 us
    pallas_call x5, Pallas kernels, final_attention(): pl.pallas_call(final_kernel, in_specs=[smem] * 3 + [anywhere] * 9, out_sp...  28 us
    pallas_call x5, Pallas kernels, pick_attention(): pl.pallas_call(pick_kernel, in_specs=[smem, smem] + [anywhere] * 5, out_s...  27.4 us
    ppermute x18, starting transfers between devices, hop(): return lax.ppermute(value, 'ctx', pairs)  23.8 us
    pallas_call x1, Pallas kernels, own_attention(): pl.pallas_call(own_kernel, grid=(count,), in_specs=[query_spec, key_spec,...  16.2 us
    select_n x3, other arithmetic, all_rows(): jnp.where(rep_index == 0, jnp.concatenate([kept, came], axis=1), jnp.conc...  8.03 us
  transfers between devices with their start and end apart: 22, of which 10 were waited for; matrix products, arithmetic and copies ran while one was open for 12% of the time, Pallas kernels for 35%

profile of v5, /device:TPU:0, one launch (start us, length us, event | category | flops | bytes accessed | tf_op | source)
XLA Modules:
  0.0 216.9 jit_solution(13244363715354295464)
XLA Ops:
  0.0 2.0 columns_kept.2.k_hbm
  2.1 3.1 %collective-permute-start.1 = (bf16[2048,256]{1,0:T(8,128)(2,1)}, bf16[2048,256]{1,0:T(8,128)(2,1)}, u32[]{:S(2)}, u32[]{:S(2)}) collective-permute-start(bf16[2048,256]{1,0:T(8,128)(2,1)} %columns_kept.2.k_hbm), channel_id=1, source_target_pairs={{0,8},{8,16},{16,24},{24,28},{28,20},{20,12},{12,4},{4,0},{1,9},{9... | collective-permute-start | bytes 3145736 | tf_op jit(solution)/shard_map/ppermute | solution.py:434
  5.3 2.0 columns_kept.3.v_hbm
  7.3 2.1 collective-permute-start.18
  9.4 0.7 constant_dynamic-slice_fusion.3
  17.7 0.8 constant_dynamic-slice_fusion.1
  19.4 10.1 %collective-permute-done.1.k_hbm = bf16[2048,256]{1,0:T(8,128)(2,1)} collective-permute-done((bf16[2048,256]{1,0:T(8,128)(2,1)}, bf16[2048,256]{1,0:T(8,128)(2,1)}, u32[]{:S(2)}, u32[]{:S(2)}) %collective-permute-start.1) | collective-permute-done | bytes 1048608 | tf_op jit(solution)/shard_map/ppermute | solution.py:434
  29.5 2.1 collective-permute-start.2
  31.7 21.0 %collective-permute-done.5.v_hbm = bf16[2048,256]{1,0:T(8,128)(2,1)} collective-permute-done((bf16[2048,256]{1,0:T(8,128)(2,1)}, bf16[2048,256]{1,0:T(8,128)(2,1)}, u32[]{:S(2)}, u32[]{:S(2)}) %collective-permute-start.5) | collective-permute-done | bytes 1048608 | tf_op jit(solution)/shard_map/ppermute | solution.py:434
  53.1 1.0 compare_select_fusion.5.ready
  54.1 1.8 collective-permute-start.19
  56.2 1.2 constant_dynamic-slice_fusion.5
  57.6 16.9 %collective-permute-done.2.k_hbm = bf16[2048,256]{1,0:T(8,128)(2,1)} collective-permute-done((bf16[2048,256]{1,0:T(8,128)(2,1)}, bf16[2048,256]{1,0:T(8,128)(2,1)}, u32[]{:S(2)}, u32[]{:S(2)}) %collective-permute-start.2) | collective-permute-done | bytes 1048608 | tf_op jit(solution)/shard_map/ppermute | solution.py:434
  74.5 2.1 collective-permute-start.3
  77.2 1.8 collective-permute-done.6.v_hbm
  80.6 2.0 maximum_select_fusion.1.k_ref
  82.6 14.3 %collective-permute-done.19.v_hbm = bf16[2048,256]{1,0:T(8,128)(2,1)} collective-permute-done((bf16[2048,256]{1,0:T(8,128)(2,1)}, bf16[2048,256]{1,0:T(8,128)(2,1)}, u32[]{:S(2)}, u32[]{:S(2)}) %collective-permute-start.19) | collective-permute-done | bytes 1048608 | tf_op jit(solution)/shard_map/ppermute | solution.py:434
  96.9 2.1 collective-permute-start.20
  99.0 2.5 %collective-permute-done.16.k_hbm = bf16[2048,256]{1,0:T(8,128)(2,1)} collective-permute-done((bf16[2048,256]{1,0:T(8,128)(2,1)}, bf16[2048,256]{1,0:T(8,128)(2,1)}, u32[]{:S(2)}, u32[]{:S(2)}) %collective-permute-start.16) | collective-permute-done | bytes 1048608 | tf_op jit(solution)/shard_map/ppermute | solution.py:434
  101.8 2.1 maximum_select_fusion.2.v_ref
  103.9 3.9 %maximum_select_fusion.q_ref.q_hbm = bf16[2,512,1024]{2,1,0:T(8,128)(2,1)} fusion(bf16[2,256,1024]{2,1,0:T(8,128)(2,1)} %collective-permute-done, bf16[2,256,1024]{2,1,0:T(8,128)(2,1)S(1)} %get-tuple-element.85, pred[]{:T(512)S(6)} %eq.226), kind=kLoop, calls=%fused_computation.1 | loop fusion | flops 9437184 | bytes 4194305 | tf_op jit(solution)/shard_map/jit(_where)/select_n | solution.py:455
  107.8 16.2 %own_attention.1 = (f32[16,128,512]{2,1,0:T(8,128)}, f32[16,1,512]{2,1,0:T(1,128)}, bf16[34,128,512]{2,1,0:T(8,128)(2,1)}, f32[34,1,512]{2,1,0:T(1,128)}, bf16[2...) custom-call(bf16[2,512,1024]{2,1,0:T(8,128)(2,1)} %maximum_select_fusion.q_ref.q_hbm, ...), custom_call_target="tpu_custom_call" | custom-call | flops 2147483648 | bytes 8388608 | tf_op jit(solution)/shard_map/own_attention/pallas_call | solution.py:72
  124.0 0.9 slice.134
  124.9 1.7 collective-permute-start.13
  126.6 6.1 %pick_attention.5 = (bf16[34,128,512]{2,1,0:T(8,128)(2,1)}, f32[34,1,512]{2,1,0:T(1,128)}) custom-call(s32[5,32]{1,0:T(8,128)} %get-tuple-element.95.table, s32[1]{0:T(128)} %get-tuple-element.109.count, bf16[2,512,1024]{2,1,0:T(8,128)(2,1)} %maximum_select_fusion.q_ref.q_hbm, ...), custom_call_target="tpu_custom_call", output_to_operand_aliasing={{0}: (5, {}), {1}: (6, {})} | custom-call | flops 536870912 | bytes 2097152 | tf_op jit(solution)/shard_map/pick_attention/pallas_call | solution.py:141
  132.8 0.9 slice.135
  134.0 0.8 fusion.13
  134.8 1.7 collective-permute-start.11
  137.3 4.6 %collective-permute-done.20.v_hbm = bf16[2048,256]{1,0:T(8,128)(2,1)} collective-permute-done((bf16[2048,256]{1,0:T(8,128)(2,1)}, bf16[2048,256]{1,0:T(8,128)(2,1)}, u32[]{:S(2)}, u32[]{:S(2)}) %collective-permute-start.20) | collective-permute-done | bytes 1048608 | tf_op jit(solution)/shard_map/ppermute | solution.py:434
  141.9 2.0 collective-permute-start.12
  143.9 2.5 %collective-permute-done.17.k_hbm = bf16[2048,256]{1,0:T(8,128)(2,1)} collective-permute-done((bf16[2048,256]{1,0:T(8,128)(2,1)}, bf16[2048,256]{1,0:T(8,128)(2,1)}, u32[]{:S(2)}, u32[]{:S(2)}) %collective-permute-start.17) | collective-permute-done | bytes 1048608 | tf_op jit(solution)/shard_map/ppermute | solution.py:434
  146.4 1.6 collective-permute-start.4
  148.0 5.0 %collective-permute-done.13.k_hbm = bf16[1024,256]{1,0:T(8,128)(2,1)S(1)} collective-permute-done((bf16[1024,256]{1,0:T(8,128)(2,1)}, bf16[1024,256]{1,0:T(8,128)(2,1)S(1)}, u32[]{:S(2)}, u32[]{:S(2)}) %collective-permute-start.13) | collective-permute-done | bytes 524320 | tf_op jit(solution)/shard_map/ppermute | solution.py:434
  153.0 2.0 collective-permute-start.8
  155.0 7.7 %pick_attention.6 = (bf16[34,128,512]{2,1,0:T(8,128)(2,1)}, f32[34,1,512]{2,1,0:T(1,128)}) custom-call(s32[5,32]{1,0:T(8,128)} %get-tuple-element.96.table, s32[1]{0:T(128)} %get-tuple-element.110.count, bf16[2,512,1024]{2,1,0:T(8,128)(2,1)} %maximum_select_fusion.q_ref.q_hbm, ...), custom_call_target="tpu_custom_call", output_to_operand_aliasing={{0}: (5, {}), {1}: (6, {})} | custom-call | flops 536870912 | bytes 2097152 | tf_op jit(solution)/shard_map/pick_attention/pallas_call | solution.py:141
  162.7 6.1 %pick_attention.7 = (bf16[34,128,512]{2,1,0:T(8,128)(2,1)}, f32[34,1,512]{2,1,0:T(1,128)}) custom-call(s32[5,32]{1,0:T(8,128)} %get-tuple-element.97.table, s32[1]{0:T(128)} %get-tuple-element.111.count, bf16[2,512,1024]{2,1,0:T(8,128)(2,1)} %maximum_select_fusion.q_ref.q_hbm, ...), custom_call_target="tpu_custom_call", output_to_operand_aliasing={{0}: (5, {}), {1}: (6, {})} | custom-call | flops 536870912 | bytes 2097152 | tf_op jit(solution)/shard_map/pick_attention/pallas_call | solution.py:141
  168.9 6.2 %pick_attention.8 = (bf16[34,128,512]{2,1,0:T(8,128)(2,1)}, f32[34,1,512]{2,1,0:T(1,128)}) custom-call(s32[5,32]{1,0:T(8,128)} %get-tuple-element.98.table, s32[1]{0:T(128)} %get-tuple-element.112.count, bf16[2,512,1024]{2,1,0:T(8,128)(2,1)} %maximum_select_fusion.q_ref.q_hbm, ...), custom_call_target="tpu_custom_call", output_to_operand_aliasing={{0}: (5, {}), {1}: (6, {})} | custom-call | flops 536870912 | bytes 2097152 | tf_op jit(solution)/shard_map/pick_attention/pallas_call | solution.py:141
  175.1 1.3 pick_attention.9
  176.4 4.4 %merge_parts.1 = (bf16[2,256,2048]{2,1,0:T(8,128)(2,1)}, bf16[2,256,1024]{2,1,0:T(8,128)(2,1)}) custom-call(s32[1]{0:T(128)} %bitcast.rep, s32[16]{0:T(128)} %compare_select_fusion.5.ready, s32[1]{0:T(128)} %bitcast.16.count, f32[16,128,512]{2,1,0:T(8,128)} %get-tuple-element.41.own_hbm, ...), custom_call_target="tpu_custom_call", output_to_operand_aliasing={{0}: (7, {}), {1}: (8, {})} | custom-call | flops 8388608 | bytes 10485760 | tf_op jit(solution)/shard_map/merge_parts/pallas_call | solution.py:213
  180.7 12.3 %final_attention.5 = (bf16[34,128,512]{2,1,0:T(8,128)(2,1)}, f32[34,1,512]{2,1,0:T(1,128)}, bf16[2,256,2048]{2,1,0:T(8,128)(2,1)}, bf16[2,256,1024]{2,1,0:T(8,128)(2,1)}) custom-call(s32[1]{0:T(128)} %bitcast.rep, s32[7,32]{1,0:T(8,128)} %get-tuple-element.100.table, ...), custom_call_target="tpu_custom_call", output_to_operand_aliasing={{0}: (8, {}), {1}: (9, {}), {2}: (10, {}), {3}: (11, {})} | custom-call | flops 268435456 | bytes 2359296 | tf_op jit(solution)/shard_map/final_attention/pallas_call | solution.py:326
  193.1 5.1 %final_attention.6 = (bf16[34,128,512]{2,1,0:T(8,128)(2,1)}, f32[34,1,512]{2,1,0:T(1,128)}, bf16[2,256,2048]{2,1,0:T(8,128)(2,1)}, bf16[2,256,1024]{2,1,0:T(8,128)(2,1)}) custom-call(s32[1]{0:T(128)} %bitcast.rep, s32[7,32]{1,0:T(8,128)} %get-tuple-element.101.table, ...), custom_call_target="tpu_custom_call", output_to_operand_aliasing={{0}: (8, {}), {1}: (9, {}), {2}: (10, {}), {3}: (11, {})} | custom-call | flops 268435456 | bytes 2359296 | tf_op jit(solution)/shard_map/final_attention/pallas_call | solution.py:326
  198.2 0.8 copy-done.5
  199.0 5.1 %final_attention.7 = (bf16[34,128,512]{2,1,0:T(8,128)(2,1)}, f32[34,1,512]{2,1,0:T(1,128)}, bf16[2,256,2048]{2,1,0:T(8,128)(2,1)}, bf16[2,256,1024]{2,1,0:T(8,128)(2,1)}) custom-call(s32[1]{0:T(128)} %bitcast.rep, s32[7,32]{1,0:T(8,128)} %get-tuple-element.102.table, ...), custom_call_target="tpu_custom_call", output_to_operand_aliasing={{0}: (8, {}), {1}: (9, {}), {2}: (10, {}), {3}: (11, {})} | custom-call | flops 268435456 | bytes 2359296 | tf_op jit(solution)/shard_map/final_attention/pallas_call | solution.py:326
  204.9 4.1 %final_attention.8 = (bf16[34,128,512]{2,1,0:T(8,128)(2,1)}, f32[34,1,512]{2,1,0:T(1,128)}, bf16[2,256,2048]{2,1,0:T(8,128)(2,1)}, bf16[2,256,1024]{2,1,0:T(8,128)(2,1)}) custom-call(s32[1]{0:T(128)} %bitcast.rep, s32[7,32]{1,0:T(8,128)} %get-tuple-element.103.table, ...), custom_call_target="tpu_custom_call", output_to_operand_aliasing={{0}: (8, {}), {1}: (9, {}), {2}: (10, {}), {3}: (11, {})} | custom-call | flops 268435456 | bytes 2359296 | tf_op jit(solution)/shard_map/final_attention/pallas_call | solution.py:326
  209.8 1.3 final_attention.9
  211.2 2.2 %collective-permute-start.21 = (bf16[2,256,1024]{2,1,0:T(8,128)(2,1)}, bf16[2,256,1024]{2,1,0:T(8,128)(2,1)S(1)}, u32[]{:S(2)}, u32[]{:S(2)}) collective-permute-start(bf16[2,256,1024]{2,1,0:T(8,128)(2,1)} %get-tuple-element.76), channel_id=1, source_target_pairs={{0,1},{1,0},{2,3},{3,2},{4,5},{5,4},{6,7},{7,6},{8,9},{9,8},{10,11... | collective-permute-start | bytes 3145736 | tf_op jit(solution)/shard_map/ppermute | solution.py:540
  213.3 2.5 %collective-permute-done.21 = bf16[2,256,1024]{2,1,0:T(8,128)(2,1)S(1)} collective-permute-done((bf16[2,256,1024]{2,1,0:T(8,128)(2,1)}, bf16[2,256,1024]{2,1,0:T(8,128)(2,1)S(1)}, u32[]{:S(2)}, u32[]{:S(2)}) %collective-permute-start.21) | collective-permute-done | bytes 1048608 | tf_op jit(solution)/shard_map/ppermute | solution.py:540
  215.8 1.0 constant_dynamic-update-slice_fusion
  (118 shorter events, 14.6 us)
Async XLA Ops:
  2.0 7.3 %copy-start.6 = (bf16[2,256,512]{2,1,0:T(8,128)(2,1)S(1)}, bf16[2,256,512]{2,1,0:T(8,128)(2,1)}, u32[]{:S(2)}) copy-start(bf16[2,256,512]{2,1,0:T(8,128)(2,1)} %param.11) | copy-start | bytes 1572868
  2.1 8.1 %copy-start.15 = (s32[8]{0:T(128)S(1)}, s32[8]{0:T(128)}, u32[]{:S(2)}) copy-start(s32[8]{0:T(128)} %constant.139.clone) | copy-start | bytes 100
  2.1 8.7 %copy-start.14 = (s32[8]{0:T(128)S(1)}, s32[8]{0:T(128)}, u32[]{:S(2)}) copy-start(s32[8]{0:T(128)} %constant.141.clone) | copy-start | bytes 100
  2.1 9.3 %copy-start = (s32[8]{0:T(128)S(1)}, s32[8]{0:T(128)}, u32[]{:S(2)}) copy-start(s32[8]{0:T(128)} %constant.140.clone) | copy-start | bytes 100
  2.1 10.7 %slice-start = ((s32[2,16,3]{1,0,2:T(2,128)}), s32[2,16,2]{1,0,2:T(2,128)S(1)}, s32[]{:S(2)}) async-start(s32[2,16,3]{1,0,2:T(2,128)} %param.15), calls=%async_computation | async-start | bytes 4096 | tf_op jit(solution)/shard_map/slice | solution.py:473
  2.1 11.7 %copy-start.13 = (s32[2]{0:T(128)S(1)}, s32[2]{0:T(128)}, u32[]{:S(2)}) copy-start(s32[2]{0:T(128)} %constant.147) | copy-start | bytes 28
  2.1 14.4 %copy-start.12 = (s32[3]{0:T(128)S(1)}, s32[3]{0:T(128)}, u32[]{:S(2)}) copy-start(s32[3]{0:T(128)} %constant.142.clone) | copy-start | bytes 40
  2.1 15.5 %copy-start.7 = (bf16[2,256,512]{2,1,0:T(8,128)(2,1)S(1)}, bf16[2,256,512]{2,1,0:T(8,128)(2,1)}, u32[]{:S(2)}) copy-start(bf16[2,256,512]{2,1,0:T(8,128)(2,1)} %param.12) | copy-start | bytes 1572868
  2.1 27.4 %collective-permute-start.1 = (bf16[2048,256]{1,0:T(8,128)(2,1)}, bf16[2048,256]{1,0:T(8,128)(2,1)}, u32[]{:S(2)}, u32[]{:S(2)}) collective-permute-start(bf16[2048,256]{1,0:T(8,128)(2,1)} %columns_kept.2.k_hbm), channel_id=1, source_target_pairs={{0,8},{8,16},{16,24},{24,28},{28,20},{20,12},{12,4},{4,0},{1,9},{9... | collective-permute-start | bytes 3145736 | tf_op jit(solution)/shard_map/ppermute | solution.py:434
  5.3 50.7 %collective-permute-start.15 = (bf16[2048,256]{1,0:T(8,128)(2,1)}, bf16[2048,256]{1,0:T(8,128)(2,1)}, u32[]{:S(2)}, u32[]{:S(2)}) collective-permute-start(bf16[2048,256]{1,0:T(8,128)(2,1)} %columns_kept.2.k_hbm), channel_id=1, source_target_pairs={{8,0},{16,8},{24,16},{28,24},{20,28},{12,20},{4,12},{0,4},{9,1},{1... | collective-permute-start | bytes 3145736 | tf_op jit(solution)/shard_map/ppermute | solution.py:434
  7.3 49.0 %copy-start.3 = (bf16[2,256,2048]{2,1,0:T(8,128)(2,1)S(1)}, bf16[2,256,2048]{2,1,0:T(8,128)(2,1)}, u32[]{:S(2)}) copy-start(bf16[2,256,2048]{2,1,0:T(8,128)(2,1)} %param.10) | copy-start | bytes 6291460
  7.3 46.9 %collective-permute-start.18 = (bf16[2048,256]{1,0:T(8,128)(2,1)}, bf16[2048,256]{1,0:T(8,128)(2,1)}, u32[]{:S(2)}, u32[]{:S(2)}) collective-permute-start(bf16[2048,256]{1,0:T(8,128)(2,1)} %columns_kept.3.v_hbm), channel_id=1, source_target_pairs={{0,8},{8,16},{16,24},{24,28},{28,20},{20,12},{12,4},{4,0},{1,9},{9... | collective-permute-start | bytes 3145736 | tf_op jit(solution)/shard_map/ppermute | solution.py:434
  9.4 43.3 %collective-permute-start.5 = (bf16[2048,256]{1,0:T(8,128)(2,1)}, bf16[2048,256]{1,0:T(8,128)(2,1)}, u32[]{:S(2)}, u32[]{:S(2)}) collective-permute-start(bf16[2048,256]{1,0:T(8,128)(2,1)} %columns_kept.3.v_hbm), channel_id=1, source_target_pairs={{8,0},{16,8},{24,16},{28,24},{20,28},{12,20},{4,12},{0,4},{9,1},{1... | collective-permute-start | bytes 3145736 | tf_op jit(solution)/shard_map/ppermute | solution.py:434
  10.1 42.9 %collective-permute-start.9 = (bf16[2,256,256]{2,1,0:T(8,128)(2,1)}, bf16[2,256,256]{2,1,0:T(8,128)(2,1)}, u32[]{:S(2)}, u32[]{:S(2)}) collective-permute-start(bf16[2,256,256]{2,1,0:T(8,128)(2,1)} %get-tuple-element.94), channel_id=1, source_target_pairs={{0,1},{1,0},{2,3},{3,2},{4,5},{5,4},{6,7},{7,6},{8,9},{9,8},{10,11... | collective-permute-start | bytes 786440 | tf_op jit(solution)/shard_map/ppermute | solution.py:454
  29.5 44.9 %collective-permute-start.2 = (bf16[2048,256]{1,0:T(8,128)(2,1)}, bf16[2048,256]{1,0:T(8,128)(2,1)}, u32[]{:S(2)}, u32[]{:S(2)}) collective-permute-start(bf16[2048,256]{1,0:T(8,128)(2,1)} %collective-permute-done.1.k_hbm), channel_id=1, source_target_pairs={{0,8},{8,16},{16,24},{24,28},{28,20},{20,12},{12,4},{4,0},{1,9},{9... | collective-permute-start | bytes 3145736 | tf_op jit(solution)/shard_map/ppermute | solution.py:434
  52.7 26.3 %collective-permute-start.6 = (bf16[2048,256]{1,0:T(8,128)(2,1)}, bf16[2048,256]{1,0:T(8,128)(2,1)}, u32[]{:S(2)}, u32[]{:S(2)}) collective-permute-start(bf16[2048,256]{1,0:T(8,128)(2,1)} %collective-permute-done.5.v_hbm), channel_id=1, source_target_pairs={{8,0},{16,8},{24,16},{28,24},{20,28},{12,20},{4,12},{0,4},{9,1},{1... | collective-permute-start | bytes 3145736 | tf_op jit(solution)/shard_map/ppermute | solution.py:434
  53.1 4.4 %collective-permute-start.10 = (bf16[2,256,256]{2,1,0:T(8,128)(2,1)}, bf16[2,256,256]{2,1,0:T(8,128)(2,1)}, u32[]{:S(2)}, u32[]{:S(2)}) collective-permute-start(bf16[2,256,256]{2,1,0:T(8,128)(2,1)} %get-tuple-element.92), channel_id=1, source_target_pairs={{0,1},{1,0},{2,3},{3,2},{4,5},{5,4},{6,7},{7,6},{8,9},{9,8},{10,11... | collective-permute-start | bytes 786440 | tf_op jit(solution)/shard_map/ppermute | solution.py:454
  54.1 42.8 %collective-permute-start.19 = (bf16[2048,256]{1,0:T(8,128)(2,1)}, bf16[2048,256]{1,0:T(8,128)(2,1)}, u32[]{:S(2)}, u32[]{:S(2)}) collective-permute-start(bf16[2048,256]{1,0:T(8,128)(2,1)} %collective-permute-done.18.v_hbm), channel_id=1, source_target_pairs={{0,8},{8,16},{16,24},{24,28},{28,20},{20,12},{12,4},{4,0},{1,9},{9... | collective-permute-start | bytes 3145736 | tf_op jit(solution)/shard_map/ppermute | solution.py:434
  55.9 45.6 %collective-permute-start.16 = (bf16[2048,256]{1,0:T(8,128)(2,1)}, bf16[2048,256]{1,0:T(8,128)(2,1)}, u32[]{:S(2)}, u32[]{:S(2)}) collective-permute-start(bf16[2048,256]{1,0:T(8,128)(2,1)} %collective-permute-done.15.k_hbm), channel_id=1, source_target_pairs={{8,0},{16,8},{24,16},{28,24},{20,28},{12,20},{4,12},{0,4},{9,1},{1... | collective-permute-start | bytes 3145736 | tf_op jit(solution)/shard_map/ppermute | solution.py:434
  57.4 46.5 %collective-permute-start = (bf16[2,256,1024]{2,1,0:T(8,128)(2,1)}, bf16[2,256,1024]{2,1,0:T(8,128)(2,1)}, u32[]{:S(2)}, u32[]{:S(2)}) collective-permute-start(bf16[2,256,1024]{2,1,0:T(8,128)(2,1)} %get-tuple-element.86), channel_id=1, source_target_pairs={{0,1},{1,0},{2,3},{3,2},{4,5},{5,4},{6,7},{7,6},{8,9},{9,8},{10,11... | collective-permute-start | bytes 3145736 | tf_op jit(solution)/shard_map/ppermute | solution.py:454
  74.5 49.5 %collective-permute-start.3 = (bf16[2048,256]{1,0:T(8,128)(2,1)}, bf16[2048,256]{1,0:T(8,128)(2,1)S(1)}, u32[]{:S(2)}, u32[]{:S(2)}) collective-permute-start(bf16[2048,256]{1,0:T(8,128)(2,1)} %collective-permute-done.2.k_hbm), channel_id=1, source_target_pairs={{0,8},{8,16},{16,24},{24,28},{28,20},{20,12},{12,4},{4,0},{1,9},{9... | collective-permute-start | bytes 3145736 | tf_op jit(solution)/shard_map/ppermute | solution.py:434
  79.0 53.8 %collective-permute-start.7 = (bf16[2048,256]{1,0:T(8,128)(2,1)}, bf16[2048,256]{1,0:T(8,128)(2,1)S(1)}, u32[]{:S(2)}, u32[]{:S(2)}) collective-permute-start(bf16[2048,256]{1,0:T(8,128)(2,1)} %collective-permute-done.6.v_hbm), channel_id=1, source_target_pairs={{8,0},{16,8},{24,16},{28,24},{20,28},{12,20},{4,12},{0,4},{9,1},{1... | collective-permute-start | bytes 3145736 | tf_op jit(solution)/shard_map/ppermute | solution.py:434
  96.9 44.9 %collective-permute-start.20 = (bf16[2048,256]{1,0:T(8,128)(2,1)}, bf16[2048,256]{1,0:T(8,128)(2,1)}, u32[]{:S(2)}, u32[]{:S(2)}) collective-permute-start(bf16[2048,256]{1,0:T(8,128)(2,1)} %collective-permute-done.19.v_hbm), channel_id=1, source_target_pairs={{0,8},{8,16},{16,24},{24,28},{28,20},{20,12},{12,4},{4,0},{1,9},{9... | collective-permute-start | bytes 3145736 | tf_op jit(solution)/shard_map/ppermute | solution.py:434
  101.5 44.9 %collective-permute-start.17 = (bf16[2048,256]{1,0:T(8,128)(2,1)}, bf16[2048,256]{1,0:T(8,128)(2,1)}, u32[]{:S(2)}, u32[]{:S(2)}) collective-permute-start(bf16[2048,256]{1,0:T(8,128)(2,1)} %collective-permute-done.16.k_hbm), channel_id=1, source_target_pairs={{8,0},{16,8},{24,16},{28,24},{20,28},{12,20},{4,12},{0,4},{9,1},{1... | collective-permute-start | bytes 3145736 | tf_op jit(solution)/shard_map/ppermute | solution.py:434
  124.0 10.0 %copy-start.1 = (bf16[2048,256]{1,0:T(8,128)(2,1)}, bf16[2048,256]{1,0:T(8,128)(2,1)S(1)}, u32[]{:S(2)}) copy-start(bf16[2048,256]{1,0:T(8,128)(2,1)S(1)} %collective-permute-done.3.k_hbm) | copy-start | bytes 3145732
  124.9 28.1 %collective-permute-start.13 = (bf16[1024,256]{1,0:T(8,128)(2,1)}, bf16[1024,256]{1,0:T(8,128)(2,1)S(1)}, u32[]{:S(2)}, u32[]{:S(2)}) collective-permute-start(bf16[1024,256]{1,0:T(8,128)(2,1)} %slice.134), channel_id=1, source_target_pairs={{0,8},{8,16},{16,24},{24,28},{28,20},{20,12},{12,4},{4,0},{1,9},{9... | collective-permute-start | bytes 1572872 | tf_op jit(solution)/shard_map/ppermute | solution.py:434
  132.8 30.0 %copy-start.2 = (bf16[2048,256]{1,0:T(8,128)(2,1)}, bf16[2048,256]{1,0:T(8,128)(2,1)S(1)}, u32[]{:S(2)}) copy-start(bf16[2048,256]{1,0:T(8,128)(2,1)S(1)} %collective-permute-done.7.v_hbm) | copy-start | bytes 3145732
  133.7 64.5 %collective-permute-start.14 = (bf16[1024,256]{1,0:T(8,128)(2,1)}, bf16[1024,256]{1,0:T(8,128)(2,1)S(1)}, u32[]{:S(2)}, u32[]{:S(2)}) collective-permute-start(bf16[1024,256]{1,0:T(8,128)(2,1)} %slice.135), channel_id=1, source_target_pairs={{8,0},{16,8},{24,16},{28,24},{20,28},{12,20},{4,12},{0,4},{9,1},{1... | collective-permute-start | bytes 1572872 | tf_op jit(solution)/shard_map/ppermute | solution.py:434
  134.8 69.3 %collective-permute-start.11 = (bf16[512,256]{1,0:T(8,128)(2,1)}, bf16[512,256]{1,0:T(8,128)(2,1)S(1)}, u32[]{:S(2)}, u32[]{:S(2)}) collective-permute-start(bf16[512,256]{1,0:T(8,128)(2,1)} %get-tuple-element.89), channel_id=1, source_target_pairs={{0,8},{8,16},{16,24},{24,28},{28,20},{20,12},{12,4},{4,0},{1,9},{9... | collective-permute-start | bytes 786440 | tf_op jit(solution)/shard_map/ppermute | solution.py:434
  141.9 62.2 %collective-permute-start.12 = (bf16[512,256]{1,0:T(8,128)(2,1)}, bf16[512,256]{1,0:T(8,128)(2,1)S(1)}, u32[]{:S(2)}, u32[]{:S(2)}) collective-permute-start(bf16[512,256]{1,0:T(8,128)(2,1)} %get-tuple-element.87), channel_id=1, source_target_pairs={{8,0},{16,8},{24,16},{28,24},{20,28},{12,20},{4,12},{0,4},{9,1},{1... | collective-permute-start | bytes 786440 | tf_op jit(solution)/shard_map/ppermute | solution.py:434
  146.4 62.6 %collective-permute-start.4 = (bf16[512,256]{1,0:T(8,128)(2,1)}, bf16[512,256]{1,0:T(8,128)(2,1)S(1)}, u32[]{:S(2)}, u32[]{:S(2)}) collective-permute-start(bf16[512,256]{1,0:T(8,128)(2,1)} %get-tuple-element.90), channel_id=1, source_target_pairs={{0,8},{8,16},{16,24},{24,28},{28,20},{20,12},{12,4},{4,0},{1,9},{9... | collective-permute-start | bytes 786440 | tf_op jit(solution)/shard_map/ppermute | solution.py:434
  153.0 9.7 %copy-start.4 = (bf16[1024,256]{1,0:T(8,128)(2,1)}, bf16[1024,256]{1,0:T(8,128)(2,1)S(1)}, u32[]{:S(2)}) copy-start(bf16[1024,256]{1,0:T(8,128)(2,1)S(1)} %collective-permute-done.13.k_hbm) | copy-start | bytes 1572868
  153.0 56.0 %collective-permute-start.8 = (bf16[512,256]{1,0:T(8,128)(2,1)S(1)}, bf16[512,256]{1,0:T(8,128)(2,1)S(1)}, u32[]{:S(2)}, u32[]{:S(2)}) collective-permute-start(bf16[512,256]{1,0:T(8,128)(2,1)S(1)} %get-tuple-element.88), channel_id=1, source_target_pairs={{8,0},{16,8},{24,16},{28,24},{20,28},{12,20},{4,12},{0,4},{9,1},{1... | collective-permute-start | bytes 786440 | tf_op jit(solution)/shard_map/ppermute | solution.py:434
  198.2 0.8 copy-start.5
  204.1 0.7 copy-start.10
  204.1 0.8 copy-start.11
  209.1 0.7 copy-start.8
  209.1 0.8 copy-start.9
  211.2 4.7 %collective-permute-start.21 = (bf16[2,256,1024]{2,1,0:T(8,128)(2,1)}, bf16[2,256,1024]{2,1,0:T(8,128)(2,1)S(1)}, u32[]{:S(2)}, u32[]{:S(2)}) collective-permute-start(bf16[2,256,1024]{2,1,0:T(8,128)(2,1)} %get-tuple-element.76), channel_id=1, source_target_pairs={{0,1},{1,0},{2,3},{3,2},{4,5},{5,4},{6,7},{7,6},{8,9},{9,8},{10,11... | collective-permute-start | bytes 3145736 | tf_op jit(solution)/shard_map/ppermute | solution.py:540

commit v6 on v5

--- a/solution.py
+++ b/solution.py
@@ -1,3 +1,5 @@
+import functools
+
 import jax
 import jax.numpy as jnp
 from jax import lax
@@ -110,36 +112,36 @@
         pipeline(*arrays)
 
 
-def pick_kernel(table, count, q_hbm, k_hbm, v_hbm, part_in, log_in, part_hbm, log_hbm):
+def pick_kernel(row, table, count, q_hbm, k_hbm, v_hbm, part_in, log_in, part_hbm, log_hbm):
     rows = q_hbm.shape[1]
 
     def attend(q_ref, k_ref, v_ref, part_ref, log_ref):
         part_ref[0], log_ref[0] = attend_tile(q_ref[0], k_ref[...], v_ref[...])
 
-    tile = fetched((BLOCK_TOKENS, HEAD_WIDTH), lambda n: (table[1, n], table[2, n]))
+    tile = fetched((BLOCK_TOKENS, HEAD_WIDTH), lambda n: (table[row, 1, n], table[row, 2, n]))
     pipeline = pltpu.emit_pipeline(
         attend,
-        grid=(count[0],),
+        grid=(count[row],),
         in_specs=[
-            fetched((1, rows, HEAD_WIDTH), lambda n: (table[3, n], 0, table[4, n])),
+            fetched((1, rows, HEAD_WIDTH), lambda n: (table[row, 3, n], 0, table[row, 4, n])),
             tile,
             tile,
         ],
         out_specs=[
-            pl.BlockSpec((1, HEAD_WIDTH, rows), lambda n: (table[0, n], 0, 0)),
-            pl.BlockSpec((1, 1, rows), lambda n: (table[0, n], 0, 0)),
-        ],
-    )
-    when_any(count[0], pipeline, q_hbm, k_hbm, v_hbm, part_hbm, log_hbm)
-
-
-def pick_attention(table, count, queries, keys, values, parts, logs):
+            pl.BlockSpec((1, HEAD_WIDTH, rows), lambda n: (table[row, 0, n], 0, 0)),
+            pl.BlockSpec((1, 1, rows), lambda n: (table[row, 0, n], 0, 0)),
+        ],
+    )
+    when_any(count[row], pipeline, q_hbm, k_hbm, v_hbm, part_hbm, log_hbm)
+
+
+def pick_attention(row, table, count, queries, keys, values, parts, logs):
     blocks, rows, width = queries.shape
     expected = 2 * blocks * (width // HEAD_WIDTH) // 8
     smem = pl.BlockSpec(memory_space=pltpu.SMEM)
     anywhere = pl.BlockSpec(memory_space=pl.ANY)
     return pl.pallas_call(
-        pick_kernel,
+        functools.partial(pick_kernel, row),
         in_specs=[smem, smem] + [anywhere] * 5,
         out_specs=[anywhere, anywhere],
         out_shape=[
@@ -153,7 +155,7 @@
             bytes_accessed=expected * rows * HEAD_WIDTH * 8,
         ),
         name="pick_attention",
-    )(table, count.reshape(1), queries, keys, values, parts, logs)
+    )(table, count, queries, keys, values, parts, logs)
 
 
 def merged_rows(rep, own, own_log, first, first_log, second, second_log):
@@ -228,104 +230,106 @@
     )(rep.reshape(1), ready, count.reshape(1), own, own_log, parts, logs, keep, send)
 
 
-def final_kernel(
-    rep,
-    table,
-    count,
-    q_hbm,
-    k_hbm,
-    v_hbm,
-    own_hbm,
-    own_log_hbm,
-    part_in,
-    log_in,
-    keep_in,
-    send_in,
-    part_hbm,
-    log_hbm,
-    keep_hbm,
-    send_hbm,
-    step,
-    held,
-    held_log,
-):
+def final_kernel(first_row, groups, rep, table, count, q_hbm, *refs):
+    arrivals, refs = refs[: 2 * groups], refs[2 * groups :]
+    own_hbm, own_log_hbm, _, _, _, _, part_hbm, log_hbm, keep_hbm, send_hbm = refs[:10]
+    step, held, held_log = refs[10:]
     rows = q_hbm.shape[1]
     half = rows // 2
     heads = send_hbm.shape[2] // HEAD_WIDTH
-    step[0] = 0
-
-    def attend(
-        q_ref,
-        k_ref,
-        v_ref,
-        own_ref,
-        own_log_ref,
-        other_ref,
-        other_log_ref,
-        part_ref,
-        log_ref,
-        keep_ref,
-        send_ref,
-    ):
-        part, log = attend_tile(q_ref[0], k_ref[...], v_ref[...])
-        second = table[6, step[0]] == 1
-        other = jnp.where(second, held[...], other_ref[0])
-        other_log = jnp.where(second, held_log[...], other_log_ref[0])
-        keep_ref[0], send_ref[0] = merged_rows(
-            rep[0], own_ref[0], own_log_ref[0], part, log, other, other_log
-        )
-        part_ref[0], log_ref[0] = part, log
-        held[...], held_log[...] = part, log
-        step[0] += 1
-
-    tile = fetched((BLOCK_TOKENS, HEAD_WIDTH), lambda n: (table[1, n], table[2, n]))
     wide = (1, HEAD_WIDTH, rows)
-    pipeline = pltpu.emit_pipeline(
-        attend,
-        grid=(count[0],),
-        in_specs=[
-            fetched((1, rows, HEAD_WIDTH), lambda n: (table[3, n], 0, table[4, n])),
-            tile,
-            tile,
-            fetched(wide, lambda n: (table[3, n] * heads + table[4, n], 0, 0)),
-            fetched((1, 1, rows), lambda n: (table[3, n] * heads + table[4, n], 0, 0)),
-            fetched(wide, lambda n: (table[5, n], 0, 0)),
-            fetched((1, 1, rows), lambda n: (table[5, n], 0, 0)),
-        ],
-        out_specs=[
-            pl.BlockSpec(wide, lambda n: (table[0, n], 0, 0)),
-            pl.BlockSpec((1, 1, rows), lambda n: (table[0, n], 0, 0)),
-            pl.BlockSpec(
-                (1, half, HEAD_WIDTH), lambda n: (table[3, n], 0, rep[0] * heads + table[4, n])
-            ),
-            pl.BlockSpec((1, half, HEAD_WIDTH), lambda n: (table[3, n], 0, table[4, n])),
-        ],
-    )
-    when_any(
-        count[0],
-        pipeline,
-        q_hbm,
-        k_hbm,
-        v_hbm,
-        own_hbm,
-        own_log_hbm,
-        part_hbm,
-        log_hbm,
-        part_hbm,
-        log_hbm,
-        keep_hbm,
-        send_hbm,
-    )
-
-
-def final_attention(rep, table, count, queries, keys, values, own, own_log, state):
+
+    def run(row, k_hbm, v_hbm):
+        def attend(
+            q_ref,
+            k_ref,
+            v_ref,
+            own_ref,
+            own_log_ref,
+            other_ref,
+            other_log_ref,
+            part_ref,
+            log_ref,
+            keep_ref,
+            send_ref,
+        ):
+            part, log = attend_tile(q_ref[0], k_ref[...], v_ref[...])
+            second = table[row, 6, step[0]] == 1
+            other = jnp.where(second, held[...], other_ref[0])
+            other_log = jnp.where(second, held_log[...], other_log_ref[0])
+            keep_ref[0], send_ref[0] = merged_rows(
+                rep[0], own_ref[0], own_log_ref[0], part, log, other, other_log
+            )
+            part_ref[0], log_ref[0] = part, log
+            held[...], held_log[...] = part, log
+            step[0] += 1
+
+        def at(column):
+            return lambda n: (table[row, column, n], 0, 0)
+
+        def own_at(n):
+            return (table[row, 3, n] * heads + table[row, 4, n], 0, 0)
+
+        tile = fetched(
+            (BLOCK_TOKENS, HEAD_WIDTH), lambda n: (table[row, 1, n], table[row, 2, n])
+        )
+        step[0] = 0
+        pipeline = pltpu.emit_pipeline(
+            attend,
+            grid=(count[row],),
+            in_specs=[
+                fetched(
+                    (1, rows, HEAD_WIDTH), lambda n: (table[row, 3, n], 0, table[row, 4, n])
+                ),
+                tile,
+                tile,
+                fetched(wide, own_at),
+                fetched((1, 1, rows), own_at),
+                fetched(wide, at(5)),
+                fetched((1, 1, rows), at(5)),
+            ],
+            out_specs=[
+                pl.BlockSpec(wide, at(0)),
+                pl.BlockSpec((1, 1, rows), at(0)),
+                pl.BlockSpec(
+                    (1, half, HEAD_WIDTH),
+                    lambda n: (table[row, 3, n], 0, rep[0] * heads + table[row, 4, n]),
+                ),
+                pl.BlockSpec(
+                    (1, half, HEAD_WIDTH), lambda n: (table[row, 3, n], 0, table[row, 4, n])
+                ),
+            ],
+        )
+        when_any(
+            count[row],
+            pipeline,
+            q_hbm,
+            k_hbm,
+            v_hbm,
+            own_hbm,
+            own_log_hbm,
+            part_hbm,
+            log_hbm,
+            part_hbm,
+            log_hbm,
+            keep_hbm,
+            send_hbm,
+        )
+
+    for n in range(groups):
+        run(first_row + n, arrivals[2 * n], arrivals[2 * n + 1])
+
+
+def final_attention(first_row, rep, table, count, queries, arrivals, own, own_log, state):
     rows = queries.shape[1]
-    expected = own.shape[0] // 8
+    groups = len(arrivals)
+    expected = own.shape[0] * groups // 8
     smem = pl.BlockSpec(memory_space=pltpu.SMEM)
     anywhere = pl.BlockSpec(memory_space=pl.ANY)
+    flat = [array for pair in arrivals for array in pair]
     return pl.pallas_call(
-        final_kernel,
-        in_specs=[smem] * 3 + [anywhere] * 9,
+        functools.partial(final_kernel, first_row, groups),
+        in_specs=[smem] * 3 + [anywhere] * (7 + len(flat)),
         out_specs=[anywhere] * 4,
         out_shape=[jax.ShapeDtypeStruct(value.shape, value.dtype) for value in state],
         scratch_shapes=[
@@ -333,14 +337,14 @@
             pltpu.VMEM((HEAD_WIDTH, rows), jnp.bfloat16),
             pltpu.VMEM((1, rows), jnp.float32),
         ],
-        input_output_aliases={8: 0, 9: 1, 10: 2, 11: 3},
+        input_output_aliases={6 + len(flat) + n: n for n in range(4)},
         cost_estimate=pl.CostEstimate(
             flops=expected * rows * BLOCK_TOKENS * HEAD_WIDTH * 4,
             transcendentals=expected * rows * BLOCK_TOKENS,
             bytes_accessed=expected * rows * HEAD_WIDTH * 18,
         ),
         name="final_attention",
-    )(rep.reshape(1), table, count.reshape(1), queries, keys, values, own, own_log, *state)
+    )(rep.reshape(1), table, count, queries, *flat, own, own_log, *state)
 
 
 def kept_kernel(rep, from_ref, to_ref, held, arrived, left):
@@ -436,16 +440,29 @@
     shards = {0: own_shard}
     ahead, behind = own_shard, own_shard
     full_steps = (ctx_size - 1) // 2
-    for step in range(1, full_steps + 1):
+    for step in range(1, full_steps):
         ahead = (hop(ahead[0], onward), hop(ahead[1], onward))
         behind = (hop(behind[0], backward), hop(behind[1], backward))
         shards[-step], shards[step] = ahead, behind
+    starts = piece_starts(blocks_here)
+    cut = starts[1] * BLOCK_TOKENS
+
+    def hop_in_parts(shard, pairs):
+        keys, values = shard
+        return [
+            (hop(keys[:cut], pairs), hop(values[:cut], pairs)),
+            (hop(keys[cut:], pairs), hop(values[cut:], pairs)),
+        ]
+
+    ahead, behind = hop_in_parts(ahead, onward), hop_in_parts(behind, backward)
     step = full_steps + 1
-    starts = piece_starts(blocks_here)
     last_pieces = []
-    for first, end in zip(starts, starts[1:] + [blocks_here]):
-        rows = slice(first * BLOCK_TOKENS, end * BLOCK_TOKENS)
-        last_pieces.append((hop(ahead[0][rows], onward), hop(behind[1][rows], backward)))
+    for n, (first, end) in enumerate(zip(starts, starts[1:] + [blocks_here])):
+        part = min(n, 1)
+        rows = slice((first - part * starts[1]) * BLOCK_TOKENS, (end - part * starts[1]) * BLOCK_TOKENS)
+        last_pieces.append(
+            (hop(ahead[part][0][rows], onward), hop(behind[part][1][rows], backward))
+        )
 
     other = rep_size - 1 - rep_index
 
@@ -467,8 +484,9 @@
         position_of[device] = position
     here = jnp.array(position_of, jnp.int32)[ctx_index]
     distances = sorted(shards, key=abs)
+    late_distances = [-full_steps, full_steps, ctx_size // 2]
     wanted = jnp.array(order, jnp.int32)[
-        (here + jnp.array([*distances, ctx_size // 2], jnp.int32)) % ctx_size
+        (here + jnp.array(distances + late_distances, jnp.int32)) % ctx_size
     ]
     mine = lax.dynamic_slice_in_dim(picks[:, :, :2], rep_index * heads, heads, axis=1).reshape(-1)
     place = jnp.arange(items)
@@ -483,24 +501,28 @@
     )
     first_tiles = jnp.array(starts, jnp.int32)
     piece_of = jnp.sum(tile[:, None] >= first_tiles[None, 1:], axis=1)
+    halfway = holders == wanted[-1]
+    reached = jnp.where(halfway, piece_of, jnp.minimum(piece_of, 1))
     piece_start = jnp.sum(
-        jnp.where(piece_of[:, None] == jnp.arange(len(starts))[None, :], first_tiles[None, :], 0),
+        jnp.where(reached[:, None] == jnp.arange(len(starts))[None, :], first_tiles[None, :], 0),
         axis=1,
     )
+    sides = holders[None, :] == wanted[-3:-1, None]
     inside = jnp.concatenate(
         [
-            holders[None, :] == wanted[-3:-1, None],
-            (holders == wanted[-1])[None, :] & (piece_of[None, :] == jnp.arange(len(starts))[:, None]),
+            sides & (reached == 0)[None, :],
+            sides & (reached == 1)[None, :],
+            halfway[None, :] & (piece_of[None, :] == jnp.arange(len(starts))[:, None]),
         ]
     )
-    both = jnp.any(jnp.all(inside.reshape(2 + len(starts), -1, 2), axis=2), axis=0)
+    both = jnp.any(jnp.all(inside.reshape(4 + len(starts), -1, 2), axis=2), axis=0)
     both = jnp.stack([both, both], axis=1).reshape(-1)
     last_tables, last_counts = compacted(
         inside,
         jnp.stack(
             [
                 place,
-                jnp.where(holders == wanted[-1], tile - piece_start, tile),
+                tile - piece_start,
                 *facts,
                 jnp.where(both, items, place + 1 - 2 * (place % 2)),
                 jnp.where(both, place % 2, 0),
@@ -517,26 +539,28 @@
     own, own_log, parts, logs, keep, send = own_attention(
         block_queries, block_keys, block_values, head_grouping, full_width
     )
-    for n, distance in enumerate(distances[:-2]):
+    for n, distance in enumerate(distances):
         keys, values = shards[distance]
-        parts, logs = pick_attention(tables[n], counts[n], block_queries, keys, values, parts, logs)
+        parts, logs = pick_attention(n, tables, counts, block_queries, keys, values, parts, logs)
     keep, send = merge(
         rep_index, ready[0, 0], ready_counts[0], own, own_log, parts, logs, keep, send
     )
     state = (parts, logs, keep, send)
-    late_arrivals = [shards[distance] for distance in distances[-2:]] + last_pieces
-    for n, (keys, values) in enumerate(late_arrivals):
+    late_arrivals = [list(pair) for pair in zip(ahead, behind)] + [[pair] for pair in last_pieces]
+    row = 0
+    for arrivals in late_arrivals:
         state = final_attention(
+            row,
             rep_index,
-            last_tables[n],
-            last_counts[n],
+            last_tables,
+            last_counts,
             block_queries,
-            keys,
-            values,
+            arrivals,
             own,
             own_log,
             state,
         )
+        row += len(arrivals)
     arriving = lax.ppermute(state[3], "rep", swap)
     return lax.dynamic_update_slice_in_dim(state[2], arriving, other * width, axis=2)
 

time: 219 us -> 221 us (level)
  the two profiles are of different devices: /device:TPU:0 before, /device:TPU:25 now
where the time goes in v6:
time: 221 us; the launch traced here: 219 us
  Pallas kernels  81.1 us (37%)
  waiting for transfers between devices  70 us (32%)
  starting transfers between devices  32.7 us (15%)
  local copies, waits for them, and re-layouts  19.2 us (9%)
  other arithmetic  15.6 us (7%)
    ppermute x22, waiting for transfers between devices, hop(): return lax.ppermute(value, 'ctx', pairs)  67.5 us
    pallas_call x5, Pallas kernels, pick_attention(): pl.pallas_call(functools.partial(pick_kernel, row), in_specs=[smem, smem]...  32.2 us
    pallas_call x5, Pallas kernels, final_attention(): pl.pallas_call(functools.partial(final_kernel, first_row, groups), in_spe...  22.3 us
    ppermute x22, starting transfers between devices, hop(): return lax.ppermute(value, 'ctx', pairs)  16.5 us
    pallas_call x1, Pallas kernels, own_attention(): pl.pallas_call(own_kernel, grid=(count,), in_specs=[query_spec, key_spec,...  16.2 us
    ppermute x1, starting transfers between devices, body(): arriving = lax.ppermute(state[3], 'rep', swap)  11.9 us
    select_n x3, other arithmetic, all_rows(): jnp.where(rep_index == 0, jnp.concatenate([kept, came], axis=1), jnp.conc...  8.25 us
    pallas_call x1, Pallas kernels, merge(): pl.pallas_call(merge_kernel, in_specs=[smem] * 3 + [anywhere] * 6, out_sp...  6.37 us
  transfers between devices with their start and end apart: 26, of which 7 were waited for; matrix products, arithmetic and copies ran while one was open for 14% of the time, Pallas kernels for 36%

profile of v6, /device:TPU:25, one launch (start us, length us, event | category | flops | bytes accessed | tf_op | source)
XLA Modules:
  0.0 219.0 jit_solution(3539813114949602343)
XLA Ops:
  0.0 2.0 columns_kept.2.k_hbm
  2.1 1.3 collective-permute-start.1
  3.6 2.0 columns_kept.3.v_hbm
  5.6 1.3 collective-permute-start.17
  7.2 1.9 collective-permute-start.9
  17.9 8.6 %collective-permute-done.1.k_hbm = bf16[2048,256]{1,0:T(8,128)(2,1)} collective-permute-done((bf16[2048,256]{1,0:T(8,128)(2,1)}, bf16[2048,256]{1,0:T(8,128)(2,1)}, u32[]{:S(2)}, u32[]{:S(2)}) %collective-permute-start.1) | collective-permute-done | bytes 1048608 | tf_op jit(solution)/shard_map/ppermute | solution.py:438
  26.5 1.2 collective-permute-start.2
  27.9 0.8 constant_dynamic-slice_fusion.1
  28.7 21.2 %collective-permute-done.5.v_hbm = bf16[2048,256]{1,0:T(8,128)(2,1)} collective-permute-done((bf16[2048,256]{1,0:T(8,128)(2,1)}, bf16[2048,256]{1,0:T(8,128)(2,1)}, u32[]{:S(2)}, u32[]{:S(2)}) %collective-permute-start.5) | collective-permute-done | bytes 1048608 | tf_op jit(solution)/shard_map/ppermute | solution.py:438
  51.0 2.1 collective-permute-start.10
  53.1 2.8 %constant_dynamic-slice_fusion.5 = (bf16[2,256,1024]{2,1,0:T(8,128)(2,1)S(1)}, bf16[2,256,1024]{2,1,0:T(8,128)(2,1)}) fusion(bf16[2,256,2048]{2,1,0:T(8,128)(2,1)} %param.10, s32[]{:T(128)S(6)} %select_n.279, s32[]{:T(128)S(6)} %select_n.280), kind=kLoop, calls=%fused_computation.51 | loop fusion | bytes 4194312 | tf_op jit(solution)/shard_map/dynamic_slice | solution.py:427
  55.9 1.3 collective-permute-start.18
  57.6 1.2 compare_select_fusion.5.ready
  58.8 2.1 maximum_select_fusion.1.k_ref
  61.1 2.2 %maximum_select_fusion.2.v_ref = bf16[2,512,256]{2,1,0:T(8,128)(2,1)} fusion(bf16[2,256,256]{2,1,0:T(8,128)(2,1)} %collective-permute-done.10, bf16[2,256,256]{2,1,0:T(8,128)(2,1)} %get-tuple-element.107, pred[]{:T(512)S(6)} %eq.253), kind=kLoop, calls=%fused_computation.4 | loop fusion | flops 2359296 | bytes 1048577 | tf_op jit(solution)/shard_map/jit(_where)/select_n | solution.py:472
  63.4 8.0 %collective-permute-done.2.k_hbm = bf16[2048,256]{1,0:T(8,128)(2,1)S(1)} collective-permute-done((bf16[2048,256]{1,0:T(8,128)(2,1)}, bf16[2048,256]{1,0:T(8,128)(2,1)S(1)}, u32[]{:S(2)}, u32[]{:S(2)}) %collective-permute-start.2) | collective-permute-done | bytes 1048608 | tf_op jit(solution)/shard_map/ppermute | solution.py:438
  71.4 1.2 fusion.16
  72.5 1.2 collective-permute-start.13
  73.8 1.1 fusion.15
  75.1 18.8 %collective-permute-done.18.v_hbm = bf16[2048,256]{1,0:T(8,128)(2,1)} collective-permute-done((bf16[2048,256]{1,0:T(8,128)(2,1)}, bf16[2048,256]{1,0:T(8,128)(2,1)}, u32[]{:S(2)}, u32[]{:S(2)}) %collective-permute-start.18) | collective-permute-done | bytes 1048608 | tf_op jit(solution)/shard_map/ppermute | solution.py:438
  93.9 2.3 %fusion.14 = (bf16[1024,256]{1,0:T(8,128)(2,1)}, bf16[1024,256]{1,0:T(8,128)(2,1)}) fusion(bf16[2048,256]{1,0:T(8,128)(2,1)} %collective-permute-done.18.v_hbm), kind=kLoop, calls=%fused_computation.106 | loop fusion | bytes 2097152 | tf_op jit(solution)/shard_map/slice | solution.py:453
  96.2 1.2 collective-permute-start.23
  97.6 3.9 %maximum_select_fusion.q_ref.q_hbm = bf16[2,512,1024]{2,1,0:T(8,128)(2,1)} fusion(bf16[2,256,1024]{2,1,0:T(8,128)(2,1)} %collective-permute-done, bf16[2,256,1024]{2,1,0:T(8,128)(2,1)S(1)} %get-tuple-element.93, pred[]{:T(512)S(6)} %eq.253), kind=kLoop, calls=%fused_computation.1 | loop fusion | flops 9437184 | bytes 4194305 | tf_op jit(solution)/shard_map/jit(_where)/select_n | solution.py:472
  101.5 1.3 collective-permute-start.7
  102.8 16.2 %own_attention.1 = (f32[16,128,512]{2,1,0:T(8,128)}, f32[16,1,512]{2,1,0:T(1,128)}, bf16[34,128,512]{2,1,0:T(8,128)(2,1)}, f32[34,1,512]{2,1,0:T(1,128)}, bf16[2...) custom-call(bf16[2,512,1024]{2,1,0:T(8,128)(2,1)} %maximum_select_fusion.q_ref.q_hbm, ...), custom_call_target="tpu_custom_call" | custom-call | flops 2147483648 | bytes 8388608 | tf_op jit(solution)/shard_map/own_attention/pallas_call | solution.py:74
  119.0 5.8 %pick_attention.5 = (bf16[34,128,512]{2,1,0:T(8,128)(2,1)}, f32[34,1,512]{2,1,0:T(1,128)}) custom-call(s32[5,5,32]{2,1,0:T(8,128)} %broadcast_select_fusion.1.table, s32[5]{0:T(128)} %copy-done.17, bf16[2,512,1024]{2,1,0:T(8,128)(2,1)} %maximum_select_fusion.q_ref.q_hbm, ...), custom_call_target="tpu_custom_call", output_to_operand_aliasing={{0}: (5, {}), {1}: (6, {})} | custom-call | flops 536870912 | bytes 2097152 | tf_op jit(solution)/shard_map/pick_attention/pallas_call | solution.py:143
  124.8 2.3 %fusion.13 = (bf16[1024,256]{1,0:T(8,128)(2,1)}, bf16[1024,256]{1,0:T(8,128)(2,1)}) fusion(bf16[2048,256]{1,0:T(8,128)(2,1)} %collective-permute-done.21.k_hbm), kind=kLoop, calls=%fused_computation.105 | loop fusion | bytes 2097152 | tf_op jit(solution)/shard_map/slice | solution.py:453
  127.1 1.5 collective-permute-start.19
  128.6 1.4 collective-permute-start.14
  130.1 5.8 %pick_attention.6 = (bf16[34,128,512]{2,1,0:T(8,128)(2,1)}, f32[34,1,512]{2,1,0:T(1,128)}) custom-call(s32[5,5,32]{2,1,0:T(8,128)} %broadcast_select_fusion.1.table, s32[5]{0:T(128)} %copy-done.17, bf16[2,512,1024]{2,1,0:T(8,128)(2,1)} %maximum_select_fusion.q_ref.q_hbm, ...), custom_call_target="tpu_custom_call", output_to_operand_aliasing={{0}: (5, {}), {1}: (6, {})} | custom-call | flops 536870912 | bytes 2097152 | tf_op jit(solution)/shard_map/pick_attention/pallas_call | solution.py:143
  135.9 1.0 fusion.18
  136.9 0.8 fusion.17
  137.8 1.1 collective-permute-done.24.refs_2_
  139.1 1.5 collective-permute-start.12
  140.6 9.7 %collective-permute-done.22.refs_2_ = bf16[1024,256]{1,0:T(8,128)(2,1)S(1)} collective-permute-done((bf16[1024,256]{1,0:T(8,128)(2,1)}, bf16[1024,256]{1,0:T(8,128)(2,1)S(1)}, u32[]{:S(2)}, u32[]{:S(2)}) %collective-permute-start.22) | collective-permute-done | bytes 524320 | tf_op jit(solution)/shard_map/ppermute | solution.py:438
  150.2 1.7 collective-permute-start.8
  151.9 4.2 %pick_attention.7 = (bf16[34,128,512]{2,1,0:T(8,128)(2,1)}, f32[34,1,512]{2,1,0:T(1,128)}) custom-call(s32[5,5,32]{2,1,0:T(8,128)} %broadcast_select_fusion.1.table, s32[5]{0:T(128)} %copy-done.17, bf16[2,512,1024]{2,1,0:T(8,128)(2,1)} %maximum_select_fusion.q_ref.q_hbm, ...), custom_call_target="tpu_custom_call", output_to_operand_aliasing={{0}: (5, {}), {1}: (6, {})} | custom-call | flops 536870912 | bytes 2097152 | tf_op jit(solution)/shard_map/pick_attention/pallas_call | solution.py:143
  156.1 6.6 %pick_attention.8 = (bf16[34,128,512]{2,1,0:T(8,128)(2,1)}, f32[34,1,512]{2,1,0:T(1,128)}) custom-call(s32[5,5,32]{2,1,0:T(8,128)} %broadcast_select_fusion.1.table, s32[5]{0:T(128)} %copy-done.17, bf16[2,512,1024]{2,1,0:T(8,128)(2,1)} %maximum_select_fusion.q_ref.q_hbm, bf16[2048,256]{1,0:T(8,128)(2,1)} %copy-done.1, ...), custom_call_target="tpu_custom_call", output_to_operand_aliasing={{0}: (5, {}), {1}: (6, {})} | custom-call | flops 536870912 | bytes 2097152 | tf_op jit(solution)/shard_map/pick_attention/pallas_call | solution.py:143
  162.7 9.8 %pick_attention.9 = (bf16[34,128,512]{2,1,0:T(8,128)(2,1)}, f32[34,1,512]{2,1,0:T(1,128)}) custom-call(s32[5,5,32]{2,1,0:T(8,128)} %broadcast_select_fusion.1.table, s32[5]{0:T(128)} %copy-done.17, bf16[2,512,1024]{2,1,0:T(8,128)(2,1)} %maximum_select_fusion.q_ref.q_hbm, ...), custom_call_target="tpu_custom_call", output_to_operand_aliasing={{0}: (5, {}), {1}: (6, {})} | custom-call | flops 536870912 | bytes 2097152 | tf_op jit(solution)/shard_map/pick_attention/pallas_call | solution.py:143
  172.5 6.4 %merge_parts.1 = (bf16[2,256,2048]{2,1,0:T(8,128)(2,1)}, bf16[2,256,1024]{2,1,0:T(8,128)(2,1)}) custom-call(s32[1]{0:T(128)} %bitcast.rep, s32[16]{0:T(128)} %compare_select_fusion.5.ready, s32[1]{0:T(128)} %bitcast.6.count, f32[16,128,512]{2,1,0:T(8,128)} %get-tuple-element.41.own_hbm.refs_4_.refs_2_, ...), custom_call_target="tpu_custom_call", output_to_operand_aliasing={{0}: (7, {}), {1}: (8, {})} | custom-call | flops 8388608 | bytes 10485760 | tf_op jit(solution)/shard_map/merge_parts/pallas_call | solution.py:215
  178.9 7.6 %final_attention.5 = (bf16[34,128,512]{2,1,0:T(8,128)(2,1)}, f32[34,1,512]{2,1,0:T(1,128)}, bf16[2,256,2048]{2,1,0:T(8,128)(2,1)}, bf16[2,256,1024]{2,1,0:T(8,128)(2,1)}) custom-call(s32[1]{0:T(128)} %bitcast.rep, s32[7,7,32]{2,1,0:T(8,128)} %broadcast_select_fusion.table, ...), custom_call_target="tpu_custom_call", output_to_operand_aliasing={{0}: (10, {}), {1}: (11, {}), {2}: (12, {}), {3}: (13, {})} | custom-call | flops 536870912 | bytes 4718592 | tf_op jit(solution)/shard_map/final_attention/pallas_call | solution.py:330
  186.5 8.6 %final_attention.6 = (bf16[34,128,512]{2,1,0:T(8,128)(2,1)}, f32[34,1,512]{2,1,0:T(1,128)}, bf16[2,256,2048]{2,1,0:T(8,128)(2,1)}, bf16[2,256,1024]{2,1,0:T(8,128)(2,1)}) custom-call(s32[1]{0:T(128)} %bitcast.rep, s32[7,7,32]{2,1,0:T(8,128)} %broadcast_select_fusion.table, ...), custom_call_target="tpu_custom_call", output_to_operand_aliasing={{0}: (10, {}), {1}: (11, {}), {2}: (12, {}), {3}: (13, {})} | custom-call | flops 536870912 | bytes 4718592 | tf_op jit(solution)/shard_map/final_attention/pallas_call | solution.py:330
  195.9 1.1 final_attention.7
  197.8 3.9 %final_attention.8 = (bf16[34,128,512]{2,1,0:T(8,128)(2,1)}, f32[34,1,512]{2,1,0:T(1,128)}, bf16[2,256,2048]{2,1,0:T(8,128)(2,1)}, bf16[2,256,1024]{2,1,0:T(8,128)(2,1)}) custom-call(s32[1]{0:T(128)} %bitcast.rep, s32[7,7,32]{2,1,0:T(8,128)} %broadcast_select_fusion.table, ...), custom_call_target="tpu_custom_call", output_to_operand_aliasing={{0}: (8, {}), {1}: (9, {}), {2}: (10, {}), {3}: (11, {})} | custom-call | flops 268435456 | bytes 2359296 | tf_op jit(solution)/shard_map/final_attention/pallas_call | solution.py:330
  202.4 1.1 final_attention.9
  203.6 11.9 %collective-permute-start.25 = (bf16[2,256,1024]{2,1,0:T(8,128)(2,1)}, bf16[2,256,1024]{2,1,0:T(8,128)(2,1)S(1)}, u32[]{:S(2)}, u32[]{:S(2)}) collective-permute-start(bf16[2,256,1024]{2,1,0:T(8,128)(2,1)} %get-tuple-element.76), channel_id=1, source_target_pairs={{0,1},{1,0},{2,3},{3,2},{4,5},{5,4},{6,7},{7,6},{8,9},{9,8},{10,11... | collective-permute-start | bytes 3145736 | tf_op jit(solution)/shard_map/ppermute | solution.py:564
  215.4 2.5 %collective-permute-done.25 = bf16[2,256,1024]{2,1,0:T(8,128)(2,1)S(1)} collective-permute-done((bf16[2,256,1024]{2,1,0:T(8,128)(2,1)}, bf16[2,256,1024]{2,1,0:T(8,128)(2,1)S(1)}, u32[]{:S(2)}, u32[]{:S(2)}) %collective-permute-start.25) | collective-permute-done | bytes 1048608 | tf_op jit(solution)/shard_map/ppermute | solution.py:564
  217.9 1.0 constant_dynamic-update-slice_fusion
  (138 shorter events, 14.1 us)
Async XLA Ops:
  2.0 5.2 %copy-start.9 = (bf16[2,256,512]{2,1,0:T(8,128)(2,1)S(1)}, bf16[2,256,512]{2,1,0:T(8,128)(2,1)}, u32[]{:S(2)}) copy-start(bf16[2,256,512]{2,1,0:T(8,128)(2,1)} %param.11) | copy-start | bytes 1572868
  2.0 7.1 %slice-start = ((s32[2,16,3]{1,0,2:T(2,128)}), s32[2,16,2]{1,0,2:T(2,128)S(1)}, s32[]{:S(2)}) async-start(s32[2,16,3]{1,0,2:T(2,128)} %param.15), calls=%async_computation | async-start | bytes 4096 | tf_op jit(solution)/shard_map/slice | solution.py:491
  2.0 7.4 %copy-start.21 = (s32[8]{0:T(128)S(1)}, s32[8]{0:T(128)}, u32[]{:S(2)}) copy-start(s32[8]{0:T(128)} %constant.143.clone) | copy-start | bytes 100
  2.0 8.0 %copy-start.20 = (s32[8]{0:T(128)S(1)}, s32[8]{0:T(128)}, u32[]{:S(2)}) copy-start(s32[8]{0:T(128)} %constant.145.clone) | copy-start | bytes 100
  2.1 8.7 %copy-start = (s32[8]{0:T(128)S(1)}, s32[8]{0:T(128)}, u32[]{:S(2)}) copy-start(s32[8]{0:T(128)} %constant.144.clone) | copy-start | bytes 100
  2.1 10.3 %copy-start.19 = (s32[2]{0:T(128)S(1)}, s32[2]{0:T(128)}, u32[]{:S(2)}) copy-start(s32[2]{0:T(128)} %constant.151) | copy-start | bytes 28
  2.1 12.1 %copy-start.18 = (s32[3]{0:T(128)S(1)}, s32[3]{0:T(128)}, u32[]{:S(2)}) copy-start(s32[3]{0:T(128)} %constant.146.clone) | copy-start | bytes 40
  2.1 25.8 %copy-start.10 = (bf16[2,256,512]{2,1,0:T(8,128)(2,1)S(1)}, bf16[2,256,512]{2,1,0:T(8,128)(2,1)}, u32[]{:S(2)}) copy-start(bf16[2,256,512]{2,1,0:T(8,128)(2,1)} %param.12) | copy-start | bytes 1572868
  2.1 24.4 %collective-permute-start.1 = (bf16[2048,256]{1,0:T(8,128)(2,1)}, bf16[2048,256]{1,0:T(8,128)(2,1)}, u32[]{:S(2)}, u32[]{:S(2)}) collective-permute-start(bf16[2048,256]{1,0:T(8,128)(2,1)} %columns_kept.2.k_hbm), channel_id=1, source_target_pairs={{0,8},{8,16},{16,24},{24,28},{28,20},{20,12},{12,4},{4,0},{1,9},{9... | collective-permute-start | bytes 3145736 | tf_op jit(solution)/shard_map/ppermute | solution.py:438
  3.4 57.5 %collective-permute-start.20 = (bf16[2048,256]{1,0:T(8,128)(2,1)}, bf16[2048,256]{1,0:T(8,128)(2,1)}, u32[]{:S(2)}, u32[]{:S(2)}) collective-permute-start(bf16[2048,256]{1,0:T(8,128)(2,1)} %columns_kept.2.k_hbm), channel_id=1, source_target_pairs={{8,0},{16,8},{24,16},{28,24},{20,28},{12,20},{4,12},{0,4},{9,1},{1... | collective-permute-start | bytes 3145736 | tf_op jit(solution)/shard_map/ppermute | solution.py:438
  5.6 50.2 %collective-permute-start.17 = (bf16[2048,256]{1,0:T(8,128)(2,1)}, bf16[2048,256]{1,0:T(8,128)(2,1)}, u32[]{:S(2)}, u32[]{:S(2)}) collective-permute-start(bf16[2048,256]{1,0:T(8,128)(2,1)} %columns_kept.3.v_hbm), channel_id=1, source_target_pairs={{0,8},{8,16},{16,24},{24,28},{28,20},{20,12},{12,4},{4,0},{1,9},{9... | collective-permute-start | bytes 3145736 | tf_op jit(solution)/shard_map/ppermute | solution.py:438
  6.9 43.0 %collective-permute-start.5 = (bf16[2048,256]{1,0:T(8,128)(2,1)}, bf16[2048,256]{1,0:T(8,128)(2,1)}, u32[]{:S(2)}, u32[]{:S(2)}) collective-permute-start(bf16[2048,256]{1,0:T(8,128)(2,1)} %columns_kept.3.v_hbm), channel_id=1, source_target_pairs={{8,0},{16,8},{24,16},{28,24},{20,28},{12,20},{4,12},{0,4},{9,1},{1... | collective-permute-start | bytes 3145736 | tf_op jit(solution)/shard_map/ppermute | solution.py:438
  7.2 43.1 %collective-permute-start.9 = (bf16[2,256,256]{2,1,0:T(8,128)(2,1)S(1)}, bf16[2,256,256]{2,1,0:T(8,128)(2,1)S(1)}, u32[]{:S(2)}, u32[]{:S(2)}) collective-permute-start(bf16[2,256,256]{2,1,0:T(8,128)(2,1)S(1)} %get-tuple-element.110), channel_id=1, source_target_pairs={{0,1},{1,0},{2,3},{3,2},{4,5},{5,4},{6,7},{7,6},{8,9},{9,8},{10,11... | collective-permute-start | bytes 786440 | tf_op jit(solution)/shard_map/ppermute | solution.py:471
  12.2 43.6 %copy-start.17 = (s32[5]{0:T(128)}, s32[5]{0:T(128)S(1)}, u32[]{:S(2)}) copy-start(s32[5]{0:T(128)S(1)} %convert_reduce_fusion.count) | copy-start | bytes 64
  14.8 41.1 %copy-start.16 = (s32[7]{0:T(128)}, s32[7]{0:T(128)S(1)}, u32[]{:S(2)}) copy-start(s32[7]{0:T(128)S(1)} %get-tuple-element.81.count) | copy-start | bytes 88
  26.5 44.8 %collective-permute-start.2 = (bf16[2048,256]{1,0:T(8,128)(2,1)}, bf16[2048,256]{1,0:T(8,128)(2,1)S(1)}, u32[]{:S(2)}, u32[]{:S(2)}) collective-permute-start(bf16[2048,256]{1,0:T(8,128)(2,1)} %collective-permute-done.1.k_hbm), channel_id=1, source_target_pairs={{0,8},{8,16},{16,24},{24,28},{28,20},{20,12},{12,4},{4,0},{1,9},{9... | collective-permute-start | bytes 3145736 | tf_op jit(solution)/shard_map/ppermute | solution.py:438
  49.9 23.8 %collective-permute-start.6 = (bf16[2048,256]{1,0:T(8,128)(2,1)}, bf16[2048,256]{1,0:T(8,128)(2,1)S(1)}, u32[]{:S(2)}, u32[]{:S(2)}) collective-permute-start(bf16[2048,256]{1,0:T(8,128)(2,1)} %collective-permute-done.5.v_hbm), channel_id=1, source_target_pairs={{8,0},{16,8},{24,16},{28,24},{20,28},{12,20},{4,12},{0,4},{9,1},{1... | collective-permute-start | bytes 3145736 | tf_op jit(solution)/shard_map/ppermute | solution.py:438
  50.3 0.7 copy-start.15
  51.0 6.3 %collective-permute-start.10 = (bf16[2,256,256]{2,1,0:T(8,128)(2,1)}, bf16[2,256,256]{2,1,0:T(8,128)(2,1)}, u32[]{:S(2)}, u32[]{:S(2)}) collective-permute-start(bf16[2,256,256]{2,1,0:T(8,128)(2,1)} %get-tuple-element.108), channel_id=1, source_target_pairs={{0,1},{1,0},{2,3},{3,2},{4,5},{5,4},{6,7},{7,6},{8,9},{9,8},{10,11... | collective-permute-start | bytes 786440 | tf_op jit(solution)/shard_map/ppermute | solution.py:471
  55.9 38.1 %collective-permute-start.18 = (bf16[2048,256]{1,0:T(8,128)(2,1)}, bf16[2048,256]{1,0:T(8,128)(2,1)}, u32[]{:S(2)}, u32[]{:S(2)}) collective-permute-start(bf16[2048,256]{1,0:T(8,128)(2,1)} %collective-permute-done.17.v_hbm), channel_id=1, source_target_pairs={{0,8},{8,16},{16,24},{24,28},{28,20},{20,12},{12,4},{4,0},{1,9},{9... | collective-permute-start | bytes 3145736 | tf_op jit(solution)/shard_map/ppermute | solution.py:438
  57.3 40.2 %collective-permute-start = (bf16[2,256,1024]{2,1,0:T(8,128)(2,1)}, bf16[2,256,1024]{2,1,0:T(8,128)(2,1)}, u32[]{:S(2)}, u32[]{:S(2)}) collective-permute-start(bf16[2,256,1024]{2,1,0:T(8,128)(2,1)} %get-tuple-element.94), channel_id=1, source_target_pairs={{0,1},{1,0},{2,3},{3,2},{4,5},{5,4},{6,7},{7,6},{8,9},{9,8},{10,11... | collective-permute-start | bytes 3145736 | tf_op jit(solution)/shard_map/ppermute | solution.py:471
  60.9 40.6 %collective-permute-start.21 = (bf16[2048,256]{1,0:T(8,128)(2,1)}, bf16[2048,256]{1,0:T(8,128)(2,1)}, u32[]{:S(2)}, u32[]{:S(2)}) collective-permute-start(bf16[2048,256]{1,0:T(8,128)(2,1)} %collective-permute-done.20.k_hbm), channel_id=1, source_target_pairs={{8,0},{16,8},{24,16},{28,24},{20,28},{12,20},{4,12},{0,4},{9,1},{1... | collective-permute-start | bytes 3145736 | tf_op jit(solution)/shard_map/ppermute | solution.py:438
  71.4 3.6 %copy-start.1 = (bf16[2048,256]{1,0:T(8,128)(2,1)}, bf16[2048,256]{1,0:T(8,128)(2,1)S(1)}, u32[]{:S(2)}) copy-start(bf16[2048,256]{1,0:T(8,128)(2,1)S(1)} %collective-permute-done.2.k_hbm) | copy-start | bytes 3145732
  72.5 54.6 %collective-permute-start.13 = (bf16[1024,256]{1,0:T(8,128)(2,1)}, bf16[1024,256]{1,0:T(8,128)(2,1)}, u32[]{:S(2)}, u32[]{:S(2)}) collective-permute-start(bf16[1024,256]{1,0:T(8,128)(2,1)} %get-tuple-element.101), channel_id=1, source_target_pairs={{0,8},{8,16},{16,24},{24,28},{28,20},{20,12},{12,4},{4,0},{1,9},{9... | collective-permute-start | bytes 1572872 | tf_op jit(solution)/shard_map/ppermute | solution.py:438
  73.8 22.4 %copy-start.2 = (bf16[2048,256]{1,0:T(8,128)(2,1)}, bf16[2048,256]{1,0:T(8,128)(2,1)S(1)}, u32[]{:S(2)}) copy-start(bf16[2048,256]{1,0:T(8,128)(2,1)S(1)} %collective-permute-done.6.v_hbm) | copy-start | bytes 3145732
  74.9 52.2 %collective-permute-start.15 = (bf16[1024,256]{1,0:T(8,128)(2,1)}, bf16[1024,256]{1,0:T(8,128)(2,1)}, u32[]{:S(2)}, u32[]{:S(2)}) collective-permute-start(bf16[1024,256]{1,0:T(8,128)(2,1)} %get-tuple-element.99), channel_id=1, source_target_pairs={{8,0},{16,8},{24,16},{28,24},{20,28},{12,20},{4,12},{0,4},{9,1},{1... | collective-permute-start | bytes 1572872 | tf_op jit(solution)/shard_map/ppermute | solution.py:438
  96.2 32.4 %collective-permute-start.23 = (bf16[1024,256]{1,0:T(8,128)(2,1)}, bf16[1024,256]{1,0:T(8,128)(2,1)S(1)}, u32[]{:S(2)}, u32[]{:S(2)}) collective-permute-start(bf16[1024,256]{1,0:T(8,128)(2,1)} %get-tuple-element.97), channel_id=1, source_target_pairs={{0,8},{8,16},{16,24},{24,28},{28,20},{20,12},{12,4},{4,0},{1,9},{9... | collective-permute-start | bytes 1572872 | tf_op jit(solution)/shard_map/ppermute | solution.py:438
  97.4 31.2 %collective-permute-start.3 = (bf16[1024,256]{1,0:T(8,128)(2,1)}, bf16[1024,256]{1,0:T(8,128)(2,1)S(1)}, u32[]{:S(2)}, u32[]{:S(2)}) collective-permute-start(bf16[1024,256]{1,0:T(8,128)(2,1)} %get-tuple-element.102), channel_id=1, source_target_pairs={{0,8},{8,16},{16,24},{24,28},{28,20},{20,12},{12,4},{4,0},{1,9},{9... | collective-permute-start | bytes 1572872 | tf_op jit(solution)/shard_map/ppermute | solution.py:438
  101.5 34.3 %collective-permute-start.7 = (bf16[1024,256]{1,0:T(8,128)(2,1)}, bf16[1024,256]{1,0:T(8,128)(2,1)S(1)}, u32[]{:S(2)}, u32[]{:S(2)}) collective-permute-start(bf16[1024,256]{1,0:T(8,128)(2,1)} %get-tuple-element.100), channel_id=1, source_target_pairs={{8,0},{16,8},{24,16},{28,24},{20,28},{12,20},{4,12},{0,4},{9,1},{1... | collective-permute-start | bytes 1572872 | tf_op jit(solution)/shard_map/ppermute | solution.py:438
  127.1 11.8 %collective-permute-start.24 = (bf16[1024,256]{1,0:T(8,128)(2,1)}, bf16[1024,256]{1,0:T(8,128)(2,1)S(1)}, u32[]{:S(2)}, u32[]{:S(2)}) collective-permute-start(bf16[1024,256]{1,0:T(8,128)(2,1)} %get-tuple-element.95), channel_id=1, source_target_pairs={{8,0},{16,8},{24,16},{28,24},{20,28},{12,20},{4,12},{0,4},{9,1},{1... | collective-permute-start | bytes 1572872 | tf_op jit(solution)/shard_map/ppermute | solution.py:438
  127.1 12.0 %collective-permute-start.19 = (bf16[1024,256]{1,0:T(8,128)(2,1)}, bf16[1024,256]{1,0:T(8,128)(2,1)S(1)}, u32[]{:S(2)}, u32[]{:S(2)}) collective-permute-start(bf16[1024,256]{1,0:T(8,128)(2,1)} %get-tuple-element.98), channel_id=1, source_target_pairs={{0,8},{8,16},{16,24},{24,28},{28,20},{20,12},{12,4},{4,0},{1,9},{9... | collective-permute-start | bytes 1572872 | tf_op jit(solution)/shard_map/ppermute | solution.py:438
  128.6 7.3 %copy-start.5 = (bf16[1024,256]{1,0:T(8,128)(2,1)}, bf16[1024,256]{1,0:T(8,128)(2,1)S(1)}, u32[]{:S(2)}) copy-start(bf16[1024,256]{1,0:T(8,128)(2,1)S(1)} %collective-permute-done.23.refs_1_) | copy-start | bytes 1572868
  128.6 21.6 %collective-permute-start.22 = (bf16[1024,256]{1,0:T(8,128)(2,1)}, bf16[1024,256]{1,0:T(8,128)(2,1)S(1)}, u32[]{:S(2)}, u32[]{:S(2)}) collective-permute-start(bf16[1024,256]{1,0:T(8,128)(2,1)} %get-tuple-element.96), channel_id=1, source_target_pairs={{8,0},{16,8},{24,16},{28,24},{20,28},{12,20},{4,12},{0,4},{9,1},{1... | collective-permute-start | bytes 1572872 | tf_op jit(solution)/shard_map/ppermute | solution.py:438
  128.6 7.3 %copy-start.3 = (bf16[1024,256]{1,0:T(8,128)(2,1)}, bf16[1024,256]{1,0:T(8,128)(2,1)S(1)}, u32[]{:S(2)}) copy-start(bf16[1024,256]{1,0:T(8,128)(2,1)S(1)} %collective-permute-done.3.refs_0_) | copy-start | bytes 1572868
  128.6 21.6 %collective-permute-start.14 = (bf16[1024,256]{1,0:T(8,128)(2,1)}, bf16[1024,256]{1,0:T(8,128)(2,1)}, u32[]{:S(2)}, u32[]{:S(2)}) collective-permute-start(bf16[1024,256]{1,0:T(8,128)(2,1)} %collective-permute-done.13.refs_0_), channel_id=1, source_target_pairs={{0,8},{8,16},{16,24},{24,28},{28,20},{20,12},{12,4},{4,0},{1,9},{9... | collective-permute-start | bytes 1572872 | tf_op jit(solution)/shard_map/ppermute | solution.py:438
  135.9 20.2 %copy-start.4 = (bf16[1024,256]{1,0:T(8,128)(2,1)}, bf16[1024,256]{1,0:T(8,128)(2,1)S(1)}, u32[]{:S(2)}) copy-start(bf16[1024,256]{1,0:T(8,128)(2,1)S(1)} %collective-permute-done.7.refs_3_) | copy-start | bytes 1572868
  135.9 59.2 %collective-permute-start.16 = (bf16[1024,256]{1,0:T(8,128)(2,1)}, bf16[1024,256]{1,0:T(8,128)(2,1)S(1)}, u32[]{:S(2)}, u32[]{:S(2)}) collective-permute-start(bf16[1024,256]{1,0:T(8,128)(2,1)} %collective-permute-done.15.refs_3_), channel_id=1, source_target_pairs={{8,0},{16,8},{24,16},{28,24},{20,28},{12,20},{4,12},{0,4},{9,1},{1... | collective-permute-start | bytes 1572872 | tf_op jit(solution)/shard_map/ppermute | solution.py:438
  138.9 17.2 %copy-start.7 = (bf16[1024,256]{1,0:T(8,128)(2,1)}, bf16[1024,256]{1,0:T(8,128)(2,1)S(1)}, u32[]{:S(2)}) copy-start(bf16[1024,256]{1,0:T(8,128)(2,1)S(1)} %collective-permute-done.24.refs_2_) | copy-start | bytes 1572868
  138.9 58.2 %collective-permute-start.11 = (bf16[512,256]{1,0:T(8,128)(2,1)}, bf16[512,256]{1,0:T(8,128)(2,1)S(1)}, u32[]{:S(2)}, u32[]{:S(2)}) collective-permute-start(bf16[512,256]{1,0:T(8,128)(2,1)} %get-tuple-element.105), channel_id=1, source_target_pairs={{0,8},{8,16},{16,24},{24,28},{28,20},{20,12},{12,4},{4,0},{1,9},{9... | collective-permute-start | bytes 786440 | tf_op jit(solution)/shard_map/ppermute | solution.py:438
  139.1 17.0 %copy-start.6 = (bf16[1024,256]{1,0:T(8,128)(2,1)}, bf16[1024,256]{1,0:T(8,128)(2,1)S(1)}, u32[]{:S(2)}) copy-start(bf16[1024,256]{1,0:T(8,128)(2,1)S(1)} %collective-permute-done.19.refs_1_) | copy-start | bytes 1572868
  139.1 58.0 %collective-permute-start.12 = (bf16[512,256]{1,0:T(8,128)(2,1)}, bf16[512,256]{1,0:T(8,128)(2,1)}, u32[]{:S(2)}, u32[]{:S(2)}) collective-permute-start(bf16[512,256]{1,0:T(8,128)(2,1)} %get-tuple-element.103), channel_id=1, source_target_pairs={{8,0},{16,8},{24,16},{28,24},{20,28},{12,20},{4,12},{0,4},{9,1},{1... | collective-permute-start | bytes 786440 | tf_op jit(solution)/shard_map/ppermute | solution.py:438
  150.2 5.9 %copy-start.8 = (bf16[1024,256]{1,0:T(8,128)(2,1)}, bf16[1024,256]{1,0:T(8,128)(2,1)S(1)}, u32[]{:S(2)}) copy-start(bf16[1024,256]{1,0:T(8,128)(2,1)S(1)} %collective-permute-done.22.refs_2_) | copy-start | bytes 1572868
  150.2 51.4 %collective-permute-start.4 = (bf16[512,256]{1,0:T(8,128)(2,1)}, bf16[512,256]{1,0:T(8,128)(2,1)S(1)}, u32[]{:S(2)}, u32[]{:S(2)}) collective-permute-start(bf16[512,256]{1,0:T(8,128)(2,1)} %get-tuple-element.106), channel_id=1, source_target_pairs={{0,8},{8,16},{16,24},{24,28},{28,20},{20,12},{12,4},{4,0},{1,9},{9... | collective-permute-start | bytes 786440 | tf_op jit(solution)/shard_map/ppermute | solution.py:438
  150.2 51.4 %collective-permute-start.8 = (bf16[512,256]{1,0:T(8,128)(2,1)}, bf16[512,256]{1,0:T(8,128)(2,1)S(1)}, u32[]{:S(2)}, u32[]{:S(2)}) collective-permute-start(bf16[512,256]{1,0:T(8,128)(2,1)} %get-tuple-element.104), channel_id=1, source_target_pairs={{8,0},{16,8},{24,16},{28,24},{20,28},{12,20},{4,12},{0,4},{9,1},{1... | collective-permute-start | bytes 786440 | tf_op jit(solution)/shard_map/ppermute | solution.py:438
  195.1 0.8 copy-start.11
  197.1 0.7 copy-start.14
  201.6 0.8 copy-start.13
  203.6 14.4 %collective-permute-start.25 = (bf16[2,256,1024]{2,1,0:T(8,128)(2,1)}, bf16[2,256,1024]{2,1,0:T(8,128)(2,1)S(1)}, u32[]{:S(2)}, u32[]{:S(2)}) collective-permute-start(bf16[2,256,1024]{2,1,0:T(8,128)(2,1)} %get-tuple-element.76), channel_id=1, source_target_pairs={{0,1},{1,0},{2,3},{3,2},{4,5},{5,4},{6,7},{7,6},{8,9},{9,8},{10,11... | collective-permute-start | bytes 3145736 | tf_op jit(solution)/shard_map/ppermute | solution.py:564
  (1 other events, 0.7 us)

commit v7 on v6

--- a/solution.py
+++ b/solution.py
@@ -46,7 +46,9 @@
     highest = jnp.max(first, axis=0, keepdims=True)
     weights = jnp.exp2((first - highest) * (SCALE * LOG2E))
     total = jnp.sum(weights, axis=0, keepdims=True)
-    part_ref[0, :, :half] = mix_by_width(v_ref[0, :half], weights) / total
+    part_ref[0, :, :half] = (mix_by_width(v_ref[0, :half], weights) / total).astype(
+        part_ref.dtype
+    )
     log_ref[0, :, :half] = highest * SCALE + jnp.log(total)
 
     before = scores_by_key(early_keys, late_queries)
@@ -58,7 +60,7 @@
     within = jnp.exp2((within - highest) * (SCALE * LOG2E))
     total = jnp.sum(before, axis=0, keepdims=True) + jnp.sum(within, axis=0, keepdims=True)
     mixed = mix_by_width(v_ref[0, :half], before) + mix_by_width(v_ref[0, half:], within)
-    part_ref[0, :, half:] = mixed / total
+    part_ref[0, :, half:] = (mixed / total).astype(part_ref.dtype)
     log_ref[0, :, half:] = highest * SCALE + jnp.log(total)
 
 
@@ -81,7 +83,7 @@
         ]
         + [pl.BlockSpec(memory_space=pl.ANY)] * 4,
         out_shape=[
-            jax.ShapeDtypeStruct((count, HEAD_WIDTH, rows), jnp.float32),
+            jax.ShapeDtypeStruct((count, HEAD_WIDTH, rows), jnp.bfloat16),
             jax.ShapeDtypeStruct((count, 1, rows), jnp.float32),
             jax.ShapeDtypeStruct((items + 2, HEAD_WIDTH, rows), jnp.bfloat16),
             jax.ShapeDtypeStruct((items + 2, 1, rows), jnp.float32),
@@ -165,7 +167,7 @@
     first_share = jnp.exp(first_log - top)
     second_share = jnp.exp(second_log - top)
     merged = (
-        own_share * own
+        own_share * own.astype(jnp.float32)
         + first_share * first.astype(jnp.float32)
         + second_share * second.astype(jnp.float32)
     ) / (own_share + first_share + second_share)
@@ -230,7 +232,7 @@
     )(rep.reshape(1), ready, count.reshape(1), own, own_log, parts, logs, keep, send)
 
 
-def final_kernel(first_row, groups, rep, table, count, q_hbm, *refs):
+def final_kernel(first_row, groups, keeps_parts, rep, table, count, q_hbm, *refs):
     arrivals, refs = refs[: 2 * groups], refs[2 * groups :]
     own_hbm, own_log_hbm, _, _, _, _, part_hbm, log_hbm, keep_hbm, send_hbm = refs[:10]
     step, held, held_log = refs[10:]
@@ -248,10 +250,9 @@
             own_log_ref,
             other_ref,
             other_log_ref,
-            part_ref,
-            log_ref,
             keep_ref,
             send_ref,
+            *part_refs,
         ):
             part, log = attend_tile(q_ref[0], k_ref[...], v_ref[...])
             second = table[row, 6, step[0]] == 1
@@ -260,7 +261,8 @@
             keep_ref[0], send_ref[0] = merged_rows(
                 rep[0], own_ref[0], own_log_ref[0], part, log, other, other_log
             )
-            part_ref[0], log_ref[0] = part, log
+            if keeps_parts:
+                part_refs[0][0], part_refs[1][0] = part, log
             held[...], held_log[...] = part, log
             step[0] += 1
 
@@ -289,8 +291,6 @@
                 fetched((1, 1, rows), at(5)),
             ],
             out_specs=[
-                pl.BlockSpec(wide, at(0)),
-                pl.BlockSpec((1, 1, rows), at(0)),
                 pl.BlockSpec(
                     (1, half, HEAD_WIDTH),
                     lambda n: (table[row, 3, n], 0, rep[0] * heads + table[row, 4, n]),
@@ -298,7 +298,9 @@
                 pl.BlockSpec(
                     (1, half, HEAD_WIDTH), lambda n: (table[row, 3, n], 0, table[row, 4, n])
                 ),
-            ],
+                pl.BlockSpec(wide, at(0)),
+                pl.BlockSpec((1, 1, rows), at(0)),
+            ][: 4 if keeps_parts else 2],
         )
         when_any(
             count[row],
@@ -310,17 +312,14 @@
             own_log_hbm,
             part_hbm,
             log_hbm,
-            part_hbm,
-            log_hbm,
-            keep_hbm,
-            send_hbm,
+            *(keep_hbm, send_hbm, part_hbm, log_hbm)[: 4 if keeps_parts else 2],
         )
 
     for n in range(groups):
         run(first_row + n, arrivals[2 * n], arrivals[2 * n + 1])
 
 
-def final_attention(first_row, rep, table, count, queries, arrivals, own, own_log, state):
+def final_attention(first_row, keeps_parts, rep, table, count, queries, arrivals, own, own_log, state):
     rows = queries.shape[1]
     groups = len(arrivals)
     expected = own.shape[0] * groups // 8
@@ -328,7 +327,7 @@
     anywhere = pl.BlockSpec(memory_space=pl.ANY)
     flat = [array for pair in arrivals for array in pair]
     return pl.pallas_call(
-        functools.partial(final_kernel, first_row, groups),
+        functools.partial(final_kernel, first_row, groups, keeps_parts),
         in_specs=[smem] * 3 + [anywhere] * (7 + len(flat)),
         out_specs=[anywhere] * 4,
         out_shape=[jax.ShapeDtypeStruct(value.shape, value.dtype) for value in state],
@@ -389,10 +388,7 @@
 
 
 def piece_starts(blocks):
-    starts = [0]
-    while blocks - starts[-1] > 1:
-        starts.append(starts[-1] + (blocks - starts[-1] + 1) // 2)
-    return starts
+    return [0, blocks - (blocks + 3) // 4]
 
 
 def ring_order(count):
@@ -456,13 +452,10 @@
 
     ahead, behind = hop_in_parts(ahead, onward), hop_in_parts(behind, backward)
     step = full_steps + 1
-    last_pieces = []
-    for n, (first, end) in enumerate(zip(starts, starts[1:] + [blocks_here])):
-        part = min(n, 1)
-        rows = slice((first - part * starts[1]) * BLOCK_TOKENS, (end - part * starts[1]) * BLOCK_TOKENS)
-        last_pieces.append(
-            (hop(ahead[part][0][rows], onward), hop(behind[part][1][rows], backward))
-        )
+    last_pieces = [
+        (hop(keys, onward), hop(values, backward))
+        for (keys, _), (_, values) in zip(ahead, behind)
+    ]
 
     other = rep_size - 1 - rep_index
 
@@ -548,9 +541,10 @@
     state = (parts, logs, keep, send)
     late_arrivals = [list(pair) for pair in zip(ahead, behind)] + [[pair] for pair in last_pieces]
     row = 0
-    for arrivals in late_arrivals:
+    for n, arrivals in enumerate(late_arrivals):
         state = final_attention(
             row,
+            n + 1 < len(late_arrivals),
             rep_index,
             last_tables,
             last_counts,

time: 221 us -> 234 us (1.059)
  the two profiles are of different devices: /device:TPU:25 before, /device:TPU:19 now
where the time goes in v7:
time: 234 us; the launch traced here: 232 us
  waiting for transfers between devices  85.4 us (36%)
  Pallas kernels  79.4 us (34%)
  starting transfers between devices  30.9 us (13%)
  local copies, waits for them, and re-layouts  19.6 us (8%)
  other arithmetic  16.6 us (7%)
    ppermute x20, waiting for transfers between devices, hop(): return lax.ppermute(value, 'ctx', pairs)  82.9 us
    pallas_call x4, Pallas kernels, final_attention(): pl.pallas_call(functools.partial(final_kernel, first_row, groups, keeps_p...  28 us
    pallas_call x5, Pallas kernels, pick_attention(): pl.pallas_call(functools.partial(pick_kernel, row), in_specs=[smem, smem]...  26.6 us
    ppermute x20, starting transfers between devices, hop(): return lax.ppermute(value, 'ctx', pairs)  17.9 us
    pallas_call x1, Pallas kernels, own_attention(): pl.pallas_call(own_kernel, grid=(count,), in_specs=[query_spec, key_spec,...  15.8 us
    select_n x3, other arithmetic, all_rows(): jnp.where(rep_index == 0, jnp.concatenate([kept, came], axis=1), jnp.conc...  8.22 us
    ppermute x3, starting transfers between devices, all_rows(): came = lax.ppermute(columns_of(value, other, size), 'rep', swap)  7.12 us
    ppermute x1, starting transfers between devices, body(): arriving = lax.ppermute(state[3], 'rep', swap)  5.82 us
  transfers between devices with their start and end apart: 24, of which 7 were waited for; matrix products, arithmetic and copies ran while one was open for 14% of the time, Pallas kernels for 33%

profile of v7, /device:TPU:19, one launch (start us, length us, event | category | flops | bytes accessed | tf_op | source)
XLA Modules:
  0.0 232.1 jit_solution(8873545903996437778)
XLA Ops:
  0.0 2.0 columns_kept.2.k_hbm
  2.0 1.3 collective-permute-start.1
  3.5 2.0 columns_kept.3.v_hbm
  5.5 1.3 collective-permute-start.15
  7.1 1.2 constant_dynamic-slice_fusion.5
  8.2 1.8 collective-permute-start
  13.7 1.3 broadcast_compare_fusion.5
  15.2 1.3 broadcast_compare_fusion.2
  18.6 7.8 %collective-permute-done.1.k_hbm = bf16[2048,256]{1,0:T(8,128)(2,1)} collective-permute-done((bf16[2048,256]{1,0:T(8,128)(2,1)}, bf16[2048,256]{1,0:T(8,128)(2,1)}, u32[]{:S(2)}, u32[]{:S(2)}) %collective-permute-start.1) | collective-permute-done | bytes 1048608 | tf_op jit(solution)/shard_map/ppermute | solution.py:434
  26.4 1.3 collective-permute-start.2
  27.7 22.2 %collective-permute-done.5.v_hbm = bf16[2048,256]{1,0:T(8,128)(2,1)} collective-permute-done((bf16[2048,256]{1,0:T(8,128)(2,1)}, bf16[2048,256]{1,0:T(8,128)(2,1)}, u32[]{:S(2)}, u32[]{:S(2)}) %collective-permute-start.5) | collective-permute-done | bytes 1048608 | tf_op jit(solution)/shard_map/ppermute | solution.py:434
  50.3 1.3 collective-permute-start.16
  51.8 1.9 constant_dynamic-slice_fusion.3
  53.9 1.8 constant_dynamic-slice_fusion.1
  55.8 15.5 %collective-permute-done.2.k_hbm = bf16[2048,256]{1,0:T(8,128)(2,1)S(1)} collective-permute-done((bf16[2048,256]{1,0:T(8,128)(2,1)}, bf16[2048,256]{1,0:T(8,128)(2,1)S(1)}, u32[]{:S(2)}, u32[]{:S(2)}) %collective-permute-start.2) | collective-permute-done | bytes 1048608 | tf_op jit(solution)/shard_map/ppermute | solution.py:434
  71.3 2.7 %collective-permute-start.9 = (bf16[2,256,256]{2,1,0:T(8,128)(2,1)}, bf16[2,256,256]{2,1,0:T(8,128)(2,1)}, u32[]{:S(2)}, u32[]{:S(2)}) collective-permute-start(bf16[2,256,256]{2,1,0:T(8,128)(2,1)} %get-tuple-element.91), channel_id=1, source_target_pairs={{0,1},{1,0},{2,3},{3,2},{4,5},{5,4},{6,7},{7,6},{8,9},{9,8},{10,11... | collective-permute-start | bytes 786440 | tf_op jit(solution)/shard_map/ppermute | solution.py:464
  74.8 1.0 slice.56
  75.8 1.3 collective-permute-start.11
  78.4 15.4 %collective-permute-done.16.v_hbm = bf16[2048,256]{1,0:T(8,128)(2,1)} collective-permute-done((bf16[2048,256]{1,0:T(8,128)(2,1)}, bf16[2048,256]{1,0:T(8,128)(2,1)}, u32[]{:S(2)}, u32[]{:S(2)}) %collective-permute-start.16) | collective-permute-done | bytes 1048608 | tf_op jit(solution)/shard_map/ppermute | solution.py:434
  93.8 2.7 %collective-permute-start.10 = (bf16[2,256,256]{2,1,0:T(8,128)(2,1)S(1)}, bf16[2,256,256]{2,1,0:T(8,128)(2,1)S(1)}, u32[]{:S(2)}, u32[]{:S(2)}) collective-permute-start(bf16[2,256,256]{2,1,0:T(8,128)(2,1)S(1)} %copy-done.9), channel_id=1, source_target_pairs={{0,1},{1,0},{2,3},{3,2},{4,5},{5,4},{6,7},{7,6},{8,9},{9,8},{10,11... | collective-permute-start | bytes 786440 | tf_op jit(solution)/shard_map/ppermute | solution.py:464
  96.5 1.3 collective-permute-start.3
  99.2 2.1 slice.60
  101.3 2.1 slice.61
  103.4 1.2 collective-permute-start.21
  104.9 11.4 %collective-permute-done.3.refs_0_ = bf16[512,256]{1,0:T(8,128)(2,1)} collective-permute-done((bf16[512,256]{1,0:T(8,128)(2,1)S(1)}, bf16[512,256]{1,0:T(8,128)(2,1)}, u32[]{:S(2)}, u32[]{:S(2)}) %collective-permute-start.3) | collective-permute-done | bytes 262176 | tf_op jit(solution)/shard_map/ppermute | solution.py:434
  116.5 1.1 compare_select_fusion.5.ready
  117.6 2.2 maximum_select_fusion.1.k_ref
  119.8 1.3 collective-permute-start.12
  121.3 2.0 maximum_select_fusion.2.v_ref
  124.3 10.6 %collective-permute-done.7.refs_3_ = bf16[512,256]{1,0:T(8,128)(2,1)S(1)} collective-permute-done((bf16[512,256]{1,0:T(8,128)(2,1)}, bf16[512,256]{1,0:T(8,128)(2,1)S(1)}, u32[]{:S(2)}, u32[]{:S(2)}) %collective-permute-start.7) | collective-permute-done | bytes 262176 | tf_op jit(solution)/shard_map/ppermute | solution.py:434
  134.8 1.2 collective-permute-start.17
  136.1 3.9 %maximum_select_fusion.q_ref.q_hbm = bf16[2,512,1024]{2,1,0:T(8,128)(2,1)} fusion(bf16[2,256,1024]{2,1,0:T(8,128)(2,1)} %collective-permute-done, bf16[2,256,1024]{2,1,0:T(8,128)(2,1)S(1)} %get-tuple-element.86, pred[]{:T(512)S(6)} %eq.253), kind=kLoop, calls=%fused_computation.1 | loop fusion | flops 9437184 | bytes 4194305 | tf_op jit(solution)/shard_map/jit(_where)/select_n | solution.py:465
  140.0 15.8 %own_attention.1 = (bf16[16,128,512]{2,1,0:T(8,128)(2,1)}, f32[16,1,512]{2,1,0:T(1,128)}, bf16[34,128,512]{2,1,0:T(8,128)(2,1)}, f32[34,1,512]{2,1,0:T(1,128)}, ...) custom-call(bf16[2,512,1024]{2,1,0:T(8,128)(2,1)} %maximum_select_fusion.q_ref.q_hbm, ...), custom_call_target="tpu_custom_call" | custom-call | flops 2147483648 | bytes 8388608 | tf_op jit(solution)/shard_map/own_attention/pallas_call | solution.py:76
  155.8 1.0 slice.59
  157.1 5.0 %pick_attention.5 = (bf16[34,128,512]{2,1,0:T(8,128)(2,1)}, f32[34,1,512]{2,1,0:T(1,128)}) custom-call(s32[5,5,32]{2,1,0:T(8,128)} %broadcast_select_fusion.1.table, s32[5]{0:T(128)} %copy-done.14, bf16[2,512,1024]{2,1,0:T(8,128)(2,1)} %maximum_select_fusion.q_ref.q_hbm, ...), custom_call_target="tpu_custom_call", output_to_operand_aliasing={{0}: (5, {}), {1}: (6, {})} | custom-call | flops 536870912 | bytes 2097152 | tf_op jit(solution)/shard_map/pick_attention/pallas_call | solution.py:145
  162.1 5.0 %pick_attention.6 = (bf16[34,128,512]{2,1,0:T(8,128)(2,1)}, f32[34,1,512]{2,1,0:T(1,128)}) custom-call(s32[5,5,32]{2,1,0:T(8,128)} %broadcast_select_fusion.1.table, s32[5]{0:T(128)} %copy-done.14, bf16[2,512,1024]{2,1,0:T(8,128)(2,1)} %maximum_select_fusion.q_ref.q_hbm, ...), custom_call_target="tpu_custom_call", output_to_operand_aliasing={{0}: (5, {}), {1}: (6, {})} | custom-call | flops 536870912 | bytes 2097152 | tf_op jit(solution)/shard_map/pick_attention/pallas_call | solution.py:145
  167.1 4.4 %collective-permute-start.4 = (bf16[512,256]{1,0:T(8,128)(2,1)}, bf16[512,256]{1,0:T(8,128)(2,1)S(1)}, u32[]{:S(2)}, u32[]{:S(2)}) collective-permute-start(bf16[512,256]{1,0:T(8,128)(2,1)} %collective-permute-done.3.refs_0_), channel_id=1, source_target_pairs={{0,8},{8,16},{16,24},{24,28},{28,20},{20,12},{12,4},{4,0},{1,9},{9... | collective-permute-start | bytes 786440 | tf_op jit(solution)/shard_map/ppermute | solution.py:434
  171.6 5.8 %pick_attention.7 = (bf16[34,128,512]{2,1,0:T(8,128)(2,1)}, f32[34,1,512]{2,1,0:T(1,128)}) custom-call(s32[5,5,32]{2,1,0:T(8,128)} %broadcast_select_fusion.1.table, s32[5]{0:T(128)} %copy-done.14, bf16[2,512,1024]{2,1,0:T(8,128)(2,1)} %maximum_select_fusion.q_ref.q_hbm, ...), custom_call_target="tpu_custom_call", output_to_operand_aliasing={{0}: (5, {}), {1}: (6, {})} | custom-call | flops 536870912 | bytes 2097152 | tf_op jit(solution)/shard_map/pick_attention/pallas_call | solution.py:145
  177.4 5.8 %pick_attention.8 = (bf16[34,128,512]{2,1,0:T(8,128)(2,1)}, f32[34,1,512]{2,1,0:T(1,128)}) custom-call(s32[5,5,32]{2,1,0:T(8,128)} %broadcast_select_fusion.1.table, s32[5]{0:T(128)} %copy-done.14, bf16[2,512,1024]{2,1,0:T(8,128)(2,1)} %maximum_select_fusion.q_ref.q_hbm, bf16[2048,256]{1,0:T(8,128)(2,1)} %copy-done.2, ...), custom_call_target="tpu_custom_call", output_to_operand_aliasing={{0}: (5, {}), {1}: (6, {})} | custom-call | flops 536870912 | bytes 2097152 | tf_op jit(solution)/shard_map/pick_attention/pallas_call | solution.py:145
  183.2 5.0 %pick_attention.9 = (bf16[34,128,512]{2,1,0:T(8,128)(2,1)}, f32[34,1,512]{2,1,0:T(1,128)}) custom-call(s32[5,5,32]{2,1,0:T(8,128)} %broadcast_select_fusion.1.table, s32[5]{0:T(128)} %copy-done.14, bf16[2,512,1024]{2,1,0:T(8,128)(2,1)} %maximum_select_fusion.q_ref.q_hbm, ...), custom_call_target="tpu_custom_call", output_to_operand_aliasing={{0}: (5, {}), {1}: (6, {})} | custom-call | flops 536870912 | bytes 2097152 | tf_op jit(solution)/shard_map/pick_attention/pallas_call | solution.py:145
  188.2 5.0 %merge_parts.1 = (bf16[2,256,2048]{2,1,0:T(8,128)(2,1)}, bf16[2,256,1024]{2,1,0:T(8,128)(2,1)}) custom-call(s32[1]{0:T(128)} %bitcast.rep, s32[16]{0:T(128)} %compare_select_fusion.5.ready, s32[1]{0:T(128)} %bitcast.7.count, bf16[16,128,512]{2,1,0:T(8,128)(2,1)} %get-tuple-element.37.own_hbm.refs_4_.refs_2_, ...), custom_call_target="tpu_custom_call", output_to_operand_aliasing={{0}: (7, {}), {1}: (8, {})} | custom-call | flops 8388608 | bytes 10485760 | tf_op jit(solution)/shard_map/merge_parts/pallas_call | solution.py:217
  193.2 11.6 %final_attention.4 = (bf16[34,128,512]{2,1,0:T(8,128)(2,1)}, f32[34,1,512]{2,1,0:T(1,128)}, bf16[2,256,2048]{2,1,0:T(8,128)(2,1)}, bf16[2,256,1024]{2,1,0:T(8,128)(2,1)}) custom-call(s32[1]{0:T(128)} %bitcast.rep, s32[6,7,32]{2,1,0:T(8,128)} %broadcast_select_fusion.table, ...), custom_call_target="tpu_custom_call", output_to_operand_aliasing={{0}: (10, {}), {1}: (11, {}), {2}: (12, {}), {3}: (13, {})} | custom-call | flops 536870912 | bytes 4718592 | tf_op jit(solution)/shard_map/final_attention/pallas_call | solution.py:329
  205.5 10.5 %final_attention.5 = (bf16[34,128,512]{2,1,0:T(8,128)(2,1)}, f32[34,1,512]{2,1,0:T(1,128)}, bf16[2,256,2048]{2,1,0:T(8,128)(2,1)}, bf16[2,256,1024]{2,1,0:T(8,128)(2,1)}) custom-call(s32[1]{0:T(128)} %bitcast.rep, s32[6,7,32]{2,1,0:T(8,128)} %broadcast_select_fusion.table, ...), custom_call_target="tpu_custom_call", output_to_operand_aliasing={{0}: (10, {}), {1}: (11, {}), {2}: (12, {}), {3}: (13, {})} | custom-call | flops 536870912 | bytes 4718592 | tf_op jit(solution)/shard_map/final_attention/pallas_call | solution.py:329
  216.0 4.8 %final_attention.6 = (bf16[34,128,512]{2,1,0:T(8,128)(2,1)}, f32[34,1,512]{2,1,0:T(1,128)}, bf16[2,256,2048]{2,1,0:T(8,128)(2,1)}, bf16[2,256,1024]{2,1,0:T(8,128)(2,1)}) custom-call(s32[1]{0:T(128)} %bitcast.rep, s32[6,7,32]{2,1,0:T(8,128)} %broadcast_select_fusion.table, ...), custom_call_target="tpu_custom_call", output_to_operand_aliasing={{0}: (8, {}), {1}: (9, {}), {2}: (10, {}), {3}: (11, {})} | custom-call | flops 268435456 | bytes 2359296 | tf_op jit(solution)/shard_map/final_attention/pallas_call | solution.py:329
  221.7 1.1 final_attention.7
  222.7 5.8 %collective-permute-start.23 = (bf16[2,256,1024]{2,1,0:T(8,128)(2,1)}, bf16[2,256,1024]{2,1,0:T(8,128)(2,1)S(1)}, u32[]{:S(2)}, u32[]{:S(2)}) collective-permute-start(bf16[2,256,1024]{2,1,0:T(8,128)(2,1)} %get-tuple-element.68), channel_id=1, source_target_pairs={{0,1},{1,0},{2,3},{3,2},{4,5},{5,4},{6,7},{7,6},{8,9},{9,8},{10,11... | collective-permute-start | bytes 3145736 | tf_op jit(solution)/shard_map/ppermute | solution.py:558
  228.6 2.5 %collective-permute-done.23 = bf16[2,256,1024]{2,1,0:T(8,128)(2,1)S(1)} collective-permute-done((bf16[2,256,1024]{2,1,0:T(8,128)(2,1)}, bf16[2,256,1024]{2,1,0:T(8,128)(2,1)S(1)}, u32[]{:S(2)}, u32[]{:S(2)}) %collective-permute-start.23) | collective-permute-done | bytes 1048608 | tf_op jit(solution)/shard_map/ppermute | solution.py:558
  231.1 1.0 constant_dynamic-update-slice_fusion
  (120 shorter events, 14.1 us)
Async XLA Ops:
  2.0 5.0 %copy-start.3 = (bf16[2,256,2048]{2,1,0:T(8,128)(2,1)S(1)}, bf16[2,256,2048]{2,1,0:T(8,128)(2,1)}, u32[]{:S(2)}) copy-start(bf16[2,256,2048]{2,1,0:T(8,128)(2,1)} %param.10) | copy-start | bytes 6291460
  2.0 24.4 %collective-permute-start.1 = (bf16[2048,256]{1,0:T(8,128)(2,1)}, bf16[2048,256]{1,0:T(8,128)(2,1)}, u32[]{:S(2)}, u32[]{:S(2)}) collective-permute-start(bf16[2048,256]{1,0:T(8,128)(2,1)} %columns_kept.2.k_hbm), channel_id=1, source_target_pairs={{0,8},{8,16},{16,24},{24,28},{28,20},{20,12},{12,4},{4,0},{1,9},{9... | collective-permute-start | bytes 3145736 | tf_op jit(solution)/shard_map/ppermute | solution.py:434
  3.4 48.3 %collective-permute-start.18 = (bf16[2048,256]{1,0:T(8,128)(2,1)}, bf16[2048,256]{1,0:T(8,128)(2,1)}, u32[]{:S(2)}, u32[]{:S(2)}) collective-permute-start(bf16[2048,256]{1,0:T(8,128)(2,1)} %columns_kept.2.k_hbm), channel_id=1, source_target_pairs={{8,0},{16,8},{24,16},{28,24},{20,28},{12,20},{4,12},{0,4},{9,1},{1... | collective-permute-start | bytes 3145736 | tf_op jit(solution)/shard_map/ppermute | solution.py:434
  5.5 44.8 %collective-permute-start.15 = (bf16[2048,256]{1,0:T(8,128)(2,1)}, bf16[2048,256]{1,0:T(8,128)(2,1)}, u32[]{:S(2)}, u32[]{:S(2)}) collective-permute-start(bf16[2048,256]{1,0:T(8,128)(2,1)} %columns_kept.3.v_hbm), channel_id=1, source_target_pairs={{0,8},{8,16},{16,24},{24,28},{28,20},{20,12},{12,4},{4,0},{1,9},{9... | collective-permute-start | bytes 3145736 | tf_op jit(solution)/shard_map/ppermute | solution.py:434
  6.9 43.1 %collective-permute-start.5 = (bf16[2048,256]{1,0:T(8,128)(2,1)}, bf16[2048,256]{1,0:T(8,128)(2,1)}, u32[]{:S(2)}, u32[]{:S(2)}) collective-permute-start(bf16[2048,256]{1,0:T(8,128)(2,1)} %columns_kept.3.v_hbm), channel_id=1, source_target_pairs={{8,0},{16,8},{24,16},{28,24},{20,28},{12,20},{4,12},{0,4},{9,1},{1... | collective-permute-start | bytes 3145736 | tf_op jit(solution)/shard_map/ppermute | solution.py:434
  7.0 3.0 %slice-start = ((s32[2,16,3]{1,0,2:T(2,128)}), s32[2,16,2]{1,0,2:T(2,128)S(1)}, s32[]{:S(2)}) async-start(s32[2,16,3]{1,0,2:T(2,128)} %param.15), calls=%async_computation | async-start | bytes 4096 | tf_op jit(solution)/shard_map/slice | solution.py:484
  7.0 3.4 %copy-start.16 = (s32[8]{0:T(128)S(1)}, s32[8]{0:T(128)}, u32[]{:S(2)}) copy-start(s32[8]{0:T(128)} %constant.144.clone) | copy-start | bytes 100
  7.0 4.0 %copy-start.15 = (s32[8]{0:T(128)S(1)}, s32[8]{0:T(128)}, u32[]{:S(2)}) copy-start(s32[8]{0:T(128)} %constant.146.clone) | copy-start | bytes 100
  7.0 4.7 %copy-start = (s32[8]{0:T(128)S(1)}, s32[8]{0:T(128)}, u32[]{:S(2)}) copy-start(s32[8]{0:T(128)} %constant.145.clone) | copy-start | bytes 100
  8.2 96.4 %collective-permute-start = (bf16[2,256,1024]{2,1,0:T(8,128)(2,1)}, bf16[2,256,1024]{2,1,0:T(8,128)(2,1)}, u32[]{:S(2)}, u32[]{:S(2)}) collective-permute-start(bf16[2,256,1024]{2,1,0:T(8,128)(2,1)} %get-tuple-element.87), channel_id=1, source_target_pairs={{0,1},{1,0},{2,3},{3,2},{4,5},{5,4},{6,7},{7,6},{8,9},{9,8},{10,11... | collective-permute-start | bytes 3145736 | tf_op jit(solution)/shard_map/ppermute | solution.py:464
  16.9 61.2 %copy-start.14 = (s32[5]{0:T(128)}, s32[5]{0:T(128)S(1)}, u32[]{:S(2)}) copy-start(s32[5]{0:T(128)S(1)} %convert_reduce_fusion.count) | copy-start | bytes 64
  18.1 60.0 %copy-start.13 = (s32[6]{0:T(128)}, s32[6]{0:T(128)S(1)}, u32[]{:S(2)}) copy-start(s32[6]{0:T(128)S(1)} %get-tuple-element.73.count) | copy-start | bytes 76
  26.4 44.8 %collective-permute-start.2 = (bf16[2048,256]{1,0:T(8,128)(2,1)}, bf16[2048,256]{1,0:T(8,128)(2,1)S(1)}, u32[]{:S(2)}, u32[]{:S(2)}) collective-permute-start(bf16[2048,256]{1,0:T(8,128)(2,1)} %collective-permute-done.1.k_hbm), channel_id=1, source_target_pairs={{0,8},{8,16},{16,24},{24,28},{28,20},{20,12},{12,4},{4,0},{1,9},{9... | collective-permute-start | bytes 3145736 | tf_op jit(solution)/shard_map/ppermute | solution.py:434
  49.9 25.9 %collective-permute-start.6 = (bf16[2048,256]{1,0:T(8,128)(2,1)}, bf16[2048,256]{1,0:T(8,128)(2,1)S(1)}, u32[]{:S(2)}, u32[]{:S(2)}) collective-permute-start(bf16[2048,256]{1,0:T(8,128)(2,1)} %collective-permute-done.5.v_hbm), channel_id=1, source_target_pairs={{8,0},{16,8},{24,16},{28,24},{20,28},{12,20},{4,12},{0,4},{9,1},{1... | collective-permute-start | bytes 3145736 | tf_op jit(solution)/shard_map/ppermute | solution.py:434
  50.3 43.6 %collective-permute-start.16 = (bf16[2048,256]{1,0:T(8,128)(2,1)}, bf16[2048,256]{1,0:T(8,128)(2,1)}, u32[]{:S(2)}, u32[]{:S(2)}) collective-permute-start(bf16[2048,256]{1,0:T(8,128)(2,1)} %collective-permute-done.15.v_hbm), channel_id=1, source_target_pairs={{0,8},{8,16},{16,24},{24,28},{28,20},{20,12},{12,4},{4,0},{1,9},{9... | collective-permute-start | bytes 3145736 | tf_op jit(solution)/shard_map/ppermute | solution.py:434
  51.6 44.9 %collective-permute-start.19 = (bf16[2048,256]{1,0:T(8,128)(2,1)}, bf16[2048,256]{1,0:T(8,128)(2,1)}, u32[]{:S(2)}, u32[]{:S(2)}) collective-permute-start(bf16[2048,256]{1,0:T(8,128)(2,1)} %collective-permute-done.18.k_hbm), channel_id=1, source_target_pairs={{8,0},{16,8},{24,16},{28,24},{20,28},{12,20},{4,12},{0,4},{9,1},{1... | collective-permute-start | bytes 3145736 | tf_op jit(solution)/shard_map/ppermute | solution.py:434
  71.3 28.0 %copy-start.2 = (bf16[2048,256]{1,0:T(8,128)(2,1)}, bf16[2048,256]{1,0:T(8,128)(2,1)S(1)}, u32[]{:S(2)}) copy-start(bf16[2048,256]{1,0:T(8,128)(2,1)S(1)} %collective-permute-done.2.k_hbm) | copy-start | bytes 3145732
  71.3 6.8 %collective-permute-start.9 = (bf16[2,256,256]{2,1,0:T(8,128)(2,1)}, bf16[2,256,256]{2,1,0:T(8,128)(2,1)}, u32[]{:S(2)}, u32[]{:S(2)}) collective-permute-start(bf16[2,256,256]{2,1,0:T(8,128)(2,1)} %get-tuple-element.91), channel_id=1, source_target_pairs={{0,1},{1,0},{2,3},{3,2},{4,5},{5,4},{6,7},{7,6},{8,9},{9,8},{10,11... | collective-permute-start | bytes 786440 | tf_op jit(solution)/shard_map/ppermute | solution.py:464
  74.2 19.7 %copy-start.9 = (bf16[2,256,256]{2,1,0:T(8,128)(2,1)S(1)}, bf16[2,256,256]{2,1,0:T(8,128)(2,1)}, u32[]{:S(2)}) copy-start(bf16[2,256,256]{2,1,0:T(8,128)(2,1)} %get-tuple-element.89) | copy-start | bytes 786436
  75.8 25.5 %copy-start.1 = (bf16[2048,256]{1,0:T(8,128)(2,1)}, bf16[2048,256]{1,0:T(8,128)(2,1)S(1)}, u32[]{:S(2)}) copy-start(bf16[2048,256]{1,0:T(8,128)(2,1)S(1)} %collective-permute-done.6.v_hbm) | copy-start | bytes 3145732
  75.8 44.0 %collective-permute-start.11 = (bf16[1536,256]{1,0:T(8,128)(2,1)}, bf16[1536,256]{1,0:T(8,128)(2,1)}, u32[]{:S(2)}, u32[]{:S(2)}) collective-permute-start(bf16[1536,256]{1,0:T(8,128)(2,1)} %slice.56), channel_id=1, source_target_pairs={{0,8},{8,16},{16,24},{24,28},{28,20},{20,12},{12,4},{4,0},{1,9},{9... | collective-permute-start | bytes 2359304 | tf_op jit(solution)/shard_map/ppermute | solution.py:434
  78.1 43.0 %collective-permute-start.13 = (bf16[1536,256]{1,0:T(8,128)(2,1)}, bf16[1536,256]{1,0:T(8,128)(2,1)}, u32[]{:S(2)}, u32[]{:S(2)}) collective-permute-start(bf16[1536,256]{1,0:T(8,128)(2,1)} %slice.57), channel_id=1, source_target_pairs={{8,0},{16,8},{24,16},{28,24},{20,28},{12,20},{4,12},{0,4},{9,1},{1... | collective-permute-start | bytes 2359304 | tf_op jit(solution)/shard_map/ppermute | solution.py:434
  93.8 9.6 %collective-permute-start.10 = (bf16[2,256,256]{2,1,0:T(8,128)(2,1)S(1)}, bf16[2,256,256]{2,1,0:T(8,128)(2,1)S(1)}, u32[]{:S(2)}, u32[]{:S(2)}) collective-permute-start(bf16[2,256,256]{2,1,0:T(8,128)(2,1)S(1)} %copy-done.9), channel_id=1, source_target_pairs={{0,1},{1,0},{2,3},{3,2},{4,5},{5,4},{6,7},{7,6},{8,9},{9,8},{10,11... | collective-permute-start | bytes 786440 | tf_op jit(solution)/shard_map/ppermute | solution.py:464
  96.5 19.8 %collective-permute-start.3 = (bf16[512,256]{1,0:T(8,128)(2,1)S(1)}, bf16[512,256]{1,0:T(8,128)(2,1)}, u32[]{:S(2)}, u32[]{:S(2)}) collective-permute-start(bf16[512,256]{1,0:T(8,128)(2,1)S(1)} %slice.54), channel_id=1, source_target_pairs={{0,8},{8,16},{16,24},{24,28},{28,20},{20,12},{12,4},{4,0},{1,9},{9... | collective-permute-start | bytes 786440 | tf_op jit(solution)/shard_map/ppermute | solution.py:434
  103.4 12.9 %copy-start.10 = (bf16[2,256,256]{2,1,0:T(8,128)(2,1)}, bf16[2,256,256]{2,1,0:T(8,128)(2,1)S(1)}, u32[]{:S(2)}) copy-start(bf16[2,256,256]{2,1,0:T(8,128)(2,1)S(1)} %collective-permute-done.10) | copy-start | bytes 786436
  103.4 63.7 %collective-permute-start.21 = (bf16[1536,256]{1,0:T(8,128)(2,1)}, bf16[1536,256]{1,0:T(8,128)(2,1)S(1)}, u32[]{:S(2)}, u32[]{:S(2)}) collective-permute-start(bf16[1536,256]{1,0:T(8,128)(2,1)} %slice.60), channel_id=1, source_target_pairs={{0,8},{8,16},{16,24},{24,28},{28,20},{20,12},{12,4},{4,0},{1,9},{9... | collective-permute-start | bytes 2359304 | tf_op jit(solution)/shard_map/ppermute | solution.py:434
  104.7 66.9 %collective-permute-start.22 = (bf16[1536,256]{1,0:T(8,128)(2,1)}, bf16[1536,256]{1,0:T(8,128)(2,1)S(1)}, u32[]{:S(2)}, u32[]{:S(2)}) collective-permute-start(bf16[1536,256]{1,0:T(8,128)(2,1)} %slice.61), channel_id=1, source_target_pairs={{8,0},{16,8},{24,16},{28,24},{20,28},{12,20},{4,12},{0,4},{9,1},{1... | collective-permute-start | bytes 2359304 | tf_op jit(solution)/shard_map/ppermute | solution.py:434
  116.3 18.5 %collective-permute-start.7 = (bf16[512,256]{1,0:T(8,128)(2,1)}, bf16[512,256]{1,0:T(8,128)(2,1)S(1)}, u32[]{:S(2)}, u32[]{:S(2)}) collective-permute-start(bf16[512,256]{1,0:T(8,128)(2,1)} %slice.55), channel_id=1, source_target_pairs={{8,0},{16,8},{24,16},{28,24},{20,28},{12,20},{4,12},{0,4},{9,1},{1... | collective-permute-start | bytes 786440 | tf_op jit(solution)/shard_map/ppermute | solution.py:434
  119.8 96.2 %collective-permute-start.12 = (bf16[1536,256]{1,0:T(8,128)(2,1)}, bf16[1536,256]{1,0:T(8,128)(2,1)}, u32[]{:S(2)}, u32[]{:S(2)}) collective-permute-start(bf16[1536,256]{1,0:T(8,128)(2,1)} %collective-permute-done.11.refs_0_), channel_id=1, source_target_pairs={{0,8},{8,16},{16,24},{24,28},{28,20},{20,12},{12,4},{4,0},{1,9},{9... | collective-permute-start | bytes 2359304 | tf_op jit(solution)/shard_map/ppermute | solution.py:434
  121.1 94.9 %collective-permute-start.14 = (bf16[1536,256]{1,0:T(8,128)(2,1)}, bf16[1536,256]{1,0:T(8,128)(2,1)}, u32[]{:S(2)}, u32[]{:S(2)}) collective-permute-start(bf16[1536,256]{1,0:T(8,128)(2,1)} %collective-permute-done.13.refs_3_), channel_id=1, source_target_pairs={{8,0},{16,8},{24,16},{28,24},{20,28},{12,20},{4,12},{0,4},{9,1},{1... | collective-permute-start | bytes 2359304 | tf_op jit(solution)/shard_map/ppermute | solution.py:434
  134.8 36.7 %copy-start.6 = (bf16[512,256]{1,0:T(8,128)(2,1)}, bf16[512,256]{1,0:T(8,128)(2,1)S(1)}, u32[]{:S(2)}) copy-start(bf16[512,256]{1,0:T(8,128)(2,1)S(1)} %collective-permute-done.7.refs_3_) | copy-start | bytes 786436
  134.8 22.0 %collective-permute-start.17 = (bf16[512,256]{1,0:T(8,128)(2,1)S(1)}, bf16[512,256]{1,0:T(8,128)(2,1)S(1)}, u32[]{:S(2)}, u32[]{:S(2)}) collective-permute-start(bf16[512,256]{1,0:T(8,128)(2,1)S(1)} %slice.58), channel_id=1, source_target_pairs={{0,8},{8,16},{16,24},{24,28},{28,20},{20,12},{12,4},{4,0},{1,9},{9... | collective-permute-start | bytes 786440 | tf_op jit(solution)/shard_map/ppermute | solution.py:434
  156.8 5.3 %copy-start.7 = (bf16[512,256]{1,0:T(8,128)(2,1)}, bf16[512,256]{1,0:T(8,128)(2,1)S(1)}, u32[]{:S(2)}) copy-start(bf16[512,256]{1,0:T(8,128)(2,1)S(1)} %collective-permute-done.17.refs_1_) | copy-start | bytes 786436
  156.8 48.0 %collective-permute-start.20 = (bf16[512,256]{1,0:T(8,128)(2,1)S(1)}, bf16[512,256]{1,0:T(8,128)(2,1)S(1)}, u32[]{:S(2)}, u32[]{:S(2)}) collective-permute-start(bf16[512,256]{1,0:T(8,128)(2,1)S(1)} %slice.59), channel_id=1, source_target_pairs={{8,0},{16,8},{24,16},{28,24},{20,28},{12,20},{4,12},{0,4},{9,1},{1... | collective-permute-start | bytes 786440 | tf_op jit(solution)/shard_map/ppermute | solution.py:434
  167.1 10.3 %copy-start.4 = (bf16[1536,256]{1,0:T(8,128)(2,1)}, bf16[1536,256]{1,0:T(8,128)(2,1)S(1)}, u32[]{:S(2)}) copy-start(bf16[1536,256]{1,0:T(8,128)(2,1)S(1)} %collective-permute-done.21.refs_1_) | copy-start | bytes 2359300
  167.1 53.7 %collective-permute-start.4 = (bf16[512,256]{1,0:T(8,128)(2,1)}, bf16[512,256]{1,0:T(8,128)(2,1)S(1)}, u32[]{:S(2)}, u32[]{:S(2)}) collective-permute-start(bf16[512,256]{1,0:T(8,128)(2,1)} %collective-permute-done.3.refs_0_), channel_id=1, source_target_pairs={{0,8},{8,16},{16,24},{24,28},{28,20},{20,12},{12,4},{4,0},{1,9},{9... | collective-permute-start | bytes 786440 | tf_op jit(solution)/shard_map/ppermute | solution.py:434
  171.5 5.9 %copy-start.5 = (bf16[1536,256]{1,0:T(8,128)(2,1)}, bf16[1536,256]{1,0:T(8,128)(2,1)S(1)}, u32[]{:S(2)}) copy-start(bf16[1536,256]{1,0:T(8,128)(2,1)S(1)} %collective-permute-done.22.refs_2_) | copy-start | bytes 2359300
  171.5 49.3 %collective-permute-start.8 = (bf16[512,256]{1,0:T(8,128)(2,1)S(1)}, bf16[512,256]{1,0:T(8,128)(2,1)S(1)}, u32[]{:S(2)}, u32[]{:S(2)}) collective-permute-start(bf16[512,256]{1,0:T(8,128)(2,1)S(1)} %collective-permute-done.7.refs_3_), channel_id=1, source_target_pairs={{8,0},{16,8},{24,16},{28,24},{20,28},{12,20},{4,12},{0,4},{9,1},{1... | collective-permute-start | bytes 786440 | tf_op jit(solution)/shard_map/ppermute | solution.py:434
  204.8 0.7 copy-start.8
  220.8 0.7 copy-start.11
  220.8 0.8 copy-start.12
  222.7 8.3 %collective-permute-start.23 = (bf16[2,256,1024]{2,1,0:T(8,128)(2,1)}, bf16[2,256,1024]{2,1,0:T(8,128)(2,1)S(1)}, u32[]{:S(2)}, u32[]{:S(2)}) collective-permute-start(bf16[2,256,1024]{2,1,0:T(8,128)(2,1)} %get-tuple-element.68), channel_id=1, source_target_pairs={{0,1},{1,0},{2,3},{3,2},{4,5},{5,4},{6,7},{7,6},{8,9},{9,8},{10,11... | collective-permute-start | bytes 3145736 | tf_op jit(solution)/shard_map/ppermute | solution.py:558

commit v8 on v7

--- a/solution.py
+++ b/solution.py
@@ -171,8 +171,8 @@
         + first_share * first.astype(jnp.float32)
         + second_share * second.astype(jnp.float32)
     ) / (own_share + first_share + second_share)
-    early = merged[:, :half].T.astype(jnp.bfloat16)
-    late = merged[:, half:].T.astype(jnp.bfloat16)
+    early = merged[:, :half].astype(jnp.bfloat16).T
+    late = merged[:, half:].astype(jnp.bfloat16).T
     return jnp.where(rep == 0, early, late), jnp.where(rep == 0, late, early)
 
 
@@ -388,7 +388,7 @@
 
 
 def piece_starts(blocks):
-    return [0, blocks - (blocks + 3) // 4]
+    return [0, (blocks + 1) // 2]
 
 
 def ring_order(count):

time: 234 us -> 226 us (0.966)
  the two profiles are of different devices: /device:TPU:19 before, /device:TPU:0 now
where the time goes in v8:
time: 226 us; the launch traced here: 222 us
  waiting for transfers between devices  87.6 us (39%)
  Pallas kernels  76.6 us (34%)
  starting transfers between devices  29.1 us (13%)
  other arithmetic  15.3 us (7%)
  local copies, waits for them, and re-layouts  13.2 us (6%)
    ppermute x20, waiting for transfers between devices, hop(): return lax.ppermute(value, 'ctx', pairs)  84.7 us
    ppermute x20, starting transfers between devices, hop(): return lax.ppermute(value, 'ctx', pairs)  29.1 us
    pallas_call x4, Pallas kernels, final_attention(): pl.pallas_call(functools.partial(final_kernel, first_row, groups, keeps_p...  26.7 us
    pallas_call x5, Pallas kernels, pick_attention(): pl.pallas_call(functools.partial(pick_kernel, row), in_specs=[smem, smem]...  25.8 us
    pallas_call x1, Pallas kernels, own_attention(): pl.pallas_call(own_kernel, grid=(count,), in_specs=[query_spec, key_spec,...  15.8 us
    select_n x3, other arithmetic, all_rows(): jnp.where(rep_index == 0, jnp.concatenate([kept, came], axis=1), jnp.conc...  6.98 us
  transfers between devices with their start and end apart: 24, of which 13 were waited for; matrix products, arithmetic and copies ran while one was open for 12% of the time, Pallas kernels for 32%

profile of v8, /device:TPU:0, one launch (start us, length us, event | category | flops | bytes accessed | tf_op | source)
XLA Modules:
  0.0 222.1 jit_solution(12294125573151245857)
XLA Ops:
  0.0 2.0 columns_kept.2.k_hbm
  2.0 3.1 %collective-permute-start.1 = (bf16[2048,256]{1,0:T(8,128)(2,1)}, bf16[2048,256]{1,0:T(8,128)(2,1)}, u32[]{:S(2)}, u32[]{:S(2)}) collective-permute-start(bf16[2048,256]{1,0:T(8,128)(2,1)} %columns_kept.2.k_hbm), channel_id=1, source_target_pairs={{0,8},{8,16},{16,24},{24,28},{28,20},{20,12},{12,4},{4,0},{1,9},{9... | collective-permute-start | bytes 3145736 | tf_op jit(solution)/shard_map/ppermute | solution.py:434
  5.1 2.0 columns_kept.3.v_hbm
  7.2 2.1 collective-permute-start.15
  9.3 1.2 constant_dynamic-slice_fusion.5
  14.2 1.3 broadcast_compare_fusion.5
  15.5 1.3 broadcast_compare_fusion.2
  18.6 1.1 constant_dynamic-slice_fusion.3
  21.3 8.1 %collective-permute-done.1.k_hbm = bf16[2048,256]{1,0:T(8,128)(2,1)} collective-permute-done((bf16[2048,256]{1,0:T(8,128)(2,1)}, bf16[2048,256]{1,0:T(8,128)(2,1)}, u32[]{:S(2)}, u32[]{:S(2)}) %collective-permute-start.1) | collective-permute-done | bytes 1048608 | tf_op jit(solution)/shard_map/ppermute | solution.py:434
  29.4 2.1 collective-permute-start.2
  31.7 20.9 %collective-permute-done.5.v_hbm = bf16[2048,256]{1,0:T(8,128)(2,1)} collective-permute-done((bf16[2048,256]{1,0:T(8,128)(2,1)}, bf16[2048,256]{1,0:T(8,128)(2,1)}, u32[]{:S(2)}, u32[]{:S(2)}) %collective-permute-start.5) | collective-permute-done | bytes 1048608 | tf_op jit(solution)/shard_map/ppermute | solution.py:434
  53.5 1.7 collective-permute-start.16
  56.3 18.0 %collective-permute-done.2.k_hbm = bf16[2048,256]{1,0:T(8,128)(2,1)S(1)} collective-permute-done((bf16[2048,256]{1,0:T(8,128)(2,1)}, bf16[2048,256]{1,0:T(8,128)(2,1)S(1)}, u32[]{:S(2)}, u32[]{:S(2)}) %collective-permute-start.2) | collective-permute-done | bytes 1048608 | tf_op jit(solution)/shard_map/ppermute | solution.py:434
  75.2 3.6 %collective-permute-done.6.v_hbm = bf16[2048,256]{1,0:T(8,128)(2,1)S(1)} collective-permute-done((bf16[2048,256]{1,0:T(8,128)(2,1)}, bf16[2048,256]{1,0:T(8,128)(2,1)S(1)}, u32[]{:S(2)}, u32[]{:S(2)}) %collective-permute-start.6) | collective-permute-done | bytes 1048608 | tf_op jit(solution)/shard_map/ppermute | solution.py:434
  78.8 1.6 collective-permute-start.11
  81.3 15.4 %collective-permute-done.16.v_hbm = bf16[2048,256]{1,0:T(8,128)(2,1)S(1)} collective-permute-done((bf16[2048,256]{1,0:T(8,128)(2,1)}, bf16[2048,256]{1,0:T(8,128)(2,1)S(1)}, u32[]{:S(2)}, u32[]{:S(2)}) %collective-permute-start.16) | collective-permute-done | bytes 1048608 | tf_op jit(solution)/shard_map/ppermute | solution.py:434
  96.7 2.0 collective-permute-start.13
  98.7 1.1 fusion.10
  100.3 1.6 collective-permute-start.21
  101.9 1.1 fusion.9
  103.6 1.5 collective-permute-start.3
  105.0 3.0 %collective-permute-done.11.refs_0_ = bf16[1024,256]{1,0:T(8,128)(2,1)} collective-permute-done((bf16[1024,256]{1,0:T(8,128)(2,1)S(1)}, bf16[1024,256]{1,0:T(8,128)(2,1)}, u32[]{:S(2)}, u32[]{:S(2)}) %collective-permute-start.11) | collective-permute-done | bytes 524320 | tf_op jit(solution)/shard_map/ppermute | solution.py:434
  108.1 2.0 collective-permute-start.7
  110.1 1.5 collective-permute-done.13.refs_3_
  111.6 2.0 collective-permute-start.17
  113.6 1.1 compare_select_fusion.5.ready
  114.7 2.0 maximum_select_fusion.1.k_ref
  117.8 1.5 collective-permute-done.21.refs_1_
  119.3 2.0 collective-permute-start.20
  121.3 3.9 %maximum_select_fusion.q_ref.q_hbm = bf16[2,512,1024]{2,1,0:T(8,128)(2,1)} fusion(bf16[2,256,1024]{2,1,0:T(8,128)(2,1)} %collective-permute-done, bf16[2,256,1024]{2,1,0:T(8,128)(2,1)S(1)} %get-tuple-element.86, pred[]{:T(512)S(6)} %eq.253), kind=kLoop, calls=%fused_computation.1 | loop fusion | flops 9437184 | bytes 4194305 | tf_op jit(solution)/shard_map/jit(_where)/select_n | solution.py:465
  125.3 5.1 %collective-permute-done.3.refs_0_ = bf16[1024,256]{1,0:T(8,128)(2,1)S(1)} collective-permute-done((bf16[1024,256]{1,0:T(8,128)(2,1)}, bf16[1024,256]{1,0:T(8,128)(2,1)S(1)}, u32[]{:S(2)}, u32[]{:S(2)}) %collective-permute-start.3) | collective-permute-done | bytes 524320 | tf_op jit(solution)/shard_map/ppermute | solution.py:434
  130.4 2.0 collective-permute-start.14
  132.4 1.6 collective-permute-done.7.refs_3_
  134.0 2.0 collective-permute-start.4
  136.1 5.7 %collective-permute-done.17.refs_1_ = bf16[1024,256]{1,0:T(8,128)(2,1)} collective-permute-done((bf16[1024,256]{1,0:T(8,128)(2,1)}, bf16[1024,256]{1,0:T(8,128)(2,1)}, u32[]{:S(2)}, u32[]{:S(2)}) %collective-permute-start.17) | collective-permute-done | bytes 524320 | tf_op jit(solution)/shard_map/ppermute | solution.py:434
  141.8 2.0 collective-permute-start.8
  143.8 15.8 %own_attention.1 = (bf16[16,128,512]{2,1,0:T(8,128)(2,1)}, f32[16,1,512]{2,1,0:T(1,128)}, bf16[34,128,512]{2,1,0:T(8,128)(2,1)}, f32[34,1,512]{2,1,0:T(1,128)}, ...) custom-call(bf16[2,512,1024]{2,1,0:T(8,128)(2,1)} %maximum_select_fusion.q_ref.q_hbm, ...), custom_call_target="tpu_custom_call" | custom-call | flops 2147483648 | bytes 8388608 | tf_op jit(solution)/shard_map/own_attention/pallas_call | solution.py:76
  159.6 5.8 %pick_attention.5 = (bf16[34,128,512]{2,1,0:T(8,128)(2,1)}, f32[34,1,512]{2,1,0:T(1,128)}) custom-call(s32[5,5,32]{2,1,0:T(8,128)} %broadcast_select_fusion.1.table, s32[5]{0:T(128)} %copy-done.14, bf16[2,512,1024]{2,1,0:T(8,128)(2,1)} %maximum_select_fusion.q_ref.q_hbm, ...), custom_call_target="tpu_custom_call", output_to_operand_aliasing={{0}: (5, {}), {1}: (6, {})} | custom-call | flops 536870912 | bytes 2097152 | tf_op jit(solution)/shard_map/pick_attention/pallas_call | solution.py:145
  165.4 7.4 %pick_attention.6 = (bf16[34,128,512]{2,1,0:T(8,128)(2,1)}, f32[34,1,512]{2,1,0:T(1,128)}) custom-call(s32[5,5,32]{2,1,0:T(8,128)} %broadcast_select_fusion.1.table, s32[5]{0:T(128)} %copy-done.14, bf16[2,512,1024]{2,1,0:T(8,128)(2,1)} %maximum_select_fusion.q_ref.q_hbm, ...), custom_call_target="tpu_custom_call", output_to_operand_aliasing={{0}: (5, {}), {1}: (6, {})} | custom-call | flops 536870912 | bytes 2097152 | tf_op jit(solution)/shard_map/pick_attention/pallas_call | solution.py:145
  172.8 5.8 %pick_attention.7 = (bf16[34,128,512]{2,1,0:T(8,128)(2,1)}, f32[34,1,512]{2,1,0:T(1,128)}) custom-call(s32[5,5,32]{2,1,0:T(8,128)} %broadcast_select_fusion.1.table, s32[5]{0:T(128)} %copy-done.14, bf16[2,512,1024]{2,1,0:T(8,128)(2,1)} %maximum_select_fusion.q_ref.q_hbm, ...), custom_call_target="tpu_custom_call", output_to_operand_aliasing={{0}: (5, {}), {1}: (6, {})} | custom-call | flops 536870912 | bytes 2097152 | tf_op jit(solution)/shard_map/pick_attention/pallas_call | solution.py:145
  178.6 5.8 %pick_attention.8 = (bf16[34,128,512]{2,1,0:T(8,128)(2,1)}, f32[34,1,512]{2,1,0:T(1,128)}) custom-call(s32[5,5,32]{2,1,0:T(8,128)} %broadcast_select_fusion.1.table, s32[5]{0:T(128)} %copy-done.14, bf16[2,512,1024]{2,1,0:T(8,128)(2,1)} %maximum_select_fusion.q_ref.q_hbm, bf16[2048,256]{1,0:T(8,128)(2,1)} %copy-done.1, ...), custom_call_target="tpu_custom_call", output_to_operand_aliasing={{0}: (5, {}), {1}: (6, {})} | custom-call | flops 536870912 | bytes 2097152 | tf_op jit(solution)/shard_map/pick_attention/pallas_call | solution.py:145
  185.4 4.3 %merge_parts.1 = (bf16[2,256,2048]{2,1,0:T(8,128)(2,1)}, bf16[2,256,1024]{2,1,0:T(8,128)(2,1)}) custom-call(s32[1]{0:T(128)} %bitcast.rep, s32[16]{0:T(128)} %compare_select_fusion.5.ready, s32[1]{0:T(128)} %bitcast.7.count, bf16[16,128,512]{2,1,0:T(8,128)(2,1)} %get-tuple-element.37.own_hbm.refs_4_.refs_2_, ...), custom_call_target="tpu_custom_call", output_to_operand_aliasing={{0}: (7, {}), {1}: (8, {})} | custom-call | flops 8388608 | bytes 10485760 | tf_op jit(solution)/shard_map/merge_parts/pallas_call | solution.py:217
  189.7 5.8 %final_attention.4 = (bf16[34,128,512]{2,1,0:T(8,128)(2,1)}, f32[34,1,512]{2,1,0:T(1,128)}, bf16[2,256,2048]{2,1,0:T(8,128)(2,1)}, bf16[2,256,1024]{2,1,0:T(8,128)(2,1)}) custom-call(s32[1]{0:T(128)} %bitcast.rep, s32[6,7,32]{2,1,0:T(8,128)} %broadcast_select_fusion.table, ...), custom_call_target="tpu_custom_call", output_to_operand_aliasing={{0}: (10, {}), {1}: (11, {}), {2}: (12, {}), {3}: (13, {})} | custom-call | flops 536870912 | bytes 4718592 | tf_op jit(solution)/shard_map/final_attention/pallas_call | solution.py:329
  195.5 12.5 %final_attention.5 = (bf16[34,128,512]{2,1,0:T(8,128)(2,1)}, f32[34,1,512]{2,1,0:T(1,128)}, bf16[2,256,2048]{2,1,0:T(8,128)(2,1)}, bf16[2,256,1024]{2,1,0:T(8,128)(2,1)}) custom-call(s32[1]{0:T(128)} %bitcast.rep, s32[6,7,32]{2,1,0:T(8,128)} %broadcast_select_fusion.table, ...), custom_call_target="tpu_custom_call", output_to_operand_aliasing={{0}: (10, {}), {1}: (11, {}), {2}: (12, {}), {3}: (13, {})} | custom-call | flops 536870912 | bytes 4718592 | tf_op jit(solution)/shard_map/final_attention/pallas_call | solution.py:329
  208.7 4.8 %final_attention.6 = (bf16[34,128,512]{2,1,0:T(8,128)(2,1)}, f32[34,1,512]{2,1,0:T(1,128)}, bf16[2,256,2048]{2,1,0:T(8,128)(2,1)}, bf16[2,256,1024]{2,1,0:T(8,128)(2,1)}) custom-call(s32[1]{0:T(128)} %bitcast.rep, s32[6,7,32]{2,1,0:T(8,128)} %broadcast_select_fusion.table, ...), custom_call_target="tpu_custom_call", output_to_operand_aliasing={{0}: (8, {}), {1}: (9, {}), {2}: (10, {}), {3}: (11, {})} | custom-call | flops 268435456 | bytes 2359296 | tf_op jit(solution)/shard_map/final_attention/pallas_call | solution.py:329
  214.5 3.7 %final_attention.7 = (bf16[34,128,512]{2,1,0:T(8,128)(2,1)}, f32[34,1,512]{2,1,0:T(1,128)}, bf16[2,256,2048]{2,1,0:T(8,128)(2,1)}, bf16[2,256,1024]{2,1,0:T(8,128)(2,1)}) custom-call(s32[1]{0:T(128)} %bitcast.rep, s32[6,7,32]{2,1,0:T(8,128)} %broadcast_select_fusion.table, ...), custom_call_target="tpu_custom_call", output_to_operand_aliasing={{0}: (8, {}), {1}: (9, {}), {2}: (10, {}), {3}: (11, {})} | custom-call | flops 268435456 | bytes 2359296 | tf_op jit(solution)/shard_map/final_attention/pallas_call | solution.py:329
  218.2 2.9 %collective-permute-done.23 = bf16[2,256,1024]{2,1,0:T(8,128)(2,1)S(1)} collective-permute-done((bf16[2,256,1024]{2,1,0:T(8,128)(2,1)}, bf16[2,256,1024]{2,1,0:T(8,128)(2,1)S(1)}, u32[]{:S(2)}, u32[]{:S(2)}) %collective-permute-start.23) | collective-permute-done | bytes 1048608 | tf_op jit(solution)/shard_map/ppermute | solution.py:558
  221.0 1.0 constant_dynamic-update-slice_fusion
  (118 shorter events, 16.1 us)
Async XLA Ops:
  2.0 7.2 %copy-start.5 = (bf16[2,256,2048]{2,1,0:T(8,128)(2,1)S(1)}, bf16[2,256,2048]{2,1,0:T(8,128)(2,1)}, u32[]{:S(2)}) copy-start(bf16[2,256,2048]{2,1,0:T(8,128)(2,1)} %param.10) | copy-start | bytes 6291460
  2.0 27.4 %collective-permute-start.1 = (bf16[2048,256]{1,0:T(8,128)(2,1)}, bf16[2048,256]{1,0:T(8,128)(2,1)}, u32[]{:S(2)}, u32[]{:S(2)}) collective-permute-start(bf16[2048,256]{1,0:T(8,128)(2,1)} %columns_kept.2.k_hbm), channel_id=1, source_target_pairs={{0,8},{8,16},{16,24},{24,28},{28,20},{20,12},{12,4},{4,0},{1,9},{9... | collective-permute-start | bytes 3145736 | tf_op jit(solution)/shard_map/ppermute | solution.py:434
  5.1 50.1 %collective-permute-start.18 = (bf16[2048,256]{1,0:T(8,128)(2,1)}, bf16[2048,256]{1,0:T(8,128)(2,1)}, u32[]{:S(2)}, u32[]{:S(2)}) collective-permute-start(bf16[2048,256]{1,0:T(8,128)(2,1)} %columns_kept.2.k_hbm), channel_id=1, source_target_pairs={{8,0},{16,8},{24,16},{28,24},{20,28},{12,20},{4,12},{0,4},{9,1},{1... | collective-permute-start | bytes 3145736 | tf_op jit(solution)/shard_map/ppermute | solution.py:434
  7.2 46.3 %collective-permute-start.15 = (bf16[2048,256]{1,0:T(8,128)(2,1)}, bf16[2048,256]{1,0:T(8,128)(2,1)}, u32[]{:S(2)}, u32[]{:S(2)}) collective-permute-start(bf16[2048,256]{1,0:T(8,128)(2,1)} %columns_kept.3.v_hbm), channel_id=1, source_target_pairs={{0,8},{8,16},{16,24},{24,28},{28,20},{20,12},{12,4},{4,0},{1,9},{9... | collective-permute-start | bytes 3145736 | tf_op jit(solution)/shard_map/ppermute | solution.py:434
  9.2 43.3 %collective-permute-start.5 = (bf16[2048,256]{1,0:T(8,128)(2,1)}, bf16[2048,256]{1,0:T(8,128)(2,1)}, u32[]{:S(2)}, u32[]{:S(2)}) collective-permute-start(bf16[2048,256]{1,0:T(8,128)(2,1)} %columns_kept.3.v_hbm), channel_id=1, source_target_pairs={{8,0},{16,8},{24,16},{28,24},{20,28},{12,20},{4,12},{0,4},{9,1},{1... | collective-permute-start | bytes 3145736 | tf_op jit(solution)/shard_map/ppermute | solution.py:434
  9.2 1.2 slice-start
  9.2 1.7 copy-start.17
  9.2 2.3 %copy-start.16 = (s32[8]{0:T(128)S(1)}, s32[8]{0:T(128)}, u32[]{:S(2)}) copy-start(s32[8]{0:T(128)} %constant.146.clone) | copy-start | bytes 100
  9.3 2.9 %copy-start = (s32[8]{0:T(128)S(1)}, s32[8]{0:T(128)}, u32[]{:S(2)}) copy-start(s32[8]{0:T(128)} %constant.145.clone) | copy-start | bytes 100
  10.4 10.0 %copy-start.13 = (bf16[2,256,512]{2,1,0:T(8,128)(2,1)S(1)}, bf16[2,256,512]{2,1,0:T(8,128)(2,1)}, u32[]{:S(2)}) copy-start(bf16[2,256,512]{2,1,0:T(8,128)(2,1)} %param.12) | copy-start | bytes 1572868
  10.5 93.1 %collective-permute-start = (bf16[2,256,1024]{2,1,0:T(8,128)(2,1)}, bf16[2,256,1024]{2,1,0:T(8,128)(2,1)}, u32[]{:S(2)}, u32[]{:S(2)}) collective-permute-start(bf16[2,256,1024]{2,1,0:T(8,128)(2,1)} %get-tuple-element.87), channel_id=1, source_target_pairs={{0,1},{1,0},{2,3},{3,2},{4,5},{5,4},{6,7},{7,6},{8,9},{9,8},{10,11... | collective-permute-start | bytes 3145736 | tf_op jit(solution)/shard_map/ppermute | solution.py:464
  18.1 57.1 %copy-start.15 = (s32[6]{0:T(128)}, s32[6]{0:T(128)S(1)}, u32[]{:S(2)}) copy-start(s32[6]{0:T(128)S(1)} %get-tuple-element.73.count) | copy-start | bytes 76
  20.2 61.0 %copy-start.14 = (s32[5]{0:T(128)}, s32[5]{0:T(128)S(1)}, u32[]{:S(2)}) copy-start(s32[5]{0:T(128)S(1)} %convert_reduce_fusion.count) | copy-start | bytes 64
  29.4 44.8 %collective-permute-start.2 = (bf16[2048,256]{1,0:T(8,128)(2,1)}, bf16[2048,256]{1,0:T(8,128)(2,1)S(1)}, u32[]{:S(2)}, u32[]{:S(2)}) collective-permute-start(bf16[2048,256]{1,0:T(8,128)(2,1)} %collective-permute-done.1.k_hbm), channel_id=1, source_target_pairs={{0,8},{8,16},{16,24},{24,28},{28,20},{20,12},{12,4},{4,0},{1,9},{9... | collective-permute-start | bytes 3145736 | tf_op jit(solution)/shard_map/ppermute | solution.py:434
  52.5 26.2 %collective-permute-start.6 = (bf16[2048,256]{1,0:T(8,128)(2,1)}, bf16[2048,256]{1,0:T(8,128)(2,1)S(1)}, u32[]{:S(2)}, u32[]{:S(2)}) collective-permute-start(bf16[2048,256]{1,0:T(8,128)(2,1)} %collective-permute-done.5.v_hbm), channel_id=1, source_target_pairs={{8,0},{16,8},{24,16},{28,24},{20,28},{12,20},{4,12},{0,4},{9,1},{1... | collective-permute-start | bytes 3145736 | tf_op jit(solution)/shard_map/ppermute | solution.py:434
  53.5 43.2 %collective-permute-start.16 = (bf16[2048,256]{1,0:T(8,128)(2,1)}, bf16[2048,256]{1,0:T(8,128)(2,1)S(1)}, u32[]{:S(2)}, u32[]{:S(2)}) collective-permute-start(bf16[2048,256]{1,0:T(8,128)(2,1)} %collective-permute-done.15.v_hbm), channel_id=1, source_target_pairs={{0,8},{8,16},{16,24},{24,28},{28,20},{20,12},{12,4},{4,0},{1,9},{9... | collective-permute-start | bytes 3145736 | tf_op jit(solution)/shard_map/ppermute | solution.py:434
  55.3 45.0 %collective-permute-start.19 = (bf16[2048,256]{1,0:T(8,128)(2,1)}, bf16[2048,256]{1,0:T(8,128)(2,1)S(1)}, u32[]{:S(2)}, u32[]{:S(2)}) collective-permute-start(bf16[2048,256]{1,0:T(8,128)(2,1)} %collective-permute-done.18.k_hbm), channel_id=1, source_target_pairs={{8,0},{16,8},{24,16},{28,24},{20,28},{12,20},{4,12},{0,4},{9,1},{1... | collective-permute-start | bytes 3145736 | tf_op jit(solution)/shard_map/ppermute | solution.py:434
  74.2 7.0 %copy-start.1 = (bf16[2048,256]{1,0:T(8,128)(2,1)}, bf16[2048,256]{1,0:T(8,128)(2,1)S(1)}, u32[]{:S(2)}) copy-start(bf16[2048,256]{1,0:T(8,128)(2,1)S(1)} %collective-permute-done.2.k_hbm) | copy-start | bytes 3145732
  74.2 25.6 %collective-permute-start.9 = (bf16[2,256,256]{2,1,0:T(8,128)(2,1)S(1)}, bf16[2,256,256]{2,1,0:T(8,128)(2,1)}, u32[]{:S(2)}, u32[]{:S(2)}) collective-permute-start(bf16[2,256,256]{2,1,0:T(8,128)(2,1)S(1)} %get-tuple-element.99), channel_id=1, source_target_pairs={{0,1},{1,0},{2,3},{3,2},{4,5},{5,4},{6,7},{7,6},{8,9},{9,8},{10,11... | collective-permute-start | bytes 786440 | tf_op jit(solution)/shard_map/ppermute | solution.py:464
  78.8 21.0 %copy-start.2 = (bf16[2048,256]{1,0:T(8,128)(2,1)}, bf16[2048,256]{1,0:T(8,128)(2,1)S(1)}, u32[]{:S(2)}) copy-start(bf16[2048,256]{1,0:T(8,128)(2,1)S(1)} %collective-permute-done.6.v_hbm) | copy-start | bytes 3145732
  78.8 29.3 %collective-permute-start.11 = (bf16[1024,256]{1,0:T(8,128)(2,1)S(1)}, bf16[1024,256]{1,0:T(8,128)(2,1)}, u32[]{:S(2)}, u32[]{:S(2)}) collective-permute-start(bf16[1024,256]{1,0:T(8,128)(2,1)S(1)} %get-tuple-element.94), channel_id=1, source_target_pairs={{0,8},{8,16},{16,24},{24,28},{28,20},{20,12},{12,4},{4,0},{1,9},{9... | collective-permute-start | bytes 1572872 | tf_op jit(solution)/shard_map/ppermute | solution.py:434
  96.7 6.3 %copy-start.4 = (bf16[2048,256]{1,0:T(8,128)(2,1)}, bf16[2048,256]{1,0:T(8,128)(2,1)S(1)}, u32[]{:S(2)}) copy-start(bf16[2048,256]{1,0:T(8,128)(2,1)S(1)} %collective-permute-done.16.v_hbm) | copy-start | bytes 3145732
  96.7 14.8 %collective-permute-start.13 = (bf16[1024,256]{1,0:T(8,128)(2,1)S(1)}, bf16[1024,256]{1,0:T(8,128)(2,1)S(1)}, u32[]{:S(2)}, u32[]{:S(2)}) collective-permute-start(bf16[1024,256]{1,0:T(8,128)(2,1)S(1)} %get-tuple-element.92), channel_id=1, source_target_pairs={{8,0},{16,8},{24,16},{28,24},{20,28},{12,20},{4,12},{0,4},{9,1},{1... | collective-permute-start | bytes 1572872 | tf_op jit(solution)/shard_map/ppermute | solution.py:434
  99.8 16.9 %copy-start.6 = (bf16[2,256,256]{2,1,0:T(8,128)(2,1)S(1)}, bf16[2,256,256]{2,1,0:T(8,128)(2,1)}, u32[]{:S(2)}) copy-start(bf16[2,256,256]{2,1,0:T(8,128)(2,1)} %get-tuple-element.96) | copy-start | bytes 786436
  99.8 3.2 %collective-permute-start.10 = (bf16[2,256,256]{2,1,0:T(8,128)(2,1)S(1)}, bf16[2,256,256]{2,1,0:T(8,128)(2,1)S(1)}, u32[]{:S(2)}, u32[]{:S(2)}) collective-permute-start(bf16[2,256,256]{2,1,0:T(8,128)(2,1)S(1)} %get-tuple-element.97), channel_id=1, source_target_pairs={{0,1},{1,0},{2,3},{3,2},{4,5},{5,4},{6,7},{7,6},{8,9},{9,8},{10,11... | collective-permute-start | bytes 786440 | tf_op jit(solution)/shard_map/ppermute | solution.py:464
  100.3 1.6 copy-start.3
  100.3 19.0 %collective-permute-start.21 = (bf16[1024,256]{1,0:T(8,128)(2,1)}, bf16[1024,256]{1,0:T(8,128)(2,1)}, u32[]{:S(2)}, u32[]{:S(2)}) collective-permute-start(bf16[1024,256]{1,0:T(8,128)(2,1)} %get-tuple-element.90), channel_id=1, source_target_pairs={{0,8},{8,16},{16,24},{24,28},{28,20},{20,12},{12,4},{4,0},{1,9},{9... | collective-permute-start | bytes 1572872 | tf_op jit(solution)/shard_map/ppermute | solution.py:434
  103.0 22.3 %collective-permute-start.22 = (bf16[1024,256]{1,0:T(8,128)(2,1)}, bf16[1024,256]{1,0:T(8,128)(2,1)}, u32[]{:S(2)}, u32[]{:S(2)}) collective-permute-start(bf16[1024,256]{1,0:T(8,128)(2,1)} %get-tuple-element.88), channel_id=1, source_target_pairs={{8,0},{16,8},{24,16},{28,24},{20,28},{12,20},{4,12},{0,4},{9,1},{1... | collective-permute-start | bytes 1572872 | tf_op jit(solution)/shard_map/ppermute | solution.py:434
  103.6 26.9 %collective-permute-start.3 = (bf16[1024,256]{1,0:T(8,128)(2,1)}, bf16[1024,256]{1,0:T(8,128)(2,1)S(1)}, u32[]{:S(2)}, u32[]{:S(2)}) collective-permute-start(bf16[1024,256]{1,0:T(8,128)(2,1)} %get-tuple-element.95), channel_id=1, source_target_pairs={{0,8},{8,16},{16,24},{24,28},{28,20},{20,12},{12,4},{4,0},{1,9},{9... | collective-permute-start | bytes 1572872 | tf_op jit(solution)/shard_map/ppermute | solution.py:434
  108.1 26.0 %collective-permute-start.7 = (bf16[1024,256]{1,0:T(8,128)(2,1)}, bf16[1024,256]{1,0:T(8,128)(2,1)S(1)}, u32[]{:S(2)}, u32[]{:S(2)}) collective-permute-start(bf16[1024,256]{1,0:T(8,128)(2,1)} %get-tuple-element.93), channel_id=1, source_target_pairs={{8,0},{16,8},{24,16},{28,24},{20,28},{12,20},{4,12},{0,4},{9,1},{1... | collective-permute-start | bytes 1572872 | tf_op jit(solution)/shard_map/ppermute | solution.py:434
  111.6 18.9 %copy-start.7 = (bf16[1024,256]{1,0:T(8,128)(2,1)}, bf16[1024,256]{1,0:T(8,128)(2,1)S(1)}, u32[]{:S(2)}) copy-start(bf16[1024,256]{1,0:T(8,128)(2,1)S(1)} %collective-permute-done.13.refs_3_) | copy-start | bytes 1572868
  111.6 30.2 %collective-permute-start.17 = (bf16[1024,256]{1,0:T(8,128)(2,1)}, bf16[1024,256]{1,0:T(8,128)(2,1)}, u32[]{:S(2)}, u32[]{:S(2)}) collective-permute-start(bf16[1024,256]{1,0:T(8,128)(2,1)} %get-tuple-element.91), channel_id=1, source_target_pairs={{0,8},{8,16},{16,24},{24,28},{28,20},{20,12},{12,4},{4,0},{1,9},{9... | collective-permute-start | bytes 1572872 | tf_op jit(solution)/shard_map/ppermute | solution.py:434
  119.3 76.2 %collective-permute-start.20 = (bf16[1024,256]{1,0:T(8,128)(2,1)}, bf16[1024,256]{1,0:T(8,128)(2,1)}, u32[]{:S(2)}, u32[]{:S(2)}) collective-permute-start(bf16[1024,256]{1,0:T(8,128)(2,1)} %get-tuple-element.89), channel_id=1, source_target_pairs={{8,0},{16,8},{24,16},{28,24},{20,28},{12,20},{4,12},{0,4},{9,1},{1... | collective-permute-start | bytes 1572872 | tf_op jit(solution)/shard_map/ppermute | solution.py:434
  125.3 82.7 %collective-permute-start.12 = (bf16[1024,256]{1,0:T(8,128)(2,1)}, bf16[1024,256]{1,0:T(8,128)(2,1)S(1)}, u32[]{:S(2)}, u32[]{:S(2)}) collective-permute-start(bf16[1024,256]{1,0:T(8,128)(2,1)} %collective-permute-done.11.refs_0_), channel_id=1, source_target_pairs={{0,8},{8,16},{16,24},{24,28},{28,20},{20,12},{12,4},{4,0},{1,9},{9... | collective-permute-start | bytes 1572872 | tf_op jit(solution)/shard_map/ppermute | solution.py:434
  130.4 29.2 %copy-start.8 = (bf16[1024,256]{1,0:T(8,128)(2,1)}, bf16[1024,256]{1,0:T(8,128)(2,1)S(1)}, u32[]{:S(2)}) copy-start(bf16[1024,256]{1,0:T(8,128)(2,1)S(1)} %collective-permute-done.3.refs_0_) | copy-start | bytes 1572868
  130.4 77.5 %collective-permute-start.14 = (bf16[1024,256]{1,0:T(8,128)(2,1)S(1)}, bf16[1024,256]{1,0:T(8,128)(2,1)}, u32[]{:S(2)}, u32[]{:S(2)}) collective-permute-start(bf16[1024,256]{1,0:T(8,128)(2,1)S(1)} %collective-permute-done.13.refs_3_), channel_id=1, source_target_pairs={{8,0},{16,8},{24,16},{28,24},{20,28},{12,20},{4,12},{0,4},{9,1},{1... | collective-permute-start | bytes 1572872 | tf_op jit(solution)/shard_map/ppermute | solution.py:434
  134.0 25.5 %copy-start.9 = (bf16[1024,256]{1,0:T(8,128)(2,1)}, bf16[1024,256]{1,0:T(8,128)(2,1)S(1)}, u32[]{:S(2)}) copy-start(bf16[1024,256]{1,0:T(8,128)(2,1)S(1)} %collective-permute-done.7.refs_3_) | copy-start | bytes 1572868
  134.0 79.4 %collective-permute-start.4 = (bf16[1024,256]{1,0:T(8,128)(2,1)S(1)}, bf16[1024,256]{1,0:T(8,128)(2,1)S(1)}, u32[]{:S(2)}, u32[]{:S(2)}) collective-permute-start(bf16[1024,256]{1,0:T(8,128)(2,1)S(1)} %collective-permute-done.3.refs_0_), channel_id=1, source_target_pairs={{0,8},{8,16},{16,24},{24,28},{28,20},{20,12},{12,4},{4,0},{1,9},{9... | collective-permute-start | bytes 1572872 | tf_op jit(solution)/shard_map/ppermute | solution.py:434
  141.8 71.7 %collective-permute-start.8 = (bf16[1024,256]{1,0:T(8,128)(2,1)S(1)}, bf16[1024,256]{1,0:T(8,128)(2,1)S(1)}, u32[]{:S(2)}, u32[]{:S(2)}) collective-permute-start(bf16[1024,256]{1,0:T(8,128)(2,1)S(1)} %collective-permute-done.7.refs_3_), channel_id=1, source_target_pairs={{8,0},{16,8},{24,16},{28,24},{20,28},{12,20},{4,12},{0,4},{9,1},{1... | collective-permute-start | bytes 1572872 | tf_op jit(solution)/shard_map/ppermute | solution.py:434
  207.9 0.8 copy-start.12
  213.5 0.8 copy-start.10
  213.5 1.0 copy-start.11
  218.2 2.9 %collective-permute-start.23 = (bf16[2,256,1024]{2,1,0:T(8,128)(2,1)}, bf16[2,256,1024]{2,1,0:T(8,128)(2,1)S(1)}, u32[]{:S(2)}, u32[]{:S(2)}) collective-permute-start(bf16[2,256,1024]{2,1,0:T(8,128)(2,1)} %get-tuple-element.68), channel_id=1, source_target_pairs={{0,1},{1,0},{2,3},{3,2},{4,5},{5,4},{6,7},{7,6},{8,9},{9,8},{10,11... | collective-permute-start | bytes 3145736 | tf_op jit(solution)/shard_map/ppermute | solution.py:558

commit v9 on v8

--- a/solution.py
+++ b/solution.py
@@ -46,7 +46,7 @@
     highest = jnp.max(first, axis=0, keepdims=True)
     weights = jnp.exp2((first - highest) * (SCALE * LOG2E))
     total = jnp.sum(weights, axis=0, keepdims=True)
-    part_ref[0, :, :half] = (mix_by_width(v_ref[0, :half], weights) / total).astype(
+    part_ref[0, :, :half] = (mix_by_width(v_ref[0, :half], weights) * (1.0 / total)).astype(
         part_ref.dtype
     )
     log_ref[0, :, :half] = highest * SCALE + jnp.log(total)
@@ -60,7 +60,7 @@
     within = jnp.exp2((within - highest) * (SCALE * LOG2E))
     total = jnp.sum(before, axis=0, keepdims=True) + jnp.sum(within, axis=0, keepdims=True)
     mixed = mix_by_width(v_ref[0, :half], before) + mix_by_width(v_ref[0, half:], within)
-    part_ref[0, :, half:] = (mixed / total).astype(part_ref.dtype)
+    part_ref[0, :, half:] = (mixed * (1.0 / total)).astype(part_ref.dtype)
     log_ref[0, :, half:] = highest * SCALE + jnp.log(total)
 
 
@@ -104,7 +104,7 @@
     highest = jnp.max(scores, axis=0, keepdims=True)
     weights = jnp.exp2((scores - highest) * (SCALE * LOG2E))
     total = jnp.sum(weights, axis=0, keepdims=True)
-    part = (mix_by_width(values, weights) / total).astype(jnp.bfloat16)
+    part = (mix_by_width(values, weights) * (1.0 / total)).astype(jnp.bfloat16)
     return part, highest * SCALE + jnp.log(total)
 
 
@@ -166,11 +166,12 @@
     own_share = jnp.exp(own_log - top)
     first_share = jnp.exp(first_log - top)
     second_share = jnp.exp(second_log - top)
+    whole = 1.0 / (own_share + first_share + second_share)
     merged = (
-        own_share * own.astype(jnp.float32)
-        + first_share * first.astype(jnp.float32)
-        + second_share * second.astype(jnp.float32)
-    ) / (own_share + first_share + second_share)
+        (own_share * whole) * own.astype(jnp.float32)
+        + (first_share * whole) * first.astype(jnp.float32)
+        + (second_share * whole) * second.astype(jnp.float32)
+    )
     early = merged[:, :half].astype(jnp.bfloat16).T
     late = merged[:, half:].astype(jnp.bfloat16).T
     return jnp.where(rep == 0, early, late), jnp.where(rep == 0, late, early)

time: 226 us -> 226 us (level)
  no operation moved by 1% of the time
where the time goes in v9:
time: 226 us; the launch traced here: 222 us
  waiting for transfers between devices  87.6 us (39%)
  Pallas kernels  76.6 us (34%)
  starting transfers between devices  29.1 us (13%)
  other arithmetic  15.3 us (7%)
  local copies, waits for them, and re-layouts  13.2 us (6%)
    ppermute x20, waiting for transfers between devices, hop(): return lax.ppermute(value, 'ctx', pairs)  84.7 us
    ppermute x20, starting transfers between devices, hop(): return lax.ppermute(value, 'ctx', pairs)  29.1 us
    pallas_call x4, Pallas kernels, final_attention(): pl.pallas_call(functools.partial(final_kernel, first_row, groups, keeps_p...  26.6 us
    pallas_call x5, Pallas kernels, pick_attention(): pl.pallas_call(functools.partial(pick_kernel, row), in_specs=[smem, smem]...  25.8 us
    pallas_call x1, Pallas kernels, own_attention(): pl.pallas_call(own_kernel, grid=(count,), in_specs=[query_spec, key_spec,...  15.8 us
    select_n x3, other arithmetic, all_rows(): jnp.where(rep_index == 0, jnp.concatenate([kept, came], axis=1), jnp.conc...  6.98 us
  transfers between devices with their start and end apart: 24, of which 13 were waited for; matrix products, arithmetic and copies ran while one was open for 12% of the time, Pallas kernels for 32%

profile of v9, /device:TPU:0, one launch (start us, length us, event | category | flops | bytes accessed | tf_op | source)
XLA Modules:
  0.0 222.0 jit_solution(2619660442645079338)
XLA Ops:
  0.0 2.0 columns_kept.2.k_hbm
  2.0 3.1 %collective-permute-start.1 = (bf16[2048,256]{1,0:T(8,128)(2,1)}, bf16[2048,256]{1,0:T(8,128)(2,1)}, u32[]{:S(2)}, u32[]{:S(2)}) collective-permute-start(bf16[2048,256]{1,0:T(8,128)(2,1)} %columns_kept.2.k_hbm), channel_id=1, source_target_pairs={{0,8},{8,16},{16,24},{24,28},{28,20},{20,12},{12,4},{4,0},{1,9},{9... | collective-permute-start | bytes 3145736 | tf_op jit(solution)/shard_map/ppermute | solution.py:435
  5.1 2.0 columns_kept.3.v_hbm
  7.2 2.1 collective-permute-start.15
  9.3 1.2 constant_dynamic-slice_fusion.5
  14.2 1.3 broadcast_compare_fusion.5
  15.5 1.3 broadcast_compare_fusion.2
  18.6 1.1 constant_dynamic-slice_fusion.3
  21.3 8.1 %collective-permute-done.1.k_hbm = bf16[2048,256]{1,0:T(8,128)(2,1)} collective-permute-done((bf16[2048,256]{1,0:T(8,128)(2,1)}, bf16[2048,256]{1,0:T(8,128)(2,1)}, u32[]{:S(2)}, u32[]{:S(2)}) %collective-permute-start.1) | collective-permute-done | bytes 1048608 | tf_op jit(solution)/shard_map/ppermute | solution.py:435
  29.4 2.1 collective-permute-start.2
  31.7 20.9 %collective-permute-done.5.v_hbm = bf16[2048,256]{1,0:T(8,128)(2,1)} collective-permute-done((bf16[2048,256]{1,0:T(8,128)(2,1)}, bf16[2048,256]{1,0:T(8,128)(2,1)}, u32[]{:S(2)}, u32[]{:S(2)}) %collective-permute-start.5) | collective-permute-done | bytes 1048608 | tf_op jit(solution)/shard_map/ppermute | solution.py:435
  53.5 1.7 collective-permute-start.16
  56.3 18.0 %collective-permute-done.2.k_hbm = bf16[2048,256]{1,0:T(8,128)(2,1)S(1)} collective-permute-done((bf16[2048,256]{1,0:T(8,128)(2,1)}, bf16[2048,256]{1,0:T(8,128)(2,1)S(1)}, u32[]{:S(2)}, u32[]{:S(2)}) %collective-permute-start.2) | collective-permute-done | bytes 1048608 | tf_op jit(solution)/shard_map/ppermute | solution.py:435
  75.2 3.6 %collective-permute-done.6.v_hbm = bf16[2048,256]{1,0:T(8,128)(2,1)S(1)} collective-permute-done((bf16[2048,256]{1,0:T(8,128)(2,1)}, bf16[2048,256]{1,0:T(8,128)(2,1)S(1)}, u32[]{:S(2)}, u32[]{:S(2)}) %collective-permute-start.6) | collective-permute-done | bytes 1048608 | tf_op jit(solution)/shard_map/ppermute | solution.py:435
  78.8 1.6 collective-permute-start.11
  81.3 15.4 %collective-permute-done.16.v_hbm = bf16[2048,256]{1,0:T(8,128)(2,1)S(1)} collective-permute-done((bf16[2048,256]{1,0:T(8,128)(2,1)}, bf16[2048,256]{1,0:T(8,128)(2,1)S(1)}, u32[]{:S(2)}, u32[]{:S(2)}) %collective-permute-start.16) | collective-permute-done | bytes 1048608 | tf_op jit(solution)/shard_map/ppermute | solution.py:435
  96.7 2.0 collective-permute-start.13
  98.7 1.1 fusion.10
  100.3 1.6 collective-permute-start.21
  101.9 1.1 fusion.9
  103.6 1.5 collective-permute-start.3
  105.0 3.0 %collective-permute-done.11.refs_0_ = bf16[1024,256]{1,0:T(8,128)(2,1)} collective-permute-done((bf16[1024,256]{1,0:T(8,128)(2,1)S(1)}, bf16[1024,256]{1,0:T(8,128)(2,1)}, u32[]{:S(2)}, u32[]{:S(2)}) %collective-permute-start.11) | collective-permute-done | bytes 524320 | tf_op jit(solution)/shard_map/ppermute | solution.py:435
  108.1 2.0 collective-permute-start.7
  110.1 1.5 collective-permute-done.13.refs_3_
  111.6 2.0 collective-permute-start.17
  113.6 1.1 compare_select_fusion.5.ready
  114.7 2.0 maximum_select_fusion.1.k_ref
  117.8 1.5 collective-permute-done.21.refs_1_
  119.3 2.0 collective-permute-start.20
  121.3 3.9 %maximum_select_fusion.q_ref.q_hbm = bf16[2,512,1024]{2,1,0:T(8,128)(2,1)} fusion(bf16[2,256,1024]{2,1,0:T(8,128)(2,1)} %collective-permute-done, bf16[2,256,1024]{2,1,0:T(8,128)(2,1)S(1)} %get-tuple-element.86, pred[]{:T(512)S(6)} %eq.253), kind=kLoop, calls=%fused_computation.1 | loop fusion | flops 9437184 | bytes 4194305 | tf_op jit(solution)/shard_map/jit(_where)/select_n | solution.py:466
  125.3 5.1 %collective-permute-done.3.refs_0_ = bf16[1024,256]{1,0:T(8,128)(2,1)S(1)} collective-permute-done((bf16[1024,256]{1,0:T(8,128)(2,1)}, bf16[1024,256]{1,0:T(8,128)(2,1)S(1)}, u32[]{:S(2)}, u32[]{:S(2)}) %collective-permute-start.3) | collective-permute-done | bytes 524320 | tf_op jit(solution)/shard_map/ppermute | solution.py:435
  130.4 2.0 collective-permute-start.14
  132.4 1.6 collective-permute-done.7.refs_3_
  134.0 2.0 collective-permute-start.4
  136.1 5.7 %collective-permute-done.17.refs_1_ = bf16[1024,256]{1,0:T(8,128)(2,1)} collective-permute-done((bf16[1024,256]{1,0:T(8,128)(2,1)}, bf16[1024,256]{1,0:T(8,128)(2,1)}, u32[]{:S(2)}, u32[]{:S(2)}) %collective-permute-start.17) | collective-permute-done | bytes 524320 | tf_op jit(solution)/shard_map/ppermute | solution.py:435
  141.8 2.0 collective-permute-start.8
  143.8 15.8 %own_attention.1 = (bf16[16,128,512]{2,1,0:T(8,128)(2,1)}, f32[16,1,512]{2,1,0:T(1,128)}, bf16[34,128,512]{2,1,0:T(8,128)(2,1)}, f32[34,1,512]{2,1,0:T(1,128)}, ...) custom-call(bf16[2,512,1024]{2,1,0:T(8,128)(2,1)} %maximum_select_fusion.q_ref.q_hbm, ...), custom_call_target="tpu_custom_call" | custom-call | flops 2147483648 | bytes 8388608 | tf_op jit(solution)/shard_map/own_attention/pallas_call | solution.py:76
  159.6 5.8 %pick_attention.5 = (bf16[34,128,512]{2,1,0:T(8,128)(2,1)}, f32[34,1,512]{2,1,0:T(1,128)}) custom-call(s32[5,5,32]{2,1,0:T(8,128)} %broadcast_select_fusion.1.table, s32[5]{0:T(128)} %copy-done.14, bf16[2,512,1024]{2,1,0:T(8,128)(2,1)} %maximum_select_fusion.q_ref.q_hbm, ...), custom_call_target="tpu_custom_call", output_to_operand_aliasing={{0}: (5, {}), {1}: (6, {})} | custom-call | flops 536870912 | bytes 2097152 | tf_op jit(solution)/shard_map/pick_attention/pallas_call | solution.py:145
  165.4 7.4 %pick_attention.6 = (bf16[34,128,512]{2,1,0:T(8,128)(2,1)}, f32[34,1,512]{2,1,0:T(1,128)}) custom-call(s32[5,5,32]{2,1,0:T(8,128)} %broadcast_select_fusion.1.table, s32[5]{0:T(128)} %copy-done.14, bf16[2,512,1024]{2,1,0:T(8,128)(2,1)} %maximum_select_fusion.q_ref.q_hbm, ...), custom_call_target="tpu_custom_call", output_to_operand_aliasing={{0}: (5, {}), {1}: (6, {})} | custom-call | flops 536870912 | bytes 2097152 | tf_op jit(solution)/shard_map/pick_attention/pallas_call | solution.py:145
  172.8 5.8 %pick_attention.7 = (bf16[34,128,512]{2,1,0:T(8,128)(2,1)}, f32[34,1,512]{2,1,0:T(1,128)}) custom-call(s32[5,5,32]{2,1,0:T(8,128)} %broadcast_select_fusion.1.table, s32[5]{0:T(128)} %copy-done.14, bf16[2,512,1024]{2,1,0:T(8,128)(2,1)} %maximum_select_fusion.q_ref.q_hbm, ...), custom_call_target="tpu_custom_call", output_to_operand_aliasing={{0}: (5, {}), {1}: (6, {})} | custom-call | flops 536870912 | bytes 2097152 | tf_op jit(solution)/shard_map/pick_attention/pallas_call | solution.py:145
  178.6 5.8 %pick_attention.8 = (bf16[34,128,512]{2,1,0:T(8,128)(2,1)}, f32[34,1,512]{2,1,0:T(1,128)}) custom-call(s32[5,5,32]{2,1,0:T(8,128)} %broadcast_select_fusion.1.table, s32[5]{0:T(128)} %copy-done.14, bf16[2,512,1024]{2,1,0:T(8,128)(2,1)} %maximum_select_fusion.q_ref.q_hbm, bf16[2048,256]{1,0:T(8,128)(2,1)} %copy-done.1, ...), custom_call_target="tpu_custom_call", output_to_operand_aliasing={{0}: (5, {}), {1}: (6, {})} | custom-call | flops 536870912 | bytes 2097152 | tf_op jit(solution)/shard_map/pick_attention/pallas_call | solution.py:145
  185.4 4.3 %merge_parts.1 = (bf16[2,256,2048]{2,1,0:T(8,128)(2,1)}, bf16[2,256,1024]{2,1,0:T(8,128)(2,1)}) custom-call(s32[1]{0:T(128)} %bitcast.rep, s32[16]{0:T(128)} %compare_select_fusion.5.ready, s32[1]{0:T(128)} %bitcast.7.count, bf16[16,128,512]{2,1,0:T(8,128)(2,1)} %get-tuple-element.37.own_hbm.refs_4_.refs_2_, ...), custom_call_target="tpu_custom_call", output_to_operand_aliasing={{0}: (7, {}), {1}: (8, {})} | custom-call | flops 8388608 | bytes 10485760 | tf_op jit(solution)/shard_map/merge_parts/pallas_call | solution.py:218
  189.7 5.8 %final_attention.4 = (bf16[34,128,512]{2,1,0:T(8,128)(2,1)}, f32[34,1,512]{2,1,0:T(1,128)}, bf16[2,256,2048]{2,1,0:T(8,128)(2,1)}, bf16[2,256,1024]{2,1,0:T(8,128)(2,1)}) custom-call(s32[1]{0:T(128)} %bitcast.rep, s32[6,7,32]{2,1,0:T(8,128)} %broadcast_select_fusion.table, ...), custom_call_target="tpu_custom_call", output_to_operand_aliasing={{0}: (10, {}), {1}: (11, {}), {2}: (12, {}), {3}: (13, {})} | custom-call | flops 536870912 | bytes 4718592 | tf_op jit(solution)/shard_map/final_attention/pallas_call | solution.py:330
  195.5 12.4 %final_attention.5 = (bf16[34,128,512]{2,1,0:T(8,128)(2,1)}, f32[34,1,512]{2,1,0:T(1,128)}, bf16[2,256,2048]{2,1,0:T(8,128)(2,1)}, bf16[2,256,1024]{2,1,0:T(8,128)(2,1)}) custom-call(s32[1]{0:T(128)} %bitcast.rep, s32[6,7,32]{2,1,0:T(8,128)} %broadcast_select_fusion.table, ...), custom_call_target="tpu_custom_call", output_to_operand_aliasing={{0}: (10, {}), {1}: (11, {}), {2}: (12, {}), {3}: (13, {})} | custom-call | flops 536870912 | bytes 4718592 | tf_op jit(solution)/shard_map/final_attention/pallas_call | solution.py:330
  208.7 4.7 %final_attention.6 = (bf16[34,128,512]{2,1,0:T(8,128)(2,1)}, f32[34,1,512]{2,1,0:T(1,128)}, bf16[2,256,2048]{2,1,0:T(8,128)(2,1)}, bf16[2,256,1024]{2,1,0:T(8,128)(2,1)}) custom-call(s32[1]{0:T(128)} %bitcast.rep, s32[6,7,32]{2,1,0:T(8,128)} %broadcast_select_fusion.table, ...), custom_call_target="tpu_custom_call", output_to_operand_aliasing={{0}: (8, {}), {1}: (9, {}), {2}: (10, {}), {3}: (11, {})} | custom-call | flops 268435456 | bytes 2359296 | tf_op jit(solution)/shard_map/final_attention/pallas_call | solution.py:330
  214.4 3.7 %final_attention.7 = (bf16[34,128,512]{2,1,0:T(8,128)(2,1)}, f32[34,1,512]{2,1,0:T(1,128)}, bf16[2,256,2048]{2,1,0:T(8,128)(2,1)}, bf16[2,256,1024]{2,1,0:T(8,128)(2,1)}) custom-call(s32[1]{0:T(128)} %bitcast.rep, s32[6,7,32]{2,1,0:T(8,128)} %broadcast_select_fusion.table, ...), custom_call_target="tpu_custom_call", output_to_operand_aliasing={{0}: (8, {}), {1}: (9, {}), {2}: (10, {}), {3}: (11, {})} | custom-call | flops 268435456 | bytes 2359296 | tf_op jit(solution)/shard_map/final_attention/pallas_call | solution.py:330
  218.1 2.9 %collective-permute-done.23 = bf16[2,256,1024]{2,1,0:T(8,128)(2,1)S(1)} collective-permute-done((bf16[2,256,1024]{2,1,0:T(8,128)(2,1)}, bf16[2,256,1024]{2,1,0:T(8,128)(2,1)S(1)}, u32[]{:S(2)}, u32[]{:S(2)}) %collective-permute-start.23) | collective-permute-done | bytes 1048608 | tf_op jit(solution)/shard_map/ppermute | solution.py:559
  221.0 1.0 constant_dynamic-update-slice_fusion
  (118 shorter events, 16.1 us)
Async XLA Ops:
  2.0 7.2 %copy-start.5 = (bf16[2,256,2048]{2,1,0:T(8,128)(2,1)S(1)}, bf16[2,256,2048]{2,1,0:T(8,128)(2,1)}, u32[]{:S(2)}) copy-start(bf16[2,256,2048]{2,1,0:T(8,128)(2,1)} %param.10) | copy-start | bytes 6291460
  2.0 27.4 %collective-permute-start.1 = (bf16[2048,256]{1,0:T(8,128)(2,1)}, bf16[2048,256]{1,0:T(8,128)(2,1)}, u32[]{:S(2)}, u32[]{:S(2)}) collective-permute-start(bf16[2048,256]{1,0:T(8,128)(2,1)} %columns_kept.2.k_hbm), channel_id=1, source_target_pairs={{0,8},{8,16},{16,24},{24,28},{28,20},{20,12},{12,4},{4,0},{1,9},{9... | collective-permute-start | bytes 3145736 | tf_op jit(solution)/shard_map/ppermute | solution.py:435
  5.1 50.1 %collective-permute-start.18 = (bf16[2048,256]{1,0:T(8,128)(2,1)}, bf16[2048,256]{1,0:T(8,128)(2,1)}, u32[]{:S(2)}, u32[]{:S(2)}) collective-permute-start(bf16[2048,256]{1,0:T(8,128)(2,1)} %columns_kept.2.k_hbm), channel_id=1, source_target_pairs={{8,0},{16,8},{24,16},{28,24},{20,28},{12,20},{4,12},{0,4},{9,1},{1... | collective-permute-start | bytes 3145736 | tf_op jit(solution)/shard_map/ppermute | solution.py:435
  7.2 46.3 %collective-permute-start.15 = (bf16[2048,256]{1,0:T(8,128)(2,1)}, bf16[2048,256]{1,0:T(8,128)(2,1)}, u32[]{:S(2)}, u32[]{:S(2)}) collective-permute-start(bf16[2048,256]{1,0:T(8,128)(2,1)} %columns_kept.3.v_hbm), channel_id=1, source_target_pairs={{0,8},{8,16},{16,24},{24,28},{28,20},{20,12},{12,4},{4,0},{1,9},{9... | collective-permute-start | bytes 3145736 | tf_op jit(solution)/shard_map/ppermute | solution.py:435
  9.2 43.3 %collective-permute-start.5 = (bf16[2048,256]{1,0:T(8,128)(2,1)}, bf16[2048,256]{1,0:T(8,128)(2,1)}, u32[]{:S(2)}, u32[]{:S(2)}) collective-permute-start(bf16[2048,256]{1,0:T(8,128)(2,1)} %columns_kept.3.v_hbm), channel_id=1, source_target_pairs={{8,0},{16,8},{24,16},{28,24},{20,28},{12,20},{4,12},{0,4},{9,1},{1... | collective-permute-start | bytes 3145736 | tf_op jit(solution)/shard_map/ppermute | solution.py:435
  9.2 1.2 slice-start
  9.2 1.7 copy-start.17
  9.2 2.3 %copy-start.16 = (s32[8]{0:T(128)S(1)}, s32[8]{0:T(128)}, u32[]{:S(2)}) copy-start(s32[8]{0:T(128)} %constant.146.clone) | copy-start | bytes 100
  9.3 2.9 %copy-start = (s32[8]{0:T(128)S(1)}, s32[8]{0:T(128)}, u32[]{:S(2)}) copy-start(s32[8]{0:T(128)} %constant.145.clone) | copy-start | bytes 100
  10.4 10.0 %copy-start.13 = (bf16[2,256,512]{2,1,0:T(8,128)(2,1)S(1)}, bf16[2,256,512]{2,1,0:T(8,128)(2,1)}, u32[]{:S(2)}) copy-start(bf16[2,256,512]{2,1,0:T(8,128)(2,1)} %param.12) | copy-start | bytes 1572868
  10.5 93.1 %collective-permute-start = (bf16[2,256,1024]{2,1,0:T(8,128)(2,1)}, bf16[2,256,1024]{2,1,0:T(8,128)(2,1)}, u32[]{:S(2)}, u32[]{:S(2)}) collective-permute-start(bf16[2,256,1024]{2,1,0:T(8,128)(2,1)} %get-tuple-element.87), channel_id=1, source_target_pairs={{0,1},{1,0},{2,3},{3,2},{4,5},{5,4},{6,7},{7,6},{8,9},{9,8},{10,11... | collective-permute-start | bytes 3145736 | tf_op jit(solution)/shard_map/ppermute | solution.py:465
  18.1 57.1 %copy-start.15 = (s32[6]{0:T(128)}, s32[6]{0:T(128)S(1)}, u32[]{:S(2)}) copy-start(s32[6]{0:T(128)S(1)} %get-tuple-element.73.count) | copy-start | bytes 76
  20.2 61.0 %copy-start.14 = (s32[5]{0:T(128)}, s32[5]{0:T(128)S(1)}, u32[]{:S(2)}) copy-start(s32[5]{0:T(128)S(1)} %convert_reduce_fusion.count) | copy-start | bytes 64
  29.4 44.8 %collective-permute-start.2 = (bf16[2048,256]{1,0:T(8,128)(2,1)}, bf16[2048,256]{1,0:T(8,128)(2,1)S(1)}, u32[]{:S(2)}, u32[]{:S(2)}) collective-permute-start(bf16[2048,256]{1,0:T(8,128)(2,1)} %collective-permute-done.1.k_hbm), channel_id=1, source_target_pairs={{0,8},{8,16},{16,24},{24,28},{28,20},{20,12},{12,4},{4,0},{1,9},{9... | collective-permute-start | bytes 3145736 | tf_op jit(solution)/shard_map/ppermute | solution.py:435
  52.5 26.2 %collective-permute-start.6 = (bf16[2048,256]{1,0:T(8,128)(2,1)}, bf16[2048,256]{1,0:T(8,128)(2,1)S(1)}, u32[]{:S(2)}, u32[]{:S(2)}) collective-permute-start(bf16[2048,256]{1,0:T(8,128)(2,1)} %collective-permute-done.5.v_hbm), channel_id=1, source_target_pairs={{8,0},{16,8},{24,16},{28,24},{20,28},{12,20},{4,12},{0,4},{9,1},{1... | collective-permute-start | bytes 3145736 | tf_op jit(solution)/shard_map/ppermute | solution.py:435
  53.5 43.2 %collective-permute-start.16 = (bf16[2048,256]{1,0:T(8,128)(2,1)}, bf16[2048,256]{1,0:T(8,128)(2,1)S(1)}, u32[]{:S(2)}, u32[]{:S(2)}) collective-permute-start(bf16[2048,256]{1,0:T(8,128)(2,1)} %collective-permute-done.15.v_hbm), channel_id=1, source_target_pairs={{0,8},{8,16},{16,24},{24,28},{28,20},{20,12},{12,4},{4,0},{1,9},{9... | collective-permute-start | bytes 3145736 | tf_op jit(solution)/shard_map/ppermute | solution.py:435
  55.3 45.0 %collective-permute-start.19 = (bf16[2048,256]{1,0:T(8,128)(2,1)}, bf16[2048,256]{1,0:T(8,128)(2,1)S(1)}, u32[]{:S(2)}, u32[]{:S(2)}) collective-permute-start(bf16[2048,256]{1,0:T(8,128)(2,1)} %collective-permute-done.18.k_hbm), channel_id=1, source_target_pairs={{8,0},{16,8},{24,16},{28,24},{20,28},{12,20},{4,12},{0,4},{9,1},{1... | collective-permute-start | bytes 3145736 | tf_op jit(solution)/shard_map/ppermute | solution.py:435
  74.2 7.0 %copy-start.1 = (bf16[2048,256]{1,0:T(8,128)(2,1)}, bf16[2048,256]{1,0:T(8,128)(2,1)S(1)}, u32[]{:S(2)}) copy-start(bf16[2048,256]{1,0:T(8,128)(2,1)S(1)} %collective-permute-done.2.k_hbm) | copy-start | bytes 3145732
  74.2 25.6 %collective-permute-start.9 = (bf16[2,256,256]{2,1,0:T(8,128)(2,1)S(1)}, bf16[2,256,256]{2,1,0:T(8,128)(2,1)}, u32[]{:S(2)}, u32[]{:S(2)}) collective-permute-start(bf16[2,256,256]{2,1,0:T(8,128)(2,1)S(1)} %get-tuple-element.99), channel_id=1, source_target_pairs={{0,1},{1,0},{2,3},{3,2},{4,5},{5,4},{6,7},{7,6},{8,9},{9,8},{10,11... | collective-permute-start | bytes 786440 | tf_op jit(solution)/shard_map/ppermute | solution.py:465
  78.8 21.0 %copy-start.2 = (bf16[2048,256]{1,0:T(8,128)(2,1)}, bf16[2048,256]{1,0:T(8,128)(2,1)S(1)}, u32[]{:S(2)}) copy-start(bf16[2048,256]{1,0:T(8,128)(2,1)S(1)} %collective-permute-done.6.v_hbm) | copy-start | bytes 3145732
  78.8 29.3 %collective-permute-start.11 = (bf16[1024,256]{1,0:T(8,128)(2,1)S(1)}, bf16[1024,256]{1,0:T(8,128)(2,1)}, u32[]{:S(2)}, u32[]{:S(2)}) collective-permute-start(bf16[1024,256]{1,0:T(8,128)(2,1)S(1)} %get-tuple-element.94), channel_id=1, source_target_pairs={{0,8},{8,16},{16,24},{24,28},{28,20},{20,12},{12,4},{4,0},{1,9},{9... | collective-permute-start | bytes 1572872 | tf_op jit(solution)/shard_map/ppermute | solution.py:435
  96.7 6.3 %copy-start.4 = (bf16[2048,256]{1,0:T(8,128)(2,1)}, bf16[2048,256]{1,0:T(8,128)(2,1)S(1)}, u32[]{:S(2)}) copy-start(bf16[2048,256]{1,0:T(8,128)(2,1)S(1)} %collective-permute-done.16.v_hbm) | copy-start | bytes 3145732
  96.7 14.8 %collective-permute-start.13 = (bf16[1024,256]{1,0:T(8,128)(2,1)S(1)}, bf16[1024,256]{1,0:T(8,128)(2,1)S(1)}, u32[]{:S(2)}, u32[]{:S(2)}) collective-permute-start(bf16[1024,256]{1,0:T(8,128)(2,1)S(1)} %get-tuple-element.92), channel_id=1, source_target_pairs={{8,0},{16,8},{24,16},{28,24},{20,28},{12,20},{4,12},{0,4},{9,1},{1... | collective-permute-start | bytes 1572872 | tf_op jit(solution)/shard_map/ppermute | solution.py:435
  99.8 16.9 %copy-start.6 = (bf16[2,256,256]{2,1,0:T(8,128)(2,1)S(1)}, bf16[2,256,256]{2,1,0:T(8,128)(2,1)}, u32[]{:S(2)}) copy-start(bf16[2,256,256]{2,1,0:T(8,128)(2,1)} %get-tuple-element.96) | copy-start | bytes 786436
  99.8 3.2 %collective-permute-start.10 = (bf16[2,256,256]{2,1,0:T(8,128)(2,1)S(1)}, bf16[2,256,256]{2,1,0:T(8,128)(2,1)S(1)}, u32[]{:S(2)}, u32[]{:S(2)}) collective-permute-start(bf16[2,256,256]{2,1,0:T(8,128)(2,1)S(1)} %get-tuple-element.97), channel_id=1, source_target_pairs={{0,1},{1,0},{2,3},{3,2},{4,5},{5,4},{6,7},{7,6},{8,9},{9,8},{10,11... | collective-permute-start | bytes 786440 | tf_op jit(solution)/shard_map/ppermute | solution.py:465
  100.3 1.6 copy-start.3
  100.3 19.0 %collective-permute-start.21 = (bf16[1024,256]{1,0:T(8,128)(2,1)}, bf16[1024,256]{1,0:T(8,128)(2,1)}, u32[]{:S(2)}, u32[]{:S(2)}) collective-permute-start(bf16[1024,256]{1,0:T(8,128)(2,1)} %get-tuple-element.90), channel_id=1, source_target_pairs={{0,8},{8,16},{16,24},{24,28},{28,20},{20,12},{12,4},{4,0},{1,9},{9... | collective-permute-start | bytes 1572872 | tf_op jit(solution)/shard_map/ppermute | solution.py:435
  103.0 22.3 %collective-permute-start.22 = (bf16[1024,256]{1,0:T(8,128)(2,1)}, bf16[1024,256]{1,0:T(8,128)(2,1)}, u32[]{:S(2)}, u32[]{:S(2)}) collective-permute-start(bf16[1024,256]{1,0:T(8,128)(2,1)} %get-tuple-element.88), channel_id=1, source_target_pairs={{8,0},{16,8},{24,16},{28,24},{20,28},{12,20},{4,12},{0,4},{9,1},{1... | collective-permute-start | bytes 1572872 | tf_op jit(solution)/shard_map/ppermute | solution.py:435
  103.6 26.9 %collective-permute-start.3 = (bf16[1024,256]{1,0:T(8,128)(2,1)}, bf16[1024,256]{1,0:T(8,128)(2,1)S(1)}, u32[]{:S(2)}, u32[]{:S(2)}) collective-permute-start(bf16[1024,256]{1,0:T(8,128)(2,1)} %get-tuple-element.95), channel_id=1, source_target_pairs={{0,8},{8,16},{16,24},{24,28},{28,20},{20,12},{12,4},{4,0},{1,9},{9... | collective-permute-start | bytes 1572872 | tf_op jit(solution)/shard_map/ppermute | solution.py:435
  108.1 26.0 %collective-permute-start.7 = (bf16[1024,256]{1,0:T(8,128)(2,1)}, bf16[1024,256]{1,0:T(8,128)(2,1)S(1)}, u32[]{:S(2)}, u32[]{:S(2)}) collective-permute-start(bf16[1024,256]{1,0:T(8,128)(2,1)} %get-tuple-element.93), channel_id=1, source_target_pairs={{8,0},{16,8},{24,16},{28,24},{20,28},{12,20},{4,12},{0,4},{9,1},{1... | collective-permute-start | bytes 1572872 | tf_op jit(solution)/shard_map/ppermute | solution.py:435
  111.6 18.9 %copy-start.7 = (bf16[1024,256]{1,0:T(8,128)(2,1)}, bf16[1024,256]{1,0:T(8,128)(2,1)S(1)}, u32[]{:S(2)}) copy-start(bf16[1024,256]{1,0:T(8,128)(2,1)S(1)} %collective-permute-done.13.refs_3_) | copy-start | bytes 1572868
  111.6 30.2 %collective-permute-start.17 = (bf16[1024,256]{1,0:T(8,128)(2,1)}, bf16[1024,256]{1,0:T(8,128)(2,1)}, u32[]{:S(2)}, u32[]{:S(2)}) collective-permute-start(bf16[1024,256]{1,0:T(8,128)(2,1)} %get-tuple-element.91), channel_id=1, source_target_pairs={{0,8},{8,16},{16,24},{24,28},{28,20},{20,12},{12,4},{4,0},{1,9},{9... | collective-permute-start | bytes 1572872 | tf_op jit(solution)/shard_map/ppermute | solution.py:435
  119.3 76.2 %collective-permute-start.20 = (bf16[1024,256]{1,0:T(8,128)(2,1)}, bf16[1024,256]{1,0:T(8,128)(2,1)}, u32[]{:S(2)}, u32[]{:S(2)}) collective-permute-start(bf16[1024,256]{1,0:T(8,128)(2,1)} %get-tuple-element.89), channel_id=1, source_target_pairs={{8,0},{16,8},{24,16},{28,24},{20,28},{12,20},{4,12},{0,4},{9,1},{1... | collective-permute-start | bytes 1572872 | tf_op jit(solution)/shard_map/ppermute | solution.py:435
  125.3 82.6 %collective-permute-start.12 = (bf16[1024,256]{1,0:T(8,128)(2,1)}, bf16[1024,256]{1,0:T(8,128)(2,1)S(1)}, u32[]{:S(2)}, u32[]{:S(2)}) collective-permute-start(bf16[1024,256]{1,0:T(8,128)(2,1)} %collective-permute-done.11.refs_0_), channel_id=1, source_target_pairs={{0,8},{8,16},{16,24},{24,28},{28,20},{20,12},{12,4},{4,0},{1,9},{9... | collective-permute-start | bytes 1572872 | tf_op jit(solution)/shard_map/ppermute | solution.py:435
  130.4 29.2 %copy-start.8 = (bf16[1024,256]{1,0:T(8,128)(2,1)}, bf16[1024,256]{1,0:T(8,128)(2,1)S(1)}, u32[]{:S(2)}) copy-start(bf16[1024,256]{1,0:T(8,128)(2,1)S(1)} %collective-permute-done.3.refs_0_) | copy-start | bytes 1572868
  130.4 77.5 %collective-permute-start.14 = (bf16[1024,256]{1,0:T(8,128)(2,1)S(1)}, bf16[1024,256]{1,0:T(8,128)(2,1)}, u32[]{:S(2)}, u32[]{:S(2)}) collective-permute-start(bf16[1024,256]{1,0:T(8,128)(2,1)S(1)} %collective-permute-done.13.refs_3_), channel_id=1, source_target_pairs={{8,0},{16,8},{24,16},{28,24},{20,28},{12,20},{4,12},{0,4},{9,1},{1... | collective-permute-start | bytes 1572872 | tf_op jit(solution)/shard_map/ppermute | solution.py:435
  134.0 25.5 %copy-start.9 = (bf16[1024,256]{1,0:T(8,128)(2,1)}, bf16[1024,256]{1,0:T(8,128)(2,1)S(1)}, u32[]{:S(2)}) copy-start(bf16[1024,256]{1,0:T(8,128)(2,1)S(1)} %collective-permute-done.7.refs_3_) | copy-start | bytes 1572868
  134.0 79.4 %collective-permute-start.4 = (bf16[1024,256]{1,0:T(8,128)(2,1)S(1)}, bf16[1024,256]{1,0:T(8,128)(2,1)S(1)}, u32[]{:S(2)}, u32[]{:S(2)}) collective-permute-start(bf16[1024,256]{1,0:T(8,128)(2,1)S(1)} %collective-permute-done.3.refs_0_), channel_id=1, source_target_pairs={{0,8},{8,16},{16,24},{24,28},{28,20},{20,12},{12,4},{4,0},{1,9},{9... | collective-permute-start | bytes 1572872 | tf_op jit(solution)/shard_map/ppermute | solution.py:435
  141.8 71.7 %collective-permute-start.8 = (bf16[1024,256]{1,0:T(8,128)(2,1)S(1)}, bf16[1024,256]{1,0:T(8,128)(2,1)S(1)}, u32[]{:S(2)}, u32[]{:S(2)}) collective-permute-start(bf16[1024,256]{1,0:T(8,128)(2,1)S(1)} %collective-permute-done.7.refs_3_), channel_id=1, source_target_pairs={{8,0},{16,8},{24,16},{28,24},{20,28},{12,20},{4,12},{0,4},{9,1},{1... | collective-permute-start | bytes 1572872 | tf_op jit(solution)/shard_map/ppermute | solution.py:435
  207.9 0.8 copy-start.12
  213.4 0.8 copy-start.10
  213.4 1.0 copy-start.11
  218.1 2.9 %collective-permute-start.23 = (bf16[2,256,1024]{2,1,0:T(8,128)(2,1)}, bf16[2,256,1024]{2,1,0:T(8,128)(2,1)S(1)}, u32[]{:S(2)}, u32[]{:S(2)}) collective-permute-start(bf16[2,256,1024]{2,1,0:T(8,128)(2,1)} %get-tuple-element.68), channel_id=1, source_target_pairs={{0,1},{1,0},{2,3},{3,2},{4,5},{5,4},{6,7},{7,6},{8,9},{9,8},{10,11... | collective-permute-start | bytes 3145736 | tf_op jit(solution)/shard_map/ppermute | solution.py:559
